TPU v7x, 32 devices: a whole 2x2x4 slice. The times are simulated.
32 devices in a mesh: dp: 4 (over y, core), tensor: 8 (over z, x).
Axes of the slice: x: 2, y: 2, z: 4, core: 2. Of those that a mesh axis runs over, the one named last changes fastest.
Arguments:
- tokens: bfloat16 [1024, 8, 1024], P('tensor', 'dp'), may hold values from -6 to 6
- conditioning: bfloat16 [8, 1024], P('dp'), may hold values from -6 to 6
- cotangent: bfloat16 [1024, 8, 1024], P('tensor', 'dp'), may hold values from -6 to 6
- w_qkv: bfloat16 [1024, 16, 192], P('dp', 'tensor'), may hold values from -0.1875 to 0.1875
- b_qkv: bfloat16 [2, 1024], P(None, 'dp'), may hold values from -3 to 3
- w_proj: bfloat16 [1024, 1024], P('tensor', 'dp'), may hold values from -1.5 to 1.5
- b_proj: bfloat16 [1024], P('dp'), may hold values from -3 to 3
- w_fc1: bfloat16 [1024, 4096], P('dp', 'tensor'), may hold values from -0.1875 to 0.1875
- b_fc1: bfloat16 [4096], P('dp'), may hold values from -3 to 3
- w_fc2: bfloat16 [4096, 1024], P('tensor', 'dp'), may hold values from -0.09375 to 0.09375
- b_fc2: bfloat16 [1024], P('dp'), may hold values from -3 to 3
- w_ada: bfloat16 [1024, 6144], P('dp'), may hold values from -0.1875 to 0.1875
- b_ada: bfloat16 [6144], P('dp'), may hold values from -3 to 3
Outputs:
- output: bfloat16 [1024, 8, 1024], P('tensor', 'dp')
- d_tokens: float32 [1024, 8, 1024], P('tensor', 'dp')
- d_conditioning: float32 [8, 1024], P('dp')
- grad_w_qkv: float32 [1024, 16, 192], P('dp', 'tensor')
- grad_b_qkv: float32 [2, 1024], P(None, 'dp')
- grad_w_proj: float32 [1024, 1024], P('tensor', 'dp')
- grad_b_proj: float32 [1024], P('dp')
- grad_w_fc1: float32 [1024, 4096], P('dp', 'tensor')
- grad_b_fc1: float32 [4096], P('dp')
- grad_w_fc2: float32 [4096, 1024], P('tensor', 'dp')
- grad_b_fc2: float32 [1024], P('dp')
- grad_w_ada: float32 [1024, 6144], P('dp', 'tensor')
- grad_b_ada: float32 [6144], P('dp')
All inputs are finite; a program needn't handle non-finite values.
Results may differ from a plain program's by a relative error of at most 0.012.
The roundings to bfloat16 on the way count: a program that leaves them out, or rounds other values in their place, can miss the bound.
Values may be sent and summed in bfloat16 or wider, within the bound.
No kernel may reach another device: no remote copies, remote signals or barrier semaphores. Data moves between devices by JAX's collectives and lax.ppermute only.
A program may use at most 192 MiB of HBM per device.

v0:
```python
import jax
import jax.numpy as jnp
from jax import lax
from jax.sharding import PartitionSpec as P

D = 1024
HD = 64
FF = 4096
MICRO = 2


highest = lax.Precision.HIGHEST
norm_eps = 1e-06


def norm_rows(block_inputs):
    center = block_inputs - jnp.mean(block_inputs, axis=-1, keepdims=True)
    return center * lax.rsqrt(jnp.mean(center * center, axis=-1, keepdims=True) + norm_eps)


def pre_norm(block_inputs, shift_vec, scale_vec):
    return norm_rows(block_inputs) * (1.0 + scale_vec) + shift_vec


def gelu_tanh(hidden):
    return jax.nn.gelu(hidden, approximate=True)


def fetch_weights(w_qkv, b_qkv, w_proj, b_proj, w_fc1, b_fc1, w_fc2, b_fc2, w_ada, b_ada):
    gathered = (
        lax.all_gather(w_qkv, "dp", axis=0, tiled=True),
        lax.all_gather(b_qkv, "dp", axis=1, tiled=True),
        lax.all_gather(w_proj, "dp", axis=1, tiled=True),
        lax.all_gather(b_proj, "dp", axis=0, tiled=True),
        lax.all_gather(w_fc1, "dp", axis=0, tiled=True),
        lax.all_gather(b_fc1, "dp", axis=0, tiled=True),
        lax.all_gather(w_fc2, "dp", axis=1, tiled=True),
        lax.all_gather(b_fc2, "dp", axis=0, tiled=True),
        lax.all_gather(w_ada, "dp", axis=0, tiled=True),
        lax.all_gather(b_ada, "dp", axis=0, tiled=True),
    )
    return gathered


def local_biases(gathered, tensor_rank, head_cols, hidden_here):
    bias_qv = lax.dynamic_slice_in_dim(gathered[1], tensor_rank * head_cols, head_cols, 1).astype(
        jnp.float32
    )
    bias_fc1 = lax.dynamic_slice_in_dim(
        gathered[5], tensor_rank * hidden_here, hidden_here, 0
    ).astype(jnp.float32)
    return (bias_qv, bias_fc1)


def attn_forward(queries, key_heads, val_heads, factor):
    seq_len = queries.shape[0]
    block_rows = min(512, seq_len)
    blocks = queries.reshape((seq_len // block_rows, block_rows) + queries.shape[1:])

    def one_block(qblock):
        scores = (
            jnp.einsum("qshe,kshe->shqk", qblock, key_heads, preferred_element_type=jnp.float32)
            * factor
        )
        top_score = jnp.max(scores, axis=-1, keepdims=True)
        exps_shift = jnp.exp(scores - top_score)
        row_total = jnp.sum(exps_shift, axis=-1, keepdims=True)
        attn_probs = (exps_shift / row_total).astype(jnp.bfloat16)
        block_out = jnp.einsum(
            "shqk,kshe->qshe", attn_probs, val_heads, preferred_element_type=jnp.float32
        )
        return (block_out, (top_score + jnp.log(row_total))[..., 0])

    block_output_list, log_norm = lax.map(one_block, blocks)
    return (block_output_list.reshape(queries.shape), log_norm)


def attn_backward(queries, key_heads, val_heads, grad_heads, log_norm, factor):
    seq_len = queries.shape[0]
    block_rows = min(512, seq_len)
    shape_blocks = (seq_len // block_rows, block_rows) + queries.shape[1:]
    q_blocks = queries.reshape(shape_blocks)
    g_blocks = grad_heads.reshape(shape_blocks)

    def one_block(running, pieces):
        qblock, gblock, norm_block = pieces
        scores = (
            jnp.einsum("qshe,kshe->shqk", qblock, key_heads, preferred_element_type=jnp.float32)
            * factor
        )
        attn_probs = jnp.exp(scores - norm_block[..., None])
        dprobs = jnp.einsum(
            "qshe,kshe->shqk", gblock, val_heads, preferred_element_type=jnp.float32
        )
        row_delta = jnp.sum(attn_probs * dprobs, axis=-1, keepdims=True)
        dscores = (attn_probs * (dprobs - row_delta)).astype(jnp.bfloat16)
        dquery = (
            jnp.einsum("shqk,kshe->qshe", dscores, key_heads, preferred_element_type=jnp.float32)
            * factor
        ).astype(jnp.bfloat16)
        dkeys_acc = (
            running[0]
            + jnp.einsum("shqk,qshe->kshe", dscores, qblock, preferred_element_type=jnp.float32)
            * factor
        )
        dvals_acc = running[1] + jnp.einsum(
            "shqk,qshe->kshe",
            attn_probs.astype(jnp.bfloat16),
            gblock,
            preferred_element_type=jnp.float32,
        )
        return ((dkeys_acc, dvals_acc), dquery)

    zero_heads = jnp.zeros(key_heads.shape, jnp.float32)
    (dkeys_acc, dvals_acc), dquery = lax.scan(
        one_block, (zero_heads, zero_heads), (q_blocks, g_blocks, log_norm)
    )
    return (
        dquery.reshape(queries.shape),
        dkeys_acc.astype(jnp.bfloat16),
        dvals_acc.astype(jnp.bfloat16),
    )


def body(
    tokens,
    conditioning,
    cotangent,
    w_qkv,
    b_qkv,
    w_proj,
    b_proj,
    w_fc1,
    b_fc1,
    w_fc2,
    b_fc2,
    w_ada,
    b_ada,
):
    tensor_rank = lax.axis_index("tensor")
    samples = tokens.shape[1] // MICRO
    heads_here = w_qkv.shape[1]
    head_cols = heads_here * HD
    hidden_here = w_fc1.shape[1]
    factor = HD ** (-0.5)
    out_parts, dinput_parts, dmod_parts = ([], [], [])
    grad_qkv = grad_proj = grad_fc1 = grad_fc2 = 0.0
    grad_bq = grad_bv = grad_bproj = grad_bfc1 = grad_bfc2 = 0.0
    for micro_index in range(MICRO):
        first_sample = micro_index * samples
        current = fetch_weights(
            w_qkv, b_qkv, w_proj, b_proj, w_fc1, b_fc1, w_fc2, b_fc2, w_ada, b_ada
        )
        full_qkv, full_proj, full_fc1, full_fc2 = (current[0], current[2], current[4], current[6])
        full_bproj = current[3].astype(jnp.float32)
        full_bfc2 = current[7].astype(jnp.float32)
        full_ada = current[8]
        bias_qv, bias_fc1 = local_biases(current, tensor_rank, head_cols, hidden_here)
        block_inputs = tokens[:, first_sample : first_sample + samples].astype(jnp.float32)
        cond_now = conditioning[first_sample : first_sample + samples].astype(jnp.float32)
        act_cond = jax.nn.silu(cond_now).astype(jnp.bfloat16)
        modulation = (
            jnp.dot(act_cond, full_ada, preferred_element_type=jnp.float32)
            + current[9].astype(jnp.float32)
        ).reshape(samples, 6, D)
        normed, norm_pull = jax.vjp(pre_norm, block_inputs, modulation[:, 0], modulation[:, 1])
        normed_low = normed.astype(jnp.bfloat16)
        gathered_in = lax.all_gather(normed_low, "tensor", axis=0, tiled=True)
        packed = jnp.einsum(
            "rsd,dhe->rshe", gathered_in, full_qkv, preferred_element_type=jnp.float32
        )
        queries = (packed[..., :HD] + bias_qv[0].reshape(heads_here, HD)).astype(jnp.bfloat16)
        key_heads = packed[..., HD : 2 * HD].astype(jnp.bfloat16)
        val_heads = (packed[..., 2 * HD :] + bias_qv[1].reshape(heads_here, HD)).astype(
            jnp.bfloat16
        )
        attn_out, log_norm = attn_forward(queries, key_heads, val_heads, factor)
        seq_len = attn_out.shape[0]
        mixed_low = attn_out.reshape(seq_len, samples, head_cols).astype(jnp.bfloat16)
        branch = (
            lax.psum_scatter(
                jnp.einsum("rsc,cd->rsd", mixed_low, full_proj, preferred_element_type=jnp.float32),
                "tensor",
                scatter_dimension=0,
                tiled=True,
            )
            + full_bproj
        )
        middle = block_inputs + modulation[:, 2] * branch
        normed_mlp, mlp_pull = jax.vjp(pre_norm, middle, modulation[:, 3], modulation[:, 4])
        mlp_low = normed_mlp.astype(jnp.bfloat16)
        gathered_mlp = lax.all_gather(mlp_low, "tensor", axis=0, tiled=True)
        hidden = (
            jnp.einsum("rsd,df->rsf", gathered_mlp, full_fc1, preferred_element_type=jnp.float32)
            + bias_fc1
        )
        activated, gelu_pull = jax.vjp(gelu_tanh, hidden)
        act_low = activated.astype(jnp.bfloat16)
        branch_mlp = (
            lax.psum_scatter(
                jnp.einsum("rsf,fd->rsd", act_low, full_fc2, preferred_element_type=jnp.float32),
                "tensor",
                scatter_dimension=0,
                tiled=True,
            )
            + full_bfc2
        )
        out_parts.append((middle + modulation[:, 5] * branch_mlp).astype(jnp.bfloat16))
        current = fetch_weights(
            w_qkv, b_qkv, w_proj, b_proj, w_fc1, b_fc1, w_fc2, b_fc2, w_ada, b_ada
        )
        full_qkv, full_proj, full_fc1, full_fc2 = (current[0], current[2], current[4], current[6])
        full_ada = current[8]
        grad_top = cotangent[:, first_sample : first_sample + samples].astype(jnp.float32)
        dgate_mlp = jnp.sum(grad_top * branch_mlp, axis=0)
        dbranch_mlp = (modulation[:, 5] * grad_top).astype(jnp.bfloat16)
        grad_bfc2 = grad_bfc2 + jnp.sum(dbranch_mlp, axis=(0, 1), dtype=jnp.float32)
        gathered_dmlp = lax.all_gather(dbranch_mlp, "tensor", axis=0, tiled=True)
        grad_fc2 = grad_fc2 + jnp.einsum(
            "rsf,rsd->fd", act_low, gathered_dmlp, preferred_element_type=jnp.float32
        )
        dactiv = jnp.einsum(
            "rsd,fd->rsf", gathered_dmlp, full_fc2, preferred_element_type=jnp.float32
        )
        dhidden = gelu_pull(dactiv)[0].astype(jnp.bfloat16)
        grad_bfc1 = grad_bfc1 + jnp.sum(dhidden, axis=(0, 1), dtype=jnp.float32)
        grad_fc1 = grad_fc1 + jnp.einsum(
            "rsd,rsf->df", gathered_mlp, dhidden, preferred_element_type=jnp.float32
        )
        mlp_normed_gradient = lax.psum_scatter(
            jnp.einsum("rsf,df->rsd", dhidden, full_fc1, preferred_element_type=jnp.float32),
            "tensor",
            scatter_dimension=0,
            tiled=True,
        )
        dmiddle_part, dshift_mlp, dscale_mlp = mlp_pull(mlp_normed_gradient)
        dmiddle = grad_top + dmiddle_part
        dgate_attn = jnp.sum(dmiddle * branch, axis=0)
        dbranch = (modulation[:, 2] * dmiddle).astype(jnp.bfloat16)
        grad_bproj = grad_bproj + jnp.sum(dbranch, axis=(0, 1), dtype=jnp.float32)
        gathered_dattn = lax.all_gather(dbranch, "tensor", axis=0, tiled=True)
        grad_proj = grad_proj + jnp.einsum(
            "rsc,rsd->cd", mixed_low, gathered_dattn, preferred_element_type=jnp.float32
        )
        dmixed = jnp.einsum(
            "rsd,cd->rsc", gathered_dattn, full_proj, preferred_element_type=jnp.float32
        ).astype(jnp.bfloat16)
        dmixed = dmixed.reshape(seq_len, samples, heads_here, HD)
        dquery, dkey_heads, dval_heads = attn_backward(
            queries, key_heads, val_heads, dmixed, log_norm, factor
        )
        grad_bq = grad_bq + jnp.sum(dquery, axis=(0, 1), dtype=jnp.float32)
        grad_bv = grad_bv + jnp.sum(dval_heads, axis=(0, 1), dtype=jnp.float32)
        dpacked = jnp.concatenate([dquery, dkey_heads, dval_heads], axis=-1)
        grad_qkv = grad_qkv + jnp.einsum(
            "rsd,rshe->dhe", gathered_in, dpacked, preferred_element_type=jnp.float32
        )
        dnormed = lax.psum_scatter(
            jnp.einsum("rshe,dhe->rsd", dpacked, full_qkv, preferred_element_type=jnp.float32),
            "tensor",
            scatter_dimension=0,
            tiled=True,
        )
        dinputs_part, dshift_attn, dscale_attn = norm_pull(dnormed)
        dinput_parts.append(dmiddle + dinputs_part)
        dmod_parts.append(
            jnp.stack(
                [dshift_attn, dscale_attn, dgate_attn, dshift_mlp, dscale_mlp, dgate_mlp], axis=1
            ).reshape(samples, 6 * D)
        )
    dmod_local = jnp.concatenate(dmod_parts, axis=0)
    bias_grads = jnp.stack([grad_bq.reshape(head_cols), grad_bv.reshape(head_cols)])
    pad_bqkv = lax.dynamic_update_slice_in_dim(
        jnp.zeros((2, D), jnp.float32), bias_grads, tensor_rank * head_cols, 1
    )
    pad_bfc1 = lax.dynamic_update_slice_in_dim(
        jnp.zeros((FF,), jnp.float32), grad_bfc1, tensor_rank * hidden_here, 0
    )
    dmod_all, sum_bqkv, sum_bproj, sum_bfc1, sum_bfc2 = lax.psum(
        (dmod_local, pad_bqkv, grad_bproj, pad_bfc1, grad_bfc2), "tensor"
    )
    cond_all = conditioning.astype(jnp.float32)
    silu_value, silu_pull = jax.vjp(jax.nn.silu, cond_all)
    act_all = silu_value.astype(jnp.bfloat16).astype(jnp.float32)
    dcond_act = jnp.dot(dmod_all, full_ada.astype(jnp.float32).T, precision=highest)
    d_conditioning = silu_pull(dcond_act)[0]
    ada_cols = full_ada.shape[1] // lax.axis_size("tensor")
    ada_slice = lax.dynamic_slice_in_dim(dmod_all, tensor_rank * ada_cols, ada_cols, 1)
    grad_ada = jnp.dot(act_all.T, ada_slice, precision=highest)
    grad_bada = jnp.sum(dmod_all, axis=0)
    (
        out_qkv,
        out_bqkv,
        out_proj,
        out_bproj,
        out_fc1,
        out_bfc1,
        out_fc2,
        out_bfc2,
        out_ada,
        out_bada,
    ) = (
        lax.psum_scatter(grad_qkv, "dp", scatter_dimension=0, tiled=True),
        lax.psum_scatter(sum_bqkv, "dp", scatter_dimension=1, tiled=True),
        lax.psum_scatter(grad_proj, "dp", scatter_dimension=1, tiled=True),
        lax.psum_scatter(sum_bproj, "dp", scatter_dimension=0, tiled=True),
        lax.psum_scatter(grad_fc1, "dp", scatter_dimension=0, tiled=True),
        lax.psum_scatter(sum_bfc1, "dp", scatter_dimension=0, tiled=True),
        lax.psum_scatter(grad_fc2, "dp", scatter_dimension=1, tiled=True),
        lax.psum_scatter(sum_bfc2, "dp", scatter_dimension=0, tiled=True),
        lax.psum_scatter(grad_ada, "dp", scatter_dimension=0, tiled=True),
        lax.psum_scatter(grad_bada, "dp", scatter_dimension=0, tiled=True),
    )
    return (
        jnp.concatenate(out_parts, axis=1),
        jnp.concatenate(dinput_parts, axis=1),
        d_conditioning,
        out_qkv,
        out_bqkv,
        out_proj,
        out_bproj,
        out_fc1,
        out_bfc1,
        out_fc2,
        out_bfc2,
        out_ada,
        out_bada,
    )


def solution(mesh):
    placed = (
        P("tensor", "dp", None),
        P("dp", None),
        P("tensor", "dp", None),
        P("dp", "tensor", None),
        P(None, "dp"),
        P("tensor", "dp"),
        P("dp"),
        P("dp", "tensor"),
        P("dp"),
        P("tensor", "dp"),
        P("dp"),
        P("dp", None),
        P("dp"),
    )
    return jax.shard_map(
        body,
        mesh=mesh,
        in_specs=placed,
        out_specs=(
            P("tensor", "dp", None),
            P("tensor", "dp", None),
            P("dp", None),
            P("dp", "tensor", None),
            P(None, "dp"),
            P("tensor", "dp"),
            P("dp"),
            P("dp", "tensor"),
            P("dp"),
            P("tensor", "dp"),
            P("dp"),
            P("dp", "tensor"),
            P("dp"),
        ),
        check_vma=False,
    )
```

profile of v0, /device:TPU:0, one launch (start us, length us, event | category | flops | bytes accessed | tf_op | source)
XLA Modules:
  0.0 1503.5 jit_solution(6698034637584246862)
XLA Ops:
  8.0 6.3 all-gather
  15.5 78.9 %all-gather.15.cloned.1.call-done = bf16[1024,6144]{1,0:T(8,128)(2,1)} async-done(((bf16[256,6144]{1,0:T(8,128)(2,1)}), bf16[1024,6144]{1,0:T(8,128)(2,1)}) %all-gather.15.cloned.1.call-update) | async-done | bytes 12582928 | tf_op jit(solution)/shard_map/all_gather | solution.py:39
  94.4 6.5 fusion.198
  119.1 9.3 all_gather.76
  128.4 26.2 %all-gather.25.cloned.1.call-done = bf16[1024,1,1024]{2,0,1:T(8,128)(2,1)} async-done(((bf16[128,1,1024]{2,0,1:T(8,128)(2,1)}), bf16[1024,1,1024]{2,0,1:T(8,128)(2,1)}) %all-gather.25.cloned.1.call-update) | async-done | bytes 2097168 | tf_op jit(solution)/shard_map/all_gather | solution.py:168
  157.4 47.5 %all-gather.17.cloned.1.call-done = bf16[1024,1,1024]{2,0,1:T(8,128)(2,1)} async-done(((bf16[128,1,1024]{2,0,1:T(8,128)(2,1)}), bf16[1024,1,1024]{2,0,1:T(8,128)(2,1)}) %all-gather.17.cloned.1.call-update) | async-done | bytes 2097168 | tf_op jit(solution)/shard_map/all_gather | solution.py:168
  219.9 5.9 while.54
  234.6 71.1 %reduce-scatter.21.cloned.1.call-done = f32[128,1,1024]{2,0,1:T(8,128)} async-done(((f32[1024,1,1024]{2,0,1:T(8,128)}), f32[128,1,1024]{2,0,1:T(8,128)}) %reduce-scatter.21.cloned.1.call-update) | async-done | bytes 524304 | tf_op jit(solution)/shard_map/reduce_scatter | solution.py:181
  305.7 91.5 %reduce-scatter.17.cloned.1.call-done = f32[128,1,1024]{2,0,1:T(8,128)} async-done(((f32[1024,1,1024]{2,0,1:T(8,128)}), f32[128,1,1024]{2,0,1:T(8,128)}) %reduce-scatter.17.cloned.1.call-update) | async-done | bytes 524304 | tf_op jit(solution)/shard_map/reduce_scatter | solution.py:181
  407.5 7.5 all-gather.21.cloned.1.call-done
  415.0 51.8 %all-gather.27.cloned.1.call-done = bf16[1024,1,1024]{2,0,1:T(8,128)(2,1)} async-done(((bf16[128,1,1024]{2,0,1:T(8,128)(2,1)}), bf16[1024,1,1024]{2,0,1:T(8,128)(2,1)}) %all-gather.27.cloned.1.call-update) | async-done | bytes 2097168 | tf_op jit(solution)/shard_map/all_gather | solution.py:192
  471.2 12.5 all-gather.23.cloned.1.call-done
  489.1 46.5 %all-gather.19.cloned.1.call-done = bf16[1024,1,1024]{2,0,1:T(8,128)(2,1)} async-done(((bf16[128,1,1024]{2,0,1:T(8,128)(2,1)}), bf16[1024,1,1024]{2,0,1:T(8,128)(2,1)}) %all-gather.19.cloned.1.call-update) | async-done | bytes 2097168 | tf_op jit(solution)/shard_map/all_gather | solution.py:192
  552.1 73.8 %reduce-scatter.23.cloned.1.call-done = f32[128,1,1024]{2,0,1:T(8,128)} async-done(((f32[1024,1,1024]{2,0,1:T(8,128)}), f32[128,1,1024]{2,0,1:T(8,128)}) %reduce-scatter.23.cloned.1.call-update) | async-done | bytes 524304 | tf_op jit(solution)/shard_map/reduce_scatter | solution.py:200
  625.9 91.6 %reduce-scatter.19.cloned.1.call-done = f32[128,1,1024]{2,0,1:T(8,128)} async-done(((f32[1024,1,1024]{2,0,1:T(8,128)}), f32[128,1,1024]{2,0,1:T(8,128)}) %reduce-scatter.19.cloned.1.call-update) | async-done | bytes 524304 | tf_op jit(solution)/shard_map/reduce_scatter | solution.py:200
  721.7 48.1 %all-gather.33.cloned.1.call-done = bf16[1024,1,1024]{2,0,1:T(8,128)(2,1)} async-done(((bf16[128,1,1024]{2,0,1:T(8,128)(2,1)}), bf16[1024,1,1024]{2,0,1:T(8,128)(2,1)}) %all-gather.33.cloned.1.call-update) | async-done | bytes 2097168 | tf_op jit(solution)/shard_map/all_gather | solution.py:218
  779.2 40.9 %all-gather.29.cloned.1.call-done = bf16[1024,1,1024]{2,0,1:T(8,128)(2,1)} async-done(((bf16[128,1,1024]{2,0,1:T(8,128)(2,1)}), bf16[1024,1,1024]{2,0,1:T(8,128)(2,1)}) %all-gather.29.cloned.1.call-update) | async-done | bytes 2097168 | tf_op jit(solution)/shard_map/all_gather | solution.py:218
  829.6 81.0 %reduce-scatter.29.cloned.1.call-done = f32[128,1,1024]{2,0,1:T(8,128)} async-done(((f32[1024,1,1024]{2,0,1:T(8,128)}), f32[128,1,1024]{2,0,1:T(8,128)}) %reduce-scatter.29.cloned.1.call-update) | async-done | bytes 524304 | tf_op jit(solution)/shard_map/reduce_scatter | solution.py:230
  914.4 87.5 %reduce-scatter.25.cloned.1.call-done = f32[128,1,1024]{2,0,1:T(8,128)} async-done(((f32[1024,1,1024]{2,0,1:T(8,128)}), f32[128,1,1024]{2,0,1:T(8,128)}) %reduce-scatter.25.cloned.1.call-update) | async-done | bytes 524304 | tf_op jit(solution)/shard_map/reduce_scatter | solution.py:230
  1006.0 46.7 %all-gather.35.cloned.1.call-done = bf16[1024,1,1024]{2,0,1:T(8,128)(2,1)} async-done(((bf16[128,1,1024]{2,0,1:T(8,128)(2,1)}), bf16[1024,1,1024]{2,0,1:T(8,128)(2,1)}) %all-gather.35.cloned.1.call-update) | async-done | bytes 2097168 | tf_op jit(solution)/shard_map/all_gather | solution.py:241
  1056.4 18.9 %while.57 = (s32[]{:T(128)}, f32[1024,1,2,64]{0,3,2,1:T(8,128)}, f32[1024,1,2,64]{0,3,2,1:T(8,128)}, bf16[2,512,1,2,64]{1,4,3,2,0:T(8,128)(2,1)}, bf16[2,512,1,2...) while((s32[]{:T(128)}, f32[1024,1,2,64]{0,3,2,1:T(8,128)}, ...), condition=%wide.region_34.35_spmd.clone, body=%wide.region_32.34_spmd.clone.sunk | while | flops 684456960 | bytes 72773944 | solution.py:115
  1077.0 25.9 %all-gather.31.cloned.1.call-done = bf16[1024,1,1024]{2,0,1:T(8,128)(2,1)} async-done(((bf16[128,1,1024]{2,0,1:T(8,128)(2,1)}), bf16[1024,1,1024]{2,0,1:T(8,128)(2,1)}) %all-gather.31.cloned.1.call-update) | async-done | bytes 2097168 | tf_op jit(solution)/shard_map/all_gather | solution.py:241
  1106.6 16.4 %while.56 = (s32[]{:T(128)}, f32[1024,1,2,64]{0,3,2,1:T(8,128)}, f32[1024,1,2,64]{0,3,2,1:T(8,128)S(1)}, bf16[2,512,1,2,64]{1,4,3,2,0:T(8,128)(2,1)}, bf16[2,512...) while((s32[]{:T(128)}, f32[1024,1,2,64]{0,3,2,1:T(8,128)}, ...), condition=%wide.region_25.26_spmd.clone, body=%wide.region_23.25_spmd.clone.sunk | while | flops 684456960 | bytes 71725344 | solution.py:115
  1162.5 11.0 all-reduce.5
  1174.7 65.5 %reduce-scatter.27.cloned.1.call-done = f32[128,1,1024]{2,0,1:T(8,128)} async-done(((f32[1024,1,1024]{2,0,1:T(8,128)}), f32[128,1,1024]{2,0,1:T(8,128)}) %reduce-scatter.27.cloned.1.call-update) | async-done | bytes 524304 | tf_op jit(solution)/shard_map/reduce_scatter | solution.py:258
  1241.6 90.2 %reduce-scatter.31.cloned.1.call-done = f32[128,1,1024]{2,0,1:T(8,128)} async-done(((f32[1024,1,1024]{2,0,1:T(8,128)}), f32[128,1,1024]{2,0,1:T(8,128)}) %reduce-scatter.31.cloned.1.call-update) | async-done | bytes 524304 | tf_op jit(solution)/shard_map/reduce_scatter | solution.py:258
  1336.8 36.6 %all-reduce.4 = (f32[2,6144]{1,0:T(2,128)S(1)}, f32[2,256]{1,0:T(2,128)}, f32[256]{0:T(256)}, f32[1024]{0:T(1024)}, f32[256]{0:T(256)}) all-reduce(f32[2,6144]{1,0:T(2,128)S(1)} %pad_maximum_fusion.4, f32[2,256]{1,0:T(2,128)S(1)} %copy.81, f32[256]{0:T(256)S(1)} %dynamic-slice.1, ...), channel_id=1, replica_groups=mesh['dp'=4,'tensor'=8] {'tensor'}, use_global_device_ids=true, to_apply=%region_50.51 | all-reduce | flops 14336 | bytes 114688 | tf_op jit(solution)/shard_map/psum | solution.py:279
  1380.9 11.2 all-reduce.3
  1392.7 13.4 fusion.191
  1406.1 18.7 %reduce-scatter.35.cloned.1.call-done = f32[128,256]{1,0:T(8,128)} async-done(((f32[128,1024]{1,0:T(8,128)}), f32[128,256]{1,0:T(8,128)}) %reduce-scatter.35.cloned.1.call-update) | async-done | bytes 131088 | tf_op jit(solution)/shard_map/reduce_scatter | solution.py:305
  1424.8 31.0 %reduce-scatter.33.cloned.1.call-done = f32[256,2,192]{0,2,1:T(8,128)} async-done(((f32[1024,2,192]{0,2,1:T(8,128)}), f32[256,2,192]{0,2,1:T(8,128)}) %reduce-scatter.33.cloned.1.call-update) | async-done | bytes 393232 | tf_op jit(solution)/shard_map/reduce_scatter | solution.py:303
  1455.7 41.0 %reduce-scatter.41.cloned.1.call-done = f32[256,768]{1,0:T(8,128)} async-done(((f32[1024,768]{1,0:T(8,128)}), f32[256,768]{1,0:T(8,128)}) %reduce-scatter.41.cloned.1.call-update) | async-done | bytes 786448 | tf_op jit(solution)/shard_map/reduce_scatter | solution.py:311
  (460 shorter events, 221.9 us)
Async XLA Ops:
  7.2 87.2 %all-gather.15.cloned.1.call-start = ((), (), s32[]{:S(2)}) async-start(), calls=%async_computation.14 | async-start | bytes 15728640 | tf_op jit(solution)/shard_map/all_gather | solution.py:39
  7.9 146.7 %all-gather.25.cloned.1.call-start = ((), (), s32[]{:S(2)}) async-start(), calls=%async_computation.21 | async-start | bytes 2359296 | tf_op jit(solution)/shard_map/all_gather | solution.py:168
  15.2 382.0 %copy-start.7 = (bf16[128,1,1024]{2,0,1:T(8,128)(2,1)}, bf16[128,1,1024]{2,0,1:T(8,128)(2,1)S(1)}, u32[]{:S(2)}) copy-start(bf16[128,1,1024]{2,0,1:T(8,128)(2,1)S(1)} %get-tuple-element.487) | copy-start | bytes 786436
  105.4 99.6 %all-gather.17.cloned.1.call-start = ((), (), s32[]{:S(2)}) async-start(), calls=%async_computation.15 | async-start | bytes 2359296 | tf_op jit(solution)/shard_map/all_gather | solution.py:168
  105.6 291.6 %copy-start.9 = (bf16[128,1,1024]{2,0,1:T(8,128)(2,1)}, bf16[128,1,1024]{2,0,1:T(8,128)(2,1)S(1)}, u32[]{:S(2)}) copy-start(bf16[128,1,1024]{2,0,1:T(8,128)(2,1)S(1)} %get-tuple-element.483) | copy-start | bytes 786436
  108.0 197.8 %reduce-scatter.21.cloned.1.call-start = ((), (), s32[]{:S(2)}) async-start(), calls=%async_computation.22 | async-start | bytes 4718592 | tf_op jit(solution)/shard_map/reduce_scatter | solution.py:181
  119.1 933.6 %copy-start.18 = (bf16[128,1024]{1,0:T(8,128)(2,1)}, bf16[128,1024]{1,0:T(8,128)(2,1)S(1)}, u32[]{:S(2)}) copy-start(bf16[128,1024]{1,0:T(8,128)(2,1)S(1)} %all_gather.78) | copy-start | bytes 786436
  218.7 178.5 %reduce-scatter.17.cloned.1.call-start = ((), (), s32[]{:S(2)}) async-start(), calls=%async_computation.16 | async-start | bytes 4718592 | tf_op jit(solution)/shard_map/reduce_scatter | solution.py:181
  228.9 186.1 %all-gather.21.cloned.1.call-start = ((), (), s32[]{:S(2)}) async-start(), calls=%async_computation.18 | async-start | bytes 1310720 | tf_op jit(solution)/shard_map/all_gather | solution.py:35
  229.5 237.3 %all-gather.27.cloned.1.call-start = ((), (), s32[]{:S(2)}) async-start(), calls=%async_computation.23 | async-start | bytes 2359296 | tf_op jit(solution)/shard_map/all_gather | solution.py:192
  399.8 83.9 %all-gather.23.cloned.1.call-start = ((), (), s32[]{:S(2)}) async-start(), calls=%async_computation.19 | async-start | bytes 1310720 | tf_op jit(solution)/shard_map/all_gather | solution.py:37
  400.6 135.0 %all-gather.19.cloned.1.call-start = ((), (), s32[]{:S(2)}) async-start(), calls=%async_computation.17 | async-start | bytes 2359296 | tf_op jit(solution)/shard_map/all_gather | solution.py:192
  401.8 224.2 %reduce-scatter.23.cloned.1.call-start = ((), (), s32[]{:S(2)}) async-start(), calls=%async_computation.24 | async-start | bytes 4718592 | tf_op jit(solution)/shard_map/reduce_scatter | solution.py:200
  489.1 228.5 %reduce-scatter.19.cloned.1.call-start = ((), (), s32[]{:S(2)}) async-start(), calls=%async_computation.20 | async-start | bytes 4718592 | tf_op jit(solution)/shard_map/reduce_scatter | solution.py:200
  543.5 226.3 %all-gather.33.cloned.1.call-start = ((), (), s32[]{:S(2)}) async-start(), calls=%async_computation.29 | async-start | bytes 2359296 | tf_op jit(solution)/shard_map/all_gather | solution.py:218
  720.9 99.2 %all-gather.29.cloned.1.call-start = ((), (), s32[]{:S(2)}) async-start(), calls=%async_computation.25 | async-start | bytes 2359296 | tf_op jit(solution)/shard_map/all_gather | solution.py:218
  721.7 188.9 %reduce-scatter.29.cloned.1.call-start = ((), (), s32[]{:S(2)}) async-start(), calls=%async_computation.30 | async-start | bytes 4718592 | tf_op jit(solution)/shard_map/reduce_scatter | solution.py:230
  779.2 222.8 %reduce-scatter.25.cloned.1.call-start = ((), (), s32[]{:S(2)}) async-start(), calls=%async_computation.26 | async-start | bytes 4718592 | tf_op jit(solution)/shard_map/reduce_scatter | solution.py:230
  829.5 223.2 %all-gather.35.cloned.1.call-start = ((), (), s32[]{:S(2)}) async-start(), calls=%async_computation.31 | async-start | bytes 2359296 | tf_op jit(solution)/shard_map/all_gather | solution.py:241
  914.4 188.5 %all-gather.31.cloned.1.call-start = ((), (), s32[]{:S(2)}) async-start(), calls=%async_computation.27 | async-start | bytes 2359296 | tf_op jit(solution)/shard_map/all_gather | solution.py:241
  1005.7 168.0 %reduce-scatter.43.cloned.1.call-start = ((), (), s32[]{:S(2)}) async-start(), calls=%async_computation.38 | async-start | bytes 655360
  1127.9 112.3 %reduce-scatter.27.cloned.1.call-start = ((), (), s32[]{:S(2)}) async-start(), calls=%async_computation.28 | async-start | bytes 4718592 | tf_op jit(solution)/shard_map/reduce_scatter | solution.py:258
  1131.2 200.5 %reduce-scatter.31.cloned.1.call-start = ((), (), s32[]{:S(2)}) async-start(), calls=%async_computation.32 | async-start | bytes 4718592 | tf_op jit(solution)/shard_map/reduce_scatter | solution.py:258
  1135.7 270.4 %reduce-scatter.39.cloned.1.call-start = ((), (), s32[]{:S(2)}) async-start(), calls=%async_computation.36 | async-start | bytes 2621440 | tf_op jit(solution)/shard_map/reduce_scatter | solution.py:309
  1143.2 263.0 %reduce-scatter.37.cloned.1.call-start = ((), (), s32[]{:S(2)}) async-start(), calls=%async_computation.35 | async-start | bytes 2621440 | tf_op jit(solution)/shard_map/reduce_scatter | solution.py:307
  1150.1 274.7 %reduce-scatter.35.cloned.1.call-start = ((), (), s32[]{:S(2)}) async-start(), calls=%async_computation.34 | async-start | bytes 655360 | tf_op jit(solution)/shard_map/reduce_scatter | solution.py:305
  1154.5 301.2 %reduce-scatter.33.cloned.1.call-start = ((), (), s32[]{:S(2)}) async-start(), calls=%async_computation.33 | async-start | bytes 1966080 | tf_op jit(solution)/shard_map/reduce_scatter | solution.py:303
  1160.3 174.6 %copy-start.31 = (f32[128,1,1024]{2,0,1:T(8,128)S(1)}, f32[128,1,1024]{2,0,1:T(8,128)}, u32[]{:S(2)}) copy-start(f32[128,1,1024]{2,0,1:T(8,128)} %reduce-scatter.21.cloned.1.call-done) | copy-start | bytes 1572868
  1160.3 174.6 %copy-start.32 = (f32[128,1,1024]{2,0,1:T(8,128)S(1)}, f32[128,1,1024]{2,0,1:T(8,128)}, u32[]{:S(2)}) copy-start(f32[128,1,1024]{2,0,1:T(8,128)} %reduce-scatter.17.cloned.1.call-done) | copy-start | bytes 1572868
  1160.3 174.6 %copy-start.34 = (f32[128,1,1024]{2,0,1:T(8,128)S(1)}, f32[128,1,1024]{2,0,1:T(8,128)}, u32[]{:S(2)}) copy-start(f32[128,1,1024]{2,0,1:T(8,128)} %get-tuple-element.468) | copy-start | bytes 1572868
  1160.3 174.6 %copy-start.35 = (f32[128,1,1024]{2,0,1:T(8,128)S(1)}, f32[128,1,1024]{2,0,1:T(8,128)}, u32[]{:S(2)}) copy-start(f32[128,1,1024]{2,0,1:T(8,128)} %get-tuple-element.471) | copy-start | bytes 1572868
  1160.4 336.4 %reduce-scatter.41.cloned.1.call-start = ((), (), s32[]{:S(2)}) async-start(), calls=%async_computation.37 | async-start | bytes 3932160 | tf_op jit(solution)/shard_map/reduce_scatter | solution.py:311
  (100 other events, 2601.8 us)
Sparse Core Ops, SparseCore 0:
  9.6 84.7 all-gather.14
  105.5 49.0 all-gather.24
  157.3 47.6 all-gather.16
  218.9 86.8 reduce-scatter.20
  309.2 87.9 reduce-scatter.16
  398.7 16.3 all-gather.20
  417.7 49.0 all-gather.26
  468.4 15.3 all-gather.22
  486.5 49.0 all-gather.18
  539.1 86.8 reduce-scatter.22
  629.6 87.8 reduce-scatter.18
  721.0 48.7 all-gather.32
  772.5 47.6 all-gather.28
  823.6 86.8 reduce-scatter.28
  914.0 87.9 reduce-scatter.24
  1004.0 48.6 all-gather.34
  1055.2 47.6 all-gather.30
  1128.0 20.1 reduce-scatter.42
  1151.9 88.2 reduce-scatter.26
  1243.7 87.9 reduce-scatter.30
  1334.8 30.8 reduce-scatter.38
  1368.8 31.4 reduce-scatter.36
  1403.3 21.3 reduce-scatter.34
  1427.7 27.9 reduce-scatter.32
  1458.8 37.8 reduce-scatter.40
where the time goes:
time: 1510 us; the launch traced here: 1500 us
  waiting for transfers between devices  1180 us (78%)
  matrix products  128 us (8%)
  blocking collectives  101 us (7%)
  other arithmetic  39.8 us (3%)
  local copies, waits for them, and re-layouts  36.6 us (2%)
  between operations  17.6 us (1%)
    reduce_scatter x2, waiting for transfers between devices, body(): lax.psum_scatter(jnp.einsum('rsf,df->rsd', dhidden, full_fc1, preferred_e...  168 us
    reduce_scatter x2, waiting for transfers between devices, body(): lax.psum_scatter(jnp.einsum('rsf,fd->rsd', act_low, full_fc2, preferred_e...  165 us
    reduce_scatter x2, waiting for transfers between devices, body(): lax.psum_scatter(jnp.einsum('rsc,cd->rsd', mixed_low, full_proj, preferre...  163 us
    reduce_scatter x2, waiting for transfers between devices, body(): lax.psum_scatter(jnp.einsum('rshe,dhe->rsd', dpacked, full_qkv, preferred...  156 us
    all_gather x2, waiting for transfers between devices, body(): gathered_mlp = lax.all_gather(mlp_low, 'tensor', axis=0, tiled=True)  98.3 us
    all_gather x2, waiting for transfers between devices, body(): gathered_dmlp = lax.all_gather(dbranch_mlp, 'tensor', axis=0, tiled=True)  89 us
    all_gather x1, waiting for transfers between devices, fetch_weights(): lax.all_gather(w_ada, 'dp', axis=0, tiled=True)  78.9 us
    all_gather x2, waiting for transfers between devices, body(): gathered_in = lax.all_gather(normed_low, 'tensor', axis=0, tiled=True)  73.7 us
  transfers between devices with their start and end apart: 25, of which 22 were waited for; matrix products, arithmetic and copies ran while one was open for 9% of the time, Pallas kernels for 0%

commit v1 on v0

v1 whole, which is shorter than its diff:
```python
import jax
import jax.numpy as jnp
from jax import lax
from jax.sharding import Mesh, PartitionSpec as P

HD = 64
NZ = 4
NC = 2
norm_eps = 1e-06
f32 = jnp.float32
bf16 = jnp.bfloat16


def flip_bits(array, axis, count, index):
    bit = 1
    while bit < count:
        shape = array.shape
        view = array.reshape(
            shape[:axis] + (count // (2 * bit), 2, bit) + shape[axis + 1 :]
        )
        swapped = jnp.flip(view, axis=axis + 1)
        on = ((index // bit) % 2) == 1
        array = jnp.where(on, swapped, view).reshape(shape)
        bit *= 2
    return array


def swap_with(array, axis_name, count, offset):
    return lax.ppermute(array, axis_name, [(i, i ^ offset) for i in range(count)])


def layer_stats(rows):
    center = rows - jnp.mean(rows, axis=-1, keepdims=True)
    scale = lax.rsqrt(jnp.mean(center * center, axis=-1, keepdims=True) + norm_eps)
    return center * scale, scale


def layer_back(grad, unit, scale):
    return scale * (
        grad
        - jnp.mean(grad, axis=-1, keepdims=True)
        - unit * jnp.mean(grad * unit, axis=-1, keepdims=True)
    )


def split_three(values):
    high = lax.reduce_precision(values, 8, 7)
    rest = values - high
    middle = lax.reduce_precision(rest, 8, 7)
    return [part.astype(bf16) for part in (high, middle, rest - middle)]


def dot(a, b, dims):
    return lax.dot_general(a, b, (dims, ((), ())), preferred_element_type=f32)


def attn_forward(queries, keys, values, factor):
    samples, rows, width = queries.shape
    heads = width // HD
    qh = queries.reshape(samples, rows, heads, HD)
    kh = keys.reshape(samples, keys.shape[1], heads, HD)
    vh = values.reshape(samples, keys.shape[1], heads, HD)
    scores = jnp.einsum("sqhe,skhe->shqk", qh, kh, preferred_element_type=f32) * factor
    top = jnp.max(scores, axis=-1, keepdims=True)
    exps = jnp.exp(scores - top)
    total = jnp.sum(exps, axis=-1, keepdims=True)
    probs = (exps / total).astype(bf16)
    mixed = jnp.einsum("shqk,skhe->sqhe", probs, vh, preferred_element_type=f32)
    return mixed.reshape(queries.shape).astype(bf16), (top + jnp.log(total))


def attn_backward(queries, keys, values, grads, log_norm, factor):
    samples, rows, width = queries.shape
    heads = width // HD
    qh = queries.reshape(samples, rows, heads, HD)
    gh = grads.reshape(samples, rows, heads, HD)
    kh = keys.reshape(samples, keys.shape[1], heads, HD)
    vh = values.reshape(samples, keys.shape[1], heads, HD)
    scores = jnp.einsum("sqhe,skhe->shqk", qh, kh, preferred_element_type=f32) * factor
    probs = jnp.exp(scores - log_norm)
    dprobs = jnp.einsum("sqhe,skhe->shqk", gh, vh, preferred_element_type=f32)
    delta = jnp.sum(probs * dprobs, axis=-1, keepdims=True)
    dscores = (probs * (dprobs - delta)).astype(bf16)
    dq = jnp.einsum("shqk,skhe->sqhe", dscores, kh, preferred_element_type=f32) * factor
    dk = jnp.einsum("shqk,sqhe->skhe", dscores, qh, preferred_element_type=f32) * factor
    dv = jnp.einsum("shqk,sqhe->skhe", probs.astype(bf16), gh, preferred_element_type=f32)
    return dq.reshape(queries.shape), dk.reshape(keys.shape), dv.reshape(keys.shape)


def make_body(ny, nx):
    def to_cores(k):
        return [
            (c * NZ + z, (z // 2) * NZ + c * 2 + ((z % 2) ^ k))
            for c in range(NC)
            for z in range(NZ)
        ]

    def body(
        tokens,
        conditioning,
        cotangent,
        w_qkv,
        b_qkv,
        w_proj,
        b_proj,
        w_fc1,
        b_fc1,
        w_fc2,
        b_fc2,
        w_ada,
        b_ada,
    ):
        y, c = lax.axis_index("y"), lax.axis_index("c")
        z, x = lax.axis_index("z"), lax.axis_index("x")
        z0, z1 = z % 2, z // 2
        place, ns, D = tokens.shape
        q = ns // 2
        L = 2 * place
        dp = ny * NC
        B = D // dp
        own = y * NC + c
        hpt = w_qkv.shape[1]
        HW = hpt * HD
        F = w_fc1.shape[1]
        FF = F * NZ * nx
        factor = HD ** (-0.5)

        def rel(array):
            shape = array.shape
            view = array.reshape(shape[:-1] + (ny, NC, B))
            view = flip_bits(view, len(shape) - 1, ny, y)
            view = flip_bits(view, len(shape), NC, c)
            return view.reshape(shape)

        def spread(array):
            view = array.reshape(place, 2, q, D)
            first = jnp.where(z0 == 0, view[:, 0], view[:, 1])
            second = jnp.where(z0 == 0, view[:, 1], view[:, 0])
            got = [
                lax.ppermute(piece, ("c", "z"), to_cores(k))
                for k, piece in enumerate((first, second))
            ]
            return jnp.concatenate([g.transpose(1, 0, 2) for g in got], axis=1)

        def collect(array):
            pieces = [
                array[:, k * place : (k + 1) * place].transpose(1, 0, 2) for k in range(2)
            ]
            got = [
                lax.ppermute(piece, ("c", "z"), [(b, a) for a, b in to_cores(k)])
                for k, piece in enumerate(pieces)
            ]
            first = jnp.where(z0 == 0, got[0], got[1])
            second = jnp.where(z0 == 0, got[1], got[0])
            return jnp.stack([first, second], axis=1).reshape(place, ns, D)

        def gather_x(array):
            return jnp.stack(
                [array] + [swap_with(array, "x", nx, k) for k in range(1, nx)]
            )

        def reduce_x(parts):
            total = parts[0]
            for k in range(1, nx):
                total = total + swap_with(parts[k].astype(bf16), "x", nx, k).astype(f32)
            return total

        def gather_w(shard, by_rows):
            along = 1 if by_rows else 0
            over_z = jnp.concatenate(
                [shard] + [swap_with(shard, "z", NZ, k) for k in range(1, NZ)], axis=along
            )
            over_y = jnp.stack(
                [over_z] + [swap_with(over_z, "y", ny, k) for k in range(1, ny)]
            )
            other = swap_with(over_y, "c", NC, 1)
            if by_rows:
                return jnp.stack([over_y, other], axis=1).reshape(D, shard.shape[1] * NZ)
            pieces = [p for k in range(ny) for p in (over_y[k], other[k])]
            return jnp.concatenate(pieces, axis=1)

        def reduce_w(grad, by_rows):
            if by_rows:
                view = grad.reshape(ny, NC, B, NZ, grad.shape[1] // NZ)
                part = lambda ky, kc, kz: view[ky, kc, :, kz]
            else:
                view = grad.reshape(NZ, grad.shape[0] // NZ, ny, NC, B)
                part = lambda ky, kc, kz: view[kz, :, ky, kc]
            pick = lambda kc: jnp.stack(
                [jnp.stack([part(ky, kc, kz) for kz in range(NZ)]) for ky in range(ny)]
            )
            got = swap_with(pick(1).astype(bf16), "c", NC, 1)
            over_c = pick(0) + got.astype(f32)
            over_y = over_c[0]
            for k in range(1, ny):
                over_y = over_y + swap_with(over_c[k].astype(bf16), "y", ny, k).astype(f32)
            over_z = over_y[0]
            for k in range(1, NZ):
                over_z = over_z + swap_with(over_y[k].astype(bf16), "z", NZ, k).astype(f32)
            return over_z

        cond_c = jnp.stack([conditioning, swap_with(conditioning, "c", NC, 1)])
        cond_c = flip_bits(cond_c, 0, NC, c)
        cond_all = jnp.stack([cond_c] + [swap_with(cond_c, "y", ny, k) for k in range(1, ny)])
        cond_all = flip_bits(cond_all.reshape(ny, NZ, q, D), 1, NZ, z)
        act_all = jax.nn.silu(cond_all.astype(f32)).astype(bf16)
        act_rows = lax.dynamic_slice_in_dim(act_all, own * B, B, 3)

        partial_mod = dot(act_rows[:, 0].reshape(ny * q, B), w_ada, ((1,), (0,)))
        pad = lambda v, n: lax.dynamic_update_slice_in_dim(
            jnp.zeros((n,), f32), v.astype(f32), own * v.shape[0], 0
        )
        partial_mod = partial_mod + pad(b_ada, 6 * D)
        bias_vec = jnp.concatenate(
            [pad(b_qkv[0], D), pad(b_qkv[1], D), pad(b_proj, D), pad(b_fc1, FF), pad(b_fc2, D)]
        )
        partial_mod = partial_mod.reshape(ny, q * 6 * D)
        packed_mod = jnp.concatenate(
            [partial_mod, jnp.broadcast_to(bias_vec, (ny,) + bias_vec.shape)], axis=1
        )
        total_mod = packed_mod[0]
        for k in range(1, ny):
            total_mod = total_mod + swap_with(packed_mod[k], "y", ny, k)
        total_mod = total_mod + swap_with(total_mod, "c", NC, 1)
        modulation = rel(total_mod[: q * 6 * D].reshape(q, 6, 1, D))
        biases = total_mod[q * 6 * D :]
        bias_heads = biases[: 2 * D].reshape(2, NZ, nx, HW)
        bias_heads = lax.dynamic_index_in_dim(bias_heads, x, 2, keepdims=False)
        bias_heads = flip_bits(bias_heads, 1, NZ, z).reshape(2, NZ * HW)
        bias_proj = rel(biases[2 * D : 3 * D])
        bias_fc1 = biases[3 * D : 3 * D + FF].reshape(NZ, nx, F)
        bias_fc1 = lax.dynamic_index_in_dim(bias_fc1, x, 1, keepdims=False)
        bias_fc1 = flip_bits(bias_fc1, 0, NZ, z).reshape(NZ * F)
        bias_fc2 = rel(biases[3 * D + FF :])
        shift_attn, scale_attn, gate_attn, shift_mlp, scale_mlp, gate_mlp = (
            modulation[:, i] for i in range(6)
        )

        block_in = rel(spread(tokens)).astype(f32)
        w_heads = w_qkv.reshape(B, hpt, 3, HD).transpose(0, 2, 1, 3).reshape(B, 3 * HW)
        full_qkv = gather_w(w_heads, True)
        full_proj = gather_w(w_proj, False)
        full_fc1 = gather_w(w_fc1, True)
        full_fc2 = gather_w(w_fc2, False)
        grad_top = rel(spread(cotangent)).astype(f32)

        unit_in, rstd_in = layer_stats(block_in)
        normed = (unit_in * (1.0 + scale_attn) + shift_attn).astype(bf16)
        normed_all = gather_x(normed).reshape(nx * q * L, D)
        T = nx * q * L
        packed = dot(normed_all, full_qkv, ((1,), (0,))).reshape(T, NZ, 3, HW)
        queries = (packed[:, :, 0].reshape(T, NZ * HW) + bias_heads[0]).astype(bf16)
        keys = packed[:, :, 1].reshape(T, NZ * HW).astype(bf16)
        vals = (packed[:, :, 2].reshape(T, NZ * HW) + bias_heads[1]).astype(bf16)

        def by_sample(array):
            return array.reshape(nx, q, L, -1).transpose(1, 0, 2, 3).reshape(q, nx * L, -1)

        def by_rank(array):
            return array.reshape(q, nx, L, -1).transpose(1, 0, 2, 3).reshape(T, -1)

        queries, keys, vals = by_sample(queries), by_sample(keys), by_sample(vals)
        key_vals = jnp.stack([keys, vals])
        other_kv = swap_with(key_vals, "c", NC, 1)
        keys_all = jnp.concatenate([keys, other_kv[0]], axis=1)
        vals_all = jnp.concatenate([vals, other_kv[1]], axis=1)
        mixed, log_norm = attn_forward(queries, keys_all, vals_all, factor)
        mixed_rows = by_rank(mixed)
        branch_part = dot(mixed_rows, full_proj, ((1,), (0,))).reshape(nx, q, L, D)
        branch = reduce_x(branch_part) + bias_proj
        middle = block_in + gate_attn * branch
        unit_mid, rstd_mid = layer_stats(middle)
        normed_mlp = (unit_mid * (1.0 + scale_mlp) + shift_mlp).astype(bf16)
        mlp_all = gather_x(normed_mlp).reshape(T, D)
        hidden = dot(mlp_all, full_fc1, ((1,), (0,))) + bias_fc1
        activated, gelu_pull = jax.vjp(lambda h: jax.nn.gelu(h, approximate=True), hidden)
        act_low = activated.astype(bf16)
        mlp_part = dot(act_low, full_fc2, ((1,), (0,))).reshape(nx, q, L, D)
        branch_mlp = reduce_x(mlp_part) + bias_fc2
        block_out = (middle + gate_mlp * branch_mlp).astype(bf16)
        out = collect(rel(block_out))

        dgate_mlp = jnp.sum(grad_top * branch_mlp, axis=1)
        dbranch_mlp = (gate_mlp * grad_top).astype(bf16)
        g_bfc2 = jnp.sum(dbranch_mlp, axis=(0, 1), dtype=f32)
        dmlp_all = gather_x(dbranch_mlp).reshape(T, D)
        g_fc2 = reduce_w(dot(act_low, dmlp_all, ((0,), (0,))), False)
        dactiv = dot(dmlp_all, full_fc2, ((1,), (1,)))
        dhidden = gelu_pull(dactiv)[0].astype(bf16)
        g_bfc1 = jnp.sum(dhidden, axis=0, dtype=f32)
        g_fc1 = reduce_w(dot(mlp_all, dhidden, ((0,), (0,))), True)
        dnormed_mlp = reduce_x(dot(dhidden, full_fc1, ((1,), (1,))).reshape(nx, q, L, D))
        dshift_mlp = jnp.sum(dnormed_mlp, axis=1)
        dscale_mlp = jnp.sum(dnormed_mlp * unit_mid, axis=1)
        dmiddle = grad_top + layer_back(dnormed_mlp * (1.0 + scale_mlp), unit_mid, rstd_mid)
        dgate_attn = jnp.sum(dmiddle * branch, axis=1)
        dbranch = (gate_attn * dmiddle).astype(bf16)
        g_bproj = jnp.sum(dbranch, axis=(0, 1), dtype=f32)
        dattn_all = gather_x(dbranch).reshape(T, D)
        g_proj = reduce_w(dot(mixed_rows, dattn_all, ((0,), (0,))), False)
        dmixed = by_sample(dot(dattn_all, full_proj, ((1,), (1,))).astype(bf16))
        dq, dk, dv = attn_backward(queries, keys_all, vals_all, dmixed, log_norm, factor)
        half = nx * L
        dkv = jnp.stack([dk, dv])
        got_dkv = swap_with(dkv[:, :, half:].astype(bf16), "c", NC, 1)
        dkv = (dkv[:, :, :half] + got_dkv.astype(f32)).astype(bf16)
        dq = dq.astype(bf16)
        g_bq = jnp.sum(dq, axis=(0, 1), dtype=f32)
        g_bv = jnp.sum(dkv[1], axis=(0, 1), dtype=f32)
        dpacked = jnp.stack(
            [by_rank(v).reshape(T, NZ, HW) for v in (dq, dkv[0], dkv[1])], axis=2
        ).reshape(T, NZ * 3 * HW)
        g_qkv = reduce_w(dot(normed_all, dpacked, ((0,), (0,))), True)
        g_qkv = g_qkv.reshape(B, 3, hpt, HD).transpose(0, 2, 1, 3).reshape(B, hpt, 3 * HD)
        dnormed = reduce_x(dot(dpacked, full_qkv, ((1,), (1,))).reshape(nx, q, L, D))
        dshift_attn = jnp.sum(dnormed, axis=1)
        dscale_attn = jnp.sum(dnormed * unit_in, axis=1)
        dblock = dmiddle + layer_back(dnormed * (1.0 + scale_attn), unit_in, rstd_in)
        d_tokens = collect(rel(dblock.astype(bf16))).astype(f32)

        dmod = jnp.stack(
            [dshift_attn, dscale_attn, dgate_attn, dshift_mlp, dscale_mlp, dgate_mlp], axis=1
        )
        here = (jnp.arange(nx) == x).astype(f32)[:, None]

        def head_bias(vec, width):
            vec = flip_bits(vec.reshape(NZ, 1, width), 0, NZ, z)
            return (vec * here).reshape(NZ * nx * width)

        small = jnp.concatenate(
            [
                rel(dmod).reshape(q * 6 * D),
                head_bias(g_bq, HW),
                head_bias(g_bv, HW),
                rel(g_bproj),
                head_bias(g_bfc1, F),
                rel(g_bfc2),
            ]
        )
        for k in range(1, nx):
            small_k = swap_with(small, "x", nx, k)
            total = small_k if k == 1 else total + small_k
        small = small + total
        small = small + swap_with(small, "c", NC, 1)
        cut = q * 6 * D
        over_z = [small] + [swap_with(small, "z", NZ, k) for k in range(1, NZ)]
        bias_sum = sum(v[cut:] for v in over_z)
        flat = jnp.concatenate([v[:cut] for v in over_z] + [bias_sum])
        over_y = [flat] + [swap_with(flat, "y", ny, k) for k in range(1, ny)]
        bias_sum = sum(v[NZ * cut :] for v in over_y)
        dmod_all = jnp.stack([v[: NZ * cut] for v in over_y]).reshape(ny * NZ * q, 6 * D)

        take = lambda v, n: lax.dynamic_slice_in_dim(v, own * n, n, 0)
        out_bqkv = jnp.stack([take(bias_sum[:D], B), take(bias_sum[D : 2 * D], B)])
        out_bproj = take(bias_sum[2 * D : 3 * D], B)
        out_bfc1 = take(bias_sum[3 * D : 3 * D + FF], FF // dp)
        out_bfc2 = take(bias_sum[3 * D + FF :], B)
        out_bada = take(jnp.sum(dmod_all, axis=0), 6 * D // dp)
        cols = 6 * D // (NZ * nx)
        dmod_cols = lax.dynamic_slice_in_dim(dmod_all, (z * nx + x) * cols, cols, 1)
        act_mine = act_rows.reshape(ny * NZ * q, B)
        out_ada = dot(
            jnp.concatenate([act_mine] * 3),
            jnp.concatenate(split_three(dmod_cols)),
            ((0,), (0,)),
        )
        dact = sum(
            dot(part, w_ada, ((1,), (1,))) for part in split_three(dmod_all)
        ).reshape(ny, NZ, q, B)
        over_y = jnp.stack([dact[0]] + [swap_with(dact[k], "y", ny, k) for k in range(1, ny)])
        over_y = flip_bits(over_y, 1, NZ, z)
        over_y = flip_bits(over_y.reshape(ny, NC, 2 * q, B), 1, NC, c)
        other = swap_with(over_y[:, 1], "c", NC, 1)
        dact_rows = jnp.stack([over_y[:, 0], other], axis=1)
        dact_rows = rel(dact_rows.transpose(2, 0, 1, 3).reshape(ns, D))
        silu_pull = jax.vjp(jax.nn.silu, conditioning.astype(f32))[1]
        d_cond = silu_pull(dact_rows)[0]
        return (
            out,
            d_tokens,
            d_cond,
            g_qkv,
            out_bqkv,
            g_proj,
            out_bproj,
            g_fc1,
            out_bfc1,
            g_fc2,
            out_bfc2,
            out_ada,
            out_bada,
        )

    return body


def solution(mesh):
    dp, tensor = mesh.shape["dp"], mesh.shape["tensor"]
    ny, nx = dp // NC, tensor // NZ
    fine = Mesh(mesh.devices.reshape(ny, NC, NZ, nx), ("y", "c", "z", "x"))
    rows, cols = ("y", "c"), ("z", "x")
    placed = (
        P(cols, rows, None),
        P(rows, None),
        P(cols, rows, None),
        P(rows, cols, None),
        P(None, rows),
        P(cols, rows),
        P(rows),
        P(rows, cols),
        P(rows),
        P(cols, rows),
        P(rows),
        P(rows, None),
        P(rows),
    )
    out_placed = (
        P(cols, rows, None),
        P(cols, rows, None),
        P(rows, None),
        P(rows, cols, None),
        P(None, rows),
        P(cols, rows),
        P(rows),
        P(rows, cols),
        P(rows),
        P(cols, rows),
        P(rows),
        P(rows, cols),
        P(rows),
    )
    return jax.shard_map(
        make_body(ny, nx), mesh=fine, in_specs=placed, out_specs=out_placed, check_vma=False
    )
```

time: 1510 us -> 640 us (0.42)
  waiting for transfers between devices: 1180 us -> 165 us
  starting transfers between devices: 1.41 us -> 106 us
  local copies, waits for them, and re-layouts: 36.6 us -> 140 us
  blocking collectives: 101 us -> 0 us
  other arithmetic: 39.8 us -> 135 us
  matrix products: 128 us -> 83.2 us
    reduce_scatter x13 -> x0, waiting for transfers between devices: 743 us -> none  [the longest x2 168 us: body(): lax.psum_scatter(jnp.einsum('rsf,df->rsd', dhidden, full_fc1, preferred_e...]
    all_gather x11 -> x0, waiting for transfers between devices: 433 us -> none  [the longest x2 98.3 us: body(): gathered_mlp = lax.all_gather(mlp_low, 'tensor', axis=0, tiled=True)]
    ppermute x0 -> x70, waiting for transfers between devices: none -> 165 us  [the longest x62 152 us: swap_with(): lax.ppermute(array, axis_name, [(i, i ^ offset) for i in range(count)])]
    ppermute x0 -> x70, starting transfers between devices: none -> 106 us  [the longest x62 88.8 us: swap_with(): lax.ppermute(array, axis_name, [(i, i ^ offset) for i in range(count)])]
    another operation x0 -> x53, other arithmetic: none -> 61.1 us  [the longest x4 14.5 us: gather_w(): return jnp.stack([over_y, other], axis=1).reshape(D, shard.shape[1] * NZ)]
    all_gather x7 -> x0, blocking collectives: 42.2 us -> none  [the longest x1 9.31 us: fetch_weights(): lax.all_gather(w_qkv, 'dp', axis=0, tiled=True)]
    dot_general x52 -> x23, matrix products: 121 us -> 83.2 us  [the longest x17 51.4 us: dot(): return lax.dot_general(a, b, (dims, ((), ())), preferred_element_type=f32)]
    psum x1 -> x0, blocking collectives: 36.6 us -> none  [body(): lax.psum((dmod_local, pad_bqkv, grad_bproj, pad_bfc1, grad_bfc2), 'tensor')]
  transfers between devices with their start and end apart: 25 -> 70, of which waited for: 22 -> 22; matrix products, arithmetic and copies ran while one was open for 9% -> 48% of each run, Pallas kernels for 0% -> 0%
where the time goes in v1:
time: 640 us; the launch traced here: 632 us
  waiting for transfers between devices  165 us (26%)
  local copies, waits for them, and re-layouts  140 us (22%)
  other arithmetic  135 us (21%)
  starting transfers between devices  106 us (17%)
  matrix products  83.2 us (13%)
    ppermute x62, waiting for transfers between devices, swap_with(): lax.ppermute(array, axis_name, [(i, i ^ offset) for i in range(count)])  152 us
    ppermute x62, starting transfers between devices, swap_with(): lax.ppermute(array, axis_name, [(i, i ^ offset) for i in range(count)])  88.8 us
    dot_general x17, matrix products, dot(): return lax.dot_general(a, b, (dims, ((), ())), preferred_element_type=f32)  51.4 us
    unnamed x191, local copies, waits for them, and re-layouts  34.6 us
    rev x9, local copies, waits for them, and re-layouts, flip_bits(): swapped = jnp.flip(view, axis=axis + 1)  23.1 us
    dot_general x7, local copies, waits for them, and re-layouts, dot(): return lax.dot_general(a, b, (dims, ((), ())), preferred_element_type=f32)  22.3 us
    convert_element_type x1, other arithmetic, attn_backward(): dscores = (probs * (dprobs - delta)).astype(bf16)  16 us
    ppermute x4, starting transfers between devices, spread(): lax.ppermute(piece, ('c', 'z'), to_cores(k))  14.7 us
  transfers between devices with their start and end apart: 70, of which 22 were waited for; matrix products, arithmetic and copies ran while one was open for 48% of the time, Pallas kernels for 0%

profile of v1, /device:TPU:0, one launch (start us, length us, event | category | flops | bytes accessed | tf_op | source)
XLA Modules:
  0.0 631.9 jit_solution(14468718540380495786)
XLA Ops:
  46.8 11.3 %collective-permute-start.26 = (bf16[512,256]{1,0:T(8,128)(2,1)}, bf16[512,256]{1,0:T(8,128)(2,1)}, u32[]{:S(2)}, u32[]{:S(2)}) collective-permute-start(bf16[512,256]{1,0:T(8,128)(2,1)} %param.22), channel_id=1, source_target_pairs={{0,4},{2,6},{4,0},{6,2},{1,5},{3,7},{5,1},{7,3},{8,12},{10,14},{12... | collective-permute-start | bytes 786440 | tf_op jit(solution)/shard_map/ppermute | solution.py:29
  60.2 7.3 %collective-permute-done.1 = bf16[128,1,1024]{2,0,1:T(8,128)(2,1)} collective-permute-done((bf16[128,1,1024]{2,0,1:T(8,128)(2,1)}, bf16[128,1,1024]{2,0,1:T(8,128)(2,1)}, u32[]{:S(2)}, u32[]{:S(2)}) %collective-permute-start.1) | collective-permute-done | bytes 262176 | tf_op jit(solution)/shard_map/ppermute | solution.py:140
  76.1 5.6 rev.124
  85.5 6.0 collective-permute-start.34
  103.7 5.6 rev.138
  118.4 5.0 collective-permute-start.27
  158.0 5.8 collective-permute-done.35
  178.8 16.1 %collective-permute-done.23 = bf16[256,2048]{1,0:T(8,128)(2,1)} collective-permute-done((bf16[256,2048]{1,0:T(8,128)(2,1)}, bf16[256,2048]{1,0:T(8,128)(2,1)}, u32[]{:S(2)}, u32[]{:S(2)}) %collective-permute-start.23) | collective-permute-done | bytes 1048608 | tf_op jit(solution)/shard_map/ppermute | solution.py:29
  202.2 4.7 copy.97
  206.9 4.7 copy.98
  228.0 4.8 fusion.38
  236.6 6.0 fusion.54
  242.6 6.3 collective-permute-done.18
  255.7 7.2 %collective-permute-done.19 = bf16[1,256,1024]{2,1,0:T(8,128)(2,1)S(1)} collective-permute-done((bf16[1,256,1024]{2,1,0:T(8,128)(2,1)S(1)}, bf16[1,256,1024]{2,1,0:T(8,128)(2,1)S(1)}, u32[]{:S(2)}, u32[]{:S(2)}) %collective-permute-start.19) | collective-permute-done | bytes 524320 | tf_op jit(solution)/shard_map/ppermute | solution.py:29
  266.2 11.0 %convert_reduce_fusion = (f32[2048]{0:T(1024)S(1)}, bf16[512,2048]{1,0:T(8,128)(2,1)S(1)}, f32[512,2048]{1,0:T(8,128)}) fusion(f32[512,2048]{1,0:T(8,128)} %fusion.54, f32[2048]{0:T(1024)S(1)} %bitcast.788, bf16[512,1024]{1,0:T(8,128)(2,1)} %bitcast.709, bf16[1024,2048]{1,0:T(8,128)(2,1)} %bitcast.700), kind=kOutput, calls=%fused_computation.44 | convolution fusion | flops 2171598848 | bytes 15745024 | tf_op jit(solution)/shard_map/dot_general | solution.py:54
  281.0 6.6 %fusion.21 = (bf16[2048,512]{0,1:T(8,128)(2,1)}, bf16[2048,512]{0,1:T(8,128)(2,1)}) fusion(f32[512,2048]{1,0:T(8,128)} %get-tuple-element.232, f32[512,2048]{1,0:T(8,128)} %fusion.54), kind=kLoop, calls=%fused_computation.39 | loop fusion | flops 23068672 | bytes 12582912 | tf_op jit(solution)/shard_map/convert_element_type | solution.py:277
  293.7 6.0 fusion.25
  338.1 5.6 rev.136
  343.8 5.0 collective-permute-done.37
  358.5 11.5 %multiply_reduce_fusion = (f32[8,512]{1,0:T(8,128)S(1)}, f32[8,512,1024]{2,1,0:T(8,128)}) fusion(f32[8,512,1024]{2,1,0:T(8,128)} %copy-done.1, f32[8,512]{1,0:T(8,128)S(1)} %log_add_fusion, bf16[512,8,64]{0,2,1:T(8,128)(2,1)S(1)} %bitcast.714, bf16[512,8,64]{0,2,1:T(8,128)(2,1)S(1)} %bitcast.717, bf16[512,8,64]{0,2,1:T(8,128)(2,1)S(1)} %copy-done.40), kind=kOutput, calls=%fused_computation.1 | convolution fusion | flops 555741184 | bytes 35160064 | tf_op jit(solution)/shard_map/sqhe,skhe->shqk/dot_general | solution.py:81
  370.1 16.0 %multiply_convert_fusion = bf16[8,512,1024]{2,1,0:T(8,128)(2,1)} fusion(f32[8,512,1024]{2,1,0:T(8,128)} %get-tuple-element.234, f32[8,512,1024]{2,1,0:T(8,128)} %copy-done.1, f32[8,512]{1,0:T(8,128)S(1)} %get-tuple-element.233, f32[8,512]{1,0:T(8,128)S(1)} %log_add_fusion), kind=kLoop, calls=%fused_computation | loop fusion | flops 20971520 | bytes 41975808 | tf_op jit(solution)/shard_map/convert_element_type | solution.py:83
  394.2 5.8 convolution_multiply_fusion
  451.2 5.6 rev.140
  475.0 5.7 collective-permute-done.44
  483.6 7.0 %collective-permute-done.45 = f32[14336]{0:T(1024)S(1)} collective-permute-done((f32[14336]{0:T(1024)S(1)}, f32[14336]{0:T(1024)S(1)}, u32[]{:S(2)}, u32[]{:S(2)}) %collective-permute-start.45) | collective-permute-done | bytes 57376 | tf_op jit(solution)/shard_map/ppermute | solution.py:29
  490.6 6.1 collective-permute-done.46
  508.2 40.0 %collective-permute-done.47 = f32[32768]{0:T(1024)S(1)} collective-permute-done((f32[32768]{0:T(1024)S(1)}, f32[32768]{0:T(1024)S(1)}, u32[]{:S(2)}, u32[]{:S(2)}) %collective-permute-start.47) | collective-permute-done | bytes 131104 | tf_op jit(solution)/shard_map/ppermute | solution.py:29
  572.6 5.0 collective-permute-done.62
  577.6 7.1 %collective-permute-start.68 = (bf16[512,256]{1,0:T(8,128)(2,1)S(1)}, bf16[512,256]{1,0:T(8,128)(2,1)S(1)}, u32[]{:S(2)}, u32[]{:S(2)}) collective-permute-start(bf16[512,256]{1,0:T(8,128)(2,1)S(1)} %get-tuple-element.154), channel_id=1, source_target_pairs={{0,4},{2,6},{4,0},{6,2},{1,5},{3,7},{5,1},{7,3},{8,12},{10,14},{12... | collective-permute-start | bytes 786440 | tf_op jit(solution)/shard_map/ppermute | solution.py:29
  584.7 16.8 %collective-permute-done.63 = bf16[256,512]{1,0:T(8,128)(2,1)S(1)} collective-permute-done((bf16[256,512]{1,0:T(8,128)(2,1)S(1)}, bf16[256,512]{1,0:T(8,128)(2,1)S(1)}, u32[]{:S(2)}, u32[]{:S(2)}) %collective-permute-start.63) | collective-permute-done | bytes 262176 | tf_op jit(solution)/shard_map/ppermute | solution.py:29
  606.3 14.9 %collective-permute-done.68 = bf16[512,256]{1,0:T(8,128)(2,1)S(1)} collective-permute-done((bf16[512,256]{1,0:T(8,128)(2,1)S(1)}, bf16[512,256]{1,0:T(8,128)(2,1)S(1)}, u32[]{:S(2)}, u32[]{:S(2)}) %collective-permute-start.68) | collective-permute-done | bytes 262176 | tf_op jit(solution)/shard_map/ppermute | solution.py:29
  622.1 6.8 %collective-permute-done.53 = bf16[256,384]{1,0:T(8,128)(2,1)S(1)} collective-permute-done((bf16[256,384]{1,0:T(8,128)(2,1)S(1)}, bf16[256,384]{1,0:T(8,128)(2,1)S(1)}, u32[]{:S(2)}, u32[]{:S(2)}) %collective-permute-start.53) | collective-permute-done | bytes 196640 | tf_op jit(solution)/shard_map/ppermute | solution.py:29
  (579 shorter events, 350.2 us)
Async XLA Ops:
  0.7 27.9 %collective-permute-start.14 = (bf16[128,256]{1,0:T(8,128)(2,1)}, bf16[128,256]{1,0:T(8,128)(2,1)}, u32[]{:S(2)}, u32[]{:S(2)}) collective-permute-start(bf16[128,256]{1,0:T(8,128)(2,1)} %param.18), channel_id=1, source_target_pairs={{0,4},{2,6},{4,0},{6,2},{1,5},{3,7},{5,1},{7,3},{8,12},{10,14},{12... | collective-permute-start | bytes 196616 | tf_op jit(solution)/shard_map/ppermute | solution.py:29
  6.4 28.7 %collective-permute-start.15 = (bf16[128,256]{1,0:T(8,128)(2,1)}, bf16[128,256]{1,0:T(8,128)(2,1)S(1)}, u32[]{:S(2)}, u32[]{:S(2)}) collective-permute-start(bf16[128,256]{1,0:T(8,128)(2,1)} %param.18), channel_id=1, source_target_pairs={{0,6},{2,4},{4,2},{6,0},{1,7},{3,5},{5,3},{7,1},{8,14},{10,12},{12... | collective-permute-start | bytes 196616 | tf_op jit(solution)/shard_map/ppermute | solution.py:29
  7.4 33.4 %collective-permute-start.9 = (bf16[256,384]{0,1:T(8,128)(2,1)S(1)}, bf16[256,384]{0,1:T(8,128)(2,1)}, u32[]{:S(2)}, u32[]{:S(2)}) collective-permute-start(bf16[256,384]{0,1:T(8,128)(2,1)S(1)} %bitcast.725), channel_id=1, source_target_pairs={{0,6},{2,4},{4,2},{6,0},{1,7},{3,5},{5,3},{7,1},{8,14},{10,12},{12... | collective-permute-start | bytes 589832 | tf_op jit(solution)/shard_map/ppermute | solution.py:29
  32.8 92.3 %collective-permute-start.21 = (bf16[256,512]{1,0:T(8,128)(2,1)}, bf16[256,512]{1,0:T(8,128)(2,1)}, u32[]{:S(2)}, u32[]{:S(2)}) collective-permute-start(bf16[256,512]{1,0:T(8,128)(2,1)} %param.20), channel_id=1, source_target_pairs={{0,4},{2,6},{4,0},{6,2},{1,5},{3,7},{5,1},{7,3},{8,12},{10,14},{12... | collective-permute-start | bytes 786440 | tf_op jit(solution)/shard_map/ppermute | solution.py:29
  40.8 77.6 %collective-permute-start.20 = (bf16[256,512]{1,0:T(8,128)(2,1)}, bf16[256,512]{1,0:T(8,128)(2,1)}, u32[]{:S(2)}, u32[]{:S(2)}) collective-permute-start(bf16[256,512]{1,0:T(8,128)(2,1)} %param.20), channel_id=1, source_target_pairs={{0,2},{2,0},{4,6},{6,4},{1,3},{3,1},{5,7},{7,5},{8,10},{10,8},{12,... | collective-permute-start | bytes 786440 | tf_op jit(solution)/shard_map/ppermute | solution.py:29
  42.8 111.1 %collective-permute-start.22 = (bf16[256,512]{1,0:T(8,128)(2,1)}, bf16[256,512]{1,0:T(8,128)(2,1)}, u32[]{:S(2)}, u32[]{:S(2)}) collective-permute-start(bf16[256,512]{1,0:T(8,128)(2,1)} %param.20), channel_id=1, source_target_pairs={{0,6},{2,4},{4,2},{6,0},{1,7},{3,5},{5,3},{7,1},{8,14},{10,12},{12... | collective-permute-start | bytes 786440 | tf_op jit(solution)/shard_map/ppermute | solution.py:29
  46.8 93.5 %collective-permute-start.26 = (bf16[512,256]{1,0:T(8,128)(2,1)}, bf16[512,256]{1,0:T(8,128)(2,1)}, u32[]{:S(2)}, u32[]{:S(2)}) collective-permute-start(bf16[512,256]{1,0:T(8,128)(2,1)} %param.22), channel_id=1, source_target_pairs={{0,4},{2,6},{4,0},{6,2},{1,5},{3,7},{5,1},{7,3},{8,12},{10,14},{12... | collective-permute-start | bytes 786440 | tf_op jit(solution)/shard_map/ppermute | solution.py:29
  96.7 31.7 %collective-permute-start.25 = (bf16[512,256]{1,0:T(8,128)(2,1)}, bf16[512,256]{1,0:T(8,128)(2,1)}, u32[]{:S(2)}, u32[]{:S(2)}) collective-permute-start(bf16[512,256]{1,0:T(8,128)(2,1)} %param.22), channel_id=1, source_target_pairs={{0,2},{2,0},{4,6},{6,4},{1,3},{3,1},{5,7},{7,5},{8,10},{10,8},{12,... | collective-permute-start | bytes 786440 | tf_op jit(solution)/shard_map/ppermute | solution.py:29
  118.4 28.7 %collective-permute-start.27 = (bf16[512,256]{1,0:T(8,128)(2,1)}, bf16[512,256]{1,0:T(8,128)(2,1)}, u32[]{:S(2)}, u32[]{:S(2)}) collective-permute-start(bf16[512,256]{1,0:T(8,128)(2,1)} %param.22), channel_id=1, source_target_pairs={{0,6},{2,4},{4,2},{6,0},{1,7},{3,5},{5,3},{7,1},{8,14},{10,12},{12... | collective-permute-start | bytes 786440 | tf_op jit(solution)/shard_map/ppermute | solution.py:29
  125.1 30.6 %collective-permute-start.16 = (bf16[512,256]{1,0:T(8,128)(2,1)S(1)}, bf16[512,256]{1,0:T(8,128)(2,1)}, u32[]{:S(2)}, u32[]{:S(2)}) collective-permute-start(bf16[512,256]{1,0:T(8,128)(2,1)S(1)} %copy-done.50), channel_id=1, source_target_pairs={{0,16},{16,0},{1,17},{17,1},{2,18},{18,2},{3,19},{19,3},{4,20},{20... | collective-permute-start | bytes 786440 | tf_op jit(solution)/shard_map/ppermute | solution.py:29
  140.3 27.0 %collective-permute-start.6 = (bf16[1,256,1024]{2,1,0:T(8,128)(2,1)}, bf16[1,256,1024]{2,1,0:T(8,128)(2,1)}, u32[]{:S(2)}, u32[]{:S(2)}) collective-permute-start(bf16[1,256,1024]{2,1,0:T(8,128)(2,1)} %add_convert_fusion.7), channel_id=1, source_target_pairs={{0,1},{1,0},{2,3},{3,2},{4,5},{5,4},{6,7},{7,6},{8,9},{9,8},{10,11... | collective-permute-start | bytes 1572872 | tf_op jit(solution)/shard_map/ppermute | solution.py:29
  149.3 26.3 %collective-permute-start.28 = (bf16[2048,256]{1,0:T(8,128)(2,1)}, bf16[2048,256]{1,0:T(8,128)(2,1)}, u32[]{:S(2)}, u32[]{:S(2)}) collective-permute-start(bf16[2048,256]{1,0:T(8,128)(2,1)} %constant_dynamic-update-slice_fusion.11), channel_id=1, source_target_pairs={{0,16},{16,0},{1,17},{17,1},{2,18},{18,2},{3,19},{19,3},{4,20},{20... | collective-permute-start | bytes 3145736 | tf_op jit(solution)/shard_map/ppermute | solution.py:29
  153.9 44.9 %collective-permute-start.11 = (bf16[2,256,1536]{1,2,0:T(8,128)(2,1)}, bf16[2,256,1536]{1,2,0:T(8,128)(2,1)}, u32[]{:S(2)}, u32[]{:S(2)}) collective-permute-start(bf16[2,256,1536]{1,2,0:T(8,128)(2,1)} %get-tuple-element.151), channel_id=1, source_target_pairs={{0,8},{8,0},{1,9},{9,1},{2,10},{10,2},{3,11},{11,3},{4,12},{12,4},... | collective-permute-start | bytes 4718600 | tf_op jit(solution)/shard_map/ppermute | solution.py:29
  155.7 39.2 %collective-permute-start.23 = (bf16[256,2048]{1,0:T(8,128)(2,1)}, bf16[256,2048]{1,0:T(8,128)(2,1)}, u32[]{:S(2)}, u32[]{:S(2)}) collective-permute-start(bf16[256,2048]{1,0:T(8,128)(2,1)} %constant_dynamic-update-slice_fusion.7), channel_id=1, source_target_pairs={{0,16},{16,0},{1,17},{17,1},{2,18},{18,2},{3,19},{19,3},{4,20},{20... | collective-permute-start | bytes 3145736 | tf_op jit(solution)/shard_map/ppermute | solution.py:29
  178.8 39.0 %collective-permute-start.29 = (bf16[2,2048,256]{2,1,0:T(8,128)(2,1)}, bf16[2,2048,256]{2,1,0:T(8,128)(2,1)}, u32[]{:S(2)}, u32[]{:S(2)}) collective-permute-start(bf16[2,2048,256]{2,1,0:T(8,128)(2,1)} %pad_maximum_fusion.5), channel_id=1, source_target_pairs={{0,8},{8,0},{1,9},{9,1},{2,10},{10,2},{3,11},{11,3},{4,12},{12,4},... | collective-permute-start | bytes 6291464 | tf_op jit(solution)/shard_map/ppermute | solution.py:29
  198.8 52.5 %collective-permute-start.24 = (bf16[2,256,2048]{2,1,0:T(8,128)(2,1)}, bf16[2,256,2048]{2,1,0:T(8,128)(2,1)}, u32[]{:S(2)}, u32[]{:S(2)}) collective-permute-start(bf16[2,256,2048]{2,1,0:T(8,128)(2,1)} %get-tuple-element.149), channel_id=1, source_target_pairs={{0,8},{8,0},{1,9},{9,1},{2,10},{10,2},{3,11},{11,3},{4,12},{12,4},... | collective-permute-start | bytes 6291464 | tf_op jit(solution)/shard_map/ppermute | solution.py:29
  301.9 26.7 %collective-permute-start.30 = (bf16[1,256,1024]{2,1,0:T(8,128)(2,1)}, bf16[1,256,1024]{2,1,0:T(8,128)(2,1)}, u32[]{:S(2)}, u32[]{:S(2)}) collective-permute-start(bf16[1,256,1024]{2,1,0:T(8,128)(2,1)} %fusion.63), channel_id=1, source_target_pairs={{0,1},{1,0},{2,3},{3,2},{4,5},{5,4},{6,7},{7,6},{8,9},{9,8},{10,11... | collective-permute-start | bytes 1572872 | tf_op jit(solution)/shard_map/ppermute | solution.py:29
  314.5 117.3 %collective-permute-start.60 = (bf16[2,4,256,512]{3,2,1,0:T(8,128)(2,1)}, bf16[2,4,256,512]{3,2,1,0:T(8,128)(2,1)}, u32[]{:S(2)}, u32[]{:S(2)}) collective-permute-start(bf16[2,4,256,512]{3,2,1,0:T(8,128)(2,1)} %pad_maximum_fusion.6), channel_id=1, source_target_pairs={{0,8},{8,0},{1,9},{9,1},{2,10},{10,2},{3,11},{11,3},{4,12},{12,4},... | collective-permute-start | bytes 6291464 | tf_op jit(solution)/shard_map/ppermute | solution.py:29
  355.7 36.6 %collective-permute-start.55 = (bf16[2,4,128,256]{3,2,1,0:T(8,128)(2,1)S(1)}, bf16[2,4,128,256]{3,2,1,0:T(8,128)(2,1)S(1)}, u32[]{:S(2)}, u32[]{:S(2)}) collective-permute-start(bf16[2,4,128,256]{3,2,1,0:T(8,128)(2,1)S(1)} %pad_maximum_fusion.21), channel_id=1, source_target_pairs={{0,8},{8,0},{1,9},{9,1},{2,10},{10,2},{3,11},{11,3},{4,12},{12,4},... | collective-permute-start | bytes 1572872 | tf_op jit(solution)/shard_map/ppermute | solution.py:29
  429.6 136.7 %collective-permute-start.50 = (bf16[2,4,256,384]{3,2,1,0:T(8,128)(2,1)}, bf16[2,4,256,384]{3,2,1,0:T(8,128)(2,1)}, u32[]{:S(2)}, u32[]{:S(2)}) collective-permute-start(bf16[2,4,256,384]{3,2,1,0:T(8,128)(2,1)} %pad_maximum_fusion.10), channel_id=1, source_target_pairs={{0,8},{8,0},{1,9},{9,1},{2,10},{10,2},{3,11},{11,3},{4,12},{12,4},... | collective-permute-start | bytes 4718600 | tf_op jit(solution)/shard_map/ppermute | solution.py:29
  465.1 32.2 %collective-permute-start.40 = (bf16[128,1,1024]{2,0,1:T(8,128)(2,1)}, bf16[128,1,1024]{2,0,1:T(8,128)(2,1)S(1)}, u32[]{:S(2)}, u32[]{:S(2)}) collective-permute-start(bf16[128,1,1024]{2,0,1:T(8,128)(2,1)} %get-tuple-element.179), channel_id=1, source_target_pairs={{0,0},{2,2},{8,4},{10,6},{4,8},{6,10},{12,12},{14,14},{1,1},{3,3},... | collective-permute-start | bytes 786440 | tf_op jit(solution)/shard_map/ppermute | solution.py:150
  466.7 32.2 %collective-permute-start.41 = (bf16[128,1,1024]{2,0,1:T(8,128)(2,1)}, bf16[128,1,1024]{2,0,1:T(8,128)(2,1)}, u32[]{:S(2)}, u32[]{:S(2)}) collective-permute-start(bf16[128,1,1024]{2,0,1:T(8,128)(2,1)} %get-tuple-element.180), channel_id=1, source_target_pairs={{2,0},{0,2},{10,4},{8,6},{6,8},{4,10},{14,12},{12,14},{3,1},{1,3},... | collective-permute-start | bytes 786440 | tf_op jit(solution)/shard_map/ppermute | solution.py:150
  472.4 27.9 %collective-permute-start.31 = (bf16[128,1,1024]{2,0,1:T(8,128)(2,1)S(1)}, bf16[128,1,1024]{2,0,1:T(8,128)(2,1)S(1)}, u32[]{:S(2)}, u32[]{:S(2)}) collective-permute-start(bf16[128,1,1024]{2,0,1:T(8,128)(2,1)S(1)} %get-tuple-element.185), channel_id=1, source_target_pairs={{0,0},{2,2},{8,4},{10,6},{4,8},{6,10},{12,12},{14,14},{1,1},{3,3},... | collective-permute-start | bytes 786440 | tf_op jit(solution)/shard_map/ppermute | solution.py:150
  497.3 62.8 %collective-permute-start.61 = (bf16[4,256,512]{2,1,0:T(8,128)(2,1)}, bf16[4,256,512]{2,1,0:T(8,128)(2,1)}, u32[]{:S(2)}, u32[]{:S(2)}) collective-permute-start(bf16[4,256,512]{2,1,0:T(8,128)(2,1)} %fusion.39), channel_id=1, source_target_pairs={{0,16},{16,0},{1,17},{17,1},{2,18},{18,2},{3,19},{19,3},{4,20},{20... | collective-permute-start | bytes 3145736 | tf_op jit(solution)/shard_map/ppermute | solution.py:29
  498.9 71.0 %collective-permute-start.66 = (bf16[4,512,256]{2,1,0:T(8,128)(2,1)}, bf16[4,512,256]{2,1,0:T(8,128)(2,1)}, u32[]{:S(2)}, u32[]{:S(2)}) collective-permute-start(bf16[4,512,256]{2,1,0:T(8,128)(2,1)} %fusion.40), channel_id=1, source_target_pairs={{0,16},{16,0},{1,17},{17,1},{2,18},{18,2},{3,19},{19,3},{4,20},{20... | collective-permute-start | bytes 3145736 | tf_op jit(solution)/shard_map/ppermute | solution.py:29
  500.3 47.8 %collective-permute-start.47 = (f32[32768]{0:T(1024)S(1)}, f32[32768]{0:T(1024)S(1)}, u32[]{:S(2)}, u32[]{:S(2)}) collective-permute-start(f32[32768]{0:T(1024)S(1)} %get-tuple-element.68), channel_id=1, source_target_pairs={{0,16},{16,0},{1,17},{17,1},{2,18},{18,2},{3,19},{19,3},{4,20},{20... | collective-permute-start | bytes 393224 | tf_op jit(solution)/shard_map/ppermute | solution.py:29
  562.9 38.6 %collective-permute-start.63 = (bf16[256,512]{1,0:T(8,128)(2,1)S(1)}, bf16[256,512]{1,0:T(8,128)(2,1)S(1)}, u32[]{:S(2)}, u32[]{:S(2)}) collective-permute-start(bf16[256,512]{1,0:T(8,128)(2,1)S(1)} %get-tuple-element.157), channel_id=1, source_target_pairs={{0,4},{2,6},{4,0},{6,2},{1,5},{3,7},{5,1},{7,3},{8,12},{10,14},{12... | collective-permute-start | bytes 786440 | tf_op jit(solution)/shard_map/ppermute | solution.py:29
  568.4 34.1 %collective-permute-start.51 = (bf16[4,256,384]{2,1,0:T(8,128)(2,1)S(1)}, bf16[4,256,384]{2,1,0:T(8,128)(2,1)S(1)}, u32[]{:S(2)}, u32[]{:S(2)}) collective-permute-start(bf16[4,256,384]{2,1,0:T(8,128)(2,1)S(1)} %fusion.53), channel_id=1, source_target_pairs={{0,16},{16,0},{1,17},{17,1},{2,18},{18,2},{3,19},{19,3},{4,20},{20... | collective-permute-start | bytes 2359304 | tf_op jit(solution)/shard_map/ppermute | solution.py:29
  571.6 32.3 %collective-permute-start.67 = (bf16[512,256]{1,0:T(8,128)(2,1)S(1)}, bf16[512,256]{1,0:T(8,128)(2,1)S(1)}, u32[]{:S(2)}, u32[]{:S(2)}) collective-permute-start(bf16[512,256]{1,0:T(8,128)(2,1)S(1)} %get-tuple-element.152), channel_id=1, source_target_pairs={{0,2},{2,0},{4,6},{6,4},{1,3},{3,1},{5,7},{7,5},{8,10},{10,8},{12,... | collective-permute-start | bytes 786440 | tf_op jit(solution)/shard_map/ppermute | solution.py:29
  577.6 28.7 %collective-permute-start.69 = (bf16[512,256]{1,0:T(8,128)(2,1)S(1)}, bf16[512,256]{1,0:T(8,128)(2,1)S(1)}, u32[]{:S(2)}, u32[]{:S(2)}) collective-permute-start(bf16[512,256]{1,0:T(8,128)(2,1)S(1)} %get-tuple-element.153), channel_id=1, source_target_pairs={{0,6},{2,4},{4,2},{6,0},{1,7},{3,5},{5,3},{7,1},{8,14},{10,12},{12... | collective-permute-start | bytes 786440 | tf_op jit(solution)/shard_map/ppermute | solution.py:29
  577.6 43.6 %collective-permute-start.68 = (bf16[512,256]{1,0:T(8,128)(2,1)S(1)}, bf16[512,256]{1,0:T(8,128)(2,1)S(1)}, u32[]{:S(2)}, u32[]{:S(2)}) collective-permute-start(bf16[512,256]{1,0:T(8,128)(2,1)S(1)} %get-tuple-element.154), channel_id=1, source_target_pairs={{0,4},{2,6},{4,0},{6,2},{1,5},{3,7},{5,1},{7,3},{8,12},{10,14},{12... | collective-permute-start | bytes 786440 | tf_op jit(solution)/shard_map/ppermute | solution.py:29
  603.8 25.0 %collective-permute-start.53 = (bf16[256,384]{1,0:T(8,128)(2,1)S(1)}, bf16[256,384]{1,0:T(8,128)(2,1)S(1)}, u32[]{:S(2)}, u32[]{:S(2)}) collective-permute-start(bf16[256,384]{1,0:T(8,128)(2,1)S(1)} %get-tuple-element.174), channel_id=1, source_target_pairs={{0,4},{2,6},{4,0},{6,2},{1,5},{3,7},{5,1},{7,3},{8,12},{10,14},{12... | collective-permute-start | bytes 589832 | tf_op jit(solution)/shard_map/ppermute | solution.py:29
  (117 other events, 1202.9 us)

commit v2 on v1

--- a/solution.py
+++ b/solution.py
@@ -1,6 +1,11 @@
+import functools
+import math
+
 import jax
 import jax.numpy as jnp
 from jax import lax
+from jax.experimental import pallas as pl
+from jax.experimental.pallas import tpu as pltpu
 from jax.sharding import Mesh, PartitionSpec as P
 
 HD = 64
@@ -394,6 +399,772 @@
     return body
 
 
+LOG2E = 1.4426950408889634
+
+
+def nn(a, b):
+    return lax.dot_general(a, b, (((1,), (0,)), ((), ())), preferred_element_type=f32)
+
+
+def nt(a, b):
+    return lax.dot_general(a, b, (((1,), (1,)), ((), ())), preferred_element_type=f32)
+
+
+def lanes(ref, block, width=256):
+    return ref[:, pl.ds(pl.multiple_of(block * width, width), width)]
+
+
+def total_rows(array):
+    return jnp.sum(array, axis=0, keepdims=True)
+
+
+def whole(shape):
+    zeros = (0,) * len(shape)
+    return pl.BlockSpec(shape, lambda *_: zeros)
+
+
+def kernel_call(body, table, operands, in_specs, out_specs, outs, steps=1, scratch=(), flops=0, name=None):
+    moved = sum(o.size * o.dtype.itemsize for o in operands)
+    listed = outs if isinstance(outs, list) else [outs]
+    moved += sum(math.prod(o.shape) * jnp.dtype(o.dtype).itemsize for o in listed)
+    return pl.pallas_call(
+        body,
+        grid_spec=pltpu.PrefetchScalarGridSpec(
+            num_scalar_prefetch=1,
+            grid=(steps,),
+            in_specs=in_specs,
+            out_specs=out_specs,
+            scratch_shapes=list(scratch),
+        ),
+        out_shape=outs,
+        cost_estimate=pl.CostEstimate(flops=flops, bytes_accessed=moved, transcendentals=0),
+        name=name,
+    )(table, *operands)
+
+
+def shaped(shape, dtype):
+    return jax.ShapeDtypeStruct(shape, dtype)
+
+
+COLS = 512
+
+
+def weight_specs():
+    spec = pl.BlockSpec((2, 1, 256, COLS), lambda j, t: (0, j, 0, 0))
+    return [spec, spec]
+
+
+def column_spec(width, rows=256):
+    return pl.BlockSpec((rows, width), lambda j, t: (0, j))
+
+
+PAIRS = [(kc, ky) for kc in range(2) for ky in range(2)]
+
+
+def mod_kernel(t, act, w_ada, b_ada, b_qkv, b_proj, b_fc1, b_fc2, out):
+    own = t[13]
+
+    def placed(vec, count):
+        tiled = jnp.concatenate([vec.astype(f32)] * count, axis=1)
+        width = vec.shape[1]
+        lane = lax.broadcasted_iota(jnp.int32, tiled.shape, 1)
+        here = (lane >= own * width) & (lane < own * width + width)
+        return jnp.where(here, tiled, 0.0)
+
+    bias_ada = placed(b_ada[...], 4)
+    rows = []
+    for i in range(6):
+        part = slice(i * 1024, (i + 1) * 1024)
+        rows.append(nn(act[...], w_ada[:, part]) + bias_ada[:, part])
+    tail = [placed(b_proj[...], 4), placed(b_fc2[...], 4), placed(b_qkv[0:1], 4), placed(b_qkv[1:2], 4)]
+    fc1 = b_fc1[...].astype(f32)
+    tail += [jnp.where(own == r, fc1, 0.0) for r in range(4)]
+    tail += [jnp.zeros((1, 1024), f32)] * 2
+    for ky in range(2):
+        out[ky] = jnp.concatenate([r[ky : ky + 1] for r in rows] + tail, axis=0)
+
+
+def norm(rows):
+    center = rows - jnp.mean(rows, axis=-1, keepdims=True)
+    scale = lax.rsqrt(jnp.mean(center * center, axis=-1, keepdims=True) + norm_eps)
+    return center * scale, scale
+
+
+def ln_kernel(t, first, second, mod, out):
+    for i, ref in enumerate((first, second)):
+        unit, _ = norm(ref[...].astype(f32))
+        out[i * 128 : (i + 1) * 128] = (unit * (1.0 + mod[1:2]) + mod[0:1]).astype(bf16)
+
+
+def dmlp_kernel(t, first, second, mod, out, sums):
+    total = jnp.zeros((1, 1024), f32)
+    for i, ref in enumerate((first, second)):
+        grad = (mod[5:6] * ref[...].astype(f32)).astype(bf16)
+        out[i * 128 : (i + 1) * 128] = grad
+        total = total + total_rows(grad.astype(f32))
+    sums[...] = total
+
+
+def qkv_kernel(t, x, wo, wt, bias, q, kv):
+    acc = jnp.zeros((256, 384), f32)
+    for kc, ky in PAIRS:
+        acc = acc + nn(lanes(x, t[kc * 2 + ky]), (wo, wt)[kc][ky, 0, :, :384])
+    q[...] = (acc[:, :128] + bias[8:9]).astype(bf16)
+    kv[0] = acc[:, 128:256].astype(bf16)
+    kv[1] = (acc[:, 256:] + bias[9:10]).astype(bf16)
+
+
+def attn_kernel(t, q, a, b, c, d, mixed, lse):
+    scale = HD**-0.5 * LOG2E
+    chunks = (a, b, c, d)
+    keys = jnp.concatenate([r[0] for r in chunks], axis=0)
+    vals_t = jnp.concatenate([r[1] for r in chunks], axis=0).T
+    lane = lax.broadcasted_iota(jnp.int32, (256, 128), 1)
+    queries = q[...]
+    parts = []
+    for h in range(2):
+        qm = jnp.where((lane // HD) == h, queries, jnp.zeros_like(queries))
+        s = nt(keys, qm)
+        top = jnp.max(s, axis=0, keepdims=True)
+        p = jnp.exp2((s - top) * scale)
+        total = jnp.sum(p, axis=0, keepdims=True)
+        o = nn(vals_t, p.astype(bf16)) / total
+        parts.append(o[h * HD : (h + 1) * HD])
+        lse[0, h : h + 1] = top * scale + jnp.log2(total)
+    mixed[...] = jnp.concatenate(parts, axis=0).T.astype(bf16)
+
+
+def attn_back_kernel(t, q, do, mixed, lse, a, b, c, d, dq, near, far):
+    factor = HD**-0.5
+    scale = factor * LOG2E
+    lane = lax.broadcasted_iota(jnp.int32, (256, 128), 1)
+    queries, grads = q[...], do[...]
+    product_t = (grads.astype(f32) * mixed[...].astype(f32)).T
+    zero = jnp.zeros_like(queries)
+    qms = [jnp.where((lane // HD) == h, queries, zero) for h in range(2)]
+    gms = [jnp.where((lane // HD) == h, grads, zero) for h in range(2)]
+    deltas = [total_rows(product_t[h * HD : (h + 1) * HD]) for h in range(2)]
+    dq_t = [jnp.zeros((128, 256), f32) for _ in range(2)]
+    for i, ref in enumerate((a, b, c, d)):
+        key, val = ref[0], ref[1]
+        key_t = key.T
+        dk = jnp.zeros((256, 128), f32)
+        dv = jnp.zeros((256, 128), f32)
+        for h in range(2):
+            p = jnp.exp2(nt(key, qms[h]) * scale - lse[0, h : h + 1])
+            ds = (p * (nt(val, gms[h]) - deltas[h])).astype(bf16)
+            dv = dv + nn(p.astype(bf16), gms[h])
+            dk = dk + nn(ds, qms[h])
+            dq_t[h] = dq_t[h] + nn(key_t, ds)
+        out = (near, far)[i // 2]
+        rows = slice((i % 2) * 256, (i % 2) * 256 + 256)
+        out[0, rows] = (dk * factor).astype(bf16)
+        out[1, rows] = dv.astype(bf16)
+    both = jnp.concatenate([dq_t[h][h * HD : (h + 1) * HD] for h in range(2)], axis=0)
+    dq[...] = (both * factor).T.astype(bf16)
+
+
+def unpack_proj(block):
+    return jnp.concatenate([block[:128, 384:], block[128:, 384:]], axis=1)
+
+
+def proj_kernel(t, mixed, wo, wt, out, acc):
+    j = pl.program_id(0)
+
+    @pl.when(j == 0)
+    def _():
+        acc[...] = jnp.zeros_like(acc)
+
+    for i, (kc, ky) in enumerate(PAIRS):
+        acc[i] += nn(mixed[...], unpack_proj((wo, wt)[kc][ky, 0]))
+
+    @pl.when(j == 3)
+    def _():
+        for i in range(4):
+            out[:, pl.ds(pl.multiple_of(t[i] * 256, 256), 256)] = acc[i].astype(out.dtype)
+
+
+def proj_back_kernel(t, grad, wo, wt, out):
+    acc = jnp.zeros((256, 128), f32)
+    for kc, ky in PAIRS:
+        acc = acc + nt(lanes(grad, t[kc * 2 + ky]), unpack_proj((wo, wt)[kc][ky, 0]))
+    out[...] = acc.astype(bf16)
+
+
+def mid_kernel(t, first, second, part, got, mod, branch, middle, out):
+    for i, ref in enumerate((first, second)):
+        rows = slice(i * 128, (i + 1) * 128)
+        br = part[rows] + got[rows].astype(f32) + mod[6:7]
+        mid = ref[...].astype(f32) + mod[2:3] * br
+        unit, _ = norm(mid)
+        branch[rows] = br
+        middle[rows] = mid
+        out[rows] = (unit * (1.0 + mod[4:5]) + mod[3:4]).astype(bf16)
+
+
+def fc1_kernel(t, x, wo, wt, bias, act, slope):
+    j = pl.program_id(0)
+    h = jnp.zeros((256, COLS), f32)
+    for kc, ky in PAIRS:
+        h = h + nn(lanes(x, t[kc * 2 + ky]), (wo, wt)[kc][ky, 0])
+    h = h + bias[pl.ds(10 + t[8 + j], 1), :]
+    root = 0.7978845608028654
+    inner = jnp.tanh(root * h * (1.0 + 0.044715 * h * h))
+    half = 0.5 * (1.0 + inner)
+    act[...] = (h * half).astype(bf16)
+    slope[...] = (half + (0.5 * root) * h * (1.0 - inner * inner) * (1.0 + 3 * 0.044715 * h * h)).astype(bf16)
+
+
+def fc2_kernel(t, act, wo, wt, out, acc):
+    j = pl.program_id(0)
+
+    @pl.when(j == 0)
+    def _():
+        acc[...] = jnp.zeros_like(acc)
+
+    for i, (kc, ky) in enumerate(PAIRS):
+        w = (wo, wt)[kc]
+        acc[i] += nn(act[:, :256], w[ky, 0, :, :256]) + nn(act[:, 256:], w[ky, 0, :, 256:])
+
+    @pl.when(j == 3)
+    def _():
+        for i in range(4):
+            out[:, pl.ds(pl.multiple_of(t[i] * 256, 256), 256)] = acc[i].astype(out.dtype)
+
+
+def mlp_back_kernel(t, grad, slope, w2o, w2t, w1o, w1t, dh, sums, out, acc):
+    j = pl.program_id(0)
+
+    @pl.when(j == 0)
+    def _():
+        acc[...] = jnp.zeros_like(acc)
+
+    left = jnp.zeros((256, 256), f32)
+    right = jnp.zeros((256, 256), f32)
+    for kc, ky in PAIRS:
+        w, g = (w2o, w2t)[kc], lanes(grad, t[kc * 2 + ky])
+        left = left + nt(g, w[ky, 0, :, :256])
+        right = right + nt(g, w[ky, 0, :, 256:])
+    dhidden = (jnp.concatenate([left, right], axis=1) * slope[...].astype(f32)).astype(bf16)
+    dh[...] = dhidden
+    sums[...] = total_rows(dhidden.astype(f32))
+    for i, (kc, ky) in enumerate(PAIRS):
+        acc[i] += nt(dhidden, (w1o, w1t)[kc][ky, 0])
+
+    @pl.when(j == 3)
+    def _():
+        for i in range(4):
+            out[:, pl.ds(pl.multiple_of(t[i] * 256, 256), 256)] = acc[i].astype(out.dtype)
+
+
+def mlp_grads_kernel(t, xo, xt, dho, dht, acto, actt, go, gt, keep, send):
+    dh = jnp.concatenate([dho[...], dht[...]], axis=0)
+    act_t = jnp.concatenate([acto[...], actt[...]], axis=0).T
+    for i, (kc, ky) in enumerate(PAIRS):
+        x_t = jnp.concatenate([lanes(xo, t[i]), lanes(xt, t[i])], axis=0).T
+        grad = jnp.concatenate([lanes(go, t[i]), lanes(gt, t[i])], axis=0)
+        out = (keep, send)[kc]
+        out[ky, 0, 0] = nn(x_t, dh).astype(bf16)
+        fc2 = nn(act_t, grad).astype(bf16)
+        out[ky, 0, 1] = jnp.concatenate([fc2[:256], fc2[256:]], axis=1)
+
+
+def attn_grads_kernel(t, xo, xt, dpo, dpt, mo, mt, go, gt, keep, send):
+    dpacked = jnp.concatenate([dpo[0], dpt[0]], axis=0)
+    mixed_t = jnp.concatenate([mo[...], mt[...]], axis=0).T
+    for i, (kc, ky) in enumerate(PAIRS):
+        x_t = jnp.concatenate([lanes(xo, t[i]), lanes(xt, t[i])], axis=0).T
+        grad = jnp.concatenate([lanes(go, t[i]), lanes(gt, t[i])], axis=0)
+        out = (keep, send)[kc]
+        proj = nn(mixed_t, grad).astype(bf16)
+        side = jnp.concatenate([proj[:, :128], proj[:, 128:]], axis=0)
+        out[ky, 0] = jnp.concatenate([nn(x_t, dpacked).astype(bf16), side], axis=1)
+
+
+def dmid_kernel(t, part, got, middle, branch, first, second, mod, dmid, out, sums):
+    rows_of = []
+    for i, ref in enumerate((first, second)):
+        rows = slice(i * 128, (i + 1) * 128)
+        dn = part[rows] + got[rows].astype(f32)
+        unit, scale = norm(middle[rows])
+        grad = dn * (1.0 + mod[4:5])
+        back = scale * (
+            grad
+            - jnp.mean(grad, axis=-1, keepdims=True)
+            - unit * jnp.mean(grad * unit, axis=-1, keepdims=True)
+        )
+        dm = ref[...].astype(f32) + back
+        dbranch = (mod[2:3] * dm).astype(bf16)
+        dmid[rows] = dm
+        out[rows] = dbranch
+        rows_of.append(
+            [dn, dn * unit, dm * branch[rows], dbranch.astype(f32)]
+        )
+    sums[...] = jnp.concatenate(
+        [total_rows(a) + total_rows(b) for a, b in zip(*rows_of)] + [jnp.zeros((4, 1024), f32)], axis=0
+    )
+
+
+def out_kernel(t, middle, part, got, first, second, mod, out0, out1, sums):
+    total = jnp.zeros((1, 1024), f32)
+    for i, (ref, out) in enumerate(((first, out0), (second, out1))):
+        rows = slice(i * 128, (i + 1) * 128)
+        branch = part[rows] + got[rows].astype(f32) + mod[7:8]
+        out[...] = (middle[rows] + mod[5:6] * branch).astype(bf16)
+        total = total + total_rows(ref[...].astype(f32) * branch)
+    sums[...] = total
+
+
+def qkv_back_kernel(t, dqo, dqt, n0, n1, f0, f1, wo, wt, packo, packt, sums, outo, outt, acco, acct):
+    j = pl.program_id(0)
+
+    @pl.when(j == 0)
+    def _():
+        acco[...] = jnp.zeros_like(acco)
+        acct[...] = jnp.zeros_like(acct)
+
+    dkv = n0[...].astype(f32) + n1[...].astype(f32) + f0[...].astype(f32) + f1[...].astype(f32)
+    dkv = dkv.astype(bf16)
+    dqs = (dqo[...], dqt[...])
+    packed = [
+        jnp.concatenate([dqs[i], dkv[0, i * 256 : i * 256 + 256], dkv[1, i * 256 : i * 256 + 256]], axis=1)
+        for i in range(2)
+    ]
+    packo[0] = packed[0]
+    packt[0] = packed[1]
+    sums[...] = jnp.concatenate(
+        [
+            total_rows(dqs[0].astype(f32)) + total_rows(dqs[1].astype(f32)),
+            total_rows(dkv[1].astype(f32)),
+            jnp.zeros((6, 128), f32),
+        ],
+        axis=0,
+    )
+    for i, (kc, ky) in enumerate(PAIRS):
+        w = (wo, wt)[kc][ky, 0, :, :384]
+        acco[i] += nt(packed[0], w)
+        acct[i] += nt(packed[1], w)
+
+    @pl.when(j == 3)
+    def _():
+        for i in range(4):
+            where = pl.ds(pl.multiple_of(t[i] * 256, 256), 256)
+            outo[:, where] = acco[i]
+            outt[:, where] = acct[i].astype(bf16)
+
+
+def din_kernel(t, part, got, dmid, first, second, mod, out0, out1, sums):
+    rows_of = []
+    for i, (ref, out) in enumerate(((first, out0), (second, out1))):
+        rows = slice(i * 128, (i + 1) * 128)
+        dn = part[rows] + got[rows].astype(f32)
+        unit, scale = norm(ref[...].astype(f32))
+        grad = dn * (1.0 + mod[1:2])
+        back = scale * (
+            grad
+            - jnp.mean(grad, axis=-1, keepdims=True)
+            - unit * jnp.mean(grad * unit, axis=-1, keepdims=True)
+        )
+        out[...] = (dmid[rows] + back).astype(bf16)
+        rows_of.append([dn, dn * unit])
+    sums[...] = jnp.concatenate([total_rows(a) + total_rows(b) for a, b in zip(*rows_of)], axis=0)
+
+
+def small_kernel(t, din_sums, dgate_mlp, dmid_sums, bfc2, qkv_sums, fc1o, fc1t, out):
+    out[...] = jnp.zeros_like(out)
+    out[0:2] = din_sums[...]
+    out[2:3] = dmid_sums[2:3]
+    out[3:5] = dmid_sums[0:2]
+    out[5:6] = dgate_mlp[...]
+    out[6:7] = dmid_sums[3:4]
+    out[7:8] = bfc2[...]
+    for j in range(4):
+        where = pl.ds(pl.multiple_of(t[4 + j] * 128, 128), 128)
+        out[8:10, where] = qkv_sums[0:2, j * 128 : (j + 1) * 128]
+        fc1 = fc1o[:, j * COLS : (j + 1) * COLS] + fc1t[:, j * COLS : (j + 1) * COLS]
+        for zz in range(4):
+            for xx in range(2):
+                @pl.when((t[8 + j] == zz) & (t[12] == xx))
+                def _(fc1=fc1, zz=zz, xx=xx):
+                    out[10 + zz : 11 + zz, xx * COLS : (xx + 1) * COLS] = fc1
+
+
+def fast_body(
+    tokens, conditioning, cotangent, w_qkv, b_qkv, w_proj, b_proj, w_fc1, b_fc1, w_fc2, b_fc2, w_ada, b_ada
+):
+    y, c = lax.axis_index("y"), lax.axis_index("c")
+    z, x = lax.axis_index("z"), lax.axis_index("x")
+    z0, z1 = z % 2, z // 2
+    D = 1024
+    own = y * 2 + c
+    blocks = [(y ^ ky) * 2 + (c ^ kc) for kc, ky in PAIRS]
+    z_of = [z ^ (kz1 * 2 + kz0) for kz0 in range(2) for kz1 in range(2)]
+    table = jnp.stack(blocks + [zz * 2 + x for zz in z_of] + z_of + [x, own]).astype(jnp.int32)
+    call = functools.partial(kernel_call)
+
+    def flip(v, axis, count, offset):
+        return lax.ppermute(v, axis, [(i, i ^ offset) for i in range(count)])
+
+    def route(k):
+        return [
+            (cc * 4 + zz, (zz // 2) * 4 + cc * 2 + ((zz % 2) ^ k)) for cc in range(2) for zz in range(4)
+        ]
+
+    def spread(array):
+        flat = array.reshape(128, 2 * D)
+        low, high = flat[:, :D], flat[:, D:]
+        first = jnp.where(z0 == 0, low, high)
+        second = jnp.where(z0 == 0, high, low)
+        return [lax.ppermute(p, ("c", "z"), route(k)) for k, p in enumerate((first, second))]
+
+    def collect(pieces, dtype):
+        got = [
+            lax.ppermute(p, ("c", "z"), [(b, a) for a, b in route(k)]) for k, p in enumerate(pieces)
+        ]
+        low = jnp.where(z0 == 0, got[0], got[1])
+        high = jnp.where(z0 == 0, got[1], got[0])
+        return jnp.concatenate([low, high], axis=1).astype(dtype).reshape(128, 2, D)
+
+    def gather_w(block):
+        v = jnp.stack([block, flip(block, "z", 4, 2)])
+        v = jnp.concatenate([v, flip(v, "z", 4, 1)])
+        v = jnp.stack([v, flip(v, "y", 2, 1)])
+        return v, flip(v, "c", 2, 1)
+
+    def reduce_w(keep, send):
+        add = lambda a, b: (a.astype(f32) + b.astype(f32)).astype(bf16)
+        got = flip(send, "c", 2, 1)
+        mine, theirs = add(keep[0], got[0]), add(keep[1], got[1])
+        got = flip(theirs, "y", 2, 1)
+        mine, theirs = add(mine[:2], got[:2]), add(mine[2:], got[2:])
+        got = flip(theirs, "z", 4, 1)
+        mine, theirs = add(mine[0], got[0]), add(mine[1], got[1])
+        return mine.astype(f32) + flip(theirs, "z", 4, 2).astype(f32)
+
+    cond_c = jnp.stack([conditioning, flip(conditioning, "c", 2, 1)])
+    cond_c = jnp.where(c == 0, cond_c, cond_c[::-1])
+    cond_all = jnp.stack([cond_c, flip(cond_c, "y", 2, 1)]).reshape(2, 4, D)
+    act_abs = jax.nn.silu(cond_all.astype(f32)).astype(bf16)
+    act_abs = lax.dynamic_slice_in_dim(act_abs, own * 256, 256, 2)
+    act_here = lax.dynamic_slice_in_dim(act_abs, z, 1, 1)[:, 0]
+    packed_mod = call(
+        mod_kernel,
+        table,
+        [
+            jnp.pad(act_here, ((0, 6), (0, 0))),
+            w_ada,
+            b_ada.reshape(1, -1),
+            b_qkv,
+            b_proj.reshape(1, -1),
+            b_fc1.reshape(1, -1),
+            b_fc2.reshape(1, -1),
+        ],
+        [whole((8, 256)), whole((256, 6144)), whole((1, 1536)), whole((2, 256)), whole((1, 256)), whole((1, 1024)), whole((1, 256))],
+        whole((2, 16, D)),
+        shaped((2, 16, D), f32),
+        flops=2 * 8 * 256 * 6144,
+        name="modulate",
+    )
+    mod = packed_mod[0] + flip(packed_mod[1], "y", 2, 1)
+    mod = mod + flip(mod, "c", 2, 1)
+    mod_spec = whole((16, D))
+
+    tok = spread(tokens)
+    heads = w_qkv.reshape(256, 2, 3, HD).transpose(0, 2, 1, 3).reshape(256, 384)
+    pack_a = jnp.concatenate(
+        [heads, jnp.concatenate([w_proj[:, :128], w_proj[:, 128:]], axis=0)], axis=1
+    )
+    wa = gather_w(pack_a)
+    w1 = gather_w(w_fc1)
+    w2 = gather_w(jnp.concatenate([w_fc2[:256], w_fc2[256:]], axis=1))
+    cot = spread(cotangent)
+
+    half, full = whole((128, D)), whole((256, D))
+    row_b, row_f = shaped((256, D), bf16), shaped((256, D), f32)
+    normed = call(ln_kernel, table, [*tok, mod], [half, half, mod_spec], full, row_b, name="norm_in")
+    normed_t = flip(normed, "x", 2, 1)
+
+    bias_spec = pl.BlockSpec((16, 128), lambda j, t: (0, t[4 + j]))
+    pair_spec = pl.BlockSpec((2, 256, 128), lambda j, t: (0, 0, j))
+
+    def make_qkv(rows):
+        return call(
+            qkv_kernel,
+            table,
+            [rows, *wa, mod],
+            [full, *weight_specs(), bias_spec],
+            [column_spec(128), pair_spec],
+            [shaped((256, 512), bf16), shaped((2, 256, 512), bf16)],
+            steps=4,
+            flops=2 * 256 * 1024 * 1536,
+            name="qkv",
+        )
+
+    q_o, kv_o = make_qkv(normed)
+    far_o = flip(kv_o, "c", 2, 1)
+    q_t, kv_t = make_qkv(normed_t)
+    far_t = flip(kv_t, "c", 2, 1)
+    chunks = [kv_o, kv_t, far_o, far_t]
+    lse_spec = pl.BlockSpec((1, 2, 256), lambda j, t: (j, 0, 0))
+
+    def attend(queries):
+        return call(
+            attn_kernel,
+            table,
+            [queries, *chunks],
+            [column_spec(128)] + [pair_spec] * 4,
+            [column_spec(128), lse_spec],
+            [shaped((256, 512), bf16), shaped((4, 2, 256), f32)],
+            steps=4,
+            flops=4 * 256 * 1024 * 64 * 8 * 4,
+            name="attend",
+        )
+
+    acc_d = pltpu.VMEM((4, 256, 256), f32)
+
+    def project(rows, kind):
+        return call(
+            proj_kernel,
+            table,
+            [rows, *wa],
+            [column_spec(128), *weight_specs()],
+            full,
+            shaped((256, D), kind),
+            steps=4,
+            scratch=[acc_d],
+            flops=2 * 256 * 512 * 1024,
+            name="project",
+        )
+
+    mixed_t, lse_t = attend(q_t)
+    got_branch = flip(project(mixed_t, bf16), "x", 2, 1)
+    mixed_o, lse_o = attend(q_o)
+    branch, middle, normed_mlp = call(
+        mid_kernel,
+        table,
+        [*tok, project(mixed_o, f32), got_branch, mod],
+        [half, half, full, full, mod_spec],
+        [full] * 3,
+        [row_f, row_f, row_b],
+        name="norm_mid",
+    )
+    dmlp_o, bfc2_sum = call(
+        dmlp_kernel, table, [*cot, mod], [half, half, mod_spec], [full, whole((1, D))], [row_b, shaped((1, D), f32)], name="dbranch_mlp"
+    )
+    dmlp_t = flip(dmlp_o, "x", 2, 1)
+    mlp_t = flip(normed_mlp, "x", 2, 1)
+    wide = shaped((256, 2048), bf16)
+    fc1_bias = pl.BlockSpec((16, COLS), lambda j, t: (0, t[12]))
+
+    def up(rows):
+        return call(
+            fc1_kernel,
+            table,
+            [rows, *w1, mod],
+            [full, *weight_specs(), fc1_bias],
+            [column_spec(COLS)] * 2,
+            [wide, wide],
+            steps=4,
+            flops=2 * 256 * 1024 * 2048,
+            name="up",
+        )
+
+    def down(act, kind):
+        return call(
+            fc2_kernel,
+            table,
+            [act, *w2],
+            [column_spec(COLS), *weight_specs()],
+            full,
+            shaped((256, D), kind),
+            steps=4,
+            scratch=[acc_d],
+            flops=2 * 256 * 1024 * 2048,
+            name="down",
+        )
+
+    def mlp_back(grad, slope, kind):
+        return call(
+            mlp_back_kernel,
+            table,
+            [grad, slope, *w2, *w1],
+            [full, column_spec(COLS), *weight_specs(), *weight_specs()],
+            [column_spec(COLS), column_spec(COLS, 1), full],
+            [wide, shaped((1, 2048), f32), shaped((256, D), kind)],
+            steps=4,
+            scratch=[acc_d],
+            flops=4 * 256 * 1024 * 2048,
+            name="mlp_back",
+        )
+
+    act_o, slope_o = up(normed_mlp)
+    act_t, slope_t = up(mlp_t)
+    dh_t, fc1_t, dn_t = mlp_back(dmlp_t, slope_t, bf16)
+    got_dn = flip(dn_t, "x", 2, 1)
+    dh_o, fc1_o, dn_o = mlp_back(dmlp_o, slope_o, f32)
+    got_mlp = flip(down(act_t, bf16), "x", 2, 1)
+    down_o = down(act_o, f32)
+    grad_specs = lambda *tail: pl.BlockSpec((2, 1) + tail, lambda j, t: (0, j) + (0,) * len(tail))
+    mlp_grad = shaped((2, 4, 2, 256, COLS), bf16)
+    keep_m, send_m = call(
+        mlp_grads_kernel,
+        table,
+        [normed_mlp, mlp_t, dh_o, dh_t, act_o, act_t, dmlp_o, dmlp_t],
+        [full, full] + [column_spec(COLS)] * 4 + [full, full],
+        [grad_specs(2, 256, COLS)] * 2,
+        [mlp_grad, mlp_grad],
+        steps=4,
+        flops=8 * 256 * 1024 * 2048,
+        name="mlp_grads",
+    )
+    g_mlp = reduce_w(keep_m, send_m)
+    g_fc1 = g_mlp[0]
+    g_fc2 = jnp.concatenate([g_mlp[1][:, :256], g_mlp[1][:, 256:]], axis=0)
+
+    sums_spec = whole((8, D))
+    dmid, dbr_o, dmid_sums = call(
+        dmid_kernel,
+        table,
+        [dn_o, got_dn, middle, branch, *cot, mod],
+        [full] * 4 + [half, half, mod_spec],
+        [full, full, sums_spec],
+        [row_f, row_b, shaped((8, D), f32)],
+        name="norm_mid_back",
+    )
+    dbr_t = flip(dbr_o, "x", 2, 1)
+    out0, out1, dgate_mlp = call(
+        out_kernel,
+        table,
+        [middle, down_o, got_mlp, *cot, mod],
+        [full] * 3 + [half, half, mod_spec],
+        [half, half, whole((1, D))],
+        [shaped((128, D), bf16)] * 2 + [shaped((1, D), f32)],
+        name="finish",
+    )
+    out = collect([out0, out1], bf16)
+
+    def attend_back(queries, grad, mixed, lse):
+        dmixed = call(
+            proj_back_kernel,
+            table,
+            [grad, *wa],
+            [full, *weight_specs()],
+            column_spec(128),
+            shaped((256, 512), bf16),
+            steps=4,
+            flops=2 * 256 * 512 * 1024,
+            name="project_back",
+        )
+        long_spec = pl.BlockSpec((2, 512, 128), lambda j, t: (0, 0, j))
+        return call(
+            attn_back_kernel,
+            table,
+            [queries, dmixed, mixed, lse, *chunks],
+            [column_spec(128)] * 3 + [lse_spec] + [pair_spec] * 4,
+            [column_spec(128), long_spec, long_spec],
+            [shaped((256, 512), bf16), shaped((2, 512, 512), bf16), shaped((2, 512, 512), bf16)],
+            steps=4,
+            flops=10 * 256 * 1024 * 64 * 8 * 4,
+            name="attend_back",
+        )
+
+    dq_o, near_o, away_o = attend_back(q_o, dbr_o, mixed_o, lse_o)
+    back_o = flip(away_o, "c", 2, 1)
+    dq_t, near_t, away_t = attend_back(q_t, dbr_t, mixed_t, lse_t)
+    back_t = flip(away_t, "c", 2, 1)
+    long_spec = pl.BlockSpec((2, 512, 128), lambda j, t: (0, 0, j))
+    pack_spec = pl.BlockSpec((1, 256, 384), lambda j, t: (j, 0, 0))
+    pack_o, pack_t, qkv_sums, din_o, din_t = call(
+        qkv_back_kernel,
+        table,
+        [dq_o, dq_t, near_o, near_t, back_o, back_t, *wa],
+        [column_spec(128)] * 2 + [long_spec] * 4 + weight_specs(),
+        [pack_spec, pack_spec, pl.BlockSpec((8, 128), lambda j, t: (0, j)), full, full],
+        [shaped((4, 256, 384), bf16)] * 2 + [shaped((8, 512), f32), row_f, row_b],
+        steps=4,
+        scratch=[acc_d, acc_d],
+        flops=4 * 256 * 1024 * 1536,
+        name="qkv_back",
+    )
+    got_din = flip(din_t, "x", 2, 1)
+    attn_grad = shaped((2, 4, 256, COLS), bf16)
+    keep_a, send_a = call(
+        attn_grads_kernel,
+        table,
+        [normed, normed_t, pack_o, pack_t, mixed_o, mixed_t, dbr_o, dbr_t],
+        [full, full, pack_spec, pack_spec, column_spec(128), column_spec(128), full, full],
+        [grad_specs(256, COLS)] * 2,
+        [attn_grad, attn_grad],
+        steps=4,
+        flops=4 * 256 * 1024 * 2048,
+        name="attn_grads",
+    )
+    g_a = reduce_w(keep_a, send_a)
+    g_qkv = g_a[:, :384].reshape(256, 3, 2, HD).transpose(0, 2, 1, 3).reshape(256, 2, 3 * HD)
+    g_proj = jnp.concatenate([g_a[:128, 384:], g_a[128:, 384:]], axis=1)
+    dt0, dt1, din_sums = call(
+        din_kernel,
+        table,
+        [din_o, got_din, dmid, *tok, mod],
+        [full] * 3 + [half, half, mod_spec],
+        [half, half, whole((2, D))],
+        [shaped((128, D), bf16)] * 2 + [shaped((2, D), f32)],
+        name="norm_in_back",
+    )
+    d_tokens = collect([dt0, dt1], f32)
+
+    small = call(
+        small_kernel,
+        table,
+        [din_sums, dgate_mlp, dmid_sums, bfc2_sum, qkv_sums, fc1_o, fc1_t],
+        [whole((2, D)), whole((1, D)), sums_spec, whole((1, D)), whole((8, 512)), whole((1, 2048)), whole((1, 2048))],
+        whole((16, D)),
+        shaped((16, D), f32),
+        name="small",
+    )
+    small = small + flip(small, "x", 2, 1)
+    small = small + flip(small, "c", 2, 1)
+    for axis, count, offset in (("z", 4, 2), ("z", 4, 1), ("y", 2, 1)):
+        got = flip(small, axis, count, offset)
+        small = jnp.concatenate([small[:-10], got[:-10], small[-10:] + got[-10:]])
+    bias_sum = small[-10:]
+    dmod_all = small[:-10].reshape(8, 6 * D)
+    take = lambda v, n: lax.dynamic_slice_in_dim(v.reshape(-1), own * n, n, 0)
+    out_bproj, out_bfc2 = take(bias_sum[0], 256), take(bias_sum[1], 256)
+    out_bqkv = lax.dynamic_slice_in_dim(bias_sum[2:4], own * 256, 256, 1)
+    out_bfc1 = take(bias_sum[4:8], 1024)
+    out_bada = take(jnp.sum(dmod_all, axis=0), 1536)
+    act_rel = jnp.swapaxes(flip_bits(act_abs, 1, 4, z).reshape(2, 2, 2, 256), 1, 2).reshape(8, 256)
+    dmod_cols = lax.dynamic_slice_in_dim(dmod_all, (z * 2 + x) * 768, 768, 1)
+    out_ada = dot(
+        jnp.concatenate([act_rel] * 3), jnp.concatenate(split_three(dmod_cols)), ((0,), (0,))
+    )
+    dact = dot(jnp.concatenate(split_three(dmod_all)), w_ada, ((1,), (1,)))
+    dact = dact[:8] + dact[8:16] + dact[16:]
+    dact = jnp.swapaxes(dact.reshape(2, 2, 2, 256), 1, 2).reshape(2, 4, 256)
+    dact = flip_bits(dact, 1, 4, z)
+    dact = jnp.stack([dact[0], flip(dact[1], "y", 2, 1)]).reshape(2, 2, 2, 256)
+    dact = jnp.where(c == 0, dact, dact[:, ::-1])
+    dact = jnp.stack([dact[:, 0], flip(dact[:, 1], "c", 2, 1)], axis=1)
+    dact = flip_bits(flip_bits(dact, 0, 2, y), 1, 2, c).transpose(2, 0, 1, 3).reshape(2, D)
+    d_cond = jax.vjp(jax.nn.silu, conditioning.astype(f32))[1](dact)[0]
+    return (
+        out,
+        d_tokens,
+        d_cond,
+        g_qkv,
+        out_bqkv,
+        g_proj,
+        out_bproj,
+        g_fc1,
+        out_bfc1,
+        g_fc2,
+        out_bfc2,
+        out_ada,
+        out_bada,
+    )
+
+
 def solution(mesh):
     dp, tensor = mesh.shape["dp"], mesh.shape["tensor"]
     ny, nx = dp // NC, tensor // NZ
@@ -429,6 +1200,7 @@
         P(rows, cols),
         P(rows),
     )
+    body = fast_body if (ny, nx) == (2, 2) else make_body(ny, nx)
     return jax.shard_map(
-        make_body(ny, nx), mesh=fine, in_specs=placed, out_specs=out_placed, check_vma=False
-    )
+        body, mesh=fine, in_specs=placed, out_specs=out_placed, check_vma=False
+    )

time: 640 us -> 501 us (0.78)
  Pallas kernels: 0 us -> 167 us
  local copies, waits for them, and re-layouts: 140 us -> 24.5 us
  other arithmetic: 135 us -> 36.6 us
  matrix products: 83.2 us -> 2.11 us
  starting transfers between devices: 106 us -> 66 us
  waiting for transfers between devices: 165 us -> 201 us
    pallas_call x0 -> x27, Pallas kernels: none -> 167 us  [kernel_call(): pl.pallas_call(body, grid_spec=pltpu.PrefetchScalarGridSpec(num_scalar_pr...]
    dot_general x17 -> x2, matrix products: 51.4 us -> 2.11 us  [dot(): return lax.dot_general(a, b, (dims, ((), ())), preferred_element_type=f32)]
    ppermute x70 -> x51, starting transfers between devices: 106 us -> 66 us  [the longest x43 57.5 us: flip(): return lax.ppermute(v, axis, [(i, i ^ offset) for i in range(count)])]
    ppermute x70 -> x51, waiting for transfers between devices: 165 us -> 201 us  [the longest x43 188 us: flip(): return lax.ppermute(v, axis, [(i, i ^ offset) for i in range(count)])]
    another operation x38 -> x14, other arithmetic: 50.8 us -> 15.8 us  [the longest x6 12.1 us: gather_w(): v = jnp.stack([v, flip(v, 'y', 2, 1)])]
    dot_general x6 -> x0, matrix products: 31.8 us -> none  [the longest x1 11.5 us: attn_backward(): dprobs = jnp.einsum('sqhe,skhe->shqk', gh, vh, preferred_element_type=f32)]
    rev x9 -> x0, local copies, waits for them, and re-layouts: 23.1 us -> none  [flip_bits(): swapped = jnp.flip(view, axis=axis + 1)]
    dot_general x7 -> x0, local copies, waits for them, and re-layouts: 22.3 us -> none  [dot(): return lax.dot_general(a, b, (dims, ((), ())), preferred_element_type=f32)]
  transfers between devices with their start and end apart: 70 -> 51, of which waited for: 22 -> 21; matrix products, arithmetic and copies ran while one was open for 48% -> 10% of each run, Pallas kernels for 0% -> 31%
where the time goes in v2:
time: 501 us; the launch traced here: 499 us
  waiting for transfers between devices  201 us (40%)
  Pallas kernels  167 us (33%)
  starting transfers between devices  66 us (13%)
  other arithmetic  36.6 us (7%)
  local copies, waits for them, and re-layouts  24.5 us (5%)
    ppermute x43, waiting for transfers between devices, flip(): return lax.ppermute(v, axis, [(i, i ^ offset) for i in range(count)])  188 us
    pallas_call x27, Pallas kernels, kernel_call(): pl.pallas_call(body, grid_spec=pltpu.PrefetchScalarGridSpec(num_scalar_pr...  167 us
    ppermute x43, starting transfers between devices, flip(): return lax.ppermute(v, axis, [(i, i ^ offset) for i in range(count)])  57.5 us
    convert_element_type x6, other arithmetic, reduce_w(): add = lambda a, b: (a.astype(f32) + b.astype(f32)).astype(bf16)  13.2 us
    unnamed x76, local copies, waits for them, and re-layouts  12.8 us
    another operation x6, other arithmetic, gather_w(): v = jnp.stack([v, flip(v, 'y', 2, 1)])  12.1 us
  transfers between devices with their start and end apart: 51, of which 21 were waited for; matrix products, arithmetic and copies ran while one was open for 10% of the time, Pallas kernels for 31%

profile of v2, /device:TPU:0, one launch (start us, length us, event | category | flops | bytes accessed | tf_op | source)
XLA Modules:
  0.0 498.6 jit_solution(14969664961681840321)
XLA Ops:
  6.7 11.9 %collective-permute-done.6 = bf16[256,512]{1,0:T(8,128)(2,1)S(1)} collective-permute-done((bf16[256,512]{1,0:T(8,128)(2,1)S(1)}, bf16[256,512]{1,0:T(8,128)(2,1)S(1)}, u32[]{:S(2)}, u32[]{:S(2)}) %collective-permute-start.6) | collective-permute-done | bytes 262176 | tf_op jit(solution)/shard_map/ppermute | solution.py:806
  19.5 12.4 %collective-permute-done.7 = bf16[2,256,512]{2,1,0:T(8,128)(2,1)S(1)} collective-permute-done((bf16[2,256,512]{2,1,0:T(8,128)(2,1)S(1)}, bf16[2,256,512]{2,1,0:T(8,128)(2,1)S(1)}, u32[]{:S(2)}, u32[]{:S(2)}) %collective-permute-start.7) | collective-permute-done | bytes 524320 | tf_op jit(solution)/shard_map/ppermute | solution.py:806
  38.2 17.0 %collective-permute-done.14 = bf16[256,512]{1,0:T(8,128)(2,1)S(1)} collective-permute-done((bf16[256,512]{1,0:T(8,128)(2,1)S(1)}, bf16[256,512]{1,0:T(8,128)(2,1)S(1)}, u32[]{:S(2)}, u32[]{:S(2)}) %collective-permute-start.14) | collective-permute-done | bytes 262176 | tf_op jit(solution)/shard_map/ppermute | solution.py:806
  76.4 6.7 %collective-permute-done.19 = bf16[2,256,512]{2,1,0:T(8,128)(2,1)} collective-permute-done((bf16[2,256,512]{2,1,0:T(8,128)(2,1)}, bf16[2,256,512]{2,1,0:T(8,128)(2,1)}, u32[]{:S(2)}, u32[]{:S(2)}) %collective-permute-start.19) | collective-permute-done | bytes 524320 | tf_op jit(solution)/shard_map/ppermute | solution.py:806
  86.3 15.7 %collective-permute-done.4 = f32[16,1024]{1,0:T(8,128)S(1)} collective-permute-done((f32[16,1024]{1,0:T(8,128)S(1)}, f32[16,1024]{1,0:T(8,128)S(1)}, u32[]{:S(2)}, u32[]{:S(2)}) %collective-permute-start.4) | collective-permute-done | bytes 65568 | tf_op jit(solution)/shard_map/ppermute | solution.py:806
  104.0 7.5 %collective-permute-done.1.second = bf16[128,1024]{1,0:T(8,128)(2,1)} collective-permute-done((bf16[128,1024]{1,0:T(8,128)(2,1)S(1)}, bf16[128,1024]{1,0:T(8,128)(2,1)}, u32[]{:S(2)}, u32[]{:S(2)}) %collective-permute-start.1) | collective-permute-done | bytes 262176 | tf_op jit(solution)/shard_map/ppermute | solution.py:818
  118.6 5.8 %collective-permute-start.17 = (bf16[2,4,256,512]{3,2,1,0:T(8,128)(2,1)}, bf16[2,4,256,512]{3,2,1,0:T(8,128)(2,1)}, u32[]{:S(2)}, u32[]{:S(2)}) collective-permute-start(bf16[2,4,256,512]{3,2,1,0:T(8,128)(2,1)} %pad_maximum_fusion.1.wo.w1o), channel_id=1, source_target_pairs={{0,8},{8,0},{1,9},{9,1},{2,10},{10,2},{3,11},{11,3},{4,12},{12,4},... | collective-permute-start | bytes 6291464 | tf_op jit(solution)/shard_map/ppermute | solution.py:806
  127.3 5.6 %qkv.3 = (bf16[256,512]{1,0:T(8,128)(2,1)}, bf16[2,256,512]{2,1,0:T(8,128)(2,1)}) custom-call(s32[14]{0:T(128)} %stack.140.t, bf16[256,1024]{1,0:T(8,128)(2,1)} %collective-permute-done.10.x.xt, bf16[2,4,256,512]{3,2,1,0:T(8,128)(2,1)} %copy-done, bf16[2,4,256,512]{3,2,1,0:T(8,128)(2,1)} %collective-permute-done.9.wt, f32[16,1024]{1,0:T(8,128)} %add.167.mod.bias), custom_call_target="tpu_custom_call" | custom-call | flops 805306368 | bytes 5570560 | tf_op jit(solution)/shard_map/qkv/pallas_call | solution.py:430
  134.9 5.6 %qkv.2 = (bf16[256,512]{1,0:T(8,128)(2,1)}, bf16[2,256,512]{2,1,0:T(8,128)(2,1)}) custom-call(s32[14]{0:T(128)} %stack.140.t, bf16[256,1024]{1,0:T(8,128)(2,1)} %norm_in.1.x.xo, bf16[2,4,256,512]{3,2,1,0:T(8,128)(2,1)} %copy-done, bf16[2,4,256,512]{3,2,1,0:T(8,128)(2,1)} %collective-permute-done.9.wt, f32[16,1024]{1,0:T(8,128)} %add.167.mod.bias), custom_call_target="tpu_custom_call" | custom-call | flops 805306368 | bytes 5570560 | tf_op jit(solution)/shard_map/qkv/pallas_call | solution.py:430
  143.3 8.8 %attend.3 = (bf16[256,512]{1,0:T(8,128)(2,1)}, f32[4,2,256]{2,1,0:T(2,128)}) custom-call(s32[14]{0:T(128)} %stack.140.t, bf16[256,512]{1,0:T(8,128)(2,1)} %get-tuple-element.64.q, bf16[2,256,512]{2,1,0:T(8,128)(2,1)} %get-tuple-element.61.a, bf16[2,256,512]{2,1,0:T(8,128)(2,1)} %get-tuple-element.62.b, bf16[2,256,512]{2,1,0:T(8,128)(2,1)} %copy-done.30, ...), custom_call_target="tpu_custom_call" | custom-call | flops 2147483648 | bytes 2629632 | tf_op jit(solution)/shard_map/attend/pallas_call | solution.py:430
  152.1 5.2 %project.3 = bf16[256,1024]{1,0:T(8,128)(2,1)} custom-call(s32[14]{0:T(128)} %stack.140.t, bf16[256,512]{1,0:T(8,128)(2,1)} %get-tuple-element.65.mixed.mt, bf16[2,4,256,512]{3,2,1,0:T(8,128)(2,1)} %copy-done, bf16[2,4,256,512]{3,2,1,0:T(8,128)(2,1)} %collective-permute-done.9.wt), custom_call_target="tpu_custom_call" | custom-call | flops 268435456 | bytes 4980736 | tf_op jit(solution)/shard_map/project/pallas_call | solution.py:430
  162.5 8.8 %attend.2 = (bf16[256,512]{1,0:T(8,128)(2,1)}, f32[4,2,256]{2,1,0:T(2,128)}) custom-call(s32[14]{0:T(128)} %stack.140.t, bf16[256,512]{1,0:T(8,128)(2,1)} %get-tuple-element.60.q, bf16[2,256,512]{2,1,0:T(8,128)(2,1)} %get-tuple-element.61.a, bf16[2,256,512]{2,1,0:T(8,128)(2,1)} %get-tuple-element.62.b, bf16[2,256,512]{2,1,0:T(8,128)(2,1)} %copy-done.30, ...), custom_call_target="tpu_custom_call" | custom-call | flops 2147483648 | bytes 2629632 | tf_op jit(solution)/shard_map/attend/pallas_call | solution.py:430
  171.3 5.3 %project.2.part = f32[256,1024]{1,0:T(8,128)} custom-call(s32[14]{0:T(128)} %stack.140.t, bf16[256,512]{1,0:T(8,128)(2,1)} %get-tuple-element.63.mixed.mo, bf16[2,4,256,512]{3,2,1,0:T(8,128)(2,1)} %copy-done, bf16[2,4,256,512]{3,2,1,0:T(8,128)(2,1)} %collective-permute-done.9.wt), custom_call_target="tpu_custom_call" | custom-call | flops 268435456 | bytes 5505024 | tf_op jit(solution)/shard_map/project/pallas_call | solution.py:430
  187.5 6.4 %collective-permute-done.22.x.xt = bf16[256,1024]{1,0:T(8,128)(2,1)S(1)} collective-permute-done((bf16[256,1024]{1,0:T(8,128)(2,1)}, bf16[256,1024]{1,0:T(8,128)(2,1)S(1)}, u32[]{:S(2)}, u32[]{:S(2)}) %collective-permute-start.22) | collective-permute-done | bytes 524320 | tf_op jit(solution)/shard_map/ppermute | solution.py:806
  194.7 6.5 %up.3 = (bf16[256,2048]{1,0:T(8,128)(2,1)}, bf16[256,2048]{1,0:T(8,128)(2,1)}) custom-call(s32[14]{0:T(128)} %stack.140.t, bf16[256,1024]{1,0:T(8,128)(2,1)} %copy-done.14, bf16[2,4,256,512]{3,2,1,0:T(8,128)(2,1)} %pad_maximum_fusion.1.wo.w1o, bf16[2,4,256,512]{3,2,1,0:T(8,128)(2,1)} %collective-permute-done.17.wt.w1t, f32[16,1024]{1,0:T(8,128)} %add.167.mod.bias), custom_call_target="tpu_custom_call" | custom-call | flops 1073741824 | bytes 6881280 | tf_op jit(solution)/shard_map/up/pallas_call | solution.py:430
  205.9 8.0 %mlp_back.3 = (bf16[256,2048]{1,0:T(8,128)(2,1)}, f32[1,2048]{1,0:T(1,128)}, bf16[256,1024]{1,0:T(8,128)(2,1)}) custom-call(s32[14]{0:T(128)} %stack.140.t, bf16[256,1024]{1,0:T(8,128)(2,1)} %copy-done.15, bf16[256,2048]{1,0:T(8,128)(2,1)} %get-tuple-element.75.slope, bf16[2,4,256,512]{3,2,1,0:T(8,128)(2,1)} %pad_maximum_fusion.2.wo.w2o, ...), custom_call_target="tpu_custom_call" | custom-call | flops 2147483648 | bytes 11542528 | tf_op jit(solution)/shard_map/mlp_back/pallas_call | solution.py:430
  214.6 6.6 %up.2 = (bf16[256,2048]{1,0:T(8,128)(2,1)}, bf16[256,2048]{1,0:T(8,128)(2,1)}) custom-call(s32[14]{0:T(128)} %stack.140.t, bf16[256,1024]{1,0:T(8,128)(2,1)} %get-tuple-element.67.x.xo, bf16[2,4,256,512]{3,2,1,0:T(8,128)(2,1)} %pad_maximum_fusion.1.wo.w1o, bf16[2,4,256,512]{3,2,1,0:T(8,128)(2,1)} %collective-permute-done.17.wt.w1t, f32[16,1024]{1,0:T(8,128)} %add.167.mod.bias), custom_call_target="tpu_custom_call" | custom-call | flops 1073741824 | bytes 6881280 | tf_op jit(solution)/shard_map/up/pallas_call | solution.py:430
  221.1 8.2 %mlp_back.2 = (bf16[256,2048]{1,0:T(8,128)(2,1)}, f32[1,2048]{1,0:T(1,128)}, f32[256,1024]{1,0:T(8,128)}) custom-call(s32[14]{0:T(128)} %stack.140.t, bf16[256,1024]{1,0:T(8,128)(2,1)} %get-tuple-element.72.grad.go, bf16[256,2048]{1,0:T(8,128)(2,1)} %get-tuple-element.73.slope, bf16[2,4,256,512]{3,2,1,0:T(8,128)(2,1)} %pad_maximum_fusion.2.wo.w2o, ...), custom_call_target="tpu_custom_call" | custom-call | flops 2147483648 | bytes 12066816 | tf_op jit(solution)/shard_map/mlp_back/pallas_call | solution.py:430
  241.8 10.8 %attend_back.2 = (bf16[256,512]{1,0:T(8,128)(2,1)}, bf16[2,512,512]{2,1,0:T(8,128)(2,1)}, bf16[2,512,512]{2,1,0:T(8,128)(2,1)}) custom-call(s32[14]{0:T(128)} %stack.140.t, bf16[256,512]{1,0:T(8,128)(2,1)} %get-tuple-element.60.q, bf16[256,512]{1,0:T(8,128)(2,1)} %project_back.2.do, bf16[256,512]{1,0:T(8,128)(2,1)} %get-tuple-element.63.mixed.mo, ...), custom_call_target="tpu_custom_call" | custom-call | flops 5368709120 | bytes 5251072 | tf_op jit(solution)/shard_map/attend_back/pallas_call | solution.py:430
  255.2 5.3 %project_back.3.do = bf16[256,512]{1,0:T(8,128)(2,1)} custom-call(s32[14]{0:T(128)} %stack.140.t, bf16[256,1024]{1,0:T(8,128)(2,1)} %copy-done.13, bf16[2,4,256,512]{3,2,1,0:T(8,128)(2,1)} %copy-done, bf16[2,4,256,512]{3,2,1,0:T(8,128)(2,1)} %collective-permute-done.9.wt), custom_call_target="tpu_custom_call" | custom-call | flops 268435456 | bytes 4980736 | tf_op jit(solution)/shard_map/project_back/pallas_call | solution.py:430
  260.5 10.8 %attend_back.3 = (bf16[256,512]{1,0:T(8,128)(2,1)}, bf16[2,512,512]{2,1,0:T(8,128)(2,1)}, bf16[2,512,512]{2,1,0:T(8,128)(2,1)}) custom-call(s32[14]{0:T(128)} %stack.140.t, bf16[256,512]{1,0:T(8,128)(2,1)} %get-tuple-element.64.q, bf16[256,512]{1,0:T(8,128)(2,1)} %project_back.3.do, bf16[256,512]{1,0:T(8,128)(2,1)} %get-tuple-element.65.mixed.mt, ...), custom_call_target="tpu_custom_call" | custom-call | flops 5368709120 | bytes 5251072 | tf_op jit(solution)/shard_map/attend_back/pallas_call | solution.py:430
  271.4 5.6 %down.3 = bf16[256,1024]{1,0:T(8,128)(2,1)} custom-call(s32[14]{0:T(128)} %stack.140.t, bf16[256,2048]{1,0:T(8,128)(2,1)} %get-tuple-element.69.act.actt, bf16[2,4,256,512]{3,2,1,0:T(8,128)(2,1)} %pad_maximum_fusion.2.wo.w2o, bf16[2,4,256,512]{3,2,1,0:T(8,128)(2,1)} %collective-permute-done.21.wt.w2t), custom_call_target="tpu_custom_call" | custom-call | flops 1073741824 | bytes 5767168 | tf_op jit(solution)/shard_map/down/pallas_call | solution.py:430
  277.5 10.2 %mlp_grads.1 = (bf16[2,4,2,256,512]{4,3,2,1,0:T(8,128)(2,1)}, bf16[2,4,2,256,512]{4,3,2,1,0:T(8,128)(2,1)}) custom-call(s32[14]{0:T(128)} %stack.140.t, bf16[256,1024]{1,0:T(8,128)(2,1)} %get-tuple-element.67.x.xo, bf16[256,1024]{1,0:T(8,128)(2,1)} %copy-done.14, bf16[256,2048]{1,0:T(8,128)(2,1)} %get-tuple-element.103.dho, ...), custom_call_target="tpu_custom_call" | custom-call | flops 4294967296 | bytes 14680064 | tf_op jit(solution)/shard_map/mlp_grads/pallas_call | solution.py:430
  289.2 8.4 %qkv_back.1 = (bf16[4,256,384]{2,1,0:T(8,128)(2,1)}, bf16[4,256,384]{2,1,0:T(8,128)(2,1)}, f32[8,512]{1,0:T(8,128)}, f32[256,1024]{1,0:T(8,128)}, bf16[256,1024]{1,0:T(8,128)(2,1)}) custom-call(s32[14]{0:T(128)} %stack.140.t, bf16[256,512]{1,0:T(8,128)(2,1)} %get-tuple-element.80.dqo, bf16[256,512]{1,0:T(8,128)(2,1)} %get-tuple-element.82.dqt, ...), custom_call_target="tpu_custom_call" | custom-call | flops 1610612736 | bytes 12075008 | tf_op jit(solution)/shard_map/qkv_back/pallas_call | solution.py:430
  299.2 5.9 %down.2.part = f32[256,1024]{1,0:T(8,128)} custom-call(s32[14]{0:T(128)} %stack.140.t, bf16[256,2048]{1,0:T(8,128)(2,1)} %get-tuple-element.68.act.acto, bf16[2,4,256,512]{3,2,1,0:T(8,128)(2,1)} %pad_maximum_fusion.2.wo.w2o, bf16[2,4,256,512]{3,2,1,0:T(8,128)(2,1)} %collective-permute-done.21.wt.w2t), custom_call_target="tpu_custom_call" | custom-call | flops 1073741824 | bytes 6291456 | tf_op jit(solution)/shard_map/down/pallas_call | solution.py:430
  335.2 8.0 %attn_grads.1 = (bf16[2,4,256,512]{3,2,1,0:T(8,128)(2,1)}, bf16[2,4,256,512]{3,2,1,0:T(8,128)(2,1)}) custom-call(s32[14]{0:T(128)} %stack.140.t, bf16[256,1024]{1,0:T(8,128)(2,1)} %norm_in.1.x.xo, bf16[256,1024]{1,0:T(8,128)(2,1)} %collective-permute-done.10.x.xt, bf16[4,256,384]{2,1,0:T(8,128)(2,1)} %get-tuple-element.99.dpo, ...), custom_call_target="tpu_custom_call" | custom-call | flops 2147483648 | bytes 8388608 | tf_op jit(solution)/shard_map/attn_grads/pallas_call | solution.py:430
  365.8 39.3 %collective-permute-done.41 = f32[4,256]{1,0:T(4,128)S(1)} collective-permute-done((f32[4,256]{1,0:T(4,128)S(1)}, f32[4,256]{1,0:T(4,128)S(1)}, u32[]{:S(2)}, u32[]{:S(2)}) %collective-permute-start.41) | collective-permute-done | bytes 4128 | tf_op jit(solution)/shard_map/ppermute | solution.py:806
  408.5 5.3 %collective-permute-start.42 = (f32[2,2,256]{2,1,0:T(2,128)S(1)}, f32[2,2,256]{2,1,0:T(2,128)S(1)}, u32[]{:S(2)}, u32[]{:S(2)}) collective-permute-start(f32[2,2,256]{2,1,0:T(2,128)S(1)} %get-tuple-element.192), channel_id=1, source_target_pairs={{0,8},{8,0},{1,9},{9,1},{2,10},{10,2},{3,11},{11,3},{4,12},{12,4},... | collective-permute-start | bytes 12296 | tf_op jit(solution)/shard_map/ppermute | solution.py:806
  421.6 8.0 %collective-permute-done.44 = bf16[4,256,512]{2,1,0:T(8,128)(2,1)S(1)} collective-permute-done((bf16[4,256,512]{2,1,0:T(8,128)(2,1)S(1)}, bf16[4,256,512]{2,1,0:T(8,128)(2,1)S(1)}, u32[]{:S(2)}, u32[]{:S(2)}) %collective-permute-start.44) | collective-permute-done | bytes 1048608 | tf_op jit(solution)/shard_map/ppermute | solution.py:806
  431.3 25.0 %collective-permute-done.45 = bf16[2,256,512]{2,1,0:T(8,128)(2,1)S(1)} collective-permute-done((bf16[2,256,512]{2,1,0:T(8,128)(2,1)}, bf16[2,256,512]{2,1,0:T(8,128)(2,1)S(1)}, u32[]{:S(2)}, u32[]{:S(2)}) %collective-permute-start.45) | collective-permute-done | bytes 524320 | tf_op jit(solution)/shard_map/ppermute | solution.py:806
  462.4 21.8 %collective-permute-done.46 = bf16[256,512]{1,0:T(8,128)(2,1)S(1)} collective-permute-done((bf16[256,512]{1,0:T(8,128)(2,1)S(1)}, bf16[256,512]{1,0:T(8,128)(2,1)S(1)}, u32[]{:S(2)}, u32[]{:S(2)}) %collective-permute-start.46) | collective-permute-done | bytes 262176 | tf_op jit(solution)/shard_map/ppermute | solution.py:806
  486.9 8.5 %collective-permute-done.50 = bf16[2,256,512]{2,1,0:T(8,128)(2,1)} collective-permute-done((bf16[2,256,512]{2,1,0:T(8,128)(2,1)}, bf16[2,256,512]{2,1,0:T(8,128)(2,1)}, u32[]{:S(2)}, u32[]{:S(2)}) %collective-permute-start.50) | collective-permute-done | bytes 524320 | tf_op jit(solution)/shard_map/ppermute | solution.py:806
  (271 shorter events, 172.6 us)
Async XLA Ops:
  2.6 16.1 %collective-permute-start.6 = (bf16[256,512]{1,0:T(8,128)(2,1)S(1)}, bf16[256,512]{1,0:T(8,128)(2,1)S(1)}, u32[]{:S(2)}, u32[]{:S(2)}) collective-permute-start(bf16[256,512]{1,0:T(8,128)(2,1)S(1)} %get-tuple-element.179), channel_id=1, source_target_pairs={{0,4},{2,6},{4,0},{6,2},{1,5},{3,7},{5,1},{7,3},{8,12},{10,14},{12... | collective-permute-start | bytes 786440 | tf_op jit(solution)/shard_map/ppermute | solution.py:806
  32.1 28.6 %collective-permute-start.8 = (bf16[4,256,512]{2,1,0:T(8,128)(2,1)S(1)}, bf16[4,256,512]{2,1,0:T(8,128)(2,1)}, u32[]{:S(2)}, u32[]{:S(2)}) collective-permute-start(bf16[4,256,512]{2,1,0:T(8,128)(2,1)S(1)} %get-tuple-element.161), channel_id=1, source_target_pairs={{0,16},{16,0},{1,17},{17,1},{2,18},{18,2},{3,19},{19,3},{4,20},{20... | collective-permute-start | bytes 3145736 | tf_op jit(solution)/shard_map/ppermute | solution.py:806
  33.5 21.8 %collective-permute-start.14 = (bf16[256,512]{1,0:T(8,128)(2,1)S(1)}, bf16[256,512]{1,0:T(8,128)(2,1)S(1)}, u32[]{:S(2)}, u32[]{:S(2)}) collective-permute-start(bf16[256,512]{1,0:T(8,128)(2,1)S(1)} %copy-done.10), channel_id=1, source_target_pairs={{0,4},{2,6},{4,0},{6,2},{1,5},{3,7},{5,1},{7,3},{8,12},{10,14},{12... | collective-permute-start | bytes 786440 | tf_op jit(solution)/shard_map/ppermute | solution.py:806
  37.6 24.5 %collective-permute-start.18 = (bf16[256,512]{1,0:T(8,128)(2,1)}, bf16[256,512]{1,0:T(8,128)(2,1)}, u32[]{:S(2)}, u32[]{:S(2)}) collective-permute-start(bf16[256,512]{1,0:T(8,128)(2,1)} %get-tuple-element.175), channel_id=1, source_target_pairs={{0,4},{2,6},{4,0},{6,2},{1,5},{3,7},{5,1},{7,3},{8,12},{10,14},{12... | collective-permute-start | bytes 786440 | tf_op jit(solution)/shard_map/ppermute | solution.py:806
  37.7 22.9 %collective-permute-start.3 = (bf16[2,2,1024]{2,1,0:T(2,128)(2,1)S(1)}, bf16[2,2,1024]{2,1,0:T(2,128)(2,1)S(1)}, u32[]{:S(2)}, u32[]{:S(2)}) collective-permute-start(bf16[2,2,1024]{2,1,0:T(2,128)(2,1)S(1)} %broadcast_select_fusion.6), channel_id=1, source_target_pairs={{0,16},{16,0},{1,17},{17,1},{2,18},{18,2},{3,19},{19,3},{4,20},{20... | collective-permute-start | bytes 24584 | tf_op jit(solution)/shard_map/ppermute | solution.py:806
  56.1 15.9 %collective-permute-start.15 = (bf16[2,256,512]{2,1,0:T(8,128)(2,1)}, bf16[2,256,512]{2,1,0:T(8,128)(2,1)}, u32[]{:S(2)}, u32[]{:S(2)}) collective-permute-start(bf16[2,256,512]{2,1,0:T(8,128)(2,1)} %pad_maximum_fusion.7), channel_id=1, source_target_pairs={{0,2},{2,0},{4,6},{6,4},{1,3},{3,1},{5,7},{7,5},{8,10},{10,8},{12,... | collective-permute-start | bytes 1572872 | tf_op jit(solution)/shard_map/ppermute | solution.py:806
  62.1 65.2 %collective-permute-start.9 = (bf16[2,4,256,512]{3,2,1,0:T(8,128)(2,1)S(1)}, bf16[2,4,256,512]{3,2,1,0:T(8,128)(2,1)}, u32[]{:S(2)}, u32[]{:S(2)}) collective-permute-start(bf16[2,4,256,512]{3,2,1,0:T(8,128)(2,1)S(1)} %pad_maximum_fusion.wo), channel_id=1, source_target_pairs={{0,8},{8,0},{1,9},{9,1},{2,10},{10,2},{3,11},{11,3},{4,12},{12,4},... | collective-permute-start | bytes 6291464 | tf_op jit(solution)/shard_map/ppermute | solution.py:806
  64.2 19.0 %collective-permute-start.19 = (bf16[2,256,512]{2,1,0:T(8,128)(2,1)}, bf16[2,256,512]{2,1,0:T(8,128)(2,1)}, u32[]{:S(2)}, u32[]{:S(2)}) collective-permute-start(bf16[2,256,512]{2,1,0:T(8,128)(2,1)} %pad_maximum_fusion.8), channel_id=1, source_target_pairs={{0,2},{2,0},{4,6},{6,4},{1,3},{3,1},{5,7},{7,5},{8,10},{10,8},{12,... | collective-permute-start | bytes 1572872 | tf_op jit(solution)/shard_map/ppermute | solution.py:806
  74.3 41.5 %collective-permute-start.16 = (bf16[4,256,512]{2,1,0:T(8,128)(2,1)}, bf16[4,256,512]{2,1,0:T(8,128)(2,1)}, u32[]{:S(2)}, u32[]{:S(2)}) collective-permute-start(bf16[4,256,512]{2,1,0:T(8,128)(2,1)} %get-tuple-element.159), channel_id=1, source_target_pairs={{0,16},{16,0},{1,17},{17,1},{2,18},{18,2},{3,19},{19,3},{4,20},{20... | collective-permute-start | bytes 3145736 | tf_op jit(solution)/shard_map/ppermute | solution.py:806
  74.9 27.1 %collective-permute-start.4 = (f32[16,1024]{1,0:T(8,128)S(1)}, f32[16,1024]{1,0:T(8,128)S(1)}, u32[]{:S(2)}, u32[]{:S(2)}) collective-permute-start(f32[16,1024]{1,0:T(8,128)S(1)} %slice_bitcast_fusion.6), channel_id=1, source_target_pairs={{0,16},{16,0},{1,17},{17,1},{2,18},{18,2},{3,19},{19,3},{4,20},{20... | collective-permute-start | bytes 196616 | tf_op jit(solution)/shard_map/ppermute | solution.py:806
  85.8 38.6 %collective-permute-start.20 = (bf16[4,256,512]{2,1,0:T(8,128)(2,1)}, bf16[4,256,512]{2,1,0:T(8,128)(2,1)}, u32[]{:S(2)}, u32[]{:S(2)}) collective-permute-start(bf16[4,256,512]{2,1,0:T(8,128)(2,1)} %get-tuple-element.157), channel_id=1, source_target_pairs={{0,16},{16,0},{1,17},{17,1},{2,18},{18,2},{3,19},{19,3},{4,20},{20... | collective-permute-start | bytes 3145736 | tf_op jit(solution)/shard_map/ppermute | solution.py:806
  118.6 68.9 %collective-permute-start.17 = (bf16[2,4,256,512]{3,2,1,0:T(8,128)(2,1)}, bf16[2,4,256,512]{3,2,1,0:T(8,128)(2,1)}, u32[]{:S(2)}, u32[]{:S(2)}) collective-permute-start(bf16[2,4,256,512]{3,2,1,0:T(8,128)(2,1)} %pad_maximum_fusion.1.wo.w1o), channel_id=1, source_target_pairs={{0,8},{8,0},{1,9},{9,1},{2,10},{10,2},{3,11},{11,3},{4,12},{12,4},... | collective-permute-start | bytes 6291464 | tf_op jit(solution)/shard_map/ppermute | solution.py:806
  127.2 77.9 %collective-permute-start.21 = (bf16[2,4,256,512]{3,2,1,0:T(8,128)(2,1)}, bf16[2,4,256,512]{3,2,1,0:T(8,128)(2,1)}, u32[]{:S(2)}, u32[]{:S(2)}) collective-permute-start(bf16[2,4,256,512]{3,2,1,0:T(8,128)(2,1)} %pad_maximum_fusion.2.wo.w2o), channel_id=1, source_target_pairs={{0,8},{8,0},{1,9},{9,1},{2,10},{10,2},{3,11},{11,3},{4,12},{12,4},... | collective-permute-start | bytes 6291464 | tf_op jit(solution)/shard_map/ppermute | solution.py:806
  157.4 19.2 %collective-permute-start.13 = (bf16[256,1024]{1,0:T(8,128)(2,1)}, bf16[256,1024]{1,0:T(8,128)(2,1)S(1)}, u32[]{:S(2)}, u32[]{:S(2)}) collective-permute-start(bf16[256,1024]{1,0:T(8,128)(2,1)} %project.3), channel_id=1, source_target_pairs={{0,1},{1,0},{2,3},{3,2},{4,5},{5,4},{6,7},{7,6},{8,9},{9,8},{10,11... | collective-permute-start | bytes 1572872 | tf_op jit(solution)/shard_map/ppermute | solution.py:806
  159.0 22.9 %collective-permute-start.24 = (bf16[128,1024]{1,0:T(8,128)(2,1)S(1)}, bf16[128,1024]{1,0:T(8,128)(2,1)S(1)}, u32[]{:S(2)}, u32[]{:S(2)}) collective-permute-start(bf16[128,1024]{1,0:T(8,128)(2,1)S(1)} %get-tuple-element.171), channel_id=1, source_target_pairs={{0,0},{2,2},{4,8},{6,10},{8,4},{10,6},{12,12},{14,14},{1,1},{3,3},... | collective-permute-start | bytes 786440 | tf_op jit(solution)/shard_map/ppermute | solution.py:818
  159.9 22.0 %collective-permute-start.25 = (bf16[128,1024]{1,0:T(8,128)(2,1)S(1)}, bf16[128,1024]{1,0:T(8,128)(2,1)S(1)}, u32[]{:S(2)}, u32[]{:S(2)}) collective-permute-start(bf16[128,1024]{1,0:T(8,128)(2,1)S(1)} %get-tuple-element.170), channel_id=1, source_target_pairs={{0,2},{2,0},{4,10},{6,8},{8,6},{10,4},{12,14},{14,12},{1,3},{3,1},... | collective-permute-start | bytes 786440 | tf_op jit(solution)/shard_map/ppermute | solution.py:818
  186.0 19.1 %collective-permute-start.28 = (bf16[256,1024]{1,0:T(8,128)(2,1)}, bf16[256,1024]{1,0:T(8,128)(2,1)S(1)}, u32[]{:S(2)}, u32[]{:S(2)}) collective-permute-start(bf16[256,1024]{1,0:T(8,128)(2,1)} %get-tuple-element.72.grad.go), channel_id=1, source_target_pairs={{0,1},{1,0},{2,3},{3,2},{4,5},{5,4},{6,7},{7,6},{8,9},{9,8},{10,11... | collective-permute-start | bytes 1572872 | tf_op jit(solution)/shard_map/ppermute | solution.py:806
  235.1 19.3 %collective-permute-start.30 = (bf16[256,1024]{1,0:T(8,128)(2,1)}, bf16[256,1024]{1,0:T(8,128)(2,1)S(1)}, u32[]{:S(2)}, u32[]{:S(2)}) collective-permute-start(bf16[256,1024]{1,0:T(8,128)(2,1)} %get-tuple-element.78.grad.go), channel_id=1, source_target_pairs={{0,1},{1,0},{2,3},{3,2},{4,5},{5,4},{6,7},{7,6},{8,9},{9,8},{10,11... | collective-permute-start | bytes 1572872 | tf_op jit(solution)/shard_map/ppermute | solution.py:806
  252.6 35.3 %collective-permute-start.31 = (bf16[2,512,512]{2,1,0:T(8,128)(2,1)}, bf16[2,512,512]{2,1,0:T(8,128)(2,1)S(1)}, u32[]{:S(2)}, u32[]{:S(2)}) collective-permute-start(bf16[2,512,512]{2,1,0:T(8,128)(2,1)} %get-tuple-element.85), channel_id=1, source_target_pairs={{0,8},{8,0},{1,9},{9,1},{2,10},{10,2},{3,11},{11,3},{4,12},{12,4},... | collective-permute-start | bytes 3145736 | tf_op jit(solution)/shard_map/ppermute | solution.py:806
  271.3 16.6 %collective-permute-start.32 = (bf16[2,512,512]{2,1,0:T(8,128)(2,1)}, bf16[2,512,512]{2,1,0:T(8,128)(2,1)S(1)}, u32[]{:S(2)}, u32[]{:S(2)}) collective-permute-start(bf16[2,512,512]{2,1,0:T(8,128)(2,1)} %get-tuple-element.86), channel_id=1, source_target_pairs={{0,8},{8,0},{1,9},{9,1},{2,10},{10,2},{3,11},{11,3},{4,12},{12,4},... | collective-permute-start | bytes 3145736 | tf_op jit(solution)/shard_map/ppermute | solution.py:806
  277.0 28.1 %collective-permute-start.23 = (bf16[256,1024]{1,0:T(8,128)(2,1)}, bf16[256,1024]{1,0:T(8,128)(2,1)S(1)}, u32[]{:S(2)}, u32[]{:S(2)}) collective-permute-start(bf16[256,1024]{1,0:T(8,128)(2,1)} %down.3), channel_id=1, source_target_pairs={{0,1},{1,0},{2,3},{3,2},{4,5},{5,4},{6,7},{7,6},{8,9},{9,8},{10,11... | collective-permute-start | bytes 1572872 | tf_op jit(solution)/shard_map/ppermute | solution.py:806
  287.7 69.1 %collective-permute-start.47 = (bf16[2,4,2,256,512]{4,3,2,1,0:T(8,128)(2,1)}, bf16[2,4,2,256,512]{4,3,2,1,0:T(8,128)(2,1)}, u32[]{:S(2)}, u32[]{:S(2)}) collective-permute-start(bf16[2,4,2,256,512]{4,3,2,1,0:T(8,128)(2,1)} %get-tuple-element.106), channel_id=1, source_target_pairs={{0,8},{8,0},{1,9},{9,1},{2,10},{10,2},{3,11},{11,3},{4,12},{12,4},... | collective-permute-start | bytes 12582920 | tf_op jit(solution)/shard_map/ppermute | solution.py:806
  309.6 17.6 %collective-permute-start.26 = (bf16[128,1024]{1,0:T(8,128)(2,1)}, bf16[128,1024]{1,0:T(8,128)(2,1)S(1)}, u32[]{:S(2)}, u32[]{:S(2)}) collective-permute-start(bf16[128,1024]{1,0:T(8,128)(2,1)} %get-tuple-element.70), channel_id=1, source_target_pairs={{0,0},{2,2},{8,4},{10,6},{4,8},{6,10},{12,12},{14,14},{1,1},{3,3},... | collective-permute-start | bytes 786440 | tf_op jit(solution)/shard_map/ppermute | solution.py:822
  311.2 16.0 %collective-permute-start.27 = (bf16[128,1024]{1,0:T(8,128)(2,1)}, bf16[128,1024]{1,0:T(8,128)(2,1)S(1)}, u32[]{:S(2)}, u32[]{:S(2)}) collective-permute-start(bf16[128,1024]{1,0:T(8,128)(2,1)} %get-tuple-element.71), channel_id=1, source_target_pairs={{2,0},{0,2},{10,4},{8,6},{6,8},{4,10},{14,12},{12,14},{3,1},{1,3},... | collective-permute-start | bytes 786440 | tf_op jit(solution)/shard_map/ppermute | solution.py:822
  343.2 62.0 %collective-permute-start.43 = (bf16[2,4,256,512]{3,2,1,0:T(8,128)(2,1)}, bf16[2,4,256,512]{3,2,1,0:T(8,128)(2,1)}, u32[]{:S(2)}, u32[]{:S(2)}) collective-permute-start(bf16[2,4,256,512]{3,2,1,0:T(8,128)(2,1)} %get-tuple-element.102), channel_id=1, source_target_pairs={{0,8},{8,0},{1,9},{9,1},{2,10},{10,2},{3,11},{11,3},{4,12},{12,4},... | collective-permute-start | bytes 6291464 | tf_op jit(solution)/shard_map/ppermute | solution.py:806
  362.0 53.7 %collective-permute-start.48 = (bf16[4,2,256,512]{3,2,1,0:T(8,128)(2,1)}, bf16[4,2,256,512]{3,2,1,0:T(8,128)(2,1)}, u32[]{:S(2)}, u32[]{:S(2)}) collective-permute-start(bf16[4,2,256,512]{3,2,1,0:T(8,128)(2,1)} %get-tuple-element.147), channel_id=1, source_target_pairs={{0,16},{16,0},{1,17},{17,1},{2,18},{18,2},{3,19},{19,3},{4,20},{20... | collective-permute-start | bytes 6291464 | tf_op jit(solution)/shard_map/ppermute | solution.py:806
  362.5 42.7 %collective-permute-start.41 = (f32[4,256]{1,0:T(4,128)S(1)}, f32[4,256]{1,0:T(4,128)S(1)}, u32[]{:S(2)}, u32[]{:S(2)}) collective-permute-start(f32[4,256]{1,0:T(4,128)S(1)} %squeeze.17), channel_id=1, source_target_pairs={{0,16},{16,0},{1,17},{17,1},{2,18},{18,2},{3,19},{19,3},{4,20},{20... | collective-permute-start | bytes 12296 | tf_op jit(solution)/shard_map/ppermute | solution.py:806
  408.0 21.6 %collective-permute-start.44 = (bf16[4,256,512]{2,1,0:T(8,128)(2,1)S(1)}, bf16[4,256,512]{2,1,0:T(8,128)(2,1)S(1)}, u32[]{:S(2)}, u32[]{:S(2)}) collective-permute-start(bf16[4,256,512]{2,1,0:T(8,128)(2,1)S(1)} %get-tuple-element.151), channel_id=1, source_target_pairs={{0,16},{16,0},{1,17},{17,1},{2,18},{18,2},{3,19},{19,3},{4,20},{20... | collective-permute-start | bytes 3145736 | tf_op jit(solution)/shard_map/ppermute | solution.py:806
  418.8 42.4 %collective-permute-start.49 = (bf16[2,2,256,512]{3,2,1,0:T(8,128)(2,1)}, bf16[2,2,256,512]{3,2,1,0:T(8,128)(2,1)S(1)}, u32[]{:S(2)}, u32[]{:S(2)}) collective-permute-start(bf16[2,2,256,512]{3,2,1,0:T(8,128)(2,1)} %get-tuple-element.149), channel_id=1, source_target_pairs={{0,2},{2,0},{4,6},{6,4},{1,3},{3,1},{5,7},{7,5},{8,10},{10,8},{12,... | collective-permute-start | bytes 3145736 | tf_op jit(solution)/shard_map/ppermute | solution.py:806
  430.7 25.7 %collective-permute-start.45 = (bf16[2,256,512]{2,1,0:T(8,128)(2,1)}, bf16[2,256,512]{2,1,0:T(8,128)(2,1)S(1)}, u32[]{:S(2)}, u32[]{:S(2)}) collective-permute-start(bf16[2,256,512]{2,1,0:T(8,128)(2,1)} %get-tuple-element.153), channel_id=1, source_target_pairs={{0,2},{2,0},{4,6},{6,4},{1,3},{3,1},{5,7},{7,5},{8,10},{10,8},{12,... | collective-permute-start | bytes 1572872 | tf_op jit(solution)/shard_map/ppermute | solution.py:806
  456.4 27.8 %collective-permute-start.46 = (bf16[256,512]{1,0:T(8,128)(2,1)S(1)}, bf16[256,512]{1,0:T(8,128)(2,1)S(1)}, u32[]{:S(2)}, u32[]{:S(2)}) collective-permute-start(bf16[256,512]{1,0:T(8,128)(2,1)S(1)} %fusion.15), channel_id=1, source_target_pairs={{0,4},{2,6},{4,0},{6,2},{1,5},{3,7},{5,1},{7,3},{8,12},{10,14},{12... | collective-permute-start | bytes 786440 | tf_op jit(solution)/shard_map/ppermute | solution.py:806
  462.2 33.2 %collective-permute-start.50 = (bf16[2,256,512]{2,1,0:T(8,128)(2,1)}, bf16[2,256,512]{2,1,0:T(8,128)(2,1)}, u32[]{:S(2)}, u32[]{:S(2)}) collective-permute-start(bf16[2,256,512]{2,1,0:T(8,128)(2,1)} %fusion.7), channel_id=1, source_target_pairs={{0,4},{2,6},{4,0},{6,2},{1,5},{3,7},{5,1},{7,3},{8,12},{10,14},{12... | collective-permute-start | bytes 1572872 | tf_op jit(solution)/shard_map/ppermute | solution.py:806
  (54 other events, 498.2 us)

commit v3 on v2

--- a/solution.py
+++ b/solution.py
@@ -449,9 +449,16 @@
 COLS = 512
 
 
-def weight_specs():
-    spec = pl.BlockSpec((2, 1, 256, COLS), lambda j, t: (0, j, 0, 0))
-    return [spec, spec]
+def block_spec(rows, cols):
+    return pl.BlockSpec((2, 1, rows, cols), lambda j, t: (0, j, 0, 0))
+
+
+def halves_specs():
+    return [block_spec(128, COLS)] * 4
+
+
+def halves(refs, kc, ky, cols):
+    return jnp.concatenate([refs[kc][ky, 0, :, cols], refs[2 + kc][ky, 0, :, cols]], axis=0)
 
 
 def column_spec(width, rows=256):
@@ -505,10 +512,11 @@
     sums[...] = total
 
 
-def qkv_kernel(t, x, wo, wt, bias, q, kv):
+def qkv_kernel(t, x, *refs):
+    ws, (bias, q, kv) = refs[:4], refs[4:]
     acc = jnp.zeros((256, 384), f32)
     for kc, ky in PAIRS:
-        acc = acc + nn(lanes(x, t[kc * 2 + ky]), (wo, wt)[kc][ky, 0, :, :384])
+        acc = acc + nn(lanes(x, t[kc * 2 + ky]), halves(ws, kc, ky, slice(0, 384)))
     q[...] = (acc[:, :128] + bias[8:9]).astype(bf16)
     kv[0] = acc[:, 128:256].astype(bf16)
     kv[1] = (acc[:, 256:] + bias[9:10]).astype(bf16)
@@ -564,11 +572,12 @@
     dq[...] = (both * factor).T.astype(bf16)
 
 
-def unpack_proj(block):
-    return jnp.concatenate([block[:128, 384:], block[128:, 384:]], axis=1)
-
-
-def proj_kernel(t, mixed, wo, wt, out, acc):
+def unpack_proj(refs, kc, ky):
+    return jnp.concatenate([refs[kc][ky, 0, :, 384:], refs[2 + kc][ky, 0, :, 384:]], axis=1)
+
+
+def proj_kernel(t, mixed, *refs):
+    ws, (out, acc) = refs[:4], refs[4:]
     j = pl.program_id(0)
 
     @pl.when(j == 0)
@@ -576,7 +585,7 @@
         acc[...] = jnp.zeros_like(acc)
 
     for i, (kc, ky) in enumerate(PAIRS):
-        acc[i] += nn(mixed[...], unpack_proj((wo, wt)[kc][ky, 0]))
+        acc[i] += nn(mixed[...], unpack_proj(ws, kc, ky))
 
     @pl.when(j == 3)
     def _():
@@ -584,10 +593,11 @@
             out[:, pl.ds(pl.multiple_of(t[i] * 256, 256), 256)] = acc[i].astype(out.dtype)
 
 
-def proj_back_kernel(t, grad, wo, wt, out):
+def proj_back_kernel(t, grad, *refs):
+    ws, out = refs[:4], refs[4]
     acc = jnp.zeros((256, 128), f32)
     for kc, ky in PAIRS:
-        acc = acc + nt(lanes(grad, t[kc * 2 + ky]), unpack_proj((wo, wt)[kc][ky, 0]))
+        acc = acc + nt(lanes(grad, t[kc * 2 + ky]), unpack_proj(ws, kc, ky))
     out[...] = acc.astype(bf16)
 
 
@@ -657,28 +667,47 @@
             out[:, pl.ds(pl.multiple_of(t[i] * 256, 256), 256)] = acc[i].astype(out.dtype)
 
 
-def mlp_grads_kernel(t, xo, xt, dho, dht, acto, actt, go, gt, keep, send):
+def keep_rows(own, other, turned):
+    @pl.when(pl.program_id(0) == 0)
+    def _():
+        for i in range(4):
+            part = slice(i * 256, (i + 1) * 256)
+            turned[part] = jnp.concatenate([own[:, part], other[:, part]], axis=0).T
+
+
+def feature_rows(turned, block):
+    return turned[pl.ds(pl.multiple_of(block * 256, 256), 256)]
+
+
+def fc1_grads_kernel(t, xo, xt, dho, dht, keep, send, turned):
+    keep_rows(xo, xt, turned)
     dh = jnp.concatenate([dho[...], dht[...]], axis=0)
+    for i, (kc, ky) in enumerate(PAIRS):
+        (keep, send)[kc][ky, 0] = nn(feature_rows(turned, t[i]), dh).astype(bf16)
+
+
+def fc2_grads_kernel(t, acto, actt, go, gt, keep, send):
     act_t = jnp.concatenate([acto[...], actt[...]], axis=0).T
     for i, (kc, ky) in enumerate(PAIRS):
-        x_t = jnp.concatenate([lanes(xo, t[i]), lanes(xt, t[i])], axis=0).T
         grad = jnp.concatenate([lanes(go, t[i]), lanes(gt, t[i])], axis=0)
-        out = (keep, send)[kc]
-        out[ky, 0, 0] = nn(x_t, dh).astype(bf16)
         fc2 = nn(act_t, grad).astype(bf16)
-        out[ky, 0, 1] = jnp.concatenate([fc2[:256], fc2[256:]], axis=1)
-
-
-def attn_grads_kernel(t, xo, xt, dpo, dpt, mo, mt, go, gt, keep, send):
-    dpacked = jnp.concatenate([dpo[0], dpt[0]], axis=0)
+        (keep, send)[kc][ky, 0] = jnp.concatenate([fc2[:256], fc2[256:]], axis=1)
+
+
+def proj_grads_kernel(t, mo, mt, go, gt, keep, send):
     mixed_t = jnp.concatenate([mo[...], mt[...]], axis=0).T
     for i, (kc, ky) in enumerate(PAIRS):
-        x_t = jnp.concatenate([lanes(xo, t[i]), lanes(xt, t[i])], axis=0).T
         grad = jnp.concatenate([lanes(go, t[i]), lanes(gt, t[i])], axis=0)
-        out = (keep, send)[kc]
-        proj = nn(mixed_t, grad).astype(bf16)
-        side = jnp.concatenate([proj[:, :128], proj[:, 128:]], axis=0)
-        out[ky, 0] = jnp.concatenate([nn(x_t, dpacked).astype(bf16), side], axis=1)
+        (keep, send)[kc][ky, 0] = nn(mixed_t, grad).astype(bf16)
+
+
+def qkv_grads_kernel(t, xo, xt, dpo, dpt, keep0, send0, keep1, send1, turned):
+    keep_rows(xo, xt, turned)
+    dpacked = jnp.concatenate([dpo[0], dpt[0]], axis=0)
+    for i, (kc, ky) in enumerate(PAIRS):
+        grad = nn(feature_rows(turned, t[i]), dpacked).astype(bf16)
+        (keep0, send0)[kc][ky, 0] = grad[:128]
+        (keep1, send1)[kc][ky, 0] = grad[128:]
 
 
 def dmid_kernel(t, part, got, middle, branch, first, second, mod, dmid, out, sums):
@@ -715,7 +744,8 @@
     sums[...] = total
 
 
-def qkv_back_kernel(t, dqo, dqt, n0, n1, f0, f1, wo, wt, packo, packt, sums, outo, outt, acco, acct):
+def qkv_back_kernel(t, dqo, dqt, n0, n1, f0, f1, *refs):
+    ws, (packo, packt, sums, outo, outt, acco, acct) = refs[:4], refs[4:]
     j = pl.program_id(0)
 
     @pl.when(j == 0)
@@ -741,7 +771,7 @@
         axis=0,
     )
     for i, (kc, ky) in enumerate(PAIRS):
-        w = (wo, wt)[kc][ky, 0, :, :384]
+        w = halves(ws, kc, ky, slice(0, 384))
         acco[i] += nt(packed[0], w)
         acct[i] += nt(packed[1], w)
 
@@ -768,6 +798,21 @@
         out[...] = (dmid[rows] + back).astype(bf16)
         rows_of.append([dn, dn * unit])
     sums[...] = jnp.concatenate([total_rows(a) + total_rows(b) for a, b in zip(*rows_of)], axis=0)
+
+
+def pack_kernel(t, qkv, proj, fc2, upper, lower, side):
+    for i, out in enumerate((upper, lower)):
+        rows = qkv[i * 128 : (i + 1) * 128]
+        parts = [rows[:, 192 * g + HD * k : 192 * g + HD * k + HD] for k in range(3) for g in range(2)]
+        out[0] = jnp.concatenate(parts + [proj[:, i * 128 : (i + 1) * 128]], axis=1)
+    side[0] = jnp.concatenate([fc2[:256], fc2[256:]], axis=1)
+
+
+def assemble_kernel(t, up, up_got, low, low_got, out):
+    for i, (own, got) in enumerate(((up, up_got), (low, low_got))):
+        rows = own[0].astype(f32) + got[0].astype(f32)
+        parts = [rows[:, 128 * k + HD * g : 128 * k + HD * g + HD] for g in range(2) for k in range(3)]
+        out[i * 128 : (i + 1) * 128] = jnp.concatenate(parts, axis=1)
 
 
 def small_kernel(t, din_sums, dgate_mlp, dmid_sums, bfc2, qkv_sums, fc1o, fc1t, out):
@@ -798,7 +843,7 @@
     D = 1024
     own = y * 2 + c
     blocks = [(y ^ ky) * 2 + (c ^ kc) for kc, ky in PAIRS]
-    z_of = [z ^ (kz1 * 2 + kz0) for kz0 in range(2) for kz1 in range(2)]
+    z_of = [z ^ k1 ^ (2 * k2) for k1 in range(2) for k2 in range(2)]
     table = jnp.stack(blocks + [zz * 2 + x for zz in z_of] + z_of + [x, own]).astype(jnp.int32)
     call = functools.partial(kernel_call)
 
@@ -810,40 +855,71 @@
             (cc * 4 + zz, (zz // 2) * 4 + cc * 2 + ((zz % 2) ^ k)) for cc in range(2) for zz in range(4)
         ]
 
-    def spread(array):
+    def spread_parts(array):
         flat = array.reshape(128, 2 * D)
         low, high = flat[:, :D], flat[:, D:]
-        first = jnp.where(z0 == 0, low, high)
-        second = jnp.where(z0 == 0, high, low)
-        return [lax.ppermute(p, ("c", "z"), route(k)) for k, p in enumerate((first, second))]
-
-    def collect(pieces, dtype):
-        got = [
-            lax.ppermute(p, ("c", "z"), [(b, a) for a, b in route(k)]) for k, p in enumerate(pieces)
-        ]
+        return jnp.where(z0 == 0, low, high), jnp.where(z0 == 0, high, low)
+
+    def spread(array):
+        return [lax.ppermute(p, ("c", "z"), route(k)) for k, p in enumerate(spread_parts(array))]
+
+    def send_back(pieces):
+        return [lax.ppermute(p, ("c", "z"), [(b, a) for a, b in route(k)]) for k, p in enumerate(pieces)]
+
+    def collect(got, dtype, *others):
+        got = lax.optimization_barrier((*got, *others))[:2]
         low = jnp.where(z0 == 0, got[0], got[1])
         high = jnp.where(z0 == 0, got[1], got[0])
         return jnp.concatenate([low, high], axis=1).astype(dtype).reshape(128, 2, D)
 
-    def gather_w(block):
-        v = jnp.stack([block, flip(block, "z", 4, 2)])
-        v = jnp.concatenate([v, flip(v, "z", 4, 1)])
-        v = jnp.stack([v, flip(v, "y", 2, 1)])
-        return v, flip(v, "c", 2, 1)
-
-    def reduce_w(keep, send):
-        add = lambda a, b: (a.astype(f32) + b.astype(f32)).astype(bf16)
-        got = flip(send, "c", 2, 1)
-        mine, theirs = add(keep[0], got[0]), add(keep[1], got[1])
-        got = flip(theirs, "y", 2, 1)
-        mine, theirs = add(mine[:2], got[:2]), add(mine[2:], got[2:])
-        got = flip(theirs, "z", 4, 1)
-        mine, theirs = add(mine[0], got[0]), add(mine[1], got[1])
-        return mine.astype(f32) + flip(theirs, "z", 4, 2).astype(f32)
+    def after(value, *others):
+        return lax.optimization_barrier((value, *others))[0]
+
+    STEPS = {"near": ("z", 4, 1), "far": ("z", 4, 2), "y": ("y", 2, 1)}
+
+    def widen(v, step, *others):
+        v, got = lax.optimization_barrier((v, flip(v, *STEPS[step]), *others))[:2]
+        return jnp.concatenate([v, got])
+
+    def both_cores(v):
+        v = v.reshape((2, 4) + v.shape[1:])
+        return [v, flip(v, "c", 2, 1)]
+
+    def cross(keep, send):
+        flat = (8,) + keep.shape[2:]
+        return keep.reshape(flat), flip(send.reshape(flat), "c", 2, 1)
+
+    def fold(pair, *others):
+        own, got = lax.optimization_barrier((*pair, *others))[:2]
+        half = own.shape[0] // 2
+        cut = lambda v, k: v[k * half : (k + 1) * half].astype(f32)
+        return [(cut(own, k) + cut(got, k)).astype(bf16) for k in range(2)]
+
+    def onward(parts, step):
+        return parts[0], flip(parts[1], *STEPS[step])
+
+    def total(pair, *others):
+        own, got = lax.optimization_barrier((*pair, *others))[:2]
+        v = own.astype(f32) + got.astype(f32)
+        return v.reshape(v.shape[-2:])
 
     cond_c = jnp.stack([conditioning, flip(conditioning, "c", 2, 1)])
     cond_c = jnp.where(c == 0, cond_c, cond_c[::-1])
     cond_all = jnp.stack([cond_c, flip(cond_c, "y", 2, 1)]).reshape(2, 4, D)
+    tok_parts = spread_parts(tokens)
+    tok = [lax.ppermute(p, ("c", "z"), route(k)) for k, p in enumerate(tok_parts)]
+    upper, lower, packed_fc2 = call(
+        pack_kernel,
+        table,
+        [w_qkv.reshape(256, 384), w_proj, w_fc2],
+        [whole((256, 384)), whole((128, 256)), whole((512, 256))],
+        [whole((1, 128, COLS)), whole((1, 128, COLS)), whole((1, 256, COLS))],
+        [shaped((1, 128, COLS), bf16), shaped((1, 128, COLS), bf16), shaped((1, 256, COLS), bf16)],
+        name="pack",
+    )
+    upper = widen(upper, "far")
+    upper, cond_all, *tok = lax.optimization_barrier((upper, cond_all, *tok))
+    upper, lower = widen(upper, "near"), widen(after(lower, upper), "far")
     act_abs = jax.nn.silu(cond_all.astype(f32)).astype(bf16)
     act_abs = lax.dynamic_slice_in_dim(act_abs, own * 256, 256, 2)
     act_here = lax.dynamic_slice_in_dim(act_abs, z, 1, 1)[:, 0]
@@ -868,21 +944,20 @@
     mod = packed_mod[0] + flip(packed_mod[1], "y", 2, 1)
     mod = mod + flip(mod, "c", 2, 1)
     mod_spec = whole((16, D))
-
-    tok = spread(tokens)
-    heads = w_qkv.reshape(256, 2, 3, HD).transpose(0, 2, 1, 3).reshape(256, 384)
-    pack_a = jnp.concatenate(
-        [heads, jnp.concatenate([w_proj[:, :128], w_proj[:, 128:]], axis=0)], axis=1
-    )
-    wa = gather_w(pack_a)
-    w1 = gather_w(w_fc1)
-    w2 = gather_w(jnp.concatenate([w_fc2[:256], w_fc2[256:]], axis=1))
-    cot = spread(cotangent)
+    upper, lower, mod = lax.optimization_barrier((upper, lower, mod))
 
     half, full = whole((128, D)), whole((256, D))
     row_b, row_f = shaped((256, D), bf16), shaped((256, D), f32)
     normed = call(ln_kernel, table, [*tok, mod], [half, half, mod_spec], full, row_b, name="norm_in")
     normed_t = flip(normed, "x", 2, 1)
+    upper = widen(upper, "y")
+    lower = widen(lower, "near")
+    w1 = after(w_fc1[None], lower)
+    lower, got_low, w1, got_w1, normed_t = lax.optimization_barrier(
+        (lower, flip(lower, *STEPS["y"]), w1, flip(w1, *STEPS["far"]), normed_t)
+    )
+    lower, w1 = jnp.concatenate([lower, got_low]), jnp.concatenate([w1, got_w1])
+    wa = both_cores(upper) + both_cores(after(lower, w1))
 
     bias_spec = pl.BlockSpec((16, 128), lambda j, t: (0, t[4 + j]))
     pair_spec = pl.BlockSpec((2, 256, 128), lambda j, t: (0, 0, j))
@@ -892,7 +967,7 @@
             qkv_kernel,
             table,
             [rows, *wa, mod],
-            [full, *weight_specs(), bias_spec],
+            [full, *halves_specs(), bias_spec],
             [column_spec(128), pair_spec],
             [shaped((256, 512), bf16), shaped((2, 256, 512), bf16)],
             steps=4,
@@ -905,6 +980,8 @@
     q_t, kv_t = make_qkv(normed_t)
     far_t = flip(kv_t, "c", 2, 1)
     chunks = [kv_o, kv_t, far_o, far_t]
+    w1 = widen(w1, "near", kv_t)
+    q_t, w1 = lax.optimization_barrier((q_t, w1))
     lse_spec = pl.BlockSpec((1, 2, 256), lambda j, t: (j, 0, 0))
 
     def attend(queries):
@@ -927,7 +1004,7 @@
             proj_kernel,
             table,
             [rows, *wa],
-            [column_spec(128), *weight_specs()],
+            [column_spec(128), *halves_specs()],
             full,
             shaped((256, D), kind),
             steps=4,
@@ -937,8 +1014,15 @@
         )
 
     mixed_t, lse_t = attend(q_t)
-    got_branch = flip(project(mixed_t, bf16), "x", 2, 1)
+    w2 = widen(after(packed_fc2, q_t), "far", mixed_t)
+    part_t = project(after(mixed_t, w2), bf16)
+    got_branch = flip(part_t, "x", 2, 1)
+    q_o, part_t = lax.optimization_barrier((q_o, part_t))
     mixed_o, lse_o = attend(q_o)
+    w1, w2 = widen(w1, "y", mixed_o), widen(w2, "near", mixed_o)
+    mixed_o, w1, w2, got_branch = lax.optimization_barrier((mixed_o, w1, w2, got_branch))
+    w1 = both_cores(w1)
+    cot = [lax.ppermute(p, ("c", "z"), route(k)) for k, p in enumerate(spread_parts(after(cotangent, mixed_o)))]
     branch, middle, normed_mlp = call(
         mid_kernel,
         table,
@@ -949,11 +1033,18 @@
         name="norm_mid",
     )
     dmlp_o, bfc2_sum = call(
-        dmlp_kernel, table, [*cot, mod], [half, half, mod_spec], [full, whole((1, D))], [row_b, shaped((1, D), f32)], name="dbranch_mlp"
+        dmlp_kernel,
+        table,
+        [*cot, after(mod, normed_mlp)],
+        [half, half, mod_spec],
+        [full, whole((1, D))],
+        [row_b, shaped((1, D), f32)],
+        name="dbranch_mlp",
     )
     dmlp_t = flip(dmlp_o, "x", 2, 1)
     mlp_t = flip(normed_mlp, "x", 2, 1)
     wide = shaped((256, 2048), bf16)
+    wide_specs = [block_spec(256, COLS)] * 2
     fc1_bias = pl.BlockSpec((16, COLS), lambda j, t: (0, t[12]))
 
     def up(rows):
@@ -961,7 +1052,7 @@
             fc1_kernel,
             table,
             [rows, *w1, mod],
-            [full, *weight_specs(), fc1_bias],
+            [full, *wide_specs, fc1_bias],
             [column_spec(COLS)] * 2,
             [wide, wide],
             steps=4,
@@ -974,7 +1065,7 @@
             fc2_kernel,
             table,
             [act, *w2],
-            [column_spec(COLS), *weight_specs()],
+            [column_spec(COLS), *wide_specs],
             full,
             shaped((256, D), kind),
             steps=4,
@@ -988,7 +1079,7 @@
             mlp_back_kernel,
             table,
             [grad, slope, *w2, *w1],
-            [full, column_spec(COLS), *weight_specs(), *weight_specs()],
+            [full, column_spec(COLS), *wide_specs, *wide_specs],
             [column_spec(COLS), column_spec(COLS, 1), full],
             [wide, shaped((1, 2048), f32), shaped((256, D), kind)],
             steps=4,
@@ -997,29 +1088,41 @@
             name="mlp_back",
         )
 
-    act_o, slope_o = up(normed_mlp)
-    act_t, slope_t = up(mlp_t)
+    act_o, slope_o = up(after(normed_mlp, dmlp_o))
+    w2 = both_cores(widen(w2, "y", act_o, mlp_t))
+    act_t, slope_t = up(after(mlp_t, act_o))
     dh_t, fc1_t, dn_t = mlp_back(dmlp_t, slope_t, bf16)
     got_dn = flip(dn_t, "x", 2, 1)
-    dh_o, fc1_o, dn_o = mlp_back(dmlp_o, slope_o, f32)
-    got_mlp = flip(down(act_t, bf16), "x", 2, 1)
-    down_o = down(act_o, f32)
-    grad_specs = lambda *tail: pl.BlockSpec((2, 1) + tail, lambda j, t: (0, j) + (0,) * len(tail))
-    mlp_grad = shaped((2, 4, 2, 256, COLS), bf16)
-    keep_m, send_m = call(
-        mlp_grads_kernel,
+    turned = pltpu.VMEM((D, 512), bf16)
+    fc2_keep, fc2_send = call(
+        fc2_grads_kernel,
         table,
-        [normed_mlp, mlp_t, dh_o, dh_t, act_o, act_t, dmlp_o, dmlp_t],
-        [full, full] + [column_spec(COLS)] * 4 + [full, full],
-        [grad_specs(2, 256, COLS)] * 2,
-        [mlp_grad, mlp_grad],
+        [act_o, act_t, after(dmlp_o, dn_t), dmlp_t],
+        [column_spec(COLS)] * 2 + [full, full],
+        [block_spec(256, COLS)] * 2,
+        [shaped((2, 4, 256, COLS), bf16)] * 2,
         steps=4,
-        flops=8 * 256 * 1024 * 2048,
-        name="mlp_grads",
-    )
-    g_mlp = reduce_w(keep_m, send_m)
-    g_fc1 = g_mlp[0]
-    g_fc2 = jnp.concatenate([g_mlp[1][:, :256], g_mlp[1][:, 256:]], axis=0)
+        flops=4 * 256 * 1024 * 2048,
+        name="fc2_grads",
+    )
+    g_fc2 = cross(fc2_keep, fc2_send)
+    dh_o, fc1_o, dn_o = mlp_back(dmlp_o, after(slope_o, fc2_send), f32)
+    g_fc2 = fold(g_fc2, dn_o)
+    fc1_keep, fc1_send = call(
+        fc1_grads_kernel,
+        table,
+        [normed_mlp, mlp_t, after(dh_o, got_dn, *g_fc2), dh_t],
+        [full, full] + [column_spec(COLS)] * 2,
+        [block_spec(256, COLS)] * 2,
+        [shaped((2, 4, 256, COLS), bf16)] * 2,
+        steps=4,
+        scratch=[turned],
+        flops=4 * 256 * 1024 * 2048,
+        name="fc1_grads",
+    )
+    g_fc1 = cross(fc1_keep, fc1_send)
+    g_fc2 = onward(g_fc2, "y")
+    dn_o = after(dn_o, fc1_send)
 
     sums_spec = whole((8, D))
     dmid, dbr_o, dmid_sums = call(
@@ -1032,7 +1135,7 @@
         name="norm_mid_back",
     )
     dbr_t = flip(dbr_o, "x", 2, 1)
-    out0, out1, dgate_mlp = call(
+    finish = lambda down_o, got_mlp: call(
         out_kernel,
         table,
         [middle, down_o, got_mlp, *cot, mod],
@@ -1041,20 +1144,21 @@
         [shaped((128, D), bf16)] * 2 + [shaped((1, D), f32)],
         name="finish",
     )
-    out = collect([out0, out1], bf16)
-
-    def attend_back(queries, grad, mixed, lse):
-        dmixed = call(
+
+    def project_back(grad):
+        return call(
             proj_back_kernel,
             table,
             [grad, *wa],
-            [full, *weight_specs()],
+            [full, *halves_specs()],
             column_spec(128),
             shaped((256, 512), bf16),
             steps=4,
             flops=2 * 256 * 512 * 1024,
             name="project_back",
         )
+
+    def attend_back(queries, dmixed, mixed, lse):
         long_spec = pl.BlockSpec((2, 512, 128), lambda j, t: (0, 0, j))
         return call(
             attn_back_kernel,
@@ -1068,17 +1172,40 @@
             name="attend_back",
         )
 
-    dq_o, near_o, away_o = attend_back(q_o, dbr_o, mixed_o, lse_o)
+    dmixed_o = project_back(dbr_o)
+    g_fc1 = fold(g_fc1, dmixed_o)
+    dmixed_o = after(dmixed_o, *g_fc1)
+    g_fc1 = onward(g_fc1, "y")
+    dq_o, near_o, away_o = attend_back(q_o, dmixed_o, mixed_o, lse_o)
     back_o = flip(away_o, "c", 2, 1)
-    dq_t, near_t, away_t = attend_back(q_t, dbr_t, mixed_t, lse_t)
+    g_fc2 = fold(g_fc2, away_o)
+    dmixed_t = project_back(after(dbr_t, *g_fc2))
+    g_fc2 = onward(g_fc2, "near")
+    p_keep, p_send = call(
+        proj_grads_kernel,
+        table,
+        [mixed_o, mixed_t, after(dbr_o, dmixed_t), dbr_t],
+        [column_spec(128)] * 2 + [full, full],
+        [block_spec(128, 256)] * 2,
+        [shaped((2, 4, 128, 256), bf16)] * 2,
+        steps=4,
+        flops=4 * 256 * 512 * 1024,
+        name="proj_grads",
+    )
+    g_proj = cross(p_keep, p_send)
+    dmixed_t = after(dmixed_t, p_send)
+    dq_t, near_t, away_t = attend_back(q_t, dmixed_t, mixed_t, lse_t)
     back_t = flip(away_t, "c", 2, 1)
+    g_fc1, g_fc2, g_proj = (fold(v, away_t) for v in (g_fc1, g_fc2, g_proj))
+    dq_t = after(dq_t, *g_fc1, *g_fc2, *g_proj)
+    g_fc2, g_fc1, g_proj = onward(g_fc2, "far"), onward(g_fc1, "near"), onward(g_proj, "y")
     long_spec = pl.BlockSpec((2, 512, 128), lambda j, t: (0, 0, j))
     pack_spec = pl.BlockSpec((1, 256, 384), lambda j, t: (j, 0, 0))
     pack_o, pack_t, qkv_sums, din_o, din_t = call(
         qkv_back_kernel,
         table,
         [dq_o, dq_t, near_o, near_t, back_o, back_t, *wa],
-        [column_spec(128)] * 2 + [long_spec] * 4 + weight_specs(),
+        [column_spec(128)] * 2 + [long_spec] * 4 + halves_specs(),
         [pack_spec, pack_spec, pl.BlockSpec((8, 128), lambda j, t: (0, j)), full, full],
         [shaped((4, 256, 384), bf16)] * 2 + [shaped((8, 512), f32), row_f, row_b],
         steps=4,
@@ -1087,21 +1214,29 @@
         name="qkv_back",
     )
     got_din = flip(din_t, "x", 2, 1)
-    attn_grad = shaped((2, 4, 256, COLS), bf16)
-    keep_a, send_a = call(
-        attn_grads_kernel,
+    qkv_out = [shaped((2, 4, 128, 384), bf16)] * 4
+    k0, s0, k1, s1 = call(
+        qkv_grads_kernel,
         table,
-        [normed, normed_t, pack_o, pack_t, mixed_o, mixed_t, dbr_o, dbr_t],
-        [full, full, pack_spec, pack_spec, column_spec(128), column_spec(128), full, full],
-        [grad_specs(256, COLS)] * 2,
-        [attn_grad, attn_grad],
+        [normed, normed_t, after(pack_o, din_t), pack_t],
+        [full, full, pack_spec, pack_spec],
+        [block_spec(128, 384)] * 4,
+        qkv_out,
         steps=4,
-        flops=4 * 256 * 1024 * 2048,
-        name="attn_grads",
-    )
-    g_a = reduce_w(keep_a, send_a)
-    g_qkv = g_a[:, :384].reshape(256, 3, 2, HD).transpose(0, 2, 1, 3).reshape(256, 2, 3 * HD)
-    g_proj = jnp.concatenate([g_a[:128, 384:], g_a[128:, 384:]], axis=1)
+        scratch=[turned],
+        flops=4 * 256 * 1024 * 1536,
+        name="qkv_grads",
+    )
+    g_up, g_low = cross(k0, s0), cross(k1, s1)
+    down_t = down(after(act_t, s0, s1), bf16)
+    got_mlp = flip(down_t, "x", 2, 1)
+    g_up, g_low = fold(g_up, down_t), fold(g_low, down_t)
+    act_o, got_din, *_ = lax.optimization_barrier((act_o, got_din, *g_up, *g_low))
+    g_up, g_low = onward(g_up, "y"), onward(g_low, "y")
+    down_o = down(act_o, f32)
+    g_proj, g_fc1 = fold(g_proj, down_o), fold(g_fc1, down_o)
+    din_o = after(din_o, *g_proj, *g_fc1)
+    g_proj, g_fc1 = onward(g_proj, "near"), onward(g_fc1, "far")
     dt0, dt1, din_sums = call(
         din_kernel,
         table,
@@ -1111,7 +1246,11 @@
         [shaped((128, D), bf16)] * 2 + [shaped((2, D), f32)],
         name="norm_in_back",
     )
-    d_tokens = collect([dt0, dt1], f32)
+    dt_got = send_back([dt0, dt1])
+    g_up = fold(g_up, dt0)
+    out0, out1, dgate_mlp = finish(after(down_o, din_sums, *g_up), got_mlp)
+    g_up = onward(g_up, "near")
+    out_got = send_back([out0, out1])
 
     small = call(
         small_kernel,
@@ -1122,11 +1261,33 @@
         shaped((16, D), f32),
         name="small",
     )
+    g_proj = onward(fold(g_proj, small), "far")
     small = small + flip(small, "x", 2, 1)
+    g_fc1, g_fc2 = total(g_fc1, small), total(g_fc2, small)
+    g_fc2 = jnp.concatenate([g_fc2[:, :256], g_fc2[:, 256:]], axis=0)
     small = small + flip(small, "c", 2, 1)
-    for axis, count, offset in (("z", 4, 2), ("z", 4, 1), ("y", 2, 1)):
-        got = flip(small, axis, count, offset)
-        small = jnp.concatenate([small[:-10], got[:-10], small[-10:] + got[-10:]])
+
+    def spread_small(v, axis, count, offset):
+        got = flip(v, axis, count, offset)
+        return jnp.concatenate([v[:-10], got[:-10], v[-10:] + got[-10:]])
+
+    g_up, g_low = onward(fold(g_up, small), "far"), onward(fold(g_low, small), "near")
+    small = spread_small(small, "z", 4, 2)
+    g_proj = total(g_proj, small)
+    small = spread_small(small, "z", 4, 1)
+    g_low = onward(fold(g_low, small), "far")
+    d_tokens = collect(dt_got, f32, small)
+    small = spread_small(small, "y", 2, 1)
+    out = collect(out_got, bf16, small)
+    g_qkv = call(
+        assemble_kernel,
+        table,
+        [*g_up, *g_low],
+        [whole((1, 128, 384))] * 4,
+        whole((256, 384)),
+        shaped((256, 384), f32),
+        name="assemble",
+    ).reshape(256, 2, 3 * HD)
     bias_sum = small[-10:]
     dmod_all = small[:-10].reshape(8, 6 * D)
     take = lambda v, n: lax.dynamic_slice_in_dim(v.reshape(-1), own * n, n, 0)

time: 501 us -> 422 us (0.84)
  waiting for transfers between devices: 201 us -> 85.5 us
  starting transfers between devices: 66 us -> 87.2 us
  Pallas kernels: 167 us -> 180 us
    ppermute x43 -> x59, waiting for transfers between devices: 188 us -> 70.9 us  [flip(): return lax.ppermute(v, axis, [(i, i ^ offset) for i in range(count)])]
    ppermute x43 -> x59, starting transfers between devices: 57.5 us -> 77.4 us  [flip(): return lax.ppermute(v, axis, [(i, i ^ offset) for i in range(count)])]
    another operation x11 -> x1, other arithmetic: 15.8 us -> 0.04 us  [fast_body(): cond_all = jnp.stack([cond_c, flip(cond_c, 'y', 2, 1)]).reshape(2, 4, D)]
    pallas_call x27 -> x31, Pallas kernels: 167 us -> 180 us  [kernel_call(): pl.pallas_call(body, grid_spec=pltpu.PrefetchScalarGridSpec(num_scalar_pr...]
    convert_element_type x6 -> x15, other arithmetic: 13.2 us -> 22.2 us  [fold(): return [(cut(own, k) + cut(got, k)).astype(bf16) for k in range(2)]]
    unnamed x76 -> x95, local copies, waits for them, and re-layouts: 12.8 us -> 11.8 us
  transfers between devices with their start and end apart: 51 -> 67, of which waited for: 21 -> 19; matrix products, arithmetic and copies ran while one was open for 10% -> 13% of each run, Pallas kernels for 31% -> 33%
where the time goes in v3:
time: 422 us; the launch traced here: 419 us
  Pallas kernels  180 us (43%)
  starting transfers between devices  87.2 us (21%)
  waiting for transfers between devices  85.5 us (20%)
  other arithmetic  34.8 us (8%)
  local copies, waits for them, and re-layouts  27.9 us (7%)
    pallas_call x31, Pallas kernels, kernel_call(): pl.pallas_call(body, grid_spec=pltpu.PrefetchScalarGridSpec(num_scalar_pr...  180 us
    ppermute x59, starting transfers between devices, flip(): return lax.ppermute(v, axis, [(i, i ^ offset) for i in range(count)])  77.4 us
    ppermute x59, waiting for transfers between devices, flip(): return lax.ppermute(v, axis, [(i, i ^ offset) for i in range(count)])  70.9 us
    convert_element_type x15, other arithmetic, fold(): return [(cut(own, k) + cut(got, k)).astype(bf16) for k in range(2)]  22.2 us
    unnamed x95, local copies, waits for them, and re-layouts  11.8 us
    ppermute x4, waiting for transfers between devices, fast_body(): lax.ppermute(p, ('c', 'z'), route(k))  9.34 us
  transfers between devices with their start and end apart: 67, of which 19 were waited for; matrix products, arithmetic and copies ran while one was open for 13% of the time, Pallas kernels for 33%

profile of v3, /device:TPU:0, one launch (start us, length us, event | category | flops | bytes accessed | tf_op | source)
XLA Modules:
  0.0 418.7 jit_solution(10359916330801198774)
XLA Ops:
  29.0 10.3 %collective-permute-start.6 = (bf16[1,128,512]{2,1,0:T(8,128)(2,1)S(1)}, bf16[1,128,512]{2,1,0:T(8,128)(2,1)S(1)}, u32[]{:S(2)}, u32[]{:S(2)}) collective-permute-start(bf16[1,128,512]{2,1,0:T(8,128)(2,1)S(1)} %copy-done.30), channel_id=1, source_target_pairs={{0,4},{2,6},{4,0},{6,2},{1,5},{3,7},{5,1},{7,3},{8,12},{10,14},{12... | collective-permute-start | bytes 393224 | tf_op jit(solution)/shard_map/ppermute | solution.py:851
  55.0 10.6 %collective-permute-done.9 = bf16[4,128,512]{2,1,0:T(8,128)(2,1)S(1)} collective-permute-done((bf16[4,128,512]{2,1,0:T(8,128)(2,1)S(1)}, bf16[4,128,512]{2,1,0:T(8,128)(2,1)S(1)}, u32[]{:S(2)}, u32[]{:S(2)}) %collective-permute-start.9) | collective-permute-done | bytes 524320 | tf_op jit(solution)/shard_map/ppermute | solution.py:851
  65.8 6.6 %collective-permute-done.12 = bf16[4,128,512]{2,1,0:T(8,128)(2,1)S(1)} collective-permute-done((bf16[4,128,512]{2,1,0:T(8,128)(2,1)S(1)}, bf16[4,128,512]{2,1,0:T(8,128)(2,1)S(1)}, u32[]{:S(2)}, u32[]{:S(2)}) %collective-permute-start.12) | collective-permute-done | bytes 524320 | tf_op jit(solution)/shard_map/ppermute | solution.py:851
  76.8 5.6 %qkv.3 = (bf16[256,512]{1,0:T(8,128)(2,1)}, bf16[2,256,512]{2,1,0:T(8,128)(2,1)}) custom-call(s32[14]{0:T(128)} %stack.86.t, bf16[256,1024]{1,0:T(8,128)(2,1)} %copy-done.18, bf16[2,4,128,512]{3,2,1,0:T(8,128)(2,1)} %bitcast.82, bf16[2,4,128,512]{3,2,1,0:T(8,128)(2,1)} %copy-done.4, bf16[2,4,128,512]{3,2,1,0:T(8,128)(2,1)} %bitcast.90, ...), custom_call_target="tpu_custom_call" | custom-call | flops 805306368 | bytes 5570560 | tf_op jit(solution)/shard_map/qkv/pallas_call | solution.py:430
  82.5 5.6 %qkv.2 = (bf16[256,512]{1,0:T(8,128)(2,1)}, bf16[2,256,512]{2,1,0:T(8,128)(2,1)}) custom-call(s32[14]{0:T(128)} %stack.86.t, bf16[256,1024]{1,0:T(8,128)(2,1)} %norm_in.1.x.xo, bf16[2,4,128,512]{3,2,1,0:T(8,128)(2,1)} %bitcast.83, bf16[2,4,128,512]{3,2,1,0:T(8,128)(2,1)} %copy-done.4, bf16[2,4,128,512]{3,2,1,0:T(8,128)(2,1)} %bitcast.91, ...), custom_call_target="tpu_custom_call" | custom-call | flops 805306368 | bytes 5570560 | tf_op jit(solution)/shard_map/qkv/pallas_call | solution.py:430
  93.9 8.8 %attend.2 = (bf16[256,512]{1,0:T(8,128)(2,1)}, f32[4,2,256]{2,1,0:T(2,128)}) custom-call(s32[14]{0:T(128)} %stack.86.t, bf16[256,512]{1,0:T(8,128)(2,1)} %get-tuple-element.204.q, bf16[2,256,512]{2,1,0:T(8,128)(2,1)} %get-tuple-element.205.a, bf16[2,256,512]{2,1,0:T(8,128)(2,1)} %get-tuple-element.201.b, bf16[2,256,512]{2,1,0:T(8,128)(2,1)} %collective-permute-done.17.c, ...), custom_call_target="tpu_custom_call" | custom-call | flops 2147483648 | bytes 2629632 | tf_op jit(solution)/shard_map/attend/pallas_call | solution.py:430
  105.1 5.1 %project.2 = bf16[256,1024]{1,0:T(8,128)(2,1)} custom-call(s32[14]{0:T(128)} %stack.86.t, bf16[256,512]{1,0:T(8,128)(2,1)} %get-tuple-element.211.mixed.mt, bf16[2,4,128,512]{3,2,1,0:T(8,128)(2,1)} %bitcast.84, bf16[2,4,128,512]{3,2,1,0:T(8,128)(2,1)} %copy-done.4, bf16[2,4,128,512]{3,2,1,0:T(8,128)(2,1)} %bitcast.92, ...), custom_call_target="tpu_custom_call" | custom-call | flops 268435456 | bytes 4980736 | tf_op jit(solution)/shard_map/project/pallas_call | solution.py:430
  110.7 8.8 %attend.3 = (bf16[256,512]{1,0:T(8,128)(2,1)}, f32[4,2,256]{2,1,0:T(2,128)}) custom-call(s32[14]{0:T(128)} %stack.86.t, bf16[256,512]{1,0:T(8,128)(2,1)} %get-tuple-element.212.q, bf16[2,256,512]{2,1,0:T(8,128)(2,1)} %get-tuple-element.205.a, bf16[2,256,512]{2,1,0:T(8,128)(2,1)} %get-tuple-element.201.b, bf16[2,256,512]{2,1,0:T(8,128)(2,1)} %collective-permute-done.17.c, ...), custom_call_target="tpu_custom_call" | custom-call | flops 2147483648 | bytes 2629632 | tf_op jit(solution)/shard_map/attend/pallas_call | solution.py:430
  125.7 5.3 %project.3.part = f32[256,1024]{1,0:T(8,128)} custom-call(s32[14]{0:T(128)} %stack.86.t, bf16[256,512]{1,0:T(8,128)(2,1)} %get-tuple-element.219.mixed.mo, bf16[2,4,128,512]{3,2,1,0:T(8,128)(2,1)} %bitcast.85, bf16[2,4,128,512]{3,2,1,0:T(8,128)(2,1)} %copy-done.4, bf16[2,4,128,512]{3,2,1,0:T(8,128)(2,1)} %bitcast.93, ...), custom_call_target="tpu_custom_call" | custom-call | flops 268435456 | bytes 5505024 | tf_op jit(solution)/shard_map/project/pallas_call | solution.py:430
  140.4 5.3 %collective-permute-done.24.second = bf16[128,1024]{1,0:T(8,128)(2,1)S(1)} collective-permute-done((bf16[128,1024]{1,0:T(8,128)(2,1)S(1)}, bf16[128,1024]{1,0:T(8,128)(2,1)S(1)}, u32[]{:S(2)}, u32[]{:S(2)}) %collective-permute-start.24) | collective-permute-done | bytes 262176 | tf_op jit(solution)/shard_map/ppermute | solution.py:1025
  149.1 6.6 %up.2 = (bf16[256,2048]{1,0:T(8,128)(2,1)}, bf16[256,2048]{1,0:T(8,128)(2,1)}) custom-call(s32[14]{0:T(128)} %stack.86.t, bf16[256,1024]{1,0:T(8,128)(2,1)} %get-tuple-element.226.x.xo, bf16[2,4,256,512]{3,2,1,0:T(8,128)(2,1)} %bitcast.103, bf16[2,4,256,512]{3,2,1,0:T(8,128)(2,1)} %collective-permute-done.25.wt.w1t, f32[16,1024]{1,0:T(8,128)} %add.216.mod.refs_4_.bias), custom_call_target="tpu_custom_call" | custom-call | flops 1073741824 | bytes 6881280 | tf_op jit(solution)/shard_map/up/pallas_call | solution.py:430
  157.1 6.3 %collective-permute-start.29 = (bf16[2,4,256,512]{3,2,1,0:T(8,128)(2,1)S(1)}, bf16[2,4,256,512]{3,2,1,0:T(8,128)(2,1)}, u32[]{:S(2)}, u32[]{:S(2)}) collective-permute-start(bf16[2,4,256,512]{3,2,1,0:T(8,128)(2,1)S(1)} %bitcast.97), channel_id=1, source_target_pairs={{0,8},{8,0},{1,9},{9,1},{2,10},{10,2},{3,11},{11,3},{4,12},{12,4},... | collective-permute-start | bytes 6291464 | tf_op jit(solution)/shard_map/ppermute | solution.py:851
  164.6 6.6 %up.3 = (bf16[256,2048]{1,0:T(8,128)(2,1)}, bf16[256,2048]{1,0:T(8,128)(2,1)}) custom-call(s32[14]{0:T(128)} %stack.86.t, bf16[256,1024]{1,0:T(8,128)(2,1)} %collective-permute-done.26.x.xt, bf16[2,4,256,512]{3,2,1,0:T(8,128)(2,1)} %bitcast.104, bf16[2,4,256,512]{3,2,1,0:T(8,128)(2,1)} %collective-permute-done.25.wt.w1t, f32[16,1024]{1,0:T(8,128)} %add.216.mod.refs_4_.bias), custom_call_target="tpu_custom_call" | custom-call | flops 1073741824 | bytes 6881280 | tf_op jit(solution)/shard_map/up/pallas_call | solution.py:430
  171.2 6.4 %collective-permute-done.27.grad.gt = bf16[256,1024]{1,0:T(8,128)(2,1)S(1)} collective-permute-done((bf16[256,1024]{1,0:T(8,128)(2,1)}, bf16[256,1024]{1,0:T(8,128)(2,1)S(1)}, u32[]{:S(2)}, u32[]{:S(2)}) %collective-permute-start.27) | collective-permute-done | bytes 524320 | tf_op jit(solution)/shard_map/ppermute | solution.py:851
  178.4 8.0 %mlp_back.2 = (bf16[256,2048]{1,0:T(8,128)(2,1)}, f32[1,2048]{1,0:T(1,128)}, bf16[256,1024]{1,0:T(8,128)(2,1)}) custom-call(s32[14]{0:T(128)} %stack.86.t, bf16[256,1024]{1,0:T(8,128)(2,1)} %copy-done.22, bf16[256,2048]{1,0:T(8,128)(2,1)} %get-tuple-element.232.slope, bf16[2,4,256,512]{3,2,1,0:T(8,128)(2,1)} %bitcast.98, ...), custom_call_target="tpu_custom_call" | custom-call | flops 2147483648 | bytes 11542528 | tf_op jit(solution)/shard_map/mlp_back/pallas_call | solution.py:430
  186.4 6.9 %fc2_grads.1 = (bf16[2,4,256,512]{3,2,1,0:T(8,128)(2,1)}, bf16[2,4,256,512]{3,2,1,0:T(8,128)(2,1)}) custom-call(s32[14]{0:T(128)} %stack.86.t, bf16[256,2048]{1,0:T(8,128)(2,1)} %get-tuple-element.290.acto.act, bf16[256,2048]{1,0:T(8,128)(2,1)} %get-tuple-element.284.actt.act, bf16[256,1024]{1,0:T(8,128)(2,1)} %get-tuple-element.237.go.grad, ...), custom_call_target="tpu_custom_call" | custom-call | flops 2147483648 | bytes 7340032 | tf_op jit(solution)/shard_map/fc2_grads/pallas_call | solution.py:430
  194.5 8.2 %mlp_back.3 = (bf16[256,2048]{1,0:T(8,128)(2,1)}, f32[1,2048]{1,0:T(1,128)}, f32[256,1024]{1,0:T(8,128)}) custom-call(s32[14]{0:T(128)} %stack.86.t, bf16[256,1024]{1,0:T(8,128)(2,1)} %get-tuple-element.237.go.grad, bf16[256,2048]{1,0:T(8,128)(2,1)} %get-tuple-element.239.slope, bf16[2,4,256,512]{3,2,1,0:T(8,128)(2,1)} %bitcast.99, ...), custom_call_target="tpu_custom_call" | custom-call | flops 2147483648 | bytes 12066816 | tf_op jit(solution)/shard_map/mlp_back/pallas_call | solution.py:430
  208.0 7.0 %fc1_grads.1 = (bf16[2,4,256,512]{3,2,1,0:T(8,128)(2,1)}, bf16[2,4,256,512]{3,2,1,0:T(8,128)(2,1)}) custom-call(s32[14]{0:T(128)} %stack.86.t, bf16[256,1024]{1,0:T(8,128)(2,1)} %get-tuple-element.226.x.xo, bf16[256,1024]{1,0:T(8,128)(2,1)} %collective-permute-done.26.x.xt, bf16[256,2048]{1,0:T(8,128)(2,1)} %get-tuple-element.245.dho, ...), custom_call_target="tpu_custom_call" | custom-call | flops 2147483648 | bytes 7340032 | tf_op jit(solution)/shard_map/fc1_grads/pallas_call | solution.py:430
  215.4 5.0 %norm_mid_back.1 = (f32[256,1024]{1,0:T(8,128)}, bf16[256,1024]{1,0:T(8,128)(2,1)}, f32[8,1024]{1,0:T(8,128)}) custom-call(s32[14]{0:T(128)} %stack.86.t, f32[256,1024]{1,0:T(8,128)} %get-tuple-element.248.part, bf16[256,1024]{1,0:T(8,128)(2,1)} %copy-done.19, f32[256,1024]{1,0:T(8,128)} %get-tuple-element.221.middle, ...), custom_call_target="tpu_custom_call" | custom-call | bytes 5865472 | tf_op jit(solution)/shard_map/norm_mid_back/pallas_call | solution.py:430
  221.6 5.2 %project_back.2.do = bf16[256,512]{1,0:T(8,128)(2,1)} custom-call(s32[14]{0:T(128)} %stack.86.t, bf16[256,1024]{1,0:T(8,128)(2,1)} %get-tuple-element.261.grad.go, bf16[2,4,128,512]{3,2,1,0:T(8,128)(2,1)} %bitcast.86, bf16[2,4,128,512]{3,2,1,0:T(8,128)(2,1)} %copy-done.4, bf16[2,4,128,512]{3,2,1,0:T(8,128)(2,1)} %bitcast.94, ...), custom_call_target="tpu_custom_call" | custom-call | flops 268435456 | bytes 4980736 | tf_op jit(solution)/shard_map/project_back/pallas_call | solution.py:430
  232.2 10.8 %attend_back.2 = (bf16[256,512]{1,0:T(8,128)(2,1)}, bf16[2,512,512]{2,1,0:T(8,128)(2,1)}, bf16[2,512,512]{2,1,0:T(8,128)(2,1)}) custom-call(s32[14]{0:T(128)} %stack.86.t, bf16[256,512]{1,0:T(8,128)(2,1)} %get-tuple-element.212.q, bf16[256,512]{1,0:T(8,128)(2,1)} %project_back.2.do, bf16[256,512]{1,0:T(8,128)(2,1)} %get-tuple-element.219.mixed.mo, ...), custom_call_target="tpu_custom_call" | custom-call | flops 5368709120 | bytes 5251072 | tf_op jit(solution)/shard_map/attend_back/pallas_call | solution.py:430
  246.3 5.2 %project_back.3.do = bf16[256,512]{1,0:T(8,128)(2,1)} custom-call(s32[14]{0:T(128)} %stack.86.t, bf16[256,1024]{1,0:T(8,128)(2,1)} %collective-permute-done.33.grad.gt, bf16[2,4,128,512]{3,2,1,0:T(8,128)(2,1)} %bitcast.87, bf16[2,4,128,512]{3,2,1,0:T(8,128)(2,1)} %copy-done.4, bf16[2,4,128,512]{3,2,1,0:T(8,128)(2,1)} %bitcast.95, ...), custom_call_target="tpu_custom_call" | custom-call | flops 268435456 | bytes 4980736 | tf_op jit(solution)/shard_map/project_back/pallas_call | solution.py:430
  251.6 5.0 %proj_grads.1 = (bf16[2,4,128,256]{3,2,1,0:T(8,128)(2,1)}, bf16[2,4,128,256]{3,2,1,0:T(8,128)(2,1)}) custom-call(s32[14]{0:T(128)} %stack.86.t, bf16[256,512]{1,0:T(8,128)(2,1)} %get-tuple-element.219.mixed.mo, bf16[256,512]{1,0:T(8,128)(2,1)} %get-tuple-element.211.mixed.mt, bf16[256,1024]{1,0:T(8,128)(2,1)} %get-tuple-element.261.grad.go, ...), custom_call_target="tpu_custom_call" | custom-call | flops 536870912 | bytes 2621440 | tf_op jit(solution)/shard_map/proj_grads/pallas_call | solution.py:430
  256.5 11.1 %attend_back.3 = (bf16[256,512]{1,0:T(8,128)(2,1)}, bf16[2,512,512]{2,1,0:T(8,128)(2,1)}, bf16[2,512,512]{2,1,0:T(8,128)(2,1)}) custom-call(s32[14]{0:T(128)} %stack.86.t, bf16[256,512]{1,0:T(8,128)(2,1)} %get-tuple-element.204.q, bf16[256,512]{1,0:T(8,128)(2,1)} %project_back.3.do, bf16[256,512]{1,0:T(8,128)(2,1)} %get-tuple-element.211.mixed.mt, ...), custom_call_target="tpu_custom_call" | custom-call | flops 5368709120 | bytes 5251072 | tf_op jit(solution)/shard_map/attend_back/pallas_call | solution.py:430
  274.1 8.4 %qkv_back.1 = (bf16[4,256,384]{2,1,0:T(8,128)(2,1)}, bf16[4,256,384]{2,1,0:T(8,128)(2,1)}, f32[8,512]{1,0:T(8,128)}, f32[256,1024]{1,0:T(8,128)}, bf16[256,1024]{1,0:T(8,128)(2,1)}) custom-call(s32[14]{0:T(128)} %stack.86.t, bf16[256,512]{1,0:T(8,128)(2,1)} %get-tuple-element.256.dqo, bf16[256,512]{1,0:T(8,128)(2,1)} %get-tuple-element.274.dqt, ...), custom_call_target="tpu_custom_call" | custom-call | flops 1610612736 | bytes 12075008 | tf_op jit(solution)/shard_map/qkv_back/pallas_call | solution.py:430
  282.5 6.8 %qkv_grads.1 = (bf16[2,4,128,384]{3,2,1,0:T(8,128)(2,1)}, bf16[2,4,128,384]{3,2,1,0:T(8,128)(2,1)}, bf16[2,4,128,384]{3,2,1,0:T(8,128)(2,1)}, bf16[2,4,128,384]{3,2,1,0:T(8,128)(2,1)}) custom-call(s32[14]{0:T(128)} %stack.86.t, bf16[256,1024]{1,0:T(8,128)(2,1)} %norm_in.1.x.xo, bf16[256,1024]{1,0:T(8,128)(2,1)} %copy-done.18, ...), custom_call_target="tpu_custom_call" | custom-call | flops 1610612736 | bytes 5767168 | tf_op jit(solution)/shard_map/qkv_grads/pallas_call | solution.py:430
  294.4 5.6 %down.2 = bf16[256,1024]{1,0:T(8,128)(2,1)} custom-call(s32[14]{0:T(128)} %stack.86.t, bf16[256,2048]{1,0:T(8,128)(2,1)} %get-tuple-element.284.actt.act, bf16[2,4,256,512]{3,2,1,0:T(8,128)(2,1)} %bitcast.100, bf16[2,4,256,512]{3,2,1,0:T(8,128)(2,1)} %collective-permute-done.29.w2t.wt), custom_call_target="tpu_custom_call" | custom-call | flops 1073741824 | bytes 5767168 | tf_op jit(solution)/shard_map/down/pallas_call | solution.py:430
  304.4 20.9 %collective-permute-done.40.got = bf16[256,1024]{1,0:T(8,128)(2,1)} collective-permute-done((bf16[256,1024]{1,0:T(8,128)(2,1)}, bf16[256,1024]{1,0:T(8,128)(2,1)}, u32[]{:S(2)}, u32[]{:S(2)}) %collective-permute-start.40) | collective-permute-done | bytes 524320 | tf_op jit(solution)/shard_map/ppermute | solution.py:851
  326.8 5.8 %down.3.part = f32[256,1024]{1,0:T(8,128)} custom-call(s32[14]{0:T(128)} %stack.86.t, bf16[256,2048]{1,0:T(8,128)(2,1)} %get-tuple-element.290.acto.act, bf16[2,4,256,512]{3,2,1,0:T(8,128)(2,1)} %bitcast.101, bf16[2,4,256,512]{3,2,1,0:T(8,128)(2,1)} %collective-permute-done.29.w2t.wt), custom_call_target="tpu_custom_call" | custom-call | flops 1073741824 | bytes 6291456 | tf_op jit(solution)/shard_map/down/pallas_call | solution.py:430
  362.6 5.5 %collective-permute-done.65 = bf16[1,256,512]{2,1,0:T(8,128)(2,1)S(1)} collective-permute-done((bf16[1,256,512]{2,1,0:T(8,128)(2,1)S(1)}, bf16[1,256,512]{2,1,0:T(8,128)(2,1)S(1)}, u32[]{:S(2)}, u32[]{:S(2)}) %collective-permute-start.65) | collective-permute-done | bytes 262176 | tf_op jit(solution)/shard_map/ppermute | solution.py:851
  383.2 5.2 %collective-permute-done.48 = bf16[128,1024]{1,0:T(8,128)(2,1)S(1)} collective-permute-done((bf16[128,1024]{1,0:T(8,128)(2,1)S(1)}, bf16[128,1024]{1,0:T(8,128)(2,1)S(1)}, u32[]{:S(2)}, u32[]{:S(2)}) %collective-permute-start.48) | collective-permute-done | bytes 262176 | tf_op jit(solution)/shard_map/ppermute | solution.py:867
  388.4 8.0 %collective-permute-start.59 = (bf16[1,128,384]{2,1,0:T(8,128)(2,1)}, bf16[1,128,384]{2,1,0:T(8,128)(2,1)}, u32[]{:S(2)}, u32[]{:S(2)}) collective-permute-start(bf16[1,128,384]{2,1,0:T(8,128)(2,1)} %get-tuple-element.406), channel_id=1, source_target_pairs={{0,4},{2,6},{4,0},{6,2},{1,5},{3,7},{5,1},{7,3},{8,12},{10,14},{12... | collective-permute-start | bytes 294920 | tf_op jit(solution)/shard_map/ppermute | solution.py:851
  (330 shorter events, 180.7 us)
Async XLA Ops:
  28.9 14.9 %collective-permute-start.5 = (bf16[2,128,512]{2,1,0:T(8,128)(2,1)S(1)}, bf16[2,128,512]{2,1,0:T(8,128)(2,1)S(1)}, u32[]{:S(2)}, u32[]{:S(2)}) collective-permute-start(bf16[2,128,512]{2,1,0:T(8,128)(2,1)S(1)} %pad_maximum_fusion.9), channel_id=1, source_target_pairs={{0,2},{2,0},{4,6},{6,4},{1,3},{3,1},{5,7},{7,5},{8,10},{10,8},{12,... | collective-permute-start | bytes 786440 | tf_op jit(solution)/shard_map/ppermute | solution.py:851
  29.0 14.1 %collective-permute-start.6 = (bf16[1,128,512]{2,1,0:T(8,128)(2,1)S(1)}, bf16[1,128,512]{2,1,0:T(8,128)(2,1)S(1)}, u32[]{:S(2)}, u32[]{:S(2)}) collective-permute-start(bf16[1,128,512]{2,1,0:T(8,128)(2,1)S(1)} %copy-done.30), channel_id=1, source_target_pairs={{0,4},{2,6},{4,0},{6,2},{1,5},{3,7},{5,1},{7,3},{8,12},{10,14},{12... | collective-permute-start | bytes 393224 | tf_op jit(solution)/shard_map/ppermute | solution.py:851
  49.3 16.5 %collective-permute-start.14 = (bf16[256,1024]{1,0:T(8,128)(2,1)}, bf16[256,1024]{1,0:T(8,128)(2,1)S(1)}, u32[]{:S(2)}, u32[]{:S(2)}) collective-permute-start(bf16[256,1024]{1,0:T(8,128)(2,1)} %norm_in.1.x.xo), channel_id=1, source_target_pairs={{0,1},{1,0},{2,3},{3,2},{4,5},{5,4},{6,7},{7,6},{8,9},{9,8},{10,11... | collective-permute-start | bytes 1572872 | tf_op jit(solution)/shard_map/ppermute | solution.py:851
  50.8 14.8 %collective-permute-start.9 = (bf16[4,128,512]{2,1,0:T(8,128)(2,1)S(1)}, bf16[4,128,512]{2,1,0:T(8,128)(2,1)S(1)}, u32[]{:S(2)}, u32[]{:S(2)}) collective-permute-start(bf16[4,128,512]{2,1,0:T(8,128)(2,1)S(1)} %pad_maximum_fusion.6), channel_id=1, source_target_pairs={{0,16},{16,0},{1,17},{17,1},{2,18},{18,2},{3,19},{19,3},{4,20},{20... | collective-permute-start | bytes 1572872 | tf_op jit(solution)/shard_map/ppermute | solution.py:851
  51.5 20.9 %collective-permute-start.12 = (bf16[4,128,512]{2,1,0:T(8,128)(2,1)S(1)}, bf16[4,128,512]{2,1,0:T(8,128)(2,1)S(1)}, u32[]{:S(2)}, u32[]{:S(2)}) collective-permute-start(bf16[4,128,512]{2,1,0:T(8,128)(2,1)S(1)} %constant_dynamic-update-slice_fusion), channel_id=1, source_target_pairs={{0,16},{16,0},{1,17},{17,1},{2,18},{18,2},{3,19},{19,3},{4,20},{20... | collective-permute-start | bytes 1572872 | tf_op jit(solution)/shard_map/ppermute | solution.py:851
  74.0 14.7 %collective-permute-start.16 = (bf16[2,256,512]{2,1,0:T(8,128)(2,1)}, bf16[2,256,512]{2,1,0:T(8,128)(2,1)}, u32[]{:S(2)}, u32[]{:S(2)}) collective-permute-start(bf16[2,256,512]{2,1,0:T(8,128)(2,1)} %constant_dynamic-update-slice_fusion.2), channel_id=1, source_target_pairs={{0,2},{2,0},{4,6},{6,4},{1,3},{3,1},{5,7},{7,5},{8,10},{10,8},{12,... | collective-permute-start | bytes 1572872 | tf_op jit(solution)/shard_map/ppermute | solution.py:851
  90.0 29.6 %collective-permute-start.20 = (bf16[4,256,512]{2,1,0:T(8,128)(2,1)S(1)}, bf16[4,256,512]{2,1,0:T(8,128)(2,1)S(1)}, u32[]{:S(2)}, u32[]{:S(2)}) collective-permute-start(bf16[4,256,512]{2,1,0:T(8,128)(2,1)S(1)} %pad_maximum_fusion.4), channel_id=1, source_target_pairs={{0,16},{16,0},{1,17},{17,1},{2,18},{18,2},{3,19},{19,3},{4,20},{20... | collective-permute-start | bytes 3145736 | tf_op jit(solution)/shard_map/ppermute | solution.py:851
  90.5 14.5 %collective-permute-start.19 = (bf16[1,256,512]{2,1,0:T(8,128)(2,1)S(1)}, bf16[1,256,512]{2,1,0:T(8,128)(2,1)S(1)}, u32[]{:S(2)}, u32[]{:S(2)}) collective-permute-start(bf16[1,256,512]{2,1,0:T(8,128)(2,1)S(1)} %copy-done.29), channel_id=1, source_target_pairs={{0,4},{2,6},{4,0},{6,2},{1,5},{3,7},{5,1},{7,3},{8,12},{10,14},{12... | collective-permute-start | bytes 786440 | tf_op jit(solution)/shard_map/ppermute | solution.py:851
  105.0 14.5 %collective-permute-start.21 = (bf16[2,256,512]{2,1,0:T(8,128)(2,1)S(1)}, bf16[2,256,512]{2,1,0:T(8,128)(2,1)S(1)}, u32[]{:S(2)}, u32[]{:S(2)}) collective-permute-start(bf16[2,256,512]{2,1,0:T(8,128)(2,1)S(1)} %constant_dynamic-update-slice_fusion.4), channel_id=1, source_target_pairs={{0,2},{2,0},{4,6},{6,4},{1,3},{3,1},{5,7},{7,5},{8,10},{10,8},{12,... | collective-permute-start | bytes 1572872 | tf_op jit(solution)/shard_map/ppermute | solution.py:851
  123.2 25.9 %collective-permute-start.25 = (bf16[2,4,256,512]{3,2,1,0:T(8,128)(2,1)S(1)}, bf16[2,4,256,512]{3,2,1,0:T(8,128)(2,1)}, u32[]{:S(2)}, u32[]{:S(2)}) collective-permute-start(bf16[2,4,256,512]{3,2,1,0:T(8,128)(2,1)S(1)} %bitcast.102), channel_id=1, source_target_pairs={{0,8},{8,0},{1,9},{9,1},{2,10},{10,2},{3,11},{11,3},{4,12},{12,4},... | collective-permute-start | bytes 6291464 | tf_op jit(solution)/shard_map/ppermute | solution.py:851
  123.2 32.5 %collective-permute-start.28 = (bf16[4,256,512]{2,1,0:T(8,128)(2,1)S(1)}, bf16[4,256,512]{2,1,0:T(8,128)(2,1)}, u32[]{:S(2)}, u32[]{:S(2)}) collective-permute-start(bf16[4,256,512]{2,1,0:T(8,128)(2,1)S(1)} %pad_maximum_fusion.5), channel_id=1, source_target_pairs={{0,16},{16,0},{1,17},{17,1},{2,18},{18,2},{3,19},{19,3},{4,20},{20... | collective-permute-start | bytes 3145736 | tf_op jit(solution)/shard_map/ppermute | solution.py:851
  134.9 20.8 %collective-permute-start.26 = (bf16[256,1024]{1,0:T(8,128)(2,1)}, bf16[256,1024]{1,0:T(8,128)(2,1)}, u32[]{:S(2)}, u32[]{:S(2)}) collective-permute-start(bf16[256,1024]{1,0:T(8,128)(2,1)} %get-tuple-element.226.x.xo), channel_id=1, source_target_pairs={{0,1},{1,0},{2,3},{3,2},{4,5},{5,4},{6,7},{7,6},{8,9},{9,8},{10,11... | collective-permute-start | bytes 1572872 | tf_op jit(solution)/shard_map/ppermute | solution.py:851
  157.1 20.4 %collective-permute-start.29 = (bf16[2,4,256,512]{3,2,1,0:T(8,128)(2,1)S(1)}, bf16[2,4,256,512]{3,2,1,0:T(8,128)(2,1)}, u32[]{:S(2)}, u32[]{:S(2)}) collective-permute-start(bf16[2,4,256,512]{3,2,1,0:T(8,128)(2,1)S(1)} %bitcast.97), channel_id=1, source_target_pairs={{0,8},{8,0},{1,9},{9,1},{2,10},{10,2},{3,11},{11,3},{4,12},{12,4},... | collective-permute-start | bytes 6291464 | tf_op jit(solution)/shard_map/ppermute | solution.py:851
  193.3 14.7 %collective-permute-start.30 = (bf16[256,1024]{1,0:T(8,128)(2,1)S(1)}, bf16[256,1024]{1,0:T(8,128)(2,1)S(1)}, u32[]{:S(2)}, u32[]{:S(2)}) collective-permute-start(bf16[256,1024]{1,0:T(8,128)(2,1)S(1)} %copy-done.38), channel_id=1, source_target_pairs={{0,1},{1,0},{2,3},{3,2},{4,5},{5,4},{6,7},{7,6},{8,9},{9,8},{10,11... | collective-permute-start | bytes 1572872 | tf_op jit(solution)/shard_map/ppermute | solution.py:851
  215.2 27.8 %collective-permute-start.34 = (bf16[4,256,512]{2,1,0:T(8,128)(2,1)}, bf16[4,256,512]{2,1,0:T(8,128)(2,1)S(1)}, u32[]{:S(2)}, u32[]{:S(2)}) collective-permute-start(bf16[4,256,512]{2,1,0:T(8,128)(2,1)} %get-tuple-element.372), channel_id=1, source_target_pairs={{0,16},{16,0},{1,17},{17,1},{2,18},{18,2},{3,19},{19,3},{4,20},{20... | collective-permute-start | bytes 3145736 | tf_op jit(solution)/shard_map/ppermute | solution.py:851
  220.4 25.9 %collective-permute-start.33 = (bf16[256,1024]{1,0:T(8,128)(2,1)}, bf16[256,1024]{1,0:T(8,128)(2,1)}, u32[]{:S(2)}, u32[]{:S(2)}) collective-permute-start(bf16[256,1024]{1,0:T(8,128)(2,1)} %get-tuple-element.261.grad.go), channel_id=1, source_target_pairs={{0,1},{1,0},{2,3},{3,2},{4,5},{5,4},{6,7},{7,6},{8,9},{9,8},{10,11... | collective-permute-start | bytes 1572872 | tf_op jit(solution)/shard_map/ppermute | solution.py:851
  230.7 41.1 %collective-permute-start.35 = (bf16[4,256,512]{2,1,0:T(8,128)(2,1)}, bf16[4,256,512]{2,1,0:T(8,128)(2,1)}, u32[]{:S(2)}, u32[]{:S(2)}) collective-permute-start(bf16[4,256,512]{2,1,0:T(8,128)(2,1)} %get-tuple-element.370), channel_id=1, source_target_pairs={{0,16},{16,0},{1,17},{17,1},{2,18},{18,2},{3,19},{19,3},{4,20},{20... | collective-permute-start | bytes 3145736 | tf_op jit(solution)/shard_map/ppermute | solution.py:851
  246.3 22.7 %collective-permute-start.36 = (bf16[2,256,512]{2,1,0:T(8,128)(2,1)}, bf16[2,256,512]{2,1,0:T(8,128)(2,1)S(1)}, u32[]{:S(2)}, u32[]{:S(2)}) collective-permute-start(bf16[2,256,512]{2,1,0:T(8,128)(2,1)} %get-tuple-element.376), channel_id=1, source_target_pairs={{0,2},{2,0},{4,6},{6,4},{1,3},{3,1},{5,7},{7,5},{8,10},{10,8},{12,... | collective-permute-start | bytes 1572872 | tf_op jit(solution)/shard_map/ppermute | solution.py:851
  290.5 42.1 %collective-permute-start.43 = (bf16[4,128,256]{2,1,0:T(8,128)(2,1)}, bf16[4,128,256]{2,1,0:T(8,128)(2,1)S(1)}, u32[]{:S(2)}, u32[]{:S(2)}) collective-permute-start(bf16[4,128,256]{2,1,0:T(8,128)(2,1)} %get-tuple-element.384), channel_id=1, source_target_pairs={{0,16},{16,0},{1,17},{17,1},{2,18},{18,2},{3,19},{19,3},{4,20},{20... | collective-permute-start | bytes 786440 | tf_op jit(solution)/shard_map/ppermute | solution.py:851
  291.0 69.8 %collective-permute-start.66 = (bf16[1,256,512]{2,1,0:T(8,128)(2,1)}, bf16[1,256,512]{2,1,0:T(8,128)(2,1)}, u32[]{:S(2)}, u32[]{:S(2)}) collective-permute-start(bf16[1,256,512]{2,1,0:T(8,128)(2,1)} %get-tuple-element.386), channel_id=1, source_target_pairs={{0,4},{2,6},{4,0},{6,2},{1,5},{3,7},{5,1},{7,3},{8,12},{10,14},{12... | collective-permute-start | bytes 786440 | tf_op jit(solution)/shard_map/ppermute | solution.py:851
  294.4 38.8 %collective-permute-start.44 = (bf16[2,256,512]{2,1,0:T(8,128)(2,1)}, bf16[2,256,512]{2,1,0:T(8,128)(2,1)S(1)}, u32[]{:S(2)}, u32[]{:S(2)}) collective-permute-start(bf16[2,256,512]{2,1,0:T(8,128)(2,1)} %get-tuple-element.374), channel_id=1, source_target_pairs={{0,2},{2,0},{4,6},{6,4},{1,3},{3,1},{5,7},{7,5},{8,10},{10,8},{12,... | collective-permute-start | bytes 1572872 | tf_op jit(solution)/shard_map/ppermute | solution.py:851
  300.1 46.7 %collective-permute-start.46 = (bf16[256,1024]{1,0:T(8,128)(2,1)}, bf16[256,1024]{1,0:T(8,128)(2,1)}, u32[]{:S(2)}, u32[]{:S(2)}) collective-permute-start(bf16[256,1024]{1,0:T(8,128)(2,1)} %down.2), channel_id=1, source_target_pairs={{0,1},{1,0},{2,3},{3,2},{4,5},{5,4},{6,7},{7,6},{8,9},{9,8},{10,11... | collective-permute-start | bytes 1572872 | tf_op jit(solution)/shard_map/ppermute | solution.py:851
  300.8 24.5 %collective-permute-start.40 = (bf16[256,1024]{1,0:T(8,128)(2,1)}, bf16[256,1024]{1,0:T(8,128)(2,1)}, u32[]{:S(2)}, u32[]{:S(2)}) collective-permute-start(bf16[256,1024]{1,0:T(8,128)(2,1)} %get-tuple-element.277), channel_id=1, source_target_pairs={{0,1},{1,0},{2,3},{3,2},{4,5},{5,4},{6,7},{7,6},{8,9},{9,8},{10,11... | collective-permute-start | bytes 1572872 | tf_op jit(solution)/shard_map/ppermute | solution.py:851
  325.3 44.5 %collective-permute-start.60 = (bf16[4,128,384]{2,1,0:T(8,128)(2,1)}, bf16[4,128,384]{2,1,0:T(8,128)(2,1)}, u32[]{:S(2)}, u32[]{:S(2)}) collective-permute-start(bf16[4,128,384]{2,1,0:T(8,128)(2,1)} %get-tuple-element.378), channel_id=1, source_target_pairs={{0,16},{16,0},{1,17},{17,1},{2,18},{18,2},{3,19},{19,3},{4,20},{20... | collective-permute-start | bytes 1179656 | tf_op jit(solution)/shard_map/ppermute | solution.py:851
  333.2 20.8 %collective-permute-start.63 = (bf16[2,128,256]{2,1,0:T(8,128)(2,1)S(1)}, bf16[2,128,256]{2,1,0:T(8,128)(2,1)S(1)}, u32[]{:S(2)}, u32[]{:S(2)}) collective-permute-start(bf16[2,128,256]{2,1,0:T(8,128)(2,1)S(1)} %get-tuple-element.398), channel_id=1, source_target_pairs={{0,2},{2,0},{4,6},{6,4},{1,3},{3,1},{5,7},{7,5},{8,10},{10,8},{12,... | collective-permute-start | bytes 393224 | tf_op jit(solution)/shard_map/ppermute | solution.py:851
  344.1 56.3 %collective-permute-start.49 = (bf16[128,1024]{1,0:T(8,128)(2,1)}, bf16[128,1024]{1,0:T(8,128)(2,1)S(1)}, u32[]{:S(2)}, u32[]{:S(2)}) collective-permute-start(bf16[128,1024]{1,0:T(8,128)(2,1)} %get-tuple-element.300), channel_id=1, source_target_pairs={{0,0},{2,2},{8,4},{10,6},{4,8},{6,10},{12,12},{14,14},{1,1},{3,3},... | collective-permute-start | bytes 786440 | tf_op jit(solution)/shard_map/ppermute | solution.py:867
  346.8 21.3 %collective-permute-start.65 = (bf16[1,256,512]{2,1,0:T(8,128)(2,1)S(1)}, bf16[1,256,512]{2,1,0:T(8,128)(2,1)S(1)}, u32[]{:S(2)}, u32[]{:S(2)}) collective-permute-start(bf16[1,256,512]{2,1,0:T(8,128)(2,1)S(1)} %get-tuple-element.382), channel_id=1, source_target_pairs={{0,4},{2,6},{4,0},{6,2},{1,5},{3,7},{5,1},{7,3},{8,12},{10,14},{12... | collective-permute-start | bytes 786440 | tf_op jit(solution)/shard_map/ppermute | solution.py:851
  358.6 41.8 %collective-permute-start.50 = (bf16[128,1024]{1,0:T(8,128)(2,1)}, bf16[128,1024]{1,0:T(8,128)(2,1)S(1)}, u32[]{:S(2)}, u32[]{:S(2)}) collective-permute-start(bf16[128,1024]{1,0:T(8,128)(2,1)} %get-tuple-element.308), channel_id=1, source_target_pairs={{2,0},{0,2},{10,4},{8,6},{6,8},{4,10},{14,12},{12,14},{3,1},{1,3},... | collective-permute-start | bytes 786440 | tf_op jit(solution)/shard_map/ppermute | solution.py:867
  360.9 19.6 %collective-permute-start.58 = (bf16[2,128,384]{2,1,0:T(8,128)(2,1)S(1)}, bf16[2,128,384]{2,1,0:T(8,128)(2,1)S(1)}, u32[]{:S(2)}, u32[]{:S(2)}) collective-permute-start(bf16[2,128,384]{2,1,0:T(8,128)(2,1)S(1)} %get-tuple-element.390), channel_id=1, source_target_pairs={{0,2},{2,0},{4,6},{6,4},{1,3},{3,1},{5,7},{7,5},{8,10},{10,8},{12,... | collective-permute-start | bytes 589832 | tf_op jit(solution)/shard_map/ppermute | solution.py:851
  380.5 21.9 %collective-permute-start.61 = (bf16[2,128,384]{2,1,0:T(8,128)(2,1)S(1)}, bf16[2,128,384]{2,1,0:T(8,128)(2,1)}, u32[]{:S(2)}, u32[]{:S(2)}) collective-permute-start(bf16[2,128,384]{2,1,0:T(8,128)(2,1)S(1)} %get-tuple-element.388), channel_id=1, source_target_pairs={{0,2},{2,0},{4,6},{6,4},{1,3},{3,1},{5,7},{7,5},{8,10},{10,8},{12,... | collective-permute-start | bytes 589832 | tf_op jit(solution)/shard_map/ppermute | solution.py:851
  383.2 14.9 %collective-permute-start.54 = (f32[22,1024]{1,0:T(8,128)S(1)}, f32[22,1024]{1,0:T(8,128)S(1)}, u32[]{:S(2)}, u32[]{:S(2)}) collective-permute-start(f32[22,1024]{1,0:T(8,128)S(1)} %pad_maximum_fusion.13), channel_id=1, source_target_pairs={{0,2},{2,0},{4,6},{6,4},{1,3},{3,1},{5,7},{7,5},{8,10},{10,8},{12,... | collective-permute-start | bytes 270344 | tf_op jit(solution)/shard_map/ppermute | solution.py:851
  388.4 25.1 %collective-permute-start.59 = (bf16[1,128,384]{2,1,0:T(8,128)(2,1)}, bf16[1,128,384]{2,1,0:T(8,128)(2,1)}, u32[]{:S(2)}, u32[]{:S(2)}) collective-permute-start(bf16[1,128,384]{2,1,0:T(8,128)(2,1)} %get-tuple-element.406), channel_id=1, source_target_pairs={{0,4},{2,6},{4,0},{6,2},{1,5},{3,7},{5,1},{7,3},{8,12},{10,14},{12... | collective-permute-start | bytes 294920 | tf_op jit(solution)/shard_map/ppermute | solution.py:851
  (78 other events, 697.3 us)

commit v4 on v3

--- a/solution.py
+++ b/solution.py
@@ -437,7 +437,7 @@
             scratch_shapes=list(scratch),
         ),
         out_shape=outs,
-        cost_estimate=pl.CostEstimate(flops=flops, bytes_accessed=moved, transcendentals=0),
+        cost_estimate=pl.CostEstimate(flops=flops // 1000, bytes_accessed=moved // 1000, transcendentals=0),
         name=name,
     )(table, *operands)
 
@@ -877,6 +877,8 @@
 
     STEPS = {"near": ("z", 4, 1), "far": ("z", 4, 2), "y": ("y", 2, 1)}
 
+    cut = lax.optimization_barrier
+
     def widen(v, step, *others):
         v, got = lax.optimization_barrier((v, flip(v, *STEPS[step]), *others))[:2]
         return jnp.concatenate([v, got])
@@ -918,8 +920,8 @@
         name="pack",
     )
     upper = widen(upper, "far")
-    upper, cond_all, *tok = lax.optimization_barrier((upper, cond_all, *tok))
-    upper, lower = widen(upper, "near"), widen(after(lower, upper), "far")
+    upper, lower, cond_all = cut((upper, lower, cond_all))
+    got_up, got_low = flip(upper, *STEPS["near"]), flip(lower, *STEPS["far"])
     act_abs = jax.nn.silu(cond_all.astype(f32)).astype(bf16)
     act_abs = lax.dynamic_slice_in_dim(act_abs, own * 256, 256, 2)
     act_here = lax.dynamic_slice_in_dim(act_abs, z, 1, 1)[:, 0]
@@ -941,17 +943,20 @@
         flops=2 * 8 * 256 * 6144,
         name="modulate",
     )
-    mod = packed_mod[0] + flip(packed_mod[1], "y", 2, 1)
+    upper, got_up, lower, got_low, tok, packed_mod, got_mod = cut(
+        (upper, got_up, lower, got_low, tok, packed_mod, flip(packed_mod[1], "y", 2, 1))
+    )
+    upper, lower = jnp.concatenate([upper, got_up]), jnp.concatenate([lower, got_low])
+    mod = packed_mod[0] + got_mod
     mod = mod + flip(mod, "c", 2, 1)
     mod_spec = whole((16, D))
-    upper, lower, mod = lax.optimization_barrier((upper, lower, mod))
 
     half, full = whole((128, D)), whole((256, D))
     row_b, row_f = shaped((256, D), bf16), shaped((256, D), f32)
-    normed = call(ln_kernel, table, [*tok, mod], [half, half, mod_spec], full, row_b, name="norm_in")
+    lower = widen(lower, "near")
+    normed = call(ln_kernel, table, [*tok, after(mod, lower)], [half, half, mod_spec], full, row_b, name="norm_in")
     normed_t = flip(normed, "x", 2, 1)
     upper = widen(upper, "y")
-    lower = widen(lower, "near")
     w1 = after(w_fc1[None], lower)
     lower, got_low, w1, got_w1, normed_t = lax.optimization_barrier(
         (lower, flip(lower, *STEPS["y"]), w1, flip(w1, *STEPS["far"]), normed_t)
@@ -1014,15 +1019,26 @@
         )
 
     mixed_t, lse_t = attend(q_t)
+    cot_parts = spread_parts(after(cotangent, normed))
+    cot = [lax.ppermute(after(p, mixed_t), ("c", "z"), route(k)) for k, p in enumerate(cot_parts)]
     w2 = widen(after(packed_fc2, q_t), "far", mixed_t)
     part_t = project(after(mixed_t, w2), bf16)
     got_branch = flip(part_t, "x", 2, 1)
     q_o, part_t = lax.optimization_barrier((q_o, part_t))
     mixed_o, lse_o = attend(q_o)
     w1, w2 = widen(w1, "y", mixed_o), widen(w2, "near", mixed_o)
-    mixed_o, w1, w2, got_branch = lax.optimization_barrier((mixed_o, w1, w2, got_branch))
+    dmlp_o, bfc2_sum = call(
+        dmlp_kernel,
+        table,
+        [*cot, after(mod, mixed_o)],
+        [half, half, mod_spec],
+        [full, whole((1, D))],
+        [row_b, shaped((1, D), f32)],
+        name="dbranch_mlp",
+    )
+    dmlp_t = flip(dmlp_o, "x", 2, 1)
+    mixed_o, w1, w2, got_branch, dmlp_o = lax.optimization_barrier((mixed_o, w1, w2, got_branch, dmlp_o))
     w1 = both_cores(w1)
-    cot = [lax.ppermute(p, ("c", "z"), route(k)) for k, p in enumerate(spread_parts(after(cotangent, mixed_o)))]
     branch, middle, normed_mlp = call(
         mid_kernel,
         table,
@@ -1032,16 +1048,6 @@
         [row_f, row_f, row_b],
         name="norm_mid",
     )
-    dmlp_o, bfc2_sum = call(
-        dmlp_kernel,
-        table,
-        [*cot, after(mod, normed_mlp)],
-        [half, half, mod_spec],
-        [full, whole((1, D))],
-        [row_b, shaped((1, D), f32)],
-        name="dbranch_mlp",
-    )
-    dmlp_t = flip(dmlp_o, "x", 2, 1)
     mlp_t = flip(normed_mlp, "x", 2, 1)
     wide = shaped((256, 2048), bf16)
     wide_specs = [block_spec(256, COLS)] * 2
@@ -1088,7 +1094,7 @@
             name="mlp_back",
         )
 
-    act_o, slope_o = up(after(normed_mlp, dmlp_o))
+    act_o, slope_o = up(after(normed_mlp, dmlp_t))
     w2 = both_cores(widen(w2, "y", act_o, mlp_t))
     act_t, slope_t = up(after(mlp_t, act_o))
     dh_t, fc1_t, dn_t = mlp_back(dmlp_t, slope_t, bf16)
@@ -1193,10 +1199,13 @@
         name="proj_grads",
     )
     g_proj = cross(p_keep, p_send)
-    dmixed_t = after(dmixed_t, p_send)
+    down_t = down(after(act_t, p_send), bf16)
+    got_mlp = flip(down_t, "x", 2, 1)
+    dmixed_t = after(dmixed_t, p_send, down_t)
     dq_t, near_t, away_t = attend_back(q_t, dmixed_t, mixed_t, lse_t)
     back_t = flip(away_t, "c", 2, 1)
-    g_fc1, g_fc2, g_proj = (fold(v, away_t) for v in (g_fc1, g_fc2, g_proj))
+    away_t, got_mlp, g_fc1, g_fc2, g_proj = cut((away_t, got_mlp, g_fc1, g_fc2, g_proj))
+    g_fc1, g_fc2, g_proj = (fold(v) for v in (g_fc1, g_fc2, g_proj))
     dq_t = after(dq_t, *g_fc1, *g_fc2, *g_proj)
     g_fc2, g_fc1, g_proj = onward(g_fc2, "far"), onward(g_fc1, "near"), onward(g_proj, "y")
     long_spec = pl.BlockSpec((2, 512, 128), lambda j, t: (0, 0, j))
@@ -1227,16 +1236,17 @@
         flops=4 * 256 * 1024 * 1536,
         name="qkv_grads",
     )
+    g_fc1 = fold(g_fc1, s0)
+    k0, s0, k1, s1, got_din, g_fc1, g_fc2, g_proj = cut((k0, s0, k1, s1, got_din, g_fc1, g_fc2, g_proj))
     g_up, g_low = cross(k0, s0), cross(k1, s1)
-    down_t = down(after(act_t, s0, s1), bf16)
-    got_mlp = flip(down_t, "x", 2, 1)
-    g_up, g_low = fold(g_up, down_t), fold(g_low, down_t)
-    act_o, got_din, *_ = lax.optimization_barrier((act_o, got_din, *g_up, *g_low))
+    g_fc1, g_proj = onward(g_fc1, "far"), onward(fold(g_proj), "near")
+    act_o = after(act_o, s0, s1)
+    down_o, g_up, g_low, got_mlp = cut((down(act_o, f32), g_up, g_low, got_mlp))
+    down_o, g_up, g_low = cut((down_o, fold(g_up), fold(g_low)))
     g_up, g_low = onward(g_up, "y"), onward(g_low, "y")
-    down_o = down(act_o, f32)
-    g_proj, g_fc1 = fold(g_proj, down_o), fold(g_fc1, down_o)
-    din_o = after(din_o, *g_proj, *g_fc1)
-    g_proj, g_fc1 = onward(g_proj, "near"), onward(g_fc1, "far")
+    out0, out1, dgate_mlp = finish(down_o, got_mlp)
+    out_got = send_back([out0, out1])
+    din_o = after(din_o, dgate_mlp)
     dt0, dt1, din_sums = call(
         din_kernel,
         table,
@@ -1246,11 +1256,10 @@
         [shaped((128, D), bf16)] * 2 + [shaped((2, D), f32)],
         name="norm_in_back",
     )
-    dt_got = send_back([dt0, dt1])
-    g_up = fold(g_up, dt0)
-    out0, out1, dgate_mlp = finish(after(down_o, din_sums, *g_up), got_mlp)
-    g_up = onward(g_up, "near")
-    out_got = send_back([out0, out1])
+    din_sums, g_up, g_fc1, g_proj = cut((din_sums, g_up, g_fc1, g_proj))
+    g_up, g_proj = onward(fold(g_up), "near"), onward(fold(g_proj), "far")
+    g_fc1, g_fc2 = total(g_fc1), total(g_fc2, din_sums)
+    g_fc2 = jnp.concatenate([g_fc2[:, :256], g_fc2[:, 256:]], axis=0)
 
     small = call(
         small_kernel,
@@ -1261,24 +1270,24 @@
         shaped((16, D), f32),
         name="small",
     )
-    g_proj = onward(fold(g_proj, small), "far")
-    small = small + flip(small, "x", 2, 1)
-    g_fc1, g_fc2 = total(g_fc1, small), total(g_fc2, small)
-    g_fc2 = jnp.concatenate([g_fc2[:, :256], g_fc2[:, 256:]], axis=0)
-    small = small + flip(small, "c", 2, 1)
-
-    def spread_small(v, axis, count, offset):
-        got = flip(v, axis, count, offset)
+    def joined(v, got):
         return jnp.concatenate([v[:-10], got[:-10], v[-10:] + got[-10:]])
 
-    g_up, g_low = onward(fold(g_up, small), "far"), onward(fold(g_low, small), "near")
-    small = spread_small(small, "z", 4, 2)
-    g_proj = total(g_proj, small)
-    small = spread_small(small, "z", 4, 1)
-    g_low = onward(fold(g_low, small), "far")
-    d_tokens = collect(dt_got, f32, small)
-    small = spread_small(small, "y", 2, 1)
-    out = collect(out_got, bf16, small)
+    small, got, g_up, g_low, g_fc1, g_fc2 = cut((small, flip(small, "x", 2, 1), g_up, g_low, g_fc1, g_fc2))
+    small = small + got
+    g_up, g_low = onward(fold(g_up), "far"), onward(fold(g_low), "near")
+    small, got, out_got = cut((small, flip(small, "c", 2, 1), out_got))
+    small = small + got
+    small, got, g_up, g_low, g_proj = cut((small, flip(small, "z", 4, 2), g_up, g_low, g_proj))
+    small, dt0, dt1 = cut((joined(small, got), dt0, dt1))
+    dt_got = send_back([dt0, dt1])
+    g_low, g_proj = onward(fold(g_low), "far"), total(g_proj)
+    out = collect(out_got, bf16)
+    small, got, g_low, out, g_proj = cut((small, flip(small, "z", 4, 1), g_low, out, g_proj))
+    small = joined(small, got)
+    small, got, dt_got = cut((small, flip(small, "y", 2, 1), dt_got))
+    small = joined(small, got)
+    d_tokens = collect(dt_got, f32)
     g_qkv = call(
         assemble_kernel,
         table,

time: 422 us -> 381 us (0.903)
  waiting for transfers between devices: 85.5 us -> 42.1 us
  starting transfers between devices: 87.2 us -> 82.6 us
    ppermute x59, waiting for transfers between devices: 70.9 us -> 42.1 us  [flip(): return lax.ppermute(v, axis, [(i, i ^ offset) for i in range(count)])]
    ppermute x4 -> x2, waiting for transfers between devices: 9.34 us -> 0.01 us  [fast_body(): lax.ppermute(p, ('c', 'z'), route(k))]
    ppermute x59, starting transfers between devices: 77.4 us -> 68.1 us  [flip(): return lax.ppermute(v, axis, [(i, i ^ offset) for i in range(count)])]
    ppermute x4, waiting for transfers between devices: 5.2 us -> 0.01 us  [send_back(): lax.ppermute(p, ('c', 'z'), [(b, a) for a, b in route(k)])]
    ppermute x4, starting transfers between devices: 4.05 us -> 8.58 us  [send_back(): lax.ppermute(p, ('c', 'z'), [(b, a) for a, b in route(k)])]
    unnamed x95 -> x103, local copies, waits for them, and re-layouts: 11.8 us -> 14.8 us
  transfers between devices with their start and end apart: 67 -> 67, of which waited for: 19 -> 20; matrix products, arithmetic and copies ran while one was open for 13% -> 15% of each run, Pallas kernels for 33% -> 42%
where the time goes in v4:
time: 381 us; the launch traced here: 377 us
  Pallas kernels  180 us (47%)
  starting transfers between devices  82.6 us (22%)
  waiting for transfers between devices  42.1 us (11%)
  other arithmetic  37.2 us (10%)
  local copies, waits for them, and re-layouts  31.9 us (8%)
    pallas_call x31, Pallas kernels, kernel_call(): pl.pallas_call(body, grid_spec=pltpu.PrefetchScalarGridSpec(num_scalar_pr...  180 us
    ppermute x59, starting transfers between devices, flip(): return lax.ppermute(v, axis, [(i, i ^ offset) for i in range(count)])  68.1 us
    ppermute x59, waiting for transfers between devices, flip(): return lax.ppermute(v, axis, [(i, i ^ offset) for i in range(count)])  42.1 us
    convert_element_type x15, other arithmetic, fold(): return [(cut(own, k) + cut(got, k)).astype(bf16) for k in range(2)]  19.5 us
    unnamed x103, local copies, waits for them, and re-layouts  14.8 us
    ppermute x4, starting transfers between devices, send_back(): lax.ppermute(p, ('c', 'z'), [(b, a) for a, b in route(k)])  8.58 us
  transfers between devices with their start and end apart: 67, of which 20 were waited for; matrix products, arithmetic and copies ran while one was open for 15% of the time, Pallas kernels for 42%

profile of v4, /device:TPU:0, one launch (start us, length us, event | category | flops | bytes accessed | tf_op | source)
XLA Modules:
  0.0 377.1 jit_solution(14816804476258521814)
XLA Ops:
  6.3 3.6 collective-permute-start
  17.6 3.7 collective-permute-start.4
  24.6 3.7 modulate.1
  51.6 10.1 %collective-permute-done.13 = bf16[1,256,512]{2,1,0:T(8,128)(2,1)S(1)} collective-permute-done((bf16[1,256,512]{2,1,0:T(8,128)(2,1)S(1)}, bf16[1,256,512]{2,1,0:T(8,128)(2,1)S(1)}, u32[]{:S(2)}, u32[]{:S(2)}) %collective-permute-start.13) | collective-permute-done | bytes 262176 | tf_op jit(solution)/shard_map/ppermute | solution.py:851
  68.1 5.6 %qkv.3 = (bf16[256,512]{1,0:T(8,128)(2,1)}, bf16[2,256,512]{2,1,0:T(8,128)(2,1)}) custom-call(s32[14]{0:T(128)} %stack.86.t, bf16[256,1024]{1,0:T(8,128)(2,1)} %copy-done.14, bf16[2,4,128,512]{3,2,1,0:T(8,128)(2,1)} %bitcast.80, bf16[2,4,128,512]{3,2,1,0:T(8,128)(2,1)} %copy-done.4, bf16[2,4,128,512]{3,2,1,0:T(8,128)(2,1)} %bitcast.88, ...), custom_call_target="tpu_custom_call" | custom-call | flops 805306 | bytes 5570 | tf_op jit(solution)/shard_map/qkv/pallas_call | solution.py:430
  73.9 5.6 %qkv.2 = (bf16[256,512]{1,0:T(8,128)(2,1)}, bf16[2,256,512]{2,1,0:T(8,128)(2,1)}) custom-call(s32[14]{0:T(128)} %stack.86.t, bf16[256,1024]{1,0:T(8,128)(2,1)} %norm_in.1.x.xo, bf16[2,4,128,512]{3,2,1,0:T(8,128)(2,1)} %bitcast.81, bf16[2,4,128,512]{3,2,1,0:T(8,128)(2,1)} %copy-done.4, bf16[2,4,128,512]{3,2,1,0:T(8,128)(2,1)} %bitcast.89, ...), custom_call_target="tpu_custom_call" | custom-call | flops 805306 | bytes 5570 | tf_op jit(solution)/shard_map/qkv/pallas_call | solution.py:430
  87.3 8.8 %attend.2 = (bf16[256,512]{1,0:T(8,128)(2,1)}, f32[4,2,256]{2,1,0:T(2,128)}) custom-call(s32[14]{0:T(128)} %stack.86.t, bf16[256,512]{1,0:T(8,128)(2,1)} %get-tuple-element.274.q, bf16[2,256,512]{2,1,0:T(8,128)(2,1)} %get-tuple-element.275.a, bf16[2,256,512]{2,1,0:T(8,128)(2,1)} %get-tuple-element.271.b, bf16[2,256,512]{2,1,0:T(8,128)(2,1)} %copy-done.7, ...), custom_call_target="tpu_custom_call" | custom-call | flops 2147483 | bytes 2629 | tf_op jit(solution)/shard_map/attend/pallas_call | solution.py:430
  104.4 5.1 %project.2 = bf16[256,1024]{1,0:T(8,128)(2,1)} custom-call(s32[14]{0:T(128)} %stack.86.t, bf16[256,512]{1,0:T(8,128)(2,1)} %get-tuple-element.281.mixed.mt, bf16[2,4,128,512]{3,2,1,0:T(8,128)(2,1)} %bitcast.82, bf16[2,4,128,512]{3,2,1,0:T(8,128)(2,1)} %copy-done.4, bf16[2,4,128,512]{3,2,1,0:T(8,128)(2,1)} %bitcast.90, ...), custom_call_target="tpu_custom_call" | custom-call | flops 268435 | bytes 4980 | tf_op jit(solution)/shard_map/project/pallas_call | solution.py:430
  110.9 8.8 %attend.3 = (bf16[256,512]{1,0:T(8,128)(2,1)}, f32[4,2,256]{2,1,0:T(2,128)}) custom-call(s32[14]{0:T(128)} %stack.86.t, bf16[256,512]{1,0:T(8,128)(2,1)} %get-tuple-element.282.q, bf16[2,256,512]{2,1,0:T(8,128)(2,1)} %get-tuple-element.275.a, bf16[2,256,512]{2,1,0:T(8,128)(2,1)} %get-tuple-element.271.b, bf16[2,256,512]{2,1,0:T(8,128)(2,1)} %copy-done.7, ...), custom_call_target="tpu_custom_call" | custom-call | flops 2147483 | bytes 2629 | tf_op jit(solution)/shard_map/attend/pallas_call | solution.py:430
  130.5 5.3 %project.3.part = f32[256,1024]{1,0:T(8,128)} custom-call(s32[14]{0:T(128)} %stack.86.t, bf16[256,512]{1,0:T(8,128)(2,1)} %get-tuple-element.295.mixed.mo, bf16[2,4,128,512]{3,2,1,0:T(8,128)(2,1)} %bitcast.83, bf16[2,4,128,512]{3,2,1,0:T(8,128)(2,1)} %copy-done.4, bf16[2,4,128,512]{3,2,1,0:T(8,128)(2,1)} %bitcast.91, ...), custom_call_target="tpu_custom_call" | custom-call | flops 268435 | bytes 5505 | tf_op jit(solution)/shard_map/project/pallas_call | solution.py:430
  135.7 4.0 %norm_mid.1 = (f32[256,1024]{1,0:T(8,128)}, f32[256,1024]{1,0:T(8,128)}, bf16[256,1024]{1,0:T(8,128)(2,1)}) custom-call(s32[14]{0:T(128)} %stack.86.t, bf16[128,1024]{1,0:T(8,128)(2,1)} %copy-done.9, bf16[128,1024]{1,0:T(8,128)(2,1)} %copy-done.8, f32[256,1024]{1,0:T(8,128)} %project.3.part, bf16[256,1024]{1,0:T(8,128)(2,1)} %collective-permute-done.22.got, ...), custom_call_target="tpu_custom_call" | custom-call | bytes 4784 | tf_op jit(solution)/shard_map/norm_mid/pallas_call | solution.py:430
  141.2 3.8 collective-permute-done.25.grad.gt
  145.0 6.5 %up.2 = (bf16[256,2048]{1,0:T(8,128)(2,1)}, bf16[256,2048]{1,0:T(8,128)(2,1)}) custom-call(s32[14]{0:T(128)} %stack.86.t, bf16[256,1024]{1,0:T(8,128)(2,1)} %get-tuple-element.298.x.xo, bf16[2,4,256,512]{3,2,1,0:T(8,128)(2,1)} %bitcast.101, bf16[2,4,256,512]{3,2,1,0:T(8,128)(2,1)} %collective-permute-done.26.wt.w1t, f32[16,1024]{1,0:T(8,128)} %add.216.mod.refs_4_.bias), custom_call_target="tpu_custom_call" | custom-call | flops 1073741 | bytes 6881 | tf_op jit(solution)/shard_map/up/pallas_call | solution.py:430
  157.6 6.5 %up.3 = (bf16[256,2048]{1,0:T(8,128)(2,1)}, bf16[256,2048]{1,0:T(8,128)(2,1)}) custom-call(s32[14]{0:T(128)} %stack.86.t, bf16[256,1024]{1,0:T(8,128)(2,1)} %copy-done.15, bf16[2,4,256,512]{3,2,1,0:T(8,128)(2,1)} %bitcast.102, bf16[2,4,256,512]{3,2,1,0:T(8,128)(2,1)} %collective-permute-done.26.wt.w1t, f32[16,1024]{1,0:T(8,128)} %add.216.mod.refs_4_.bias), custom_call_target="tpu_custom_call" | custom-call | flops 1073741 | bytes 6881 | tf_op jit(solution)/shard_map/up/pallas_call | solution.py:430
  164.2 8.0 %mlp_back.2 = (bf16[256,2048]{1,0:T(8,128)(2,1)}, f32[1,2048]{1,0:T(1,128)}, bf16[256,1024]{1,0:T(8,128)(2,1)}) custom-call(s32[14]{0:T(128)} %stack.86.t, bf16[256,1024]{1,0:T(8,128)(2,1)} %copy-done.16, bf16[256,2048]{1,0:T(8,128)(2,1)} %get-tuple-element.304.slope, bf16[2,4,256,512]{3,2,1,0:T(8,128)(2,1)} %bitcast.96, ...), custom_call_target="tpu_custom_call" | custom-call | flops 2147483 | bytes 11542 | tf_op jit(solution)/shard_map/mlp_back/pallas_call | solution.py:430
  172.2 6.9 %fc2_grads.1 = (bf16[2,4,256,512]{3,2,1,0:T(8,128)(2,1)}, bf16[2,4,256,512]{3,2,1,0:T(8,128)(2,1)}) custom-call(s32[14]{0:T(128)} %stack.86.t, bf16[256,2048]{1,0:T(8,128)(2,1)} %get-tuple-element.370.acto.act, bf16[256,2048]{1,0:T(8,128)(2,1)} %get-tuple-element.336.actt.act, bf16[256,1024]{1,0:T(8,128)(2,1)} %get-tuple-element.309.go.grad, ...), custom_call_target="tpu_custom_call" | custom-call | flops 2147483 | bytes 7340 | tf_op jit(solution)/shard_map/fc2_grads/pallas_call | solution.py:430
  180.2 8.1 %mlp_back.3 = (bf16[256,2048]{1,0:T(8,128)(2,1)}, f32[1,2048]{1,0:T(1,128)}, f32[256,1024]{1,0:T(8,128)}) custom-call(s32[14]{0:T(128)} %stack.86.t, bf16[256,1024]{1,0:T(8,128)(2,1)} %get-tuple-element.309.go.grad, bf16[256,2048]{1,0:T(8,128)(2,1)} %get-tuple-element.311.slope, bf16[2,4,256,512]{3,2,1,0:T(8,128)(2,1)} %bitcast.97, ...), custom_call_target="tpu_custom_call" | custom-call | flops 2147483 | bytes 12066 | tf_op jit(solution)/shard_map/mlp_back/pallas_call | solution.py:430
  189.7 3.8 %add_convert_fusion.2 = (bf16[4,256,512]{2,1,0:T(8,128)(2,1)}, bf16[4,256,512]{2,1,0:T(8,128)(2,1)S(1)}) fusion(bf16[8,256,512]{2,1,0:T(8,128)(2,1)} %copy-done.12, bf16[8,256,512]{2,1,0:T(8,128)(2,1)} %bitcast.106), kind=kLoop, calls=%fused_computation.4 | loop fusion | flops 4194304 | bytes 6291456 | tf_op jit(solution)/shard_map/convert_element_type | solution.py:898
  193.6 7.0 %fc1_grads.1 = (bf16[2,4,256,512]{3,2,1,0:T(8,128)(2,1)}, bf16[2,4,256,512]{3,2,1,0:T(8,128)(2,1)}) custom-call(s32[14]{0:T(128)} %stack.86.t, bf16[256,1024]{1,0:T(8,128)(2,1)} %get-tuple-element.298.x.xo, bf16[256,1024]{1,0:T(8,128)(2,1)} %copy-done.15, bf16[256,2048]{1,0:T(8,128)(2,1)} %get-tuple-element.317.dho, bf16[256,2048]{1,0:T(8,128)(2,1)} %get-tuple-element.318.dht), custom_call_target="tpu_custom_call" | custom-call | flops 2147483 | bytes 7340 | tf_op jit(solution)/shard_map/fc1_grads/pallas_call | solution.py:430
  202.3 5.0 %norm_mid_back.1 = (f32[256,1024]{1,0:T(8,128)}, bf16[256,1024]{1,0:T(8,128)(2,1)}, f32[8,1024]{1,0:T(8,128)}) custom-call(s32[14]{0:T(128)} %stack.86.t, f32[256,1024]{1,0:T(8,128)} %get-tuple-element.320.part, bf16[256,1024]{1,0:T(8,128)(2,1)} %copy-done.26, f32[256,1024]{1,0:T(8,128)} %get-tuple-element.321.middle, ...), custom_call_target="tpu_custom_call" | custom-call | bytes 5865 | tf_op jit(solution)/shard_map/norm_mid_back/pallas_call | solution.py:430
  208.8 5.2 %project_back.2.do = bf16[256,512]{1,0:T(8,128)(2,1)} custom-call(s32[14]{0:T(128)} %stack.86.t, bf16[256,1024]{1,0:T(8,128)(2,1)} %get-tuple-element.334.grad.go, bf16[2,4,128,512]{3,2,1,0:T(8,128)(2,1)} %bitcast.84, bf16[2,4,128,512]{3,2,1,0:T(8,128)(2,1)} %copy-done.4, bf16[2,4,128,512]{3,2,1,0:T(8,128)(2,1)} %bitcast.92, ...), custom_call_target="tpu_custom_call" | custom-call | flops 268435 | bytes 4980 | tf_op jit(solution)/shard_map/project_back/pallas_call | solution.py:430
  214.0 3.9 %add_convert_fusion = (bf16[4,256,512]{2,1,0:T(8,128)(2,1)}, bf16[4,256,512]{2,1,0:T(8,128)(2,1)S(1)}) fusion(bf16[8,256,512]{2,1,0:T(8,128)(2,1)} %collective-permute-done.32, bf16[8,256,512]{2,1,0:T(8,128)(2,1)} %bitcast.105), kind=kLoop, calls=%fused_computation.2 | loop fusion | flops 4194304 | bytes 6291456 | tf_op jit(solution)/shard_map/convert_element_type | solution.py:898
  218.3 11.0 %attend_back.2 = (bf16[256,512]{1,0:T(8,128)(2,1)}, bf16[2,512,512]{2,1,0:T(8,128)(2,1)}, bf16[2,512,512]{2,1,0:T(8,128)(2,1)}) custom-call(s32[14]{0:T(128)} %stack.86.t, bf16[256,512]{1,0:T(8,128)(2,1)} %get-tuple-element.282.q, bf16[256,512]{1,0:T(8,128)(2,1)} %project_back.2.do, bf16[256,512]{1,0:T(8,128)(2,1)} %get-tuple-element.295.mixed.mo, ...), custom_call_target="tpu_custom_call" | custom-call | flops 5368709 | bytes 5251 | tf_op jit(solution)/shard_map/attend_back/pallas_call | solution.py:430
  232.4 5.2 %project_back.3.do = bf16[256,512]{1,0:T(8,128)(2,1)} custom-call(s32[14]{0:T(128)} %stack.86.t, bf16[256,1024]{1,0:T(8,128)(2,1)} %copy-done.13, bf16[2,4,128,512]{3,2,1,0:T(8,128)(2,1)} %bitcast.85, bf16[2,4,128,512]{3,2,1,0:T(8,128)(2,1)} %copy-done.4, bf16[2,4,128,512]{3,2,1,0:T(8,128)(2,1)} %bitcast.93, ...), custom_call_target="tpu_custom_call" | custom-call | flops 268435 | bytes 4980 | tf_op jit(solution)/shard_map/project_back/pallas_call | solution.py:430
  237.6 4.9 %proj_grads.1 = (bf16[2,4,128,256]{3,2,1,0:T(8,128)(2,1)}, bf16[2,4,128,256]{3,2,1,0:T(8,128)(2,1)}) custom-call(s32[14]{0:T(128)} %stack.86.t, bf16[256,512]{1,0:T(8,128)(2,1)} %get-tuple-element.295.mixed.mo, bf16[256,512]{1,0:T(8,128)(2,1)} %get-tuple-element.281.mixed.mt, bf16[256,1024]{1,0:T(8,128)(2,1)} %get-tuple-element.334.grad.go, ...), custom_call_target="tpu_custom_call" | custom-call | flops 536870 | bytes 2621 | tf_op jit(solution)/shard_map/proj_grads/pallas_call | solution.py:430
  242.5 5.7 %down.2 = bf16[256,1024]{1,0:T(8,128)(2,1)} custom-call(s32[14]{0:T(128)} %stack.86.t, bf16[256,2048]{1,0:T(8,128)(2,1)} %get-tuple-element.336.actt.act, bf16[2,4,256,512]{3,2,1,0:T(8,128)(2,1)} %bitcast.98, bf16[2,4,256,512]{3,2,1,0:T(8,128)(2,1)} %collective-permute-done.29.w2t.wt), custom_call_target="tpu_custom_call" | custom-call | flops 1073741 | bytes 5767 | tf_op jit(solution)/shard_map/down/pallas_call | solution.py:430
  249.3 10.8 %attend_back.3 = (bf16[256,512]{1,0:T(8,128)(2,1)}, bf16[2,512,512]{2,1,0:T(8,128)(2,1)}, bf16[2,512,512]{2,1,0:T(8,128)(2,1)}) custom-call(s32[14]{0:T(128)} %stack.86.t, bf16[256,512]{1,0:T(8,128)(2,1)} %get-tuple-element.274.q, bf16[256,512]{1,0:T(8,128)(2,1)} %project_back.3.do, bf16[256,512]{1,0:T(8,128)(2,1)} %get-tuple-element.281.mixed.mt, ...), custom_call_target="tpu_custom_call" | custom-call | flops 5368709 | bytes 5251 | tf_op jit(solution)/shard_map/attend_back/pallas_call | solution.py:430
  270.2 8.4 %qkv_back.1 = (bf16[4,256,384]{2,1,0:T(8,128)(2,1)}, bf16[4,256,384]{2,1,0:T(8,128)(2,1)}, f32[8,512]{1,0:T(8,128)}, f32[256,1024]{1,0:T(8,128)}, bf16[256,1024]{1,0:T(8,128)(2,1)}) custom-call(s32[14]{0:T(128)} %stack.86.t, bf16[256,512]{1,0:T(8,128)(2,1)} %get-tuple-element.329.dqo, bf16[256,512]{1,0:T(8,128)(2,1)} %get-tuple-element.354.dqt, ...), custom_call_target="tpu_custom_call" | custom-call | flops 1610612 | bytes 12075 | tf_op jit(solution)/shard_map/qkv_back/pallas_call | solution.py:430
  281.8 4.1 %collective-permute-start.43 = (bf16[1,256,512]{2,1,0:T(8,128)(2,1)}, bf16[1,256,512]{2,1,0:T(8,128)(2,1)S(1)}, u32[]{:S(2)}, u32[]{:S(2)}) collective-permute-start(bf16[1,256,512]{2,1,0:T(8,128)(2,1)} %get-tuple-element.526), channel_id=1, source_target_pairs={{0,4},{2,6},{4,0},{6,2},{1,5},{3,7},{5,1},{7,3},{8,12},{10,14},{12... | collective-permute-start | bytes 786440 | tf_op jit(solution)/shard_map/ppermute | solution.py:851
  285.9 6.8 %qkv_grads.1 = (bf16[2,4,128,384]{3,2,1,0:T(8,128)(2,1)}, bf16[2,4,128,384]{3,2,1,0:T(8,128)(2,1)}, bf16[2,4,128,384]{3,2,1,0:T(8,128)(2,1)}, bf16[2,4,128,384]{3,2,1,0:T(8,128)(2,1)}) custom-call(s32[14]{0:T(128)} %stack.86.t, bf16[256,1024]{1,0:T(8,128)(2,1)} %norm_in.1.x.xo, bf16[256,1024]{1,0:T(8,128)(2,1)} %copy-done.14, ...), custom_call_target="tpu_custom_call" | custom-call | flops 1610612 | bytes 5767 | tf_op jit(solution)/shard_map/qkv_grads/pallas_call | solution.py:430
  297.8 5.8 %down.3.part = f32[256,1024]{1,0:T(8,128)} custom-call(s32[14]{0:T(128)} %stack.86.t, bf16[256,2048]{1,0:T(8,128)(2,1)} %get-tuple-element.370.acto.act, bf16[2,4,256,512]{3,2,1,0:T(8,128)(2,1)} %bitcast.99, bf16[2,4,256,512]{3,2,1,0:T(8,128)(2,1)} %collective-permute-done.29.w2t.wt), custom_call_target="tpu_custom_call" | custom-call | flops 1073741 | bytes 6291 | tf_op jit(solution)/shard_map/down/pallas_call | solution.py:430
  317.1 4.1 %norm_in_back.1 = (bf16[128,1024]{1,0:T(8,128)(2,1)}, bf16[128,1024]{1,0:T(8,128)(2,1)}, f32[2,1024]{1,0:T(2,128)}) custom-call(s32[14]{0:T(128)} %stack.86.t, f32[256,1024]{1,0:T(8,128)} %get-tuple-element.386.part, bf16[256,1024]{1,0:T(8,128)(2,1)} %copy-done.27, f32[256,1024]{1,0:T(8,128)} %get-tuple-element.388.dmid, bf16[128,1024]{1,0:T(8,128)(2,1)} %copy-done.9, ...), custom_call_target="tpu_custom_call" | custom-call | bytes 3743 | tf_op jit(solution)/shard_map/norm_in_back/pallas_call | solution.py:430
  (340 shorter events, 179.7 us)
Async XLA Ops:
  12.8 21.3 %collective-permute-start.6 = (bf16[128,1024]{1,0:T(8,128)(2,1)S(1)}, bf16[128,1024]{1,0:T(8,128)(2,1)S(1)}, u32[]{:S(2)}, u32[]{:S(2)}) collective-permute-start(bf16[128,1024]{1,0:T(8,128)(2,1)S(1)} %get-tuple-element.542), channel_id=1, source_target_pairs={{0,2},{2,0},{4,10},{6,8},{8,6},{10,4},{12,14},{14,12},{1,3},{3,1},... | collective-permute-start | bytes 786440 | tf_op jit(solution)/shard_map/ppermute | solution.py:912
  14.4 19.7 %collective-permute-start.5 = (bf16[128,1024]{1,0:T(8,128)(2,1)S(1)}, bf16[128,1024]{1,0:T(8,128)(2,1)S(1)}, u32[]{:S(2)}, u32[]{:S(2)}) collective-permute-start(bf16[128,1024]{1,0:T(8,128)(2,1)S(1)} %get-tuple-element.543), channel_id=1, source_target_pairs={{0,0},{2,2},{4,8},{6,10},{8,4},{10,6},{12,12},{14,14},{1,1},{3,3},... | collective-permute-start | bytes 786440 | tf_op jit(solution)/shard_map/ppermute | solution.py:912
  17.6 16.4 %collective-permute-start.4 = (bf16[1,128,512]{2,1,0:T(8,128)(2,1)S(1)}, bf16[1,128,512]{2,1,0:T(8,128)(2,1)S(1)}, u32[]{:S(2)}, u32[]{:S(2)}) collective-permute-start(bf16[1,128,512]{2,1,0:T(8,128)(2,1)S(1)} %copy-done.34), channel_id=1, source_target_pairs={{0,4},{2,6},{4,0},{6,2},{1,5},{3,7},{5,1},{7,3},{8,12},{10,14},{12... | collective-permute-start | bytes 393224 | tf_op jit(solution)/shard_map/ppermute | solution.py:851
  21.4 14.1 %collective-permute-start.3 = (bf16[2,128,512]{2,1,0:T(8,128)(2,1)S(1)}, bf16[2,128,512]{2,1,0:T(8,128)(2,1)S(1)}, u32[]{:S(2)}, u32[]{:S(2)}) collective-permute-start(bf16[2,128,512]{2,1,0:T(8,128)(2,1)S(1)} %pad_maximum_fusion.8), channel_id=1, source_target_pairs={{0,2},{2,0},{4,6},{6,4},{1,3},{3,1},{5,7},{7,5},{8,10},{10,8},{12,... | collective-permute-start | bytes 786440 | tf_op jit(solution)/shard_map/ppermute | solution.py:851
  36.6 14.9 %collective-permute-start.10 = (bf16[4,128,512]{2,1,0:T(8,128)(2,1)S(1)}, bf16[4,128,512]{2,1,0:T(8,128)(2,1)S(1)}, u32[]{:S(2)}, u32[]{:S(2)}) collective-permute-start(bf16[4,128,512]{2,1,0:T(8,128)(2,1)S(1)} %constant_dynamic-update-slice_fusion.4), channel_id=1, source_target_pairs={{0,16},{16,0},{1,17},{17,1},{2,18},{18,2},{3,19},{19,3},{4,20},{20... | collective-permute-start | bytes 1572872 | tf_op jit(solution)/shard_map/ppermute | solution.py:851
  45.8 15.9 %collective-permute-start.14 = (bf16[256,1024]{1,0:T(8,128)(2,1)}, bf16[256,1024]{1,0:T(8,128)(2,1)S(1)}, u32[]{:S(2)}, u32[]{:S(2)}) collective-permute-start(bf16[256,1024]{1,0:T(8,128)(2,1)} %norm_in.1.x.xo), channel_id=1, source_target_pairs={{0,1},{1,0},{2,3},{3,2},{4,5},{5,4},{6,7},{7,6},{8,9},{9,8},{10,11... | collective-permute-start | bytes 1572872 | tf_op jit(solution)/shard_map/ppermute | solution.py:851
  47.3 15.1 %collective-permute-start.12 = (bf16[4,128,512]{2,1,0:T(8,128)(2,1)S(1)}, bf16[4,128,512]{2,1,0:T(8,128)(2,1)S(1)}, u32[]{:S(2)}, u32[]{:S(2)}) collective-permute-start(bf16[4,128,512]{2,1,0:T(8,128)(2,1)S(1)} %constant_dynamic-update-slice_fusion.2), channel_id=1, source_target_pairs={{0,16},{16,0},{1,17},{17,1},{2,18},{18,2},{3,19},{19,3},{4,20},{20... | collective-permute-start | bytes 1572872 | tf_op jit(solution)/shard_map/ppermute | solution.py:851
  51.5 15.6 %collective-permute-start.11 = (bf16[2,4,128,512]{3,2,1,0:T(8,128)(2,1)S(1)}, bf16[2,4,128,512]{3,2,1,0:T(8,128)(2,1)S(1)}, u32[]{:S(2)}, u32[]{:S(2)}) collective-permute-start(bf16[2,4,128,512]{3,2,1,0:T(8,128)(2,1)S(1)} %bitcast.79), channel_id=1, source_target_pairs={{0,8},{8,0},{1,9},{9,1},{2,10},{10,2},{3,11},{11,3},{4,12},{12,4},... | collective-permute-start | bytes 3145736 | tf_op jit(solution)/shard_map/ppermute | solution.py:851
  65.1 14.9 %collective-permute-start.16 = (bf16[2,256,512]{2,1,0:T(8,128)(2,1)}, bf16[2,256,512]{2,1,0:T(8,128)(2,1)}, u32[]{:S(2)}, u32[]{:S(2)}) collective-permute-start(bf16[2,256,512]{2,1,0:T(8,128)(2,1)} %constant_dynamic-update-slice_fusion.6), channel_id=1, source_target_pairs={{0,2},{2,0},{4,6},{6,4},{1,3},{3,1},{5,7},{7,5},{8,10},{10,8},{12,... | collective-permute-start | bytes 1572872 | tf_op jit(solution)/shard_map/ppermute | solution.py:851
  81.3 42.5 %collective-permute-start.20 = (bf16[4,256,512]{2,1,0:T(8,128)(2,1)S(1)}, bf16[4,256,512]{2,1,0:T(8,128)(2,1)S(1)}, u32[]{:S(2)}, u32[]{:S(2)}) collective-permute-start(bf16[4,256,512]{2,1,0:T(8,128)(2,1)S(1)} %pad_maximum_fusion.4), channel_id=1, source_target_pairs={{0,16},{16,0},{1,17},{17,1},{2,18},{18,2},{3,19},{19,3},{4,20},{20... | collective-permute-start | bytes 3145736 | tf_op jit(solution)/shard_map/ppermute | solution.py:851
  83.1 14.6 %collective-permute-start.19 = (bf16[1,256,512]{2,1,0:T(8,128)(2,1)S(1)}, bf16[1,256,512]{2,1,0:T(8,128)(2,1)}, u32[]{:S(2)}, u32[]{:S(2)}) collective-permute-start(bf16[1,256,512]{2,1,0:T(8,128)(2,1)S(1)} %copy-done.32), channel_id=1, source_target_pairs={{0,4},{2,6},{4,0},{6,2},{1,5},{3,7},{5,1},{7,3},{8,12},{10,14},{12... | collective-permute-start | bytes 786440 | tf_op jit(solution)/shard_map/ppermute | solution.py:851
  98.8 25.0 %collective-permute-start.21 = (bf16[2,256,512]{2,1,0:T(8,128)(2,1)S(1)}, bf16[2,256,512]{2,1,0:T(8,128)(2,1)}, u32[]{:S(2)}, u32[]{:S(2)}) collective-permute-start(bf16[2,256,512]{2,1,0:T(8,128)(2,1)S(1)} %constant_dynamic-update-slice_fusion.8), channel_id=1, source_target_pairs={{0,2},{2,0},{4,6},{6,4},{1,3},{3,1},{5,7},{7,5},{8,10},{10,8},{12,... | collective-permute-start | bytes 1572872 | tf_op jit(solution)/shard_map/ppermute | solution.py:851
  100.8 18.9 %collective-permute-start.23 = (bf16[128,1024]{1,0:T(8,128)(2,1)}, bf16[128,1024]{1,0:T(8,128)(2,1)S(1)}, u32[]{:S(2)}, u32[]{:S(2)}) collective-permute-start(bf16[128,1024]{1,0:T(8,128)(2,1)} %get-tuple-element.290), channel_id=1, source_target_pairs={{0,0},{2,2},{4,8},{6,10},{8,4},{10,6},{12,12},{14,14},{1,1},{3,3},... | collective-permute-start | bytes 786440 | tf_op jit(solution)/shard_map/ppermute | solution.py:1023
  102.4 17.4 %collective-permute-start.24 = (bf16[128,1024]{1,0:T(8,128)(2,1)S(1)}, bf16[128,1024]{1,0:T(8,128)(2,1)S(1)}, u32[]{:S(2)}, u32[]{:S(2)}) collective-permute-start(bf16[128,1024]{1,0:T(8,128)(2,1)S(1)} %get-tuple-element.291), channel_id=1, source_target_pairs={{0,2},{2,0},{4,10},{6,8},{8,6},{10,4},{12,14},{14,12},{1,3},{3,1},... | collective-permute-start | bytes 786440 | tf_op jit(solution)/shard_map/ppermute | solution.py:1023
  109.4 18.8 %collective-permute-start.22 = (bf16[256,1024]{1,0:T(8,128)(2,1)}, bf16[256,1024]{1,0:T(8,128)(2,1)}, u32[]{:S(2)}, u32[]{:S(2)}) collective-permute-start(bf16[256,1024]{1,0:T(8,128)(2,1)} %project.2), channel_id=1, source_target_pairs={{0,1},{1,0},{2,3},{3,2},{4,5},{5,4},{6,7},{7,6},{8,9},{9,8},{10,11... | collective-permute-start | bytes 1572872 | tf_op jit(solution)/shard_map/ppermute | solution.py:851
  128.3 16.7 %collective-permute-start.26 = (bf16[2,4,256,512]{3,2,1,0:T(8,128)(2,1)S(1)}, bf16[2,4,256,512]{3,2,1,0:T(8,128)(2,1)}, u32[]{:S(2)}, u32[]{:S(2)}) collective-permute-start(bf16[2,4,256,512]{3,2,1,0:T(8,128)(2,1)S(1)} %bitcast.100), channel_id=1, source_target_pairs={{0,8},{8,0},{1,9},{9,1},{2,10},{10,2},{3,11},{11,3},{4,12},{12,4},... | collective-permute-start | bytes 6291464 | tf_op jit(solution)/shard_map/ppermute | solution.py:851
  129.6 25.5 %collective-permute-start.28 = (bf16[4,256,512]{2,1,0:T(8,128)(2,1)}, bf16[4,256,512]{2,1,0:T(8,128)(2,1)}, u32[]{:S(2)}, u32[]{:S(2)}) collective-permute-start(bf16[4,256,512]{2,1,0:T(8,128)(2,1)} %pad_maximum_fusion.5), channel_id=1, source_target_pairs={{0,16},{16,0},{1,17},{17,1},{2,18},{18,2},{3,19},{19,3},{4,20},{20... | collective-permute-start | bytes 3145736 | tf_op jit(solution)/shard_map/ppermute | solution.py:851
  129.9 15.0 %collective-permute-start.25 = (bf16[256,1024]{1,0:T(8,128)(2,1)}, bf16[256,1024]{1,0:T(8,128)(2,1)S(1)}, u32[]{:S(2)}, u32[]{:S(2)}) collective-permute-start(bf16[256,1024]{1,0:T(8,128)(2,1)} %get-tuple-element.309.go.grad), channel_id=1, source_target_pairs={{0,1},{1,0},{2,3},{3,2},{4,5},{5,4},{6,7},{7,6},{8,9},{9,8},{10,11... | collective-permute-start | bytes 1572872 | tf_op jit(solution)/shard_map/ppermute | solution.py:851
  139.7 15.3 %collective-permute-start.27 = (bf16[256,1024]{1,0:T(8,128)(2,1)}, bf16[256,1024]{1,0:T(8,128)(2,1)S(1)}, u32[]{:S(2)}, u32[]{:S(2)}) collective-permute-start(bf16[256,1024]{1,0:T(8,128)(2,1)} %get-tuple-element.298.x.xo), channel_id=1, source_target_pairs={{0,1},{1,0},{2,3},{3,2},{4,5},{5,4},{6,7},{7,6},{8,9},{9,8},{10,11... | collective-permute-start | bytes 1572872 | tf_op jit(solution)/shard_map/ppermute | solution.py:851
  179.6 13.9 %collective-permute-start.30 = (bf16[256,1024]{1,0:T(8,128)(2,1)S(1)}, bf16[256,1024]{1,0:T(8,128)(2,1)S(1)}, u32[]{:S(2)}, u32[]{:S(2)}) collective-permute-start(bf16[256,1024]{1,0:T(8,128)(2,1)S(1)} %copy-done.43), channel_id=1, source_target_pairs={{0,1},{1,0},{2,3},{3,2},{4,5},{5,4},{6,7},{7,6},{8,9},{9,8},{10,11... | collective-permute-start | bytes 1572872 | tf_op jit(solution)/shard_map/ppermute | solution.py:851
  200.6 28.8 %collective-permute-start.34 = (bf16[4,256,512]{2,1,0:T(8,128)(2,1)}, bf16[4,256,512]{2,1,0:T(8,128)(2,1)}, u32[]{:S(2)}, u32[]{:S(2)}) collective-permute-start(bf16[4,256,512]{2,1,0:T(8,128)(2,1)} %get-tuple-element.512), channel_id=1, source_target_pairs={{0,16},{16,0},{1,17},{17,1},{2,18},{18,2},{3,19},{19,3},{4,20},{20... | collective-permute-start | bytes 3145736 | tf_op jit(solution)/shard_map/ppermute | solution.py:851
  207.3 24.3 %collective-permute-start.33 = (bf16[256,1024]{1,0:T(8,128)(2,1)}, bf16[256,1024]{1,0:T(8,128)(2,1)S(1)}, u32[]{:S(2)}, u32[]{:S(2)}) collective-permute-start(bf16[256,1024]{1,0:T(8,128)(2,1)} %get-tuple-element.334.grad.go), channel_id=1, source_target_pairs={{0,1},{1,0},{2,3},{3,2},{4,5},{5,4},{6,7},{7,6},{8,9},{9,8},{10,11... | collective-permute-start | bytes 1572872 | tf_op jit(solution)/shard_map/ppermute | solution.py:851
  217.9 45.5 %collective-permute-start.36 = (bf16[4,256,512]{2,1,0:T(8,128)(2,1)}, bf16[4,256,512]{2,1,0:T(8,128)(2,1)}, u32[]{:S(2)}, u32[]{:S(2)}) collective-permute-start(bf16[4,256,512]{2,1,0:T(8,128)(2,1)} %get-tuple-element.510), channel_id=1, source_target_pairs={{0,16},{16,0},{1,17},{17,1},{2,18},{18,2},{3,19},{19,3},{4,20},{20... | collective-permute-start | bytes 3145736 | tf_op jit(solution)/shard_map/ppermute | solution.py:851
  248.7 14.7 %collective-permute-start.37 = (bf16[2,256,512]{2,1,0:T(8,128)(2,1)}, bf16[2,256,512]{2,1,0:T(8,128)(2,1)}, u32[]{:S(2)}, u32[]{:S(2)}) collective-permute-start(bf16[2,256,512]{2,1,0:T(8,128)(2,1)} %get-tuple-element.516), channel_id=1, source_target_pairs={{0,2},{2,0},{4,6},{6,4},{1,3},{3,1},{5,7},{7,5},{8,10},{10,8},{12,... | collective-permute-start | bytes 1572872 | tf_op jit(solution)/shard_map/ppermute | solution.py:851
  265.9 26.9 %collective-permute-start.42 = (bf16[2,256,512]{2,1,0:T(8,128)(2,1)}, bf16[2,256,512]{2,1,0:T(8,128)(2,1)S(1)}, u32[]{:S(2)}, u32[]{:S(2)}) collective-permute-start(bf16[2,256,512]{2,1,0:T(8,128)(2,1)} %get-tuple-element.514), channel_id=1, source_target_pairs={{0,2},{2,0},{4,6},{6,4},{1,3},{3,1},{5,7},{7,5},{8,10},{10,8},{12,... | collective-permute-start | bytes 1572872 | tf_op jit(solution)/shard_map/ppermute | solution.py:851
  278.6 18.5 %collective-permute-start.41 = (bf16[256,1024]{1,0:T(8,128)(2,1)}, bf16[256,1024]{1,0:T(8,128)(2,1)S(1)}, u32[]{:S(2)}, u32[]{:S(2)}) collective-permute-start(bf16[256,1024]{1,0:T(8,128)(2,1)} %get-tuple-element.359), channel_id=1, source_target_pairs={{0,1},{1,0},{2,3},{3,2},{4,5},{5,4},{6,7},{7,6},{8,9},{9,8},{10,11... | collective-permute-start | bytes 1572872 | tf_op jit(solution)/shard_map/ppermute | solution.py:851
  281.8 15.2 %collective-permute-start.43 = (bf16[1,256,512]{2,1,0:T(8,128)(2,1)}, bf16[1,256,512]{2,1,0:T(8,128)(2,1)S(1)}, u32[]{:S(2)}, u32[]{:S(2)}) collective-permute-start(bf16[1,256,512]{2,1,0:T(8,128)(2,1)} %get-tuple-element.526), channel_id=1, source_target_pairs={{0,4},{2,6},{4,0},{6,2},{1,5},{3,7},{5,1},{7,3},{8,12},{10,14},{12... | collective-permute-start | bytes 786440 | tf_op jit(solution)/shard_map/ppermute | solution.py:851
  297.6 25.2 %collective-permute-start.48 = (bf16[1,256,512]{2,1,0:T(8,128)(2,1)}, bf16[1,256,512]{2,1,0:T(8,128)(2,1)}, u32[]{:S(2)}, u32[]{:S(2)}) collective-permute-start(bf16[1,256,512]{2,1,0:T(8,128)(2,1)} %get-tuple-element.393), channel_id=1, source_target_pairs={{0,4},{2,6},{4,0},{6,2},{1,5},{3,7},{5,1},{7,3},{8,12},{10,14},{12... | collective-permute-start | bytes 786440 | tf_op jit(solution)/shard_map/ppermute | solution.py:851
  306.3 16.5 %collective-permute-start.47 = (bf16[4,128,384]{2,1,0:T(8,128)(2,1)S(1)}, bf16[4,128,384]{2,1,0:T(8,128)(2,1)S(1)}, u32[]{:S(2)}, u32[]{:S(2)}) collective-permute-start(bf16[4,128,384]{2,1,0:T(8,128)(2,1)S(1)} %get-tuple-element.391), channel_id=1, source_target_pairs={{0,16},{16,0},{1,17},{17,1},{2,18},{18,2},{3,19},{19,3},{4,20},{20... | collective-permute-start | bytes 1179656 | tf_op jit(solution)/shard_map/ppermute | solution.py:851
  307.3 13.9 %collective-permute-start.49 = (bf16[2,128,256]{2,1,0:T(8,128)(2,1)S(1)}, bf16[2,128,256]{2,1,0:T(8,128)(2,1)S(1)}, u32[]{:S(2)}, u32[]{:S(2)}) collective-permute-start(bf16[2,128,256]{2,1,0:T(8,128)(2,1)S(1)} %get-tuple-element.538), channel_id=1, source_target_pairs={{0,2},{2,0},{4,6},{6,4},{1,3},{3,1},{5,7},{7,5},{8,10},{10,8},{12,... | collective-permute-start | bytes 393224 | tf_op jit(solution)/shard_map/ppermute | solution.py:851
  313.4 22.5 %collective-permute-start.54 = (bf16[128,1024]{1,0:T(8,128)(2,1)}, bf16[128,1024]{1,0:T(8,128)(2,1)}, u32[]{:S(2)}, u32[]{:S(2)}) collective-permute-start(bf16[128,1024]{1,0:T(8,128)(2,1)} %get-tuple-element.420), channel_id=1, source_target_pairs={{0,0},{2,2},{8,4},{10,6},{4,8},{6,10},{12,12},{14,14},{1,1},{3,3},... | collective-permute-start | bytes 786440 | tf_op jit(solution)/shard_map/ppermute | solution.py:867
  317.0 19.9 %collective-permute-start.55 = (bf16[128,1024]{1,0:T(8,128)(2,1)}, bf16[128,1024]{1,0:T(8,128)(2,1)}, u32[]{:S(2)}, u32[]{:S(2)}) collective-permute-start(bf16[128,1024]{1,0:T(8,128)(2,1)} %get-tuple-element.421), channel_id=1, source_target_pairs={{2,0},{0,2},{10,4},{8,6},{6,8},{4,10},{14,12},{12,14},{3,1},{1,3},... | collective-permute-start | bytes 786440 | tf_op jit(solution)/shard_map/ppermute | solution.py:867
  (81 other events, 591.7 us)

commit v5 on v4

--- a/solution.py
+++ b/solution.py
@@ -453,12 +453,16 @@
     return pl.BlockSpec((2, 1, rows, cols), lambda j, t: (0, j, 0, 0))
 
 
-def halves_specs():
-    return [block_spec(128, COLS)] * 4
-
-
-def halves(refs, kc, ky, cols):
-    return jnp.concatenate([refs[kc][ky, 0, :, cols], refs[2 + kc][ky, 0, :, cols]], axis=0)
+def qkv_specs():
+    return [block_spec(128, 384)] * 4
+
+
+def proj_specs():
+    return [pl.BlockSpec((2, 1, 128, 128), lambda j, t: (0, j, 0, 3))] * 4
+
+
+def halves(refs, kc, ky):
+    return jnp.concatenate([refs[kc][ky, 0], refs[2 + kc][ky, 0]], axis=0)
 
 
 def column_spec(width, rows=256):
@@ -516,7 +520,7 @@
     ws, (bias, q, kv) = refs[:4], refs[4:]
     acc = jnp.zeros((256, 384), f32)
     for kc, ky in PAIRS:
-        acc = acc + nn(lanes(x, t[kc * 2 + ky]), halves(ws, kc, ky, slice(0, 384)))
+        acc = acc + nn(lanes(x, t[kc * 2 + ky]), halves(ws, kc, ky))
     q[...] = (acc[:, :128] + bias[8:9]).astype(bf16)
     kv[0] = acc[:, 128:256].astype(bf16)
     kv[1] = (acc[:, 256:] + bias[9:10]).astype(bf16)
@@ -542,11 +546,15 @@
     mixed[...] = jnp.concatenate(parts, axis=0).T.astype(bf16)
 
 
-def attn_back_kernel(t, q, do, mixed, lse, a, b, c, d, dq, near, far):
+def attn_back_kernel(t, q, grad, mixed, lse, a, b, c, d, *refs):
+    ws, (dq, near, far) = refs[:4], refs[4:]
+    dmixed = jnp.zeros((256, 128), f32)
+    for kc, ky in PAIRS:
+        dmixed = dmixed + nt(lanes(grad, t[kc * 2 + ky]), unpack_proj(ws, kc, ky))
     factor = HD**-0.5
     scale = factor * LOG2E
     lane = lax.broadcasted_iota(jnp.int32, (256, 128), 1)
-    queries, grads = q[...], do[...]
+    queries, grads = q[...], dmixed.astype(bf16)
     product_t = (grads.astype(f32) * mixed[...].astype(f32)).T
     zero = jnp.zeros_like(queries)
     qms = [jnp.where((lane // HD) == h, queries, zero) for h in range(2)]
@@ -573,7 +581,7 @@
 
 
 def unpack_proj(refs, kc, ky):
-    return jnp.concatenate([refs[kc][ky, 0, :, 384:], refs[2 + kc][ky, 0, :, 384:]], axis=1)
+    return jnp.concatenate([refs[kc][ky, 0], refs[2 + kc][ky, 0]], axis=1)
 
 
 def proj_kernel(t, mixed, *refs):
@@ -591,14 +599,6 @@
     def _():
         for i in range(4):
             out[:, pl.ds(pl.multiple_of(t[i] * 256, 256), 256)] = acc[i].astype(out.dtype)
-
-
-def proj_back_kernel(t, grad, *refs):
-    ws, out = refs[:4], refs[4]
-    acc = jnp.zeros((256, 128), f32)
-    for kc, ky in PAIRS:
-        acc = acc + nt(lanes(grad, t[kc * 2 + ky]), unpack_proj(ws, kc, ky))
-    out[...] = acc.astype(bf16)
 
 
 def mid_kernel(t, first, second, part, got, mod, branch, middle, out):
@@ -771,7 +771,7 @@
         axis=0,
     )
     for i, (kc, ky) in enumerate(PAIRS):
-        w = halves(ws, kc, ky, slice(0, 384))
+        w = halves(ws, kc, ky)
         acco[i] += nt(packed[0], w)
         acct[i] += nt(packed[1], w)
 
@@ -972,7 +972,7 @@
             qkv_kernel,
             table,
             [rows, *wa, mod],
-            [full, *halves_specs(), bias_spec],
+            [full, *qkv_specs(), bias_spec],
             [column_spec(128), pair_spec],
             [shaped((256, 512), bf16), shaped((2, 256, 512), bf16)],
             steps=4,
@@ -1009,7 +1009,7 @@
             proj_kernel,
             table,
             [rows, *wa],
-            [column_spec(128), *halves_specs()],
+            [column_spec(128), *proj_specs()],
             full,
             shaped((256, D), kind),
             steps=4,
@@ -1151,26 +1151,13 @@
         name="finish",
     )
 
-    def project_back(grad):
-        return call(
-            proj_back_kernel,
-            table,
-            [grad, *wa],
-            [full, *halves_specs()],
-            column_spec(128),
-            shaped((256, 512), bf16),
-            steps=4,
-            flops=2 * 256 * 512 * 1024,
-            name="project_back",
-        )
-
-    def attend_back(queries, dmixed, mixed, lse):
+    def attend_back(queries, grad, mixed, lse):
         long_spec = pl.BlockSpec((2, 512, 128), lambda j, t: (0, 0, j))
         return call(
             attn_back_kernel,
             table,
-            [queries, dmixed, mixed, lse, *chunks],
-            [column_spec(128)] * 3 + [lse_spec] + [pair_spec] * 4,
+            [queries, grad, mixed, lse, *chunks, *wa],
+            [column_spec(128), full, column_spec(128), lse_spec] + [pair_spec] * 4 + proj_specs(),
             [column_spec(128), long_spec, long_spec],
             [shaped((256, 512), bf16), shaped((2, 512, 512), bf16), shaped((2, 512, 512), bf16)],
             steps=4,
@@ -1178,19 +1165,17 @@
             name="attend_back",
         )
 
-    dmixed_o = project_back(dbr_o)
-    g_fc1 = fold(g_fc1, dmixed_o)
-    dmixed_o = after(dmixed_o, *g_fc1)
+    g_fc1 = fold(g_fc1, dbr_o)
+    dq_o, near_o, away_o = attend_back(q_o, after(dbr_o, *g_fc1), mixed_o, lse_o)
     g_fc1 = onward(g_fc1, "y")
-    dq_o, near_o, away_o = attend_back(q_o, dmixed_o, mixed_o, lse_o)
     back_o = flip(away_o, "c", 2, 1)
     g_fc2 = fold(g_fc2, away_o)
-    dmixed_t = project_back(after(dbr_t, *g_fc2))
+    dbr_t = after(dbr_t, away_o, *g_fc2)
     g_fc2 = onward(g_fc2, "near")
     p_keep, p_send = call(
         proj_grads_kernel,
         table,
-        [mixed_o, mixed_t, after(dbr_o, dmixed_t), dbr_t],
+        [mixed_o, mixed_t, dbr_o, dbr_t],
         [column_spec(128)] * 2 + [full, full],
         [block_spec(128, 256)] * 2,
         [shaped((2, 4, 128, 256), bf16)] * 2,
@@ -1201,8 +1186,8 @@
     g_proj = cross(p_keep, p_send)
     down_t = down(after(act_t, p_send), bf16)
     got_mlp = flip(down_t, "x", 2, 1)
-    dmixed_t = after(dmixed_t, p_send, down_t)
-    dq_t, near_t, away_t = attend_back(q_t, dmixed_t, mixed_t, lse_t)
+    dbr_t = after(dbr_t, p_send, down_t)
+    dq_t, near_t, away_t = attend_back(q_t, dbr_t, mixed_t, lse_t)
     back_t = flip(away_t, "c", 2, 1)
     away_t, got_mlp, g_fc1, g_fc2, g_proj = cut((away_t, got_mlp, g_fc1, g_fc2, g_proj))
     g_fc1, g_fc2, g_proj = (fold(v) for v in (g_fc1, g_fc2, g_proj))
@@ -1214,7 +1199,7 @@
         qkv_back_kernel,
         table,
         [dq_o, dq_t, near_o, near_t, back_o, back_t, *wa],
-        [column_spec(128)] * 2 + [long_spec] * 4 + halves_specs(),
+        [column_spec(128)] * 2 + [long_spec] * 4 + qkv_specs(),
         [pack_spec, pack_spec, pl.BlockSpec((8, 128), lambda j, t: (0, j)), full, full],
         [shaped((4, 256, 384), bf16)] * 2 + [shaped((8, 512), f32), row_f, row_b],
         steps=4,

time: 381 us -> 374 us (0.982)
  Pallas kernels: 180 us -> 172 us
    pallas_call x31 -> x29, Pallas kernels: 180 us -> 172 us  [kernel_call(): pl.pallas_call(body, grid_spec=pltpu.PrefetchScalarGridSpec(num_scalar_pr...]
  transfers between devices with their start and end apart: 67 -> 67, of which waited for: 20 -> 20; matrix products, arithmetic and copies ran while one was open for 15% -> 15% of each run, Pallas kernels for 42% -> 40%
where the time goes in v5:
time: 374 us; the launch traced here: 370 us
  Pallas kernels  172 us (46%)
  starting transfers between devices  83.4 us (22%)
  waiting for transfers between devices  42 us (11%)
  other arithmetic  37.1 us (10%)
  local copies, waits for them, and re-layouts  31.9 us (9%)
    pallas_call x29, Pallas kernels, kernel_call(): pl.pallas_call(body, grid_spec=pltpu.PrefetchScalarGridSpec(num_scalar_pr...  172 us
    ppermute x59, starting transfers between devices, flip(): return lax.ppermute(v, axis, [(i, i ^ offset) for i in range(count)])  68.4 us
    ppermute x59, waiting for transfers between devices, flip(): return lax.ppermute(v, axis, [(i, i ^ offset) for i in range(count)])  39.8 us
    convert_element_type x15, other arithmetic, fold(): return [(cut(own, k) + cut(got, k)).astype(bf16) for k in range(2)]  19.5 us
    unnamed x103, local copies, waits for them, and re-layouts  14.8 us
    ppermute x4, starting transfers between devices, send_back(): lax.ppermute(p, ('c', 'z'), [(b, a) for a, b in route(k)])  9.17 us
  transfers between devices with their start and end apart: 67, of which 20 were waited for; matrix products, arithmetic and copies ran while one was open for 15% of the time, Pallas kernels for 40%

profile of v5, /device:TPU:0, one launch (start us, length us, event | category | flops | bytes accessed | tf_op | source)
XLA Modules:
  0.0 369.8 jit_solution(12015525029141368660)
XLA Ops:
  6.3 3.6 collective-permute-start
  17.6 3.7 %collective-permute-start.4 = (bf16[1,128,512]{2,1,0:T(8,128)(2,1)S(1)}, bf16[1,128,512]{2,1,0:T(8,128)(2,1)S(1)}, u32[]{:S(2)}, u32[]{:S(2)}) collective-permute-start(bf16[1,128,512]{2,1,0:T(8,128)(2,1)S(1)} %copy-done.34), channel_id=1, source_target_pairs={{0,4},{2,6},{4,0},{6,2},{1,5},{3,7},{5,1},{7,3},{8,12},{10,14},{12... | collective-permute-start | bytes 393224 | tf_op jit(solution)/shard_map/ppermute | solution.py:851
  24.6 3.7 %modulate.1 = f32[2,16,1024]{2,1,0:T(8,128)} custom-call(s32[14]{0:T(128)} %stack.86.t, bf16[8,256]{1,0:T(8,128)(2,1)} %pad.4.act, bf16[256,6144]{1,0:T(8,128)(2,1)} %w_ada.1, bf16[1,1536]{1,0:T(2,128)(2,1)} %reshape.160.b_ada, bf16[2,256]{1,0:T(2,128)(2,1)} %b_qkv.1, bf16[1,256]{1,0:T(2,128)(2,1)} %reshape.161.b_proj, bf16[1,1024]{1,0:T(2,128)(2,1)} %reshape.162.b_fc1, ...), custom_call_target="tpu_custom_call" | custom-call | flops 25165 | bytes 3288 | tf_op jit(solution)/shard_map/modulate/pallas_call | solution.py:430
  51.6 10.1 %collective-permute-done.13 = bf16[1,256,512]{2,1,0:T(8,128)(2,1)S(1)} collective-permute-done((bf16[1,256,512]{2,1,0:T(8,128)(2,1)S(1)}, bf16[1,256,512]{2,1,0:T(8,128)(2,1)S(1)}, u32[]{:S(2)}, u32[]{:S(2)}) %collective-permute-start.13) | collective-permute-done | bytes 262176 | tf_op jit(solution)/shard_map/ppermute | solution.py:851
  68.1 5.6 %qkv.3 = (bf16[256,512]{1,0:T(8,128)(2,1)}, bf16[2,256,512]{2,1,0:T(8,128)(2,1)}) custom-call(s32[14]{0:T(128)} %stack.86.t, bf16[256,1024]{1,0:T(8,128)(2,1)} %copy-done.14, bf16[2,4,128,512]{3,2,1,0:T(8,128)(2,1)} %bitcast.80, bf16[2,4,128,512]{3,2,1,0:T(8,128)(2,1)} %copy-done.4, bf16[2,4,128,512]{3,2,1,0:T(8,128)(2,1)} %bitcast.88, ...), custom_call_target="tpu_custom_call" | custom-call | flops 805306 | bytes 5570 | tf_op jit(solution)/shard_map/qkv/pallas_call | solution.py:430
  73.9 5.6 %qkv.2 = (bf16[256,512]{1,0:T(8,128)(2,1)}, bf16[2,256,512]{2,1,0:T(8,128)(2,1)}) custom-call(s32[14]{0:T(128)} %stack.86.t, bf16[256,1024]{1,0:T(8,128)(2,1)} %norm_in.1.x.xo, bf16[2,4,128,512]{3,2,1,0:T(8,128)(2,1)} %bitcast.81, bf16[2,4,128,512]{3,2,1,0:T(8,128)(2,1)} %copy-done.4, bf16[2,4,128,512]{3,2,1,0:T(8,128)(2,1)} %bitcast.89, ...), custom_call_target="tpu_custom_call" | custom-call | flops 805306 | bytes 5570 | tf_op jit(solution)/shard_map/qkv/pallas_call | solution.py:430
  87.3 8.8 %attend.2 = (bf16[256,512]{1,0:T(8,128)(2,1)}, f32[4,2,256]{2,1,0:T(2,128)}) custom-call(s32[14]{0:T(128)} %stack.86.t, bf16[256,512]{1,0:T(8,128)(2,1)} %get-tuple-element.273.q, bf16[2,256,512]{2,1,0:T(8,128)(2,1)} %get-tuple-element.274.a, bf16[2,256,512]{2,1,0:T(8,128)(2,1)} %get-tuple-element.270.b, bf16[2,256,512]{2,1,0:T(8,128)(2,1)} %copy-done.7, ...), custom_call_target="tpu_custom_call" | custom-call | flops 2147483 | bytes 2629 | tf_op jit(solution)/shard_map/attend/pallas_call | solution.py:430
  104.3 4.5 %project.2 = bf16[256,1024]{1,0:T(8,128)(2,1)} custom-call(s32[14]{0:T(128)} %stack.86.t, bf16[256,512]{1,0:T(8,128)(2,1)} %get-tuple-element.280.mixed.mt, bf16[2,4,128,512]{3,2,1,0:T(8,128)(2,1)} %bitcast.82, bf16[2,4,128,512]{3,2,1,0:T(8,128)(2,1)} %copy-done.4, bf16[2,4,128,512]{3,2,1,0:T(8,128)(2,1)} %bitcast.90, ...), custom_call_target="tpu_custom_call" | custom-call | flops 268435 | bytes 4980 | tf_op jit(solution)/shard_map/project/pallas_call | solution.py:430
  110.3 8.8 %attend.3 = (bf16[256,512]{1,0:T(8,128)(2,1)}, f32[4,2,256]{2,1,0:T(2,128)}) custom-call(s32[14]{0:T(128)} %stack.86.t, bf16[256,512]{1,0:T(8,128)(2,1)} %get-tuple-element.281.q, bf16[2,256,512]{2,1,0:T(8,128)(2,1)} %get-tuple-element.274.a, bf16[2,256,512]{2,1,0:T(8,128)(2,1)} %get-tuple-element.270.b, bf16[2,256,512]{2,1,0:T(8,128)(2,1)} %copy-done.7, ...), custom_call_target="tpu_custom_call" | custom-call | flops 2147483 | bytes 2629 | tf_op jit(solution)/shard_map/attend/pallas_call | solution.py:430
  130.1 4.7 %project.3.part = f32[256,1024]{1,0:T(8,128)} custom-call(s32[14]{0:T(128)} %stack.86.t, bf16[256,512]{1,0:T(8,128)(2,1)} %get-tuple-element.294.mixed.mo, bf16[2,4,128,512]{3,2,1,0:T(8,128)(2,1)} %bitcast.83, bf16[2,4,128,512]{3,2,1,0:T(8,128)(2,1)} %copy-done.4, bf16[2,4,128,512]{3,2,1,0:T(8,128)(2,1)} %bitcast.91, ...), custom_call_target="tpu_custom_call" | custom-call | flops 268435 | bytes 5505 | tf_op jit(solution)/shard_map/project/pallas_call | solution.py:430
  134.9 4.0 %norm_mid.1 = (f32[256,1024]{1,0:T(8,128)}, f32[256,1024]{1,0:T(8,128)}, bf16[256,1024]{1,0:T(8,128)(2,1)}) custom-call(s32[14]{0:T(128)} %stack.86.t, bf16[128,1024]{1,0:T(8,128)(2,1)} %copy-done.9, bf16[128,1024]{1,0:T(8,128)(2,1)} %copy-done.8, f32[256,1024]{1,0:T(8,128)} %project.3.part, bf16[256,1024]{1,0:T(8,128)(2,1)} %collective-permute-done.22.got, ...), custom_call_target="tpu_custom_call" | custom-call | bytes 4784 | tf_op jit(solution)/shard_map/norm_mid/pallas_call | solution.py:430
  140.0 4.3 %collective-permute-done.25.grad.gt = bf16[256,1024]{1,0:T(8,128)(2,1)S(1)} collective-permute-done((bf16[256,1024]{1,0:T(8,128)(2,1)}, bf16[256,1024]{1,0:T(8,128)(2,1)S(1)}, u32[]{:S(2)}, u32[]{:S(2)}) %collective-permute-start.25) | collective-permute-done | bytes 524320 | tf_op jit(solution)/shard_map/ppermute | solution.py:851
  144.3 6.5 %up.2 = (bf16[256,2048]{1,0:T(8,128)(2,1)}, bf16[256,2048]{1,0:T(8,128)(2,1)}) custom-call(s32[14]{0:T(128)} %stack.86.t, bf16[256,1024]{1,0:T(8,128)(2,1)} %get-tuple-element.297.x.xo, bf16[2,4,256,512]{3,2,1,0:T(8,128)(2,1)} %bitcast.101, bf16[2,4,256,512]{3,2,1,0:T(8,128)(2,1)} %collective-permute-done.26.wt.w1t, f32[16,1024]{1,0:T(8,128)} %add.216.mod.refs_4_.bias), custom_call_target="tpu_custom_call" | custom-call | flops 1073741 | bytes 6881 | tf_op jit(solution)/shard_map/up/pallas_call | solution.py:430
  157.0 6.5 %up.3 = (bf16[256,2048]{1,0:T(8,128)(2,1)}, bf16[256,2048]{1,0:T(8,128)(2,1)}) custom-call(s32[14]{0:T(128)} %stack.86.t, bf16[256,1024]{1,0:T(8,128)(2,1)} %copy-done.15, bf16[2,4,256,512]{3,2,1,0:T(8,128)(2,1)} %bitcast.102, bf16[2,4,256,512]{3,2,1,0:T(8,128)(2,1)} %collective-permute-done.26.wt.w1t, f32[16,1024]{1,0:T(8,128)} %add.216.mod.refs_4_.bias), custom_call_target="tpu_custom_call" | custom-call | flops 1073741 | bytes 6881 | tf_op jit(solution)/shard_map/up/pallas_call | solution.py:430
  163.6 8.0 %mlp_back.2 = (bf16[256,2048]{1,0:T(8,128)(2,1)}, f32[1,2048]{1,0:T(1,128)}, bf16[256,1024]{1,0:T(8,128)(2,1)}) custom-call(s32[14]{0:T(128)} %stack.86.t, bf16[256,1024]{1,0:T(8,128)(2,1)} %copy-done.16, bf16[256,2048]{1,0:T(8,128)(2,1)} %get-tuple-element.303.slope, bf16[2,4,256,512]{3,2,1,0:T(8,128)(2,1)} %bitcast.96, ...), custom_call_target="tpu_custom_call" | custom-call | flops 2147483 | bytes 11542 | tf_op jit(solution)/shard_map/mlp_back/pallas_call | solution.py:430
  171.6 6.9 %fc2_grads.1 = (bf16[2,4,256,512]{3,2,1,0:T(8,128)(2,1)}, bf16[2,4,256,512]{3,2,1,0:T(8,128)(2,1)}) custom-call(s32[14]{0:T(128)} %stack.86.t, bf16[256,2048]{1,0:T(8,128)(2,1)} %get-tuple-element.368.acto.act, bf16[256,2048]{1,0:T(8,128)(2,1)} %get-tuple-element.334.actt.act, bf16[256,1024]{1,0:T(8,128)(2,1)} %get-tuple-element.308.go.grad, ...), custom_call_target="tpu_custom_call" | custom-call | flops 2147483 | bytes 7340 | tf_op jit(solution)/shard_map/fc2_grads/pallas_call | solution.py:430
  179.9 8.1 %mlp_back.3 = (bf16[256,2048]{1,0:T(8,128)(2,1)}, f32[1,2048]{1,0:T(1,128)}, f32[256,1024]{1,0:T(8,128)}) custom-call(s32[14]{0:T(128)} %stack.86.t, bf16[256,1024]{1,0:T(8,128)(2,1)} %get-tuple-element.308.go.grad, bf16[256,2048]{1,0:T(8,128)(2,1)} %get-tuple-element.310.slope, bf16[2,4,256,512]{3,2,1,0:T(8,128)(2,1)} %bitcast.97, ...), custom_call_target="tpu_custom_call" | custom-call | flops 2147483 | bytes 12066 | tf_op jit(solution)/shard_map/mlp_back/pallas_call | solution.py:430
  189.4 3.8 %add_convert_fusion.2 = (bf16[4,256,512]{2,1,0:T(8,128)(2,1)}, bf16[4,256,512]{2,1,0:T(8,128)(2,1)S(1)}) fusion(bf16[8,256,512]{2,1,0:T(8,128)(2,1)} %copy-done.12, bf16[8,256,512]{2,1,0:T(8,128)(2,1)} %bitcast.106), kind=kLoop, calls=%fused_computation.4 | loop fusion | flops 4194304 | bytes 6291456 | tf_op jit(solution)/shard_map/convert_element_type | solution.py:898
  193.2 7.0 %fc1_grads.1 = (bf16[2,4,256,512]{3,2,1,0:T(8,128)(2,1)}, bf16[2,4,256,512]{3,2,1,0:T(8,128)(2,1)}) custom-call(s32[14]{0:T(128)} %stack.86.t, bf16[256,1024]{1,0:T(8,128)(2,1)} %get-tuple-element.297.x.xo, bf16[256,1024]{1,0:T(8,128)(2,1)} %copy-done.15, bf16[256,2048]{1,0:T(8,128)(2,1)} %get-tuple-element.316.dho, bf16[256,2048]{1,0:T(8,128)(2,1)} %get-tuple-element.317.dht), custom_call_target="tpu_custom_call" | custom-call | flops 2147483 | bytes 7340 | tf_op jit(solution)/shard_map/fc1_grads/pallas_call | solution.py:430
  201.9 5.0 %norm_mid_back.1 = (f32[256,1024]{1,0:T(8,128)}, bf16[256,1024]{1,0:T(8,128)(2,1)}, f32[8,1024]{1,0:T(8,128)}) custom-call(s32[14]{0:T(128)} %stack.86.t, f32[256,1024]{1,0:T(8,128)} %get-tuple-element.319.part, bf16[256,1024]{1,0:T(8,128)(2,1)} %copy-done.26, f32[256,1024]{1,0:T(8,128)} %get-tuple-element.320.middle, ...), custom_call_target="tpu_custom_call" | custom-call | bytes 5865 | tf_op jit(solution)/shard_map/norm_mid_back/pallas_call | solution.py:430
  208.2 3.9 %add_convert_fusion = (bf16[4,256,512]{2,1,0:T(8,128)(2,1)}, bf16[4,256,512]{2,1,0:T(8,128)(2,1)S(1)}) fusion(bf16[8,256,512]{2,1,0:T(8,128)(2,1)} %collective-permute-done.32, bf16[8,256,512]{2,1,0:T(8,128)(2,1)} %bitcast.105), kind=kLoop, calls=%fused_computation.2 | loop fusion | flops 4194304 | bytes 6291456 | tf_op jit(solution)/shard_map/convert_element_type | solution.py:898
  212.5 12.9 %attend_back.2 = (bf16[256,512]{1,0:T(8,128)(2,1)}, bf16[2,512,512]{2,1,0:T(8,128)(2,1)}, bf16[2,512,512]{2,1,0:T(8,128)(2,1)}) custom-call(s32[14]{0:T(128)} %stack.86.t, bf16[256,512]{1,0:T(8,128)(2,1)} %get-tuple-element.281.q, bf16[256,1024]{1,0:T(8,128)(2,1)} %get-tuple-element.326.grad.go, bf16[256,512]{1,0:T(8,128)(2,1)} %get-tuple-element.294.mixed.mo, ...), custom_call_target="tpu_custom_call" | custom-call | flops 5368709 | bytes 9707 | tf_op jit(solution)/shard_map/attend_back/pallas_call | solution.py:430
  229.8 4.9 %proj_grads.1 = (bf16[2,4,128,256]{3,2,1,0:T(8,128)(2,1)}, bf16[2,4,128,256]{3,2,1,0:T(8,128)(2,1)}) custom-call(s32[14]{0:T(128)} %stack.86.t, bf16[256,512]{1,0:T(8,128)(2,1)} %get-tuple-element.294.mixed.mo, bf16[256,512]{1,0:T(8,128)(2,1)} %get-tuple-element.280.mixed.mt, bf16[256,1024]{1,0:T(8,128)(2,1)} %get-tuple-element.326.grad.go, ...), custom_call_target="tpu_custom_call" | custom-call | flops 536870 | bytes 2621 | tf_op jit(solution)/shard_map/proj_grads/pallas_call | solution.py:430
  234.7 5.6 %down.2 = bf16[256,1024]{1,0:T(8,128)(2,1)} custom-call(s32[14]{0:T(128)} %stack.86.t, bf16[256,2048]{1,0:T(8,128)(2,1)} %get-tuple-element.334.actt.act, bf16[2,4,256,512]{3,2,1,0:T(8,128)(2,1)} %bitcast.98, bf16[2,4,256,512]{3,2,1,0:T(8,128)(2,1)} %collective-permute-done.29.w2t.wt), custom_call_target="tpu_custom_call" | custom-call | flops 1073741 | bytes 5767 | tf_op jit(solution)/shard_map/down/pallas_call | solution.py:430
  242.1 12.6 %attend_back.3 = (bf16[256,512]{1,0:T(8,128)(2,1)}, bf16[2,512,512]{2,1,0:T(8,128)(2,1)}, bf16[2,512,512]{2,1,0:T(8,128)(2,1)}) custom-call(s32[14]{0:T(128)} %stack.86.t, bf16[256,512]{1,0:T(8,128)(2,1)} %get-tuple-element.273.q, bf16[256,1024]{1,0:T(8,128)(2,1)} %copy-done.13, bf16[256,512]{1,0:T(8,128)(2,1)} %get-tuple-element.280.mixed.mt, ...), custom_call_target="tpu_custom_call" | custom-call | flops 5368709 | bytes 9707 | tf_op jit(solution)/shard_map/attend_back/pallas_call | solution.py:430
  263.7 8.2 %qkv_back.1 = (bf16[4,256,384]{2,1,0:T(8,128)(2,1)}, bf16[4,256,384]{2,1,0:T(8,128)(2,1)}, f32[8,512]{1,0:T(8,128)}, f32[256,1024]{1,0:T(8,128)}, bf16[256,1024]{1,0:T(8,128)(2,1)}) custom-call(s32[14]{0:T(128)} %stack.86.t, bf16[256,512]{1,0:T(8,128)(2,1)} %get-tuple-element.328.dqo, bf16[256,512]{1,0:T(8,128)(2,1)} %get-tuple-element.352.dqt, ...), custom_call_target="tpu_custom_call" | custom-call | flops 1610612 | bytes 12075 | tf_op jit(solution)/shard_map/qkv_back/pallas_call | solution.py:430
  277.6 6.8 %qkv_grads.1 = (bf16[2,4,128,384]{3,2,1,0:T(8,128)(2,1)}, bf16[2,4,128,384]{3,2,1,0:T(8,128)(2,1)}, bf16[2,4,128,384]{3,2,1,0:T(8,128)(2,1)}, bf16[2,4,128,384]{3,2,1,0:T(8,128)(2,1)}) custom-call(s32[14]{0:T(128)} %stack.86.t, bf16[256,1024]{1,0:T(8,128)(2,1)} %norm_in.1.x.xo, bf16[256,1024]{1,0:T(8,128)(2,1)} %copy-done.14, ...), custom_call_target="tpu_custom_call" | custom-call | flops 1610612 | bytes 5767 | tf_op jit(solution)/shard_map/qkv_grads/pallas_call | solution.py:430
  285.2 3.6 collective-permute-done.43
  289.6 5.8 %down.3.part = f32[256,1024]{1,0:T(8,128)} custom-call(s32[14]{0:T(128)} %stack.86.t, bf16[256,2048]{1,0:T(8,128)(2,1)} %get-tuple-element.368.acto.act, bf16[2,4,256,512]{3,2,1,0:T(8,128)(2,1)} %bitcast.99, bf16[2,4,256,512]{3,2,1,0:T(8,128)(2,1)} %collective-permute-done.29.w2t.wt), custom_call_target="tpu_custom_call" | custom-call | flops 1073741 | bytes 6291 | tf_op jit(solution)/shard_map/down/pallas_call | solution.py:430
  306.2 3.6 collective-permute-start.54
  309.8 4.1 %norm_in_back.1 = (bf16[128,1024]{1,0:T(8,128)(2,1)}, bf16[128,1024]{1,0:T(8,128)(2,1)}, f32[2,1024]{1,0:T(2,128)}) custom-call(s32[14]{0:T(128)} %stack.86.t, f32[256,1024]{1,0:T(8,128)} %get-tuple-element.384.part, bf16[256,1024]{1,0:T(8,128)(2,1)} %copy-done.27, f32[256,1024]{1,0:T(8,128)} %get-tuple-element.386.dmid, bf16[128,1024]{1,0:T(8,128)(2,1)} %copy-done.9, ...), custom_call_target="tpu_custom_call" | custom-call | bytes 3743 | tf_op jit(solution)/shard_map/norm_in_back/pallas_call | solution.py:430
  342.0 3.6 collective-permute-start.63
  (338 shorter events, 173.2 us)
Async XLA Ops:
  12.8 21.3 %collective-permute-start.6 = (bf16[128,1024]{1,0:T(8,128)(2,1)S(1)}, bf16[128,1024]{1,0:T(8,128)(2,1)S(1)}, u32[]{:S(2)}, u32[]{:S(2)}) collective-permute-start(bf16[128,1024]{1,0:T(8,128)(2,1)S(1)} %get-tuple-element.540), channel_id=1, source_target_pairs={{0,2},{2,0},{4,10},{6,8},{8,6},{10,4},{12,14},{14,12},{1,3},{3,1},... | collective-permute-start | bytes 786440 | tf_op jit(solution)/shard_map/ppermute | solution.py:912
  14.4 19.7 %collective-permute-start.5 = (bf16[128,1024]{1,0:T(8,128)(2,1)S(1)}, bf16[128,1024]{1,0:T(8,128)(2,1)S(1)}, u32[]{:S(2)}, u32[]{:S(2)}) collective-permute-start(bf16[128,1024]{1,0:T(8,128)(2,1)S(1)} %get-tuple-element.541), channel_id=1, source_target_pairs={{0,0},{2,2},{4,8},{6,10},{8,4},{10,6},{12,12},{14,14},{1,1},{3,3},... | collective-permute-start | bytes 786440 | tf_op jit(solution)/shard_map/ppermute | solution.py:912
  17.6 16.4 %collective-permute-start.4 = (bf16[1,128,512]{2,1,0:T(8,128)(2,1)S(1)}, bf16[1,128,512]{2,1,0:T(8,128)(2,1)S(1)}, u32[]{:S(2)}, u32[]{:S(2)}) collective-permute-start(bf16[1,128,512]{2,1,0:T(8,128)(2,1)S(1)} %copy-done.34), channel_id=1, source_target_pairs={{0,4},{2,6},{4,0},{6,2},{1,5},{3,7},{5,1},{7,3},{8,12},{10,14},{12... | collective-permute-start | bytes 393224 | tf_op jit(solution)/shard_map/ppermute | solution.py:851
  21.4 14.1 %collective-permute-start.3 = (bf16[2,128,512]{2,1,0:T(8,128)(2,1)S(1)}, bf16[2,128,512]{2,1,0:T(8,128)(2,1)S(1)}, u32[]{:S(2)}, u32[]{:S(2)}) collective-permute-start(bf16[2,128,512]{2,1,0:T(8,128)(2,1)S(1)} %pad_maximum_fusion.8), channel_id=1, source_target_pairs={{0,2},{2,0},{4,6},{6,4},{1,3},{3,1},{5,7},{7,5},{8,10},{10,8},{12,... | collective-permute-start | bytes 786440 | tf_op jit(solution)/shard_map/ppermute | solution.py:851
  36.6 14.9 %collective-permute-start.10 = (bf16[4,128,512]{2,1,0:T(8,128)(2,1)S(1)}, bf16[4,128,512]{2,1,0:T(8,128)(2,1)S(1)}, u32[]{:S(2)}, u32[]{:S(2)}) collective-permute-start(bf16[4,128,512]{2,1,0:T(8,128)(2,1)S(1)} %constant_dynamic-update-slice_fusion.4), channel_id=1, source_target_pairs={{0,16},{16,0},{1,17},{17,1},{2,18},{18,2},{3,19},{19,3},{4,20},{20... | collective-permute-start | bytes 1572872 | tf_op jit(solution)/shard_map/ppermute | solution.py:851
  45.8 15.9 %collective-permute-start.14 = (bf16[256,1024]{1,0:T(8,128)(2,1)}, bf16[256,1024]{1,0:T(8,128)(2,1)S(1)}, u32[]{:S(2)}, u32[]{:S(2)}) collective-permute-start(bf16[256,1024]{1,0:T(8,128)(2,1)} %norm_in.1.x.xo), channel_id=1, source_target_pairs={{0,1},{1,0},{2,3},{3,2},{4,5},{5,4},{6,7},{7,6},{8,9},{9,8},{10,11... | collective-permute-start | bytes 1572872 | tf_op jit(solution)/shard_map/ppermute | solution.py:851
  47.3 15.1 %collective-permute-start.12 = (bf16[4,128,512]{2,1,0:T(8,128)(2,1)S(1)}, bf16[4,128,512]{2,1,0:T(8,128)(2,1)S(1)}, u32[]{:S(2)}, u32[]{:S(2)}) collective-permute-start(bf16[4,128,512]{2,1,0:T(8,128)(2,1)S(1)} %constant_dynamic-update-slice_fusion.2), channel_id=1, source_target_pairs={{0,16},{16,0},{1,17},{17,1},{2,18},{18,2},{3,19},{19,3},{4,20},{20... | collective-permute-start | bytes 1572872 | tf_op jit(solution)/shard_map/ppermute | solution.py:851
  51.5 15.6 %collective-permute-start.11 = (bf16[2,4,128,512]{3,2,1,0:T(8,128)(2,1)S(1)}, bf16[2,4,128,512]{3,2,1,0:T(8,128)(2,1)S(1)}, u32[]{:S(2)}, u32[]{:S(2)}) collective-permute-start(bf16[2,4,128,512]{3,2,1,0:T(8,128)(2,1)S(1)} %bitcast.79), channel_id=1, source_target_pairs={{0,8},{8,0},{1,9},{9,1},{2,10},{10,2},{3,11},{11,3},{4,12},{12,4},... | collective-permute-start | bytes 3145736 | tf_op jit(solution)/shard_map/ppermute | solution.py:851
  65.1 14.9 %collective-permute-start.16 = (bf16[2,256,512]{2,1,0:T(8,128)(2,1)}, bf16[2,256,512]{2,1,0:T(8,128)(2,1)}, u32[]{:S(2)}, u32[]{:S(2)}) collective-permute-start(bf16[2,256,512]{2,1,0:T(8,128)(2,1)} %constant_dynamic-update-slice_fusion.6), channel_id=1, source_target_pairs={{0,2},{2,0},{4,6},{6,4},{1,3},{3,1},{5,7},{7,5},{8,10},{10,8},{12,... | collective-permute-start | bytes 1572872 | tf_op jit(solution)/shard_map/ppermute | solution.py:851
  81.3 41.9 %collective-permute-start.20 = (bf16[4,256,512]{2,1,0:T(8,128)(2,1)S(1)}, bf16[4,256,512]{2,1,0:T(8,128)(2,1)S(1)}, u32[]{:S(2)}, u32[]{:S(2)}) collective-permute-start(bf16[4,256,512]{2,1,0:T(8,128)(2,1)S(1)} %pad_maximum_fusion.4), channel_id=1, source_target_pairs={{0,16},{16,0},{1,17},{17,1},{2,18},{18,2},{3,19},{19,3},{4,20},{20... | collective-permute-start | bytes 3145736 | tf_op jit(solution)/shard_map/ppermute | solution.py:851
  83.1 14.6 %collective-permute-start.19 = (bf16[1,256,512]{2,1,0:T(8,128)(2,1)S(1)}, bf16[1,256,512]{2,1,0:T(8,128)(2,1)}, u32[]{:S(2)}, u32[]{:S(2)}) collective-permute-start(bf16[1,256,512]{2,1,0:T(8,128)(2,1)S(1)} %copy-done.32), channel_id=1, source_target_pairs={{0,4},{2,6},{4,0},{6,2},{1,5},{3,7},{5,1},{7,3},{8,12},{10,14},{12... | collective-permute-start | bytes 786440 | tf_op jit(solution)/shard_map/ppermute | solution.py:851
  98.7 24.5 %collective-permute-start.21 = (bf16[2,256,512]{2,1,0:T(8,128)(2,1)S(1)}, bf16[2,256,512]{2,1,0:T(8,128)(2,1)}, u32[]{:S(2)}, u32[]{:S(2)}) collective-permute-start(bf16[2,256,512]{2,1,0:T(8,128)(2,1)S(1)} %constant_dynamic-update-slice_fusion.8), channel_id=1, source_target_pairs={{0,2},{2,0},{4,6},{6,4},{1,3},{3,1},{5,7},{7,5},{8,10},{10,8},{12,... | collective-permute-start | bytes 1572872 | tf_op jit(solution)/shard_map/ppermute | solution.py:851
  100.7 18.4 %collective-permute-start.23 = (bf16[128,1024]{1,0:T(8,128)(2,1)}, bf16[128,1024]{1,0:T(8,128)(2,1)S(1)}, u32[]{:S(2)}, u32[]{:S(2)}) collective-permute-start(bf16[128,1024]{1,0:T(8,128)(2,1)} %get-tuple-element.289), channel_id=1, source_target_pairs={{0,0},{2,2},{4,8},{6,10},{8,4},{10,6},{12,12},{14,14},{1,1},{3,3},... | collective-permute-start | bytes 786440 | tf_op jit(solution)/shard_map/ppermute | solution.py:1023
  102.3 16.8 %collective-permute-start.24 = (bf16[128,1024]{1,0:T(8,128)(2,1)S(1)}, bf16[128,1024]{1,0:T(8,128)(2,1)S(1)}, u32[]{:S(2)}, u32[]{:S(2)}) collective-permute-start(bf16[128,1024]{1,0:T(8,128)(2,1)S(1)} %get-tuple-element.290), channel_id=1, source_target_pairs={{0,2},{2,0},{4,10},{6,8},{8,6},{10,4},{12,14},{14,12},{1,3},{3,1},... | collective-permute-start | bytes 786440 | tf_op jit(solution)/shard_map/ppermute | solution.py:1023
  108.8 18.8 %collective-permute-start.22 = (bf16[256,1024]{1,0:T(8,128)(2,1)}, bf16[256,1024]{1,0:T(8,128)(2,1)}, u32[]{:S(2)}, u32[]{:S(2)}) collective-permute-start(bf16[256,1024]{1,0:T(8,128)(2,1)} %project.2), channel_id=1, source_target_pairs={{0,1},{1,0},{2,3},{3,2},{4,5},{5,4},{6,7},{7,6},{8,9},{9,8},{10,11... | collective-permute-start | bytes 1572872 | tf_op jit(solution)/shard_map/ppermute | solution.py:851
  127.7 16.7 %collective-permute-start.26 = (bf16[2,4,256,512]{3,2,1,0:T(8,128)(2,1)S(1)}, bf16[2,4,256,512]{3,2,1,0:T(8,128)(2,1)}, u32[]{:S(2)}, u32[]{:S(2)}) collective-permute-start(bf16[2,4,256,512]{3,2,1,0:T(8,128)(2,1)S(1)} %bitcast.100), channel_id=1, source_target_pairs={{0,8},{8,0},{1,9},{9,1},{2,10},{10,2},{3,11},{11,3},{4,12},{12,4},... | collective-permute-start | bytes 6291464 | tf_op jit(solution)/shard_map/ppermute | solution.py:851
  129.0 25.5 %collective-permute-start.28 = (bf16[4,256,512]{2,1,0:T(8,128)(2,1)}, bf16[4,256,512]{2,1,0:T(8,128)(2,1)}, u32[]{:S(2)}, u32[]{:S(2)}) collective-permute-start(bf16[4,256,512]{2,1,0:T(8,128)(2,1)} %pad_maximum_fusion.5), channel_id=1, source_target_pairs={{0,16},{16,0},{1,17},{17,1},{2,18},{18,2},{3,19},{19,3},{4,20},{20... | collective-permute-start | bytes 3145736 | tf_op jit(solution)/shard_map/ppermute | solution.py:851
  129.3 15.0 %collective-permute-start.25 = (bf16[256,1024]{1,0:T(8,128)(2,1)}, bf16[256,1024]{1,0:T(8,128)(2,1)S(1)}, u32[]{:S(2)}, u32[]{:S(2)}) collective-permute-start(bf16[256,1024]{1,0:T(8,128)(2,1)} %get-tuple-element.308.go.grad), channel_id=1, source_target_pairs={{0,1},{1,0},{2,3},{3,2},{4,5},{5,4},{6,7},{7,6},{8,9},{9,8},{10,11... | collective-permute-start | bytes 1572872 | tf_op jit(solution)/shard_map/ppermute | solution.py:851
  138.8 15.6 %collective-permute-start.27 = (bf16[256,1024]{1,0:T(8,128)(2,1)}, bf16[256,1024]{1,0:T(8,128)(2,1)S(1)}, u32[]{:S(2)}, u32[]{:S(2)}) collective-permute-start(bf16[256,1024]{1,0:T(8,128)(2,1)} %get-tuple-element.297.x.xo), channel_id=1, source_target_pairs={{0,1},{1,0},{2,3},{3,2},{4,5},{5,4},{6,7},{7,6},{8,9},{9,8},{10,11... | collective-permute-start | bytes 1572872 | tf_op jit(solution)/shard_map/ppermute | solution.py:851
  179.1 14.2 %collective-permute-start.30 = (bf16[256,1024]{1,0:T(8,128)(2,1)S(1)}, bf16[256,1024]{1,0:T(8,128)(2,1)S(1)}, u32[]{:S(2)}, u32[]{:S(2)}) collective-permute-start(bf16[256,1024]{1,0:T(8,128)(2,1)S(1)} %copy-done.43), channel_id=1, source_target_pairs={{0,1},{1,0},{2,3},{3,2},{4,5},{5,4},{6,7},{7,6},{8,9},{9,8},{10,11... | collective-permute-start | bytes 1572872 | tf_op jit(solution)/shard_map/ppermute | solution.py:851
  200.3 26.4 %collective-permute-start.34 = (bf16[4,256,512]{2,1,0:T(8,128)(2,1)}, bf16[4,256,512]{2,1,0:T(8,128)(2,1)}, u32[]{:S(2)}, u32[]{:S(2)}) collective-permute-start(bf16[4,256,512]{2,1,0:T(8,128)(2,1)} %get-tuple-element.510), channel_id=1, source_target_pairs={{0,16},{16,0},{1,17},{17,1},{2,18},{18,2},{3,19},{19,3},{4,20},{20... | collective-permute-start | bytes 3145736 | tf_op jit(solution)/shard_map/ppermute | solution.py:851
  206.9 22.0 %collective-permute-start.33 = (bf16[256,1024]{1,0:T(8,128)(2,1)}, bf16[256,1024]{1,0:T(8,128)(2,1)S(1)}, u32[]{:S(2)}, u32[]{:S(2)}) collective-permute-start(bf16[256,1024]{1,0:T(8,128)(2,1)} %get-tuple-element.326.grad.go), channel_id=1, source_target_pairs={{0,1},{1,0},{2,3},{3,2},{4,5},{5,4},{6,7},{7,6},{8,9},{9,8},{10,11... | collective-permute-start | bytes 1572872 | tf_op jit(solution)/shard_map/ppermute | solution.py:851
  212.1 44.1 %collective-permute-start.36 = (bf16[4,256,512]{2,1,0:T(8,128)(2,1)}, bf16[4,256,512]{2,1,0:T(8,128)(2,1)}, u32[]{:S(2)}, u32[]{:S(2)}) collective-permute-start(bf16[4,256,512]{2,1,0:T(8,128)(2,1)} %get-tuple-element.508), channel_id=1, source_target_pairs={{0,16},{16,0},{1,17},{17,1},{2,18},{18,2},{3,19},{19,3},{4,20},{20... | collective-permute-start | bytes 3145736 | tf_op jit(solution)/shard_map/ppermute | solution.py:851
  240.3 14.7 %collective-permute-start.35 = (bf16[256,1024]{1,0:T(8,128)(2,1)}, bf16[256,1024]{1,0:T(8,128)(2,1)}, u32[]{:S(2)}, u32[]{:S(2)}) collective-permute-start(bf16[256,1024]{1,0:T(8,128)(2,1)} %down.2), channel_id=1, source_target_pairs={{0,1},{1,0},{2,3},{3,2},{4,5},{5,4},{6,7},{7,6},{8,9},{9,8},{10,11... | collective-permute-start | bytes 1572872 | tf_op jit(solution)/shard_map/ppermute | solution.py:851
  241.5 14.7 %collective-permute-start.37 = (bf16[2,256,512]{2,1,0:T(8,128)(2,1)}, bf16[2,256,512]{2,1,0:T(8,128)(2,1)}, u32[]{:S(2)}, u32[]{:S(2)}) collective-permute-start(bf16[2,256,512]{2,1,0:T(8,128)(2,1)} %get-tuple-element.514), channel_id=1, source_target_pairs={{0,2},{2,0},{4,6},{6,4},{1,3},{3,1},{5,7},{7,5},{8,10},{10,8},{12,... | collective-permute-start | bytes 1572872 | tf_op jit(solution)/shard_map/ppermute | solution.py:851
  258.6 25.8 %collective-permute-start.42 = (bf16[2,256,512]{2,1,0:T(8,128)(2,1)}, bf16[2,256,512]{2,1,0:T(8,128)(2,1)S(1)}, u32[]{:S(2)}, u32[]{:S(2)}) collective-permute-start(bf16[2,256,512]{2,1,0:T(8,128)(2,1)} %get-tuple-element.512), channel_id=1, source_target_pairs={{0,2},{2,0},{4,6},{6,4},{1,3},{3,1},{5,7},{7,5},{8,10},{10,8},{12,... | collective-permute-start | bytes 1572872 | tf_op jit(solution)/shard_map/ppermute | solution.py:851
  272.0 16.9 %collective-permute-start.41 = (bf16[256,1024]{1,0:T(8,128)(2,1)}, bf16[256,1024]{1,0:T(8,128)(2,1)S(1)}, u32[]{:S(2)}, u32[]{:S(2)}) collective-permute-start(bf16[256,1024]{1,0:T(8,128)(2,1)} %get-tuple-element.357), channel_id=1, source_target_pairs={{0,1},{1,0},{2,3},{3,2},{4,5},{5,4},{6,7},{7,6},{8,9},{9,8},{10,11... | collective-permute-start | bytes 1572872 | tf_op jit(solution)/shard_map/ppermute | solution.py:851
  274.4 14.5 %collective-permute-start.43 = (bf16[1,256,512]{2,1,0:T(8,128)(2,1)}, bf16[1,256,512]{2,1,0:T(8,128)(2,1)S(1)}, u32[]{:S(2)}, u32[]{:S(2)}) collective-permute-start(bf16[1,256,512]{2,1,0:T(8,128)(2,1)} %get-tuple-element.524), channel_id=1, source_target_pairs={{0,4},{2,6},{4,0},{6,2},{1,5},{3,7},{5,1},{7,3},{8,12},{10,14},{12... | collective-permute-start | bytes 786440 | tf_op jit(solution)/shard_map/ppermute | solution.py:851
  289.5 26.1 %collective-permute-start.48 = (bf16[1,256,512]{2,1,0:T(8,128)(2,1)}, bf16[1,256,512]{2,1,0:T(8,128)(2,1)}, u32[]{:S(2)}, u32[]{:S(2)}) collective-permute-start(bf16[1,256,512]{2,1,0:T(8,128)(2,1)} %get-tuple-element.391), channel_id=1, source_target_pairs={{0,4},{2,6},{4,0},{6,2},{1,5},{3,7},{5,1},{7,3},{8,12},{10,14},{12... | collective-permute-start | bytes 786440 | tf_op jit(solution)/shard_map/ppermute | solution.py:851
  298.1 17.4 %collective-permute-start.47 = (bf16[4,128,384]{2,1,0:T(8,128)(2,1)S(1)}, bf16[4,128,384]{2,1,0:T(8,128)(2,1)S(1)}, u32[]{:S(2)}, u32[]{:S(2)}) collective-permute-start(bf16[4,128,384]{2,1,0:T(8,128)(2,1)S(1)} %get-tuple-element.389), channel_id=1, source_target_pairs={{0,16},{16,0},{1,17},{17,1},{2,18},{18,2},{3,19},{19,3},{4,20},{20... | collective-permute-start | bytes 1179656 | tf_op jit(solution)/shard_map/ppermute | solution.py:851
  306.2 23.3 %collective-permute-start.54 = (bf16[128,1024]{1,0:T(8,128)(2,1)}, bf16[128,1024]{1,0:T(8,128)(2,1)}, u32[]{:S(2)}, u32[]{:S(2)}) collective-permute-start(bf16[128,1024]{1,0:T(8,128)(2,1)} %get-tuple-element.418), channel_id=1, source_target_pairs={{0,0},{2,2},{8,4},{10,6},{4,8},{6,10},{12,12},{14,14},{1,1},{3,3},... | collective-permute-start | bytes 786440 | tf_op jit(solution)/shard_map/ppermute | solution.py:867
  309.7 19.9 %collective-permute-start.55 = (bf16[128,1024]{1,0:T(8,128)(2,1)}, bf16[128,1024]{1,0:T(8,128)(2,1)}, u32[]{:S(2)}, u32[]{:S(2)}) collective-permute-start(bf16[128,1024]{1,0:T(8,128)(2,1)} %get-tuple-element.419), channel_id=1, source_target_pairs={{2,0},{0,2},{10,4},{8,6},{6,8},{4,10},{14,12},{12,14},{3,1},{1,3},... | collective-permute-start | bytes 786440 | tf_op jit(solution)/shard_map/ppermute | solution.py:867
  (81 other events, 586.5 us)

commit v6 on v5

--- a/solution.py
+++ b/solution.py
@@ -526,7 +526,8 @@
     kv[1] = (acc[:, 256:] + bias[9:10]).astype(bf16)
 
 
-def attn_kernel(t, q, a, b, c, d, mixed, lse):
+def attn_kernel(t, q, a, b, c, d, *refs):
+    mixed, lse = refs[-4:-2] if len(refs) > 2 else refs
     scale = HD**-0.5 * LOG2E
     chunks = (a, b, c, d)
     keys = jnp.concatenate([r[0] for r in chunks], axis=0)
@@ -543,7 +544,10 @@
         o = nn(vals_t, p.astype(bf16)) / total
         parts.append(o[h * HD : (h + 1) * HD])
         lse[0, h : h + 1] = top * scale + jnp.log2(total)
-    mixed[...] = jnp.concatenate(parts, axis=0).T.astype(bf16)
+    rows = jnp.concatenate(parts, axis=0).T.astype(bf16)
+    mixed[...] = rows
+    if len(refs) > 2:
+        add_projection(t, rows, refs[:4], *refs[-2:])
 
 
 def attn_back_kernel(t, q, grad, mixed, lse, a, b, c, d, *refs):
@@ -585,7 +589,10 @@
 
 
 def proj_kernel(t, mixed, *refs):
-    ws, (out, acc) = refs[:4], refs[4:]
+    add_projection(t, mixed[...], refs[:4], *refs[4:])
+
+
+def add_projection(t, rows, ws, out, acc):
     j = pl.program_id(0)
 
     @pl.when(j == 0)
@@ -593,7 +600,7 @@
         acc[...] = jnp.zeros_like(acc)
 
     for i, (kc, ky) in enumerate(PAIRS):
-        acc[i] += nn(mixed[...], unpack_proj(ws, kc, ky))
+        acc[i] += nn(rows, unpack_proj(ws, kc, ky))
 
     @pl.when(j == 3)
     def _():
@@ -985,8 +992,6 @@
     q_t, kv_t = make_qkv(normed_t)
     far_t = flip(kv_t, "c", 2, 1)
     chunks = [kv_o, kv_t, far_o, far_t]
-    w1 = widen(w1, "near", kv_t)
-    q_t, w1 = lax.optimization_barrier((q_t, w1))
     lse_spec = pl.BlockSpec((1, 2, 256), lambda j, t: (j, 0, 0))
 
     def attend(queries):
@@ -1003,6 +1008,20 @@
         )
 
     acc_d = pltpu.VMEM((4, 256, 256), f32)
+
+    def attend_project(queries, kind):
+        return call(
+            attn_kernel,
+            table,
+            [queries, *chunks, *wa],
+            [column_spec(128)] + [pair_spec] * 4 + proj_specs(),
+            [column_spec(128), lse_spec, full],
+            [shaped((256, 512), bf16), shaped((4, 2, 256), f32), shaped((256, D), kind)],
+            steps=4,
+            scratch=[acc_d],
+            flops=4 * 256 * 1024 * 64 * 8 * 4,
+            name="attend_project",
+        )
 
     def project(rows, kind):
         return call(
@@ -1018,31 +1037,33 @@
             name="project",
         )
 
-    mixed_t, lse_t = attend(q_t)
+    mixed_t, lse_t, part_t = attend_project(q_t, bf16)
     cot_parts = spread_parts(after(cotangent, normed))
     cot = [lax.ppermute(after(p, mixed_t), ("c", "z"), route(k)) for k, p in enumerate(cot_parts)]
     w2 = widen(after(packed_fc2, q_t), "far", mixed_t)
-    part_t = project(after(mixed_t, w2), bf16)
     got_branch = flip(part_t, "x", 2, 1)
-    q_o, part_t = lax.optimization_barrier((q_o, part_t))
+    w1 = widen(w1, "near", mixed_t)
+    q_o, part_t, w1, w2 = lax.optimization_barrier((q_o, part_t, w1, w2))
     mixed_o, lse_o = attend(q_o)
     w1, w2 = widen(w1, "y", mixed_o), widen(w2, "near", mixed_o)
+    mixed_o, w1, w2, got_branch = lax.optimization_barrier((mixed_o, w1, w2, got_branch))
+    part_o = project(mixed_o, f32)
     dmlp_o, bfc2_sum = call(
         dmlp_kernel,
         table,
-        [*cot, after(mod, mixed_o)],
+        [*cot, after(mod, part_o)],
         [half, half, mod_spec],
         [full, whole((1, D))],
         [row_b, shaped((1, D), f32)],
         name="dbranch_mlp",
     )
     dmlp_t = flip(dmlp_o, "x", 2, 1)
-    mixed_o, w1, w2, got_branch, dmlp_o = lax.optimization_barrier((mixed_o, w1, w2, got_branch, dmlp_o))
+    part_o = after(part_o, dmlp_o)
     w1 = both_cores(w1)
     branch, middle, normed_mlp = call(
         mid_kernel,
         table,
-        [*tok, project(mixed_o, f32), got_branch, mod],
+        [*tok, part_o, got_branch, mod],
         [half, half, full, full, mod_spec],
         [full] * 3,
         [row_f, row_f, row_b],

time: 374 us -> 386 us (1.032)
  waiting for transfers between devices: 42 us -> 69 us
  starting transfers between devices: 83.4 us -> 78.1 us
  local copies, waits for them, and re-layouts: 31.9 us -> 27.5 us
    ppermute x59, waiting for transfers between devices: 39.8 us -> 66.3 us  [flip(): return lax.ppermute(v, axis, [(i, i ^ offset) for i in range(count)])]
    ppermute x59, starting transfers between devices: 68.4 us -> 62.6 us  [flip(): return lax.ppermute(v, axis, [(i, i ^ offset) for i in range(count)])]
    pallas_call x29 -> x28, Pallas kernels: 172 us -> 169 us  [kernel_call(): pl.pallas_call(body, grid_spec=pltpu.PrefetchScalarGridSpec(num_scalar_pr...]
    unnamed x103 -> x104, local copies, waits for them, and re-layouts: 14.8 us -> 12.1 us
  transfers between devices with their start and end apart: 67 -> 67, of which waited for: 20 -> 24; matrix products, arithmetic and copies ran while one was open for 15% -> 13% of each run, Pallas kernels for 40% -> 37%
where the time goes in v6:
time: 386 us; the launch traced here: 382 us
  Pallas kernels  169 us (44%)
  starting transfers between devices  78.1 us (20%)
  waiting for transfers between devices  69 us (18%)
  other arithmetic  35.1 us (9%)
  local copies, waits for them, and re-layouts  27.5 us (7%)
    pallas_call x28, Pallas kernels, kernel_call(): pl.pallas_call(body, grid_spec=pltpu.PrefetchScalarGridSpec(num_scalar_pr...  169 us
    ppermute x59, waiting for transfers between devices, flip(): return lax.ppermute(v, axis, [(i, i ^ offset) for i in range(count)])  66.3 us
    ppermute x59, starting transfers between devices, flip(): return lax.ppermute(v, axis, [(i, i ^ offset) for i in range(count)])  62.6 us
    convert_element_type x15, other arithmetic, fold(): return [(cut(own, k) + cut(got, k)).astype(bf16) for k in range(2)]  19.5 us
    unnamed x104, local copies, waits for them, and re-layouts  12.1 us
    ppermute x4, starting transfers between devices, send_back(): lax.ppermute(p, ('c', 'z'), [(b, a) for a, b in route(k)])  9.33 us
  transfers between devices with their start and end apart: 67, of which 24 were waited for; matrix products, arithmetic and copies ran while one was open for 13% of the time, Pallas kernels for 37%

profile of v6, /device:TPU:0, one launch (start us, length us, event | category | flops | bytes accessed | tf_op | source)
XLA Modules:
  0.0 382.3 jit_solution(1476223597436704883)
XLA Ops:
  6.3 3.6 collective-permute-start
  17.6 3.7 collective-permute-start.4
  24.6 3.7 modulate.1
  51.6 10.1 %collective-permute-done.13 = bf16[1,256,512]{2,1,0:T(8,128)(2,1)S(1)} collective-permute-done((bf16[1,256,512]{2,1,0:T(8,128)(2,1)S(1)}, bf16[1,256,512]{2,1,0:T(8,128)(2,1)S(1)}, u32[]{:S(2)}, u32[]{:S(2)}) %collective-permute-start.13) | collective-permute-done | bytes 262176 | tf_op jit(solution)/shard_map/ppermute | solution.py:858
  66.5 5.6 %qkv.3 = (bf16[256,512]{1,0:T(8,128)(2,1)}, bf16[2,256,512]{2,1,0:T(8,128)(2,1)}) custom-call(s32[14]{0:T(128)} %stack.86.t, bf16[256,1024]{1,0:T(8,128)(2,1)} %copy-done.14, bf16[2,4,128,512]{3,2,1,0:T(8,128)(2,1)} %bitcast.80, bf16[2,4,128,512]{3,2,1,0:T(8,128)(2,1)} %copy-done.4, bf16[2,4,128,512]{3,2,1,0:T(8,128)(2,1)} %bitcast.88, ...), custom_call_target="tpu_custom_call" | custom-call | flops 805306 | bytes 5570 | tf_op jit(solution)/shard_map/qkv/pallas_call | solution.py:430
  72.3 5.7 %qkv.2 = (bf16[256,512]{1,0:T(8,128)(2,1)}, bf16[2,256,512]{2,1,0:T(8,128)(2,1)}) custom-call(s32[14]{0:T(128)} %stack.86.t, bf16[256,1024]{1,0:T(8,128)(2,1)} %norm_in.1.x.xo, bf16[2,4,128,512]{3,2,1,0:T(8,128)(2,1)} %bitcast.81, bf16[2,4,128,512]{3,2,1,0:T(8,128)(2,1)} %copy-done.4, bf16[2,4,128,512]{3,2,1,0:T(8,128)(2,1)} %bitcast.89, ...), custom_call_target="tpu_custom_call" | custom-call | flops 805306 | bytes 5570 | tf_op jit(solution)/shard_map/qkv/pallas_call | solution.py:430
  82.8 10.5 %attend_project.1 = (bf16[256,512]{1,0:T(8,128)(2,1)}, f32[4,2,256]{2,1,0:T(2,128)}, bf16[256,1024]{1,0:T(8,128)(2,1)}) custom-call(s32[14]{0:T(128)} %stack.86.t, bf16[256,512]{1,0:T(8,128)(2,1)} %get-tuple-element.269.q, bf16[2,256,512]{2,1,0:T(8,128)(2,1)} %get-tuple-element.270.a, bf16[2,256,512]{2,1,0:T(8,128)(2,1)} %get-tuple-element.271.b, ...), custom_call_target="tpu_custom_call" | custom-call | flops 2147483 | bytes 7348 | tf_op jit(solution)/shard_map/attend_project/pallas_call | solution.py:430
  93.3 4.2 %collective-permute-done.19 = bf16[1,256,512]{2,1,0:T(8,128)(2,1)S(1)} collective-permute-done((bf16[1,256,512]{2,1,0:T(8,128)(2,1)S(1)}, bf16[1,256,512]{2,1,0:T(8,128)(2,1)S(1)}, u32[]{:S(2)}, u32[]{:S(2)}) %collective-permute-start.19) | collective-permute-done | bytes 262176 | tf_op jit(solution)/shard_map/ppermute | solution.py:858
  106.1 8.8 %attend.1 = (bf16[256,512]{1,0:T(8,128)(2,1)}, f32[4,2,256]{2,1,0:T(2,128)}) custom-call(s32[14]{0:T(128)} %stack.86.t, bf16[256,512]{1,0:T(8,128)(2,1)} %get-tuple-element.280.q, bf16[2,256,512]{2,1,0:T(8,128)(2,1)} %get-tuple-element.270.a, bf16[2,256,512]{2,1,0:T(8,128)(2,1)} %get-tuple-element.271.b, bf16[2,256,512]{2,1,0:T(8,128)(2,1)} %copy-done.7, ...), custom_call_target="tpu_custom_call" | custom-call | flops 2147483 | bytes 2629 | tf_op jit(solution)/shard_map/attend/pallas_call | solution.py:430
  115.9 9.2 %collective-permute-done.22 = bf16[4,256,512]{2,1,0:T(8,128)(2,1)} collective-permute-done((bf16[4,256,512]{2,1,0:T(8,128)(2,1)S(1)}, bf16[4,256,512]{2,1,0:T(8,128)(2,1)}, u32[]{:S(2)}, u32[]{:S(2)}) %collective-permute-start.22) | collective-permute-done | bytes 1048608 | tf_op jit(solution)/shard_map/ppermute | solution.py:858
  133.6 4.7 %project.1.part = f32[256,1024]{1,0:T(8,128)} custom-call(s32[14]{0:T(128)} %stack.86.t, bf16[256,512]{1,0:T(8,128)(2,1)} %get-tuple-element.291.mixed.mo, bf16[2,4,128,512]{3,2,1,0:T(8,128)(2,1)} %bitcast.83, bf16[2,4,128,512]{3,2,1,0:T(8,128)(2,1)} %copy-done.4, bf16[2,4,128,512]{3,2,1,0:T(8,128)(2,1)} %bitcast.91, ...), custom_call_target="tpu_custom_call" | custom-call | flops 268435 | bytes 5505 | tf_op jit(solution)/shard_map/project/pallas_call | solution.py:430
  145.3 4.0 %norm_mid.1 = (f32[256,1024]{1,0:T(8,128)}, f32[256,1024]{1,0:T(8,128)}, bf16[256,1024]{1,0:T(8,128)(2,1)}) custom-call(s32[14]{0:T(128)} %stack.86.t, bf16[128,1024]{1,0:T(8,128)(2,1)} %copy-done.10, bf16[128,1024]{1,0:T(8,128)(2,1)} %copy-done.9, f32[256,1024]{1,0:T(8,128)} %project.1.part, bf16[256,1024]{1,0:T(8,128)(2,1)} %collective-permute-done.24.got, ...), custom_call_target="tpu_custom_call" | custom-call | bytes 4784 | tf_op jit(solution)/shard_map/norm_mid/pallas_call | solution.py:430
  149.8 6.6 %collective-permute-done.25.grad.gt = bf16[256,1024]{1,0:T(8,128)(2,1)} collective-permute-done((bf16[256,1024]{1,0:T(8,128)(2,1)}, bf16[256,1024]{1,0:T(8,128)(2,1)}, u32[]{:S(2)}, u32[]{:S(2)}) %collective-permute-start.25) | collective-permute-done | bytes 524320 | tf_op jit(solution)/shard_map/ppermute | solution.py:858
  156.4 6.6 %up.2 = (bf16[256,2048]{1,0:T(8,128)(2,1)}, bf16[256,2048]{1,0:T(8,128)(2,1)}) custom-call(s32[14]{0:T(128)} %stack.86.t, bf16[256,1024]{1,0:T(8,128)(2,1)} %get-tuple-element.297.x.xo, bf16[2,4,256,512]{3,2,1,0:T(8,128)(2,1)} %bitcast.101, bf16[2,4,256,512]{3,2,1,0:T(8,128)(2,1)} %collective-permute-done.26.wt.w1t, f32[16,1024]{1,0:T(8,128)} %add.216.mod.refs_4_.bias), custom_call_target="tpu_custom_call" | custom-call | flops 1073741 | bytes 6881 | tf_op jit(solution)/shard_map/up/pallas_call | solution.py:430
  163.0 4.7 %collective-permute-done.27.x.xt = bf16[256,1024]{1,0:T(8,128)(2,1)} collective-permute-done((bf16[256,1024]{1,0:T(8,128)(2,1)}, bf16[256,1024]{1,0:T(8,128)(2,1)}, u32[]{:S(2)}, u32[]{:S(2)}) %collective-permute-start.27) | collective-permute-done | bytes 524320 | tf_op jit(solution)/shard_map/ppermute | solution.py:858
  171.4 6.6 %up.3 = (bf16[256,2048]{1,0:T(8,128)(2,1)}, bf16[256,2048]{1,0:T(8,128)(2,1)}) custom-call(s32[14]{0:T(128)} %stack.86.t, bf16[256,1024]{1,0:T(8,128)(2,1)} %collective-permute-done.27.x.xt, bf16[2,4,256,512]{3,2,1,0:T(8,128)(2,1)} %bitcast.102, bf16[2,4,256,512]{3,2,1,0:T(8,128)(2,1)} %collective-permute-done.26.wt.w1t, f32[16,1024]{1,0:T(8,128)} %add.216.mod.refs_4_.bias), custom_call_target="tpu_custom_call" | custom-call | flops 1073741 | bytes 6881 | tf_op jit(solution)/shard_map/up/pallas_call | solution.py:430
  178.0 8.0 %mlp_back.2 = (bf16[256,2048]{1,0:T(8,128)(2,1)}, f32[1,2048]{1,0:T(1,128)}, bf16[256,1024]{1,0:T(8,128)(2,1)}) custom-call(s32[14]{0:T(128)} %stack.86.t, bf16[256,1024]{1,0:T(8,128)(2,1)} %collective-permute-done.25.grad.gt, bf16[256,2048]{1,0:T(8,128)(2,1)} %get-tuple-element.303.slope, bf16[2,4,256,512]{3,2,1,0:T(8,128)(2,1)} %bitcast.96, ...), custom_call_target="tpu_custom_call" | custom-call | flops 2147483 | bytes 11542 | tf_op jit(solution)/shard_map/mlp_back/pallas_call | solution.py:430
  186.0 6.9 %fc2_grads.1 = (bf16[2,4,256,512]{3,2,1,0:T(8,128)(2,1)}, bf16[2,4,256,512]{3,2,1,0:T(8,128)(2,1)}) custom-call(s32[14]{0:T(128)} %stack.86.t, bf16[256,2048]{1,0:T(8,128)(2,1)} %get-tuple-element.368.acto.act, bf16[256,2048]{1,0:T(8,128)(2,1)} %get-tuple-element.334.actt.act, bf16[256,1024]{1,0:T(8,128)(2,1)} %get-tuple-element.308.go.grad, ...), custom_call_target="tpu_custom_call" | custom-call | flops 2147483 | bytes 7340 | tf_op jit(solution)/shard_map/fc2_grads/pallas_call | solution.py:430
  194.5 8.1 %mlp_back.3 = (bf16[256,2048]{1,0:T(8,128)(2,1)}, f32[1,2048]{1,0:T(1,128)}, f32[256,1024]{1,0:T(8,128)}) custom-call(s32[14]{0:T(128)} %stack.86.t, bf16[256,1024]{1,0:T(8,128)(2,1)} %get-tuple-element.308.go.grad, bf16[256,2048]{1,0:T(8,128)(2,1)} %get-tuple-element.310.slope, bf16[2,4,256,512]{3,2,1,0:T(8,128)(2,1)} %bitcast.97, ...), custom_call_target="tpu_custom_call" | custom-call | flops 2147483 | bytes 12066 | tf_op jit(solution)/shard_map/mlp_back/pallas_call | solution.py:430
  204.1 3.8 add_convert_fusion.2
  207.9 7.0 %fc1_grads.1 = (bf16[2,4,256,512]{3,2,1,0:T(8,128)(2,1)}, bf16[2,4,256,512]{3,2,1,0:T(8,128)(2,1)}) custom-call(s32[14]{0:T(128)} %stack.86.t, bf16[256,1024]{1,0:T(8,128)(2,1)} %get-tuple-element.297.x.xo, bf16[256,1024]{1,0:T(8,128)(2,1)} %collective-permute-done.27.x.xt, bf16[256,2048]{1,0:T(8,128)(2,1)} %get-tuple-element.316.dho, ...), custom_call_target="tpu_custom_call" | custom-call | flops 2147483 | bytes 7340 | tf_op jit(solution)/shard_map/fc1_grads/pallas_call | solution.py:430
  215.4 5.1 %norm_mid_back.1 = (f32[256,1024]{1,0:T(8,128)}, bf16[256,1024]{1,0:T(8,128)(2,1)}, f32[8,1024]{1,0:T(8,128)}) custom-call(s32[14]{0:T(128)} %stack.86.t, f32[256,1024]{1,0:T(8,128)} %get-tuple-element.319.part, bf16[256,1024]{1,0:T(8,128)(2,1)} %copy-done.25, f32[256,1024]{1,0:T(8,128)} %get-tuple-element.320.middle, ...), custom_call_target="tpu_custom_call" | custom-call | bytes 5865 | tf_op jit(solution)/shard_map/norm_mid_back/pallas_call | solution.py:430
  221.3 3.9 %add_convert_fusion = (bf16[4,256,512]{2,1,0:T(8,128)(2,1)}, bf16[4,256,512]{2,1,0:T(8,128)(2,1)S(1)}) fusion(bf16[8,256,512]{2,1,0:T(8,128)(2,1)} %collective-permute-done.32, bf16[8,256,512]{2,1,0:T(8,128)(2,1)} %bitcast.105), kind=kLoop, calls=%fused_computation.2 | loop fusion | flops 4194304 | bytes 6291456 | tf_op jit(solution)/shard_map/convert_element_type | solution.py:905
  226.9 12.7 %attend_back.2 = (bf16[256,512]{1,0:T(8,128)(2,1)}, bf16[2,512,512]{2,1,0:T(8,128)(2,1)}, bf16[2,512,512]{2,1,0:T(8,128)(2,1)}) custom-call(s32[14]{0:T(128)} %stack.86.t, bf16[256,512]{1,0:T(8,128)(2,1)} %get-tuple-element.280.q, bf16[256,1024]{1,0:T(8,128)(2,1)} %get-tuple-element.326.grad.go, bf16[256,512]{1,0:T(8,128)(2,1)} %get-tuple-element.291.mixed.mo, ...), custom_call_target="tpu_custom_call" | custom-call | flops 5368709 | bytes 9707 | tf_op jit(solution)/shard_map/attend_back/pallas_call | solution.py:430
  244.5 5.0 %proj_grads.1 = (bf16[2,4,128,256]{3,2,1,0:T(8,128)(2,1)}, bf16[2,4,128,256]{3,2,1,0:T(8,128)(2,1)}) custom-call(s32[14]{0:T(128)} %stack.86.t, bf16[256,512]{1,0:T(8,128)(2,1)} %get-tuple-element.291.mixed.mo, bf16[256,512]{1,0:T(8,128)(2,1)} %get-tuple-element.273.mt.mixed, bf16[256,1024]{1,0:T(8,128)(2,1)} %get-tuple-element.326.grad.go, ...), custom_call_target="tpu_custom_call" | custom-call | flops 536870 | bytes 2621 | tf_op jit(solution)/shard_map/proj_grads/pallas_call | solution.py:430
  249.5 5.6 %down.2 = bf16[256,1024]{1,0:T(8,128)(2,1)} custom-call(s32[14]{0:T(128)} %stack.86.t, bf16[256,2048]{1,0:T(8,128)(2,1)} %get-tuple-element.334.actt.act, bf16[2,4,256,512]{3,2,1,0:T(8,128)(2,1)} %bitcast.98, bf16[2,4,256,512]{3,2,1,0:T(8,128)(2,1)} %collective-permute-done.29.w2t.wt), custom_call_target="tpu_custom_call" | custom-call | flops 1073741 | bytes 5767 | tf_op jit(solution)/shard_map/down/pallas_call | solution.py:430
  258.0 12.6 %attend_back.3 = (bf16[256,512]{1,0:T(8,128)(2,1)}, bf16[2,512,512]{2,1,0:T(8,128)(2,1)}, bf16[2,512,512]{2,1,0:T(8,128)(2,1)}) custom-call(s32[14]{0:T(128)} %stack.86.t, bf16[256,512]{1,0:T(8,128)(2,1)} %get-tuple-element.269.q, bf16[256,1024]{1,0:T(8,128)(2,1)} %copy-done.13, bf16[256,512]{1,0:T(8,128)(2,1)} %get-tuple-element.273.mt.mixed, ...), custom_call_target="tpu_custom_call" | custom-call | flops 5368709 | bytes 9707 | tf_op jit(solution)/shard_map/attend_back/pallas_call | solution.py:430
  278.9 8.2 %qkv_back.1 = (bf16[4,256,384]{2,1,0:T(8,128)(2,1)}, bf16[4,256,384]{2,1,0:T(8,128)(2,1)}, f32[8,512]{1,0:T(8,128)}, f32[256,1024]{1,0:T(8,128)}, bf16[256,1024]{1,0:T(8,128)(2,1)}) custom-call(s32[14]{0:T(128)} %stack.86.t, bf16[256,512]{1,0:T(8,128)(2,1)} %get-tuple-element.328.dqo, bf16[256,512]{1,0:T(8,128)(2,1)} %get-tuple-element.352.dqt, ...), custom_call_target="tpu_custom_call" | custom-call | flops 1610612 | bytes 12075 | tf_op jit(solution)/shard_map/qkv_back/pallas_call | solution.py:430
  288.7 6.9 %qkv_grads.1 = (bf16[2,4,128,384]{3,2,1,0:T(8,128)(2,1)}, bf16[2,4,128,384]{3,2,1,0:T(8,128)(2,1)}, bf16[2,4,128,384]{3,2,1,0:T(8,128)(2,1)}, bf16[2,4,128,384]{3,2,1,0:T(8,128)(2,1)}) custom-call(s32[14]{0:T(128)} %stack.86.t, bf16[256,1024]{1,0:T(8,128)(2,1)} %norm_in.1.x.xo, bf16[256,1024]{1,0:T(8,128)(2,1)} %copy-done.14, ...), custom_call_target="tpu_custom_call" | custom-call | flops 1610612 | bytes 5767 | tf_op jit(solution)/shard_map/qkv_grads/pallas_call | solution.py:430
  296.5 6.2 %collective-permute-done.43 = bf16[1,256,512]{2,1,0:T(8,128)(2,1)S(1)} collective-permute-done((bf16[1,256,512]{2,1,0:T(8,128)(2,1)}, bf16[1,256,512]{2,1,0:T(8,128)(2,1)S(1)}, u32[]{:S(2)}, u32[]{:S(2)}) %collective-permute-start.43) | collective-permute-done | bytes 262176 | tf_op jit(solution)/shard_map/ppermute | solution.py:858
  303.4 5.8 %down.3.part = f32[256,1024]{1,0:T(8,128)} custom-call(s32[14]{0:T(128)} %stack.86.t, bf16[256,2048]{1,0:T(8,128)(2,1)} %get-tuple-element.368.acto.act, bf16[2,4,256,512]{3,2,1,0:T(8,128)(2,1)} %bitcast.99, bf16[2,4,256,512]{3,2,1,0:T(8,128)(2,1)} %collective-permute-done.29.w2t.wt), custom_call_target="tpu_custom_call" | custom-call | flops 1073741 | bytes 6291 | tf_op jit(solution)/shard_map/down/pallas_call | solution.py:430
  323.0 4.1 %norm_in_back.1 = (bf16[128,1024]{1,0:T(8,128)(2,1)}, bf16[128,1024]{1,0:T(8,128)(2,1)}, f32[2,1024]{1,0:T(2,128)}) custom-call(s32[14]{0:T(128)} %stack.86.t, f32[256,1024]{1,0:T(8,128)} %get-tuple-element.384.part, bf16[256,1024]{1,0:T(8,128)(2,1)} %copy-done.27, f32[256,1024]{1,0:T(8,128)} %get-tuple-element.386.dmid, bf16[128,1024]{1,0:T(8,128)(2,1)} %copy-done.10, ...), custom_call_target="tpu_custom_call" | custom-call | bytes 3743 | tf_op jit(solution)/shard_map/norm_in_back/pallas_call | solution.py:430
  (338 shorter events, 172.4 us)
Async XLA Ops:
  12.7 21.3 %collective-permute-start.6 = (bf16[128,1024]{1,0:T(8,128)(2,1)S(1)}, bf16[128,1024]{1,0:T(8,128)(2,1)S(1)}, u32[]{:S(2)}, u32[]{:S(2)}) collective-permute-start(bf16[128,1024]{1,0:T(8,128)(2,1)S(1)} %get-tuple-element.540), channel_id=1, source_target_pairs={{0,2},{2,0},{4,10},{6,8},{8,6},{10,4},{12,14},{14,12},{1,3},{3,1},... | collective-permute-start | bytes 786440 | tf_op jit(solution)/shard_map/ppermute | solution.py:919
  14.4 19.7 %collective-permute-start.5 = (bf16[128,1024]{1,0:T(8,128)(2,1)S(1)}, bf16[128,1024]{1,0:T(8,128)(2,1)S(1)}, u32[]{:S(2)}, u32[]{:S(2)}) collective-permute-start(bf16[128,1024]{1,0:T(8,128)(2,1)S(1)} %get-tuple-element.541), channel_id=1, source_target_pairs={{0,0},{2,2},{4,8},{6,10},{8,4},{10,6},{12,12},{14,14},{1,1},{3,3},... | collective-permute-start | bytes 786440 | tf_op jit(solution)/shard_map/ppermute | solution.py:919
  17.6 16.4 %collective-permute-start.4 = (bf16[1,128,512]{2,1,0:T(8,128)(2,1)S(1)}, bf16[1,128,512]{2,1,0:T(8,128)(2,1)S(1)}, u32[]{:S(2)}, u32[]{:S(2)}) collective-permute-start(bf16[1,128,512]{2,1,0:T(8,128)(2,1)S(1)} %copy-done.35), channel_id=1, source_target_pairs={{0,4},{2,6},{4,0},{6,2},{1,5},{3,7},{5,1},{7,3},{8,12},{10,14},{12... | collective-permute-start | bytes 393224 | tf_op jit(solution)/shard_map/ppermute | solution.py:858
  21.3 14.1 %collective-permute-start.3 = (bf16[2,128,512]{2,1,0:T(8,128)(2,1)S(1)}, bf16[2,128,512]{2,1,0:T(8,128)(2,1)S(1)}, u32[]{:S(2)}, u32[]{:S(2)}) collective-permute-start(bf16[2,128,512]{2,1,0:T(8,128)(2,1)S(1)} %pad_maximum_fusion.9), channel_id=1, source_target_pairs={{0,2},{2,0},{4,6},{6,4},{1,3},{3,1},{5,7},{7,5},{8,10},{10,8},{12,... | collective-permute-start | bytes 786440 | tf_op jit(solution)/shard_map/ppermute | solution.py:858
  36.5 14.9 %collective-permute-start.10 = (bf16[4,128,512]{2,1,0:T(8,128)(2,1)S(1)}, bf16[4,128,512]{2,1,0:T(8,128)(2,1)S(1)}, u32[]{:S(2)}, u32[]{:S(2)}) collective-permute-start(bf16[4,128,512]{2,1,0:T(8,128)(2,1)S(1)} %constant_dynamic-update-slice_fusion.4), channel_id=1, source_target_pairs={{0,16},{16,0},{1,17},{17,1},{2,18},{18,2},{3,19},{19,3},{4,20},{20... | collective-permute-start | bytes 1572872 | tf_op jit(solution)/shard_map/ppermute | solution.py:858
  45.8 15.9 %collective-permute-start.14 = (bf16[256,1024]{1,0:T(8,128)(2,1)}, bf16[256,1024]{1,0:T(8,128)(2,1)S(1)}, u32[]{:S(2)}, u32[]{:S(2)}) collective-permute-start(bf16[256,1024]{1,0:T(8,128)(2,1)} %norm_in.1.x.xo), channel_id=1, source_target_pairs={{0,1},{1,0},{2,3},{3,2},{4,5},{5,4},{6,7},{7,6},{8,9},{9,8},{10,11... | collective-permute-start | bytes 1572872 | tf_op jit(solution)/shard_map/ppermute | solution.py:858
  47.2 15.1 %collective-permute-start.12 = (bf16[4,128,512]{2,1,0:T(8,128)(2,1)S(1)}, bf16[4,128,512]{2,1,0:T(8,128)(2,1)S(1)}, u32[]{:S(2)}, u32[]{:S(2)}) collective-permute-start(bf16[4,128,512]{2,1,0:T(8,128)(2,1)S(1)} %constant_dynamic-update-slice_fusion.2), channel_id=1, source_target_pairs={{0,16},{16,0},{1,17},{17,1},{2,18},{18,2},{3,19},{19,3},{4,20},{20... | collective-permute-start | bytes 1572872 | tf_op jit(solution)/shard_map/ppermute | solution.py:858
  78.2 20.0 %collective-permute-start.18 = (bf16[2,256,512]{2,1,0:T(8,128)(2,1)S(1)}, bf16[2,256,512]{2,1,0:T(8,128)(2,1)S(1)}, u32[]{:S(2)}, u32[]{:S(2)}) collective-permute-start(bf16[2,256,512]{2,1,0:T(8,128)(2,1)S(1)} %copy-done.16), channel_id=1, source_target_pairs={{0,2},{2,0},{4,6},{6,4},{1,3},{3,1},{5,7},{7,5},{8,10},{10,8},{12,... | collective-permute-start | bytes 1572872 | tf_op jit(solution)/shard_map/ppermute | solution.py:858
  80.3 17.2 %collective-permute-start.19 = (bf16[1,256,512]{2,1,0:T(8,128)(2,1)S(1)}, bf16[1,256,512]{2,1,0:T(8,128)(2,1)S(1)}, u32[]{:S(2)}, u32[]{:S(2)}) collective-permute-start(bf16[1,256,512]{2,1,0:T(8,128)(2,1)S(1)} %copy-done.34), channel_id=1, source_target_pairs={{0,4},{2,6},{4,0},{6,2},{1,5},{3,7},{5,1},{7,3},{8,12},{10,14},{12... | collective-permute-start | bytes 786440 | tf_op jit(solution)/shard_map/ppermute | solution.py:858
  100.2 24.9 %collective-permute-start.22 = (bf16[4,256,512]{2,1,0:T(8,128)(2,1)S(1)}, bf16[4,256,512]{2,1,0:T(8,128)(2,1)}, u32[]{:S(2)}, u32[]{:S(2)}) collective-permute-start(bf16[4,256,512]{2,1,0:T(8,128)(2,1)S(1)} %pad_maximum_fusion.4), channel_id=1, source_target_pairs={{0,16},{16,0},{1,17},{17,1},{2,18},{18,2},{3,19},{19,3},{4,20},{20... | collective-permute-start | bytes 3145736 | tf_op jit(solution)/shard_map/ppermute | solution.py:858
  102.0 13.8 %collective-permute-start.23 = (bf16[2,256,512]{2,1,0:T(8,128)(2,1)S(1)}, bf16[2,256,512]{2,1,0:T(8,128)(2,1)S(1)}, u32[]{:S(2)}, u32[]{:S(2)}) collective-permute-start(bf16[2,256,512]{2,1,0:T(8,128)(2,1)S(1)} %pad_maximum_fusion.6), channel_id=1, source_target_pairs={{0,2},{2,0},{4,6},{6,4},{1,3},{3,1},{5,7},{7,5},{8,10},{10,8},{12,... | collective-permute-start | bytes 1572872 | tf_op jit(solution)/shard_map/ppermute | solution.py:858
  104.6 22.3 %collective-permute-start.24 = (bf16[256,1024]{1,0:T(8,128)(2,1)}, bf16[256,1024]{1,0:T(8,128)(2,1)}, u32[]{:S(2)}, u32[]{:S(2)}) collective-permute-start(bf16[256,1024]{1,0:T(8,128)(2,1)} %get-tuple-element.272), channel_id=1, source_target_pairs={{0,1},{1,0},{2,3},{3,2},{4,5},{5,4},{6,7},{7,6},{8,9},{9,8},{10,11... | collective-permute-start | bytes 1572872 | tf_op jit(solution)/shard_map/ppermute | solution.py:858
  126.9 29.5 %collective-permute-start.26 = (bf16[2,4,256,512]{3,2,1,0:T(8,128)(2,1)S(1)}, bf16[2,4,256,512]{3,2,1,0:T(8,128)(2,1)}, u32[]{:S(2)}, u32[]{:S(2)}) collective-permute-start(bf16[2,4,256,512]{3,2,1,0:T(8,128)(2,1)S(1)} %bitcast.100), channel_id=1, source_target_pairs={{0,8},{8,0},{1,9},{9,1},{2,10},{10,2},{3,11},{11,3},{4,12},{12,4},... | collective-permute-start | bytes 6291464 | tf_op jit(solution)/shard_map/ppermute | solution.py:858
  127.0 40.7 %collective-permute-start.28 = (bf16[4,256,512]{2,1,0:T(8,128)(2,1)S(1)}, bf16[4,256,512]{2,1,0:T(8,128)(2,1)}, u32[]{:S(2)}, u32[]{:S(2)}) collective-permute-start(bf16[4,256,512]{2,1,0:T(8,128)(2,1)S(1)} %pad_maximum_fusion.5), channel_id=1, source_target_pairs={{0,16},{16,0},{1,17},{17,1},{2,18},{18,2},{3,19},{19,3},{4,20},{20... | collective-permute-start | bytes 3145736 | tf_op jit(solution)/shard_map/ppermute | solution.py:858
  143.8 12.6 %collective-permute-start.25 = (bf16[256,1024]{1,0:T(8,128)(2,1)}, bf16[256,1024]{1,0:T(8,128)(2,1)}, u32[]{:S(2)}, u32[]{:S(2)}) collective-permute-start(bf16[256,1024]{1,0:T(8,128)(2,1)} %get-tuple-element.308.go.grad), channel_id=1, source_target_pairs={{0,1},{1,0},{2,3},{3,2},{4,5},{5,4},{6,7},{7,6},{8,9},{9,8},{10,11... | collective-permute-start | bytes 1572872 | tf_op jit(solution)/shard_map/ppermute | solution.py:858
  149.2 18.4 %collective-permute-start.27 = (bf16[256,1024]{1,0:T(8,128)(2,1)}, bf16[256,1024]{1,0:T(8,128)(2,1)}, u32[]{:S(2)}, u32[]{:S(2)}) collective-permute-start(bf16[256,1024]{1,0:T(8,128)(2,1)} %get-tuple-element.297.x.xo), channel_id=1, source_target_pairs={{0,1},{1,0},{2,3},{3,2},{4,5},{5,4},{6,7},{7,6},{8,9},{9,8},{10,11... | collective-permute-start | bytes 1572872 | tf_op jit(solution)/shard_map/ppermute | solution.py:858
  193.0 14.9 %collective-permute-start.30 = (bf16[256,1024]{1,0:T(8,128)(2,1)S(1)}, bf16[256,1024]{1,0:T(8,128)(2,1)S(1)}, u32[]{:S(2)}, u32[]{:S(2)}) collective-permute-start(bf16[256,1024]{1,0:T(8,128)(2,1)S(1)} %copy-done.44), channel_id=1, source_target_pairs={{0,1},{1,0},{2,3},{3,2},{4,5},{5,4},{6,7},{7,6},{8,9},{9,8},{10,11... | collective-permute-start | bytes 1572872 | tf_op jit(solution)/shard_map/ppermute | solution.py:858
  215.1 26.3 %collective-permute-start.34 = (bf16[4,256,512]{2,1,0:T(8,128)(2,1)}, bf16[4,256,512]{2,1,0:T(8,128)(2,1)}, u32[]{:S(2)}, u32[]{:S(2)}) collective-permute-start(bf16[4,256,512]{2,1,0:T(8,128)(2,1)} %get-tuple-element.510), channel_id=1, source_target_pairs={{0,16},{16,0},{1,17},{17,1},{2,18},{18,2},{3,19},{19,3},{4,20},{20... | collective-permute-start | bytes 3145736 | tf_op jit(solution)/shard_map/ppermute | solution.py:858
  220.5 23.2 %collective-permute-start.33 = (bf16[256,1024]{1,0:T(8,128)(2,1)}, bf16[256,1024]{1,0:T(8,128)(2,1)S(1)}, u32[]{:S(2)}, u32[]{:S(2)}) collective-permute-start(bf16[256,1024]{1,0:T(8,128)(2,1)} %get-tuple-element.326.grad.go), channel_id=1, source_target_pairs={{0,1},{1,0},{2,3},{3,2},{4,5},{5,4},{6,7},{7,6},{8,9},{9,8},{10,11... | collective-permute-start | bytes 1572872 | tf_op jit(solution)/shard_map/ppermute | solution.py:858
  225.2 46.0 %collective-permute-start.36 = (bf16[4,256,512]{2,1,0:T(8,128)(2,1)}, bf16[4,256,512]{2,1,0:T(8,128)(2,1)}, u32[]{:S(2)}, u32[]{:S(2)}) collective-permute-start(bf16[4,256,512]{2,1,0:T(8,128)(2,1)} %get-tuple-element.508), channel_id=1, source_target_pairs={{0,16},{16,0},{1,17},{17,1},{2,18},{18,2},{3,19},{19,3},{4,20},{20... | collective-permute-start | bytes 3145736 | tf_op jit(solution)/shard_map/ppermute | solution.py:858
  255.2 15.7 %collective-permute-start.35 = (bf16[256,1024]{1,0:T(8,128)(2,1)}, bf16[256,1024]{1,0:T(8,128)(2,1)}, u32[]{:S(2)}, u32[]{:S(2)}) collective-permute-start(bf16[256,1024]{1,0:T(8,128)(2,1)} %down.2), channel_id=1, source_target_pairs={{0,1},{1,0},{2,3},{3,2},{4,5},{5,4},{6,7},{7,6},{8,9},{9,8},{10,11... | collective-permute-start | bytes 1572872 | tf_op jit(solution)/shard_map/ppermute | solution.py:858
  256.0 15.2 %collective-permute-start.38 = (bf16[8,128,256]{2,1,0:T(8,128)(2,1)}, bf16[8,128,256]{2,1,0:T(8,128)(2,1)S(1)}, u32[]{:S(2)}, u32[]{:S(2)}) collective-permute-start(bf16[8,128,256]{2,1,0:T(8,128)(2,1)} %bitcast.29), channel_id=1, source_target_pairs={{0,8},{8,0},{1,9},{9,1},{2,10},{10,2},{3,11},{11,3},{4,12},{12,4},... | collective-permute-start | bytes 1572872 | tf_op jit(solution)/shard_map/ppermute | solution.py:858
  256.0 15.2 %collective-permute-start.37 = (bf16[2,256,512]{2,1,0:T(8,128)(2,1)}, bf16[2,256,512]{2,1,0:T(8,128)(2,1)}, u32[]{:S(2)}, u32[]{:S(2)}) collective-permute-start(bf16[2,256,512]{2,1,0:T(8,128)(2,1)} %get-tuple-element.514), channel_id=1, source_target_pairs={{0,2},{2,0},{4,6},{6,4},{1,3},{3,1},{5,7},{7,5},{8,10},{10,8},{12,... | collective-permute-start | bytes 1572872 | tf_op jit(solution)/shard_map/ppermute | solution.py:858
  274.4 21.2 %collective-permute-start.42 = (bf16[2,256,512]{2,1,0:T(8,128)(2,1)}, bf16[2,256,512]{2,1,0:T(8,128)(2,1)S(1)}, u32[]{:S(2)}, u32[]{:S(2)}) collective-permute-start(bf16[2,256,512]{2,1,0:T(8,128)(2,1)} %get-tuple-element.512), channel_id=1, source_target_pairs={{0,2},{2,0},{4,6},{6,4},{1,3},{3,1},{5,7},{7,5},{8,10},{10,8},{12,... | collective-permute-start | bytes 1572872 | tf_op jit(solution)/shard_map/ppermute | solution.py:858
  287.1 15.6 %collective-permute-start.41 = (bf16[256,1024]{1,0:T(8,128)(2,1)}, bf16[256,1024]{1,0:T(8,128)(2,1)S(1)}, u32[]{:S(2)}, u32[]{:S(2)}) collective-permute-start(bf16[256,1024]{1,0:T(8,128)(2,1)} %get-tuple-element.357), channel_id=1, source_target_pairs={{0,1},{1,0},{2,3},{3,2},{4,5},{5,4},{6,7},{7,6},{8,9},{9,8},{10,11... | collective-permute-start | bytes 1572872 | tf_op jit(solution)/shard_map/ppermute | solution.py:858
  288.7 13.9 %collective-permute-start.43 = (bf16[1,256,512]{2,1,0:T(8,128)(2,1)}, bf16[1,256,512]{2,1,0:T(8,128)(2,1)S(1)}, u32[]{:S(2)}, u32[]{:S(2)}) collective-permute-start(bf16[1,256,512]{2,1,0:T(8,128)(2,1)} %get-tuple-element.524), channel_id=1, source_target_pairs={{0,4},{2,6},{4,0},{6,2},{1,5},{3,7},{5,1},{7,3},{8,12},{10,14},{12... | collective-permute-start | bytes 786440 | tf_op jit(solution)/shard_map/ppermute | solution.py:858
  303.3 24.2 %collective-permute-start.48 = (bf16[1,256,512]{2,1,0:T(8,128)(2,1)}, bf16[1,256,512]{2,1,0:T(8,128)(2,1)}, u32[]{:S(2)}, u32[]{:S(2)}) collective-permute-start(bf16[1,256,512]{2,1,0:T(8,128)(2,1)} %get-tuple-element.391), channel_id=1, source_target_pairs={{0,4},{2,6},{4,0},{6,2},{1,5},{3,7},{5,1},{7,3},{8,12},{10,14},{12... | collective-permute-start | bytes 786440 | tf_op jit(solution)/shard_map/ppermute | solution.py:858
  312.0 15.5 %collective-permute-start.47 = (bf16[4,128,384]{2,1,0:T(8,128)(2,1)S(1)}, bf16[4,128,384]{2,1,0:T(8,128)(2,1)S(1)}, u32[]{:S(2)}, u32[]{:S(2)}) collective-permute-start(bf16[4,128,384]{2,1,0:T(8,128)(2,1)S(1)} %get-tuple-element.389), channel_id=1, source_target_pairs={{0,16},{16,0},{1,17},{17,1},{2,18},{18,2},{3,19},{19,3},{4,20},{20... | collective-permute-start | bytes 1179656 | tf_op jit(solution)/shard_map/ppermute | solution.py:858
  313.8 13.3 %collective-permute-start.49 = (bf16[2,128,256]{2,1,0:T(8,128)(2,1)S(1)}, bf16[2,128,256]{2,1,0:T(8,128)(2,1)S(1)}, u32[]{:S(2)}, u32[]{:S(2)}) collective-permute-start(bf16[2,128,256]{2,1,0:T(8,128)(2,1)S(1)} %get-tuple-element.536), channel_id=1, source_target_pairs={{0,2},{2,0},{4,6},{6,4},{1,3},{3,1},{5,7},{7,5},{8,10},{10,8},{12,... | collective-permute-start | bytes 393224 | tf_op jit(solution)/shard_map/ppermute | solution.py:858
  318.9 23.7 %collective-permute-start.54 = (bf16[128,1024]{1,0:T(8,128)(2,1)}, bf16[128,1024]{1,0:T(8,128)(2,1)}, u32[]{:S(2)}, u32[]{:S(2)}) collective-permute-start(bf16[128,1024]{1,0:T(8,128)(2,1)} %get-tuple-element.418), channel_id=1, source_target_pairs={{0,0},{2,2},{8,4},{10,6},{4,8},{6,10},{12,12},{14,14},{1,1},{3,3},... | collective-permute-start | bytes 786440 | tf_op jit(solution)/shard_map/ppermute | solution.py:874
  322.6 20.7 %collective-permute-start.55 = (bf16[128,1024]{1,0:T(8,128)(2,1)}, bf16[128,1024]{1,0:T(8,128)(2,1)}, u32[]{:S(2)}, u32[]{:S(2)}) collective-permute-start(bf16[128,1024]{1,0:T(8,128)(2,1)} %get-tuple-element.419), channel_id=1, source_target_pairs={{2,0},{0,2},{10,4},{8,6},{6,8},{4,10},{14,12},{12,14},{3,1},{1,3},... | collective-permute-start | bytes 786440 | tf_op jit(solution)/shard_map/ppermute | solution.py:874
  355.4 13.2 %collective-permute-start.63 = (bf16[128,1024]{1,0:T(8,128)(2,1)}, bf16[128,1024]{1,0:T(8,128)(2,1)}, u32[]{:S(2)}, u32[]{:S(2)}) collective-permute-start(bf16[128,1024]{1,0:T(8,128)(2,1)} %get-tuple-element.454), channel_id=1, source_target_pairs={{0,0},{2,2},{8,4},{10,6},{4,8},{6,10},{12,12},{14,14},{1,1},{3,3},... | collective-permute-start | bytes 786440 | tf_op jit(solution)/shard_map/ppermute | solution.py:874
  (82 other events, 605.4 us)
